TPU v7x, 128 devices: a whole 4x4x4 slice. The times are simulated.
128 devices in a mesh: patch: 128 (over z, y, x, core).
Axes of the slice: x: 4, y: 4, z: 4, core: 2. Of those that a mesh axis runs over, the one named last changes fastest.
Arguments:
- fine_state: bfloat16 [4096, 32, 512], P('patch'), may hold values from -6 to 6
- weight_in: bfloat16 [7, 32, 32], replicated, may hold values from -0.375 to 0.375
- weight_out: bfloat16 [7, 32, 32], replicated, may hold values from -0.375 to 0.375
- weight_coarse: bfloat16 [7, 32, 32], replicated, may hold values from -0.375 to 0.375
- cotangent: bfloat16 [4096, 32, 512], P('patch'), may hold values from -6 to 6
- owner_count: int32 [128], replicated, may hold values from 8 to 32, as said below
- neighbour: int32 [4096, 6], P('patch'), may hold values from 0 to 4095, as said below
- level_tag: int32 [4096, 6], P('patch'), may hold values from 0 to 1, as said below
- octant: int32 [4096], P('patch'), may hold values from -1 to 7, as said below
Outputs:
- output: bfloat16 [4096, 32, 512], P('patch')
- grad_state: bfloat16 [4096, 32, 512], P('patch')
- grad_in: float32 [7, 32, 32], replicated
- grad_out: float32 [7, 32, 32], replicated
- grad_coarse: float32 [7, 32, 32], replicated
Inputs may be any that keep to these rules, and one draw needn't show every extreme that they name: `owner_count`: an owner's live patches take its first slots; the total over all owners is a multiple of 8. Where level_tag is 0 this names a live slot whose neighbour across face f XOR 1 is this slot; it lies earlier on the Morton curve across a low face and later across a high face, on an owner at most 2 indices away (exactly 2 for some pair). The Morton positions of two face neighbours differ by exactly 3 across dimension 0, 8 across dimension 1 and 16 across dimension 2. Elsewhere it names the slot itself. `level_tag`: 1 where the face borders a coarser region or the domain's edge (the patch's own layer stands in for the neighbour's) and on every face of an empty slot. `octant`: live patches at Morton positions 8q to 8q+7 form parent q and take the octants 0 to 7 once each; -1 in empty slots.
All inputs are finite; a program needn't handle non-finite values.
Results may differ from a plain program's by a relative error of at most 0.018.
Values may be sent and summed in bfloat16 or wider, within the bound.
No kernel may reach another device: no remote copies, remote signals or barrier semaphores. Data moves between devices by JAX's collectives and lax.ppermute only.
A program may use at most 320 MiB of HBM per device.

v0:
```python
import math

import jax
import jax.numpy as jnp
from jax import lax
from jax.sharding import PartitionSpec as P

EDGE = 8
REACH = 2
QSLOTS = 4


def from_behind(block, axis, distance):
    devices = range(lax.axis_size(axis))
    route = [(i - distance, i) for i in devices if i - distance in devices]
    return lax.ppermute(block, axis, route)


def face_mask(face_id):
    cell_ids = jnp.arange(EDGE**3)
    coords = [cell_ids // (EDGE * EDGE), cell_ids // EDGE % EDGE, cell_ids % EDGE]
    return coords[face_id // 2] == (EDGE - 1 if face_id % 2 else 0)


def face_step(face_id):
    stride = EDGE ** (2 - face_id // 2)
    return stride if face_id % 2 else -stride


def face_layer(field, face_id):
    lead_dims = field.shape[:-1]
    cube = field.reshape(lead_dims + (EDGE, EDGE, EDGE))
    side = EDGE - 1 if face_id % 2 else 0
    if face_id // 2 == 0:
        sheet = cube[..., side, :, :]
    elif face_id // 2 == 1:
        sheet = cube[..., :, side, :]
    else:
        sheet = cube[..., side]
    return sheet.reshape(lead_dims + (EDGE * EDGE,))


def spread_layer(sheet, face_id):
    lead_dims = sheet.shape[:-1]
    square = sheet.reshape(lead_dims + (EDGE, EDGE))
    if face_id // 2 == 0:
        square = square[..., None, :, :]
    elif face_id // 2 == 1:
        square = square[..., :, None, :]
    else:
        square = square[..., :, :, None]
    return jnp.broadcast_to(square, lead_dims + (EDGE, EDGE, EDGE)).reshape(lead_dims + (EDGE**3,))


def all_layers(field):
    return jnp.stack([face_layer(field, face_id) for face_id in range(6)], axis=1)


def tap_field(field, ghost, face_id):
    return jnp.where(
        face_mask(face_id),
        spread_layer(ghost, face_id),
        jnp.roll(field, -face_step(face_id), axis=-1),
    )


def tap_stack(field, ghosts):
    return jnp.stack(
        [field] + [tap_field(field, ghosts[:, face_id], face_id) for face_id in range(6)], axis=1
    )


def conv_forward(field, ghosts, weight):
    return jnp.einsum(
        "fio,sfic->soc", weight, tap_stack(field, ghosts), preferred_element_type=jnp.float32
    )


def conv_backward(field, ghosts, weight, cotan, owned):
    weighed = cotan * owned[:, None, None]
    grad_field = jnp.einsum("io,soc->sic", weight[0], cotan, preferred_element_type=jnp.float32)
    sheets = []
    for face_id in range(6):
        moved = jnp.einsum(
            "io,soc->sic", weight[face_id + 1], cotan, preferred_element_type=jnp.float32
        )
        grad_field = grad_field + jnp.roll(
            jnp.where(face_mask(face_id), 0.0, moved), face_step(face_id), axis=-1
        )
        sheets.append(face_layer(moved, face_id))
    grad_weight = jnp.einsum(
        "sfic,soc->fio", tap_stack(field, ghosts), weighed, preferred_element_type=jnp.float32
    )
    return (grad_field, jnp.stack(sheets, axis=1), grad_weight)


def settle(grad_field, sheets):
    for face_id in range(6):
        grad_field = grad_field + jnp.where(
            face_mask(face_id), spread_layer(sheets[:, face_id].astype(jnp.float32), face_id), 0.0
        )
    return grad_field


def restrict_sum(field):
    lead_dims = field.shape[:-1]
    half = EDGE // 2
    groups = field.astype(jnp.float32).reshape(lead_dims + (half, 2, half, 2, half, 2))
    return groups.sum(axis=(-5, -3, -1)).reshape(lead_dims + (half**3,))


def spread_block(block):
    lead_dims = block.shape[:-1]
    half = EDGE // 2
    small = block.reshape(lead_dims + (half, 1, half, 1, half, 1))
    return jnp.broadcast_to(small, lead_dims + (half, 2, half, 2, half, 2)).reshape(
        lead_dims + (EDGE**3,)
    )


def octants_to_cells(rows):
    lead_dims = rows.shape[:-3]
    width = rows.shape[-2]
    half = EDGE // 2
    count = len(lead_dims)
    parts = rows.reshape(lead_dims + (2, 2, 2, width, half, half, half))
    order = list(range(count)) + [
        count + 3,
        count,
        count + 4,
        count + 1,
        count + 5,
        count + 2,
        count + 6,
    ]
    return parts.transpose(order).reshape(lead_dims + (width, EDGE**3))


def cells_to_octants(field):
    lead_dims = field.shape[:-2]
    width = field.shape[-2]
    half = EDGE // 2
    count = len(lead_dims)
    parts = field.reshape(lead_dims + (width, 2, half, 2, half, 2, half))
    order = list(range(count)) + [
        count + 1,
        count + 3,
        count + 5,
        count,
        count + 2,
        count + 4,
        count + 6,
    ]
    return parts.transpose(order).reshape(lead_dims + (8, width, half**3))


def silu_slope(value):
    sigma = jax.nn.sigmoid(value)
    return sigma * (1.0 + value * (1.0 - sigma))


def exchange_faces(layer_pack, neighbour, tag_high, rank_here):
    slot_count = layer_pack.shape[0]
    width = layer_pack.shape[2]
    sheet_cells = layer_pack.shape[3]
    opposite = jnp.array([1, 0, 3, 2, 5, 4], jnp.int32)[None, :]
    owner_dev = neighbour // slot_count
    local_slot = neighbour % slot_count
    distance = owner_dev - rank_here
    gathered = []
    for offset in range(-REACH, REACH + 1):
        if offset == 0:
            gathered.append(layer_pack)
        else:
            gathered.append(from_behind(layer_pack, "patch", -offset))
    rows_table = jnp.stack(gathered).reshape(-1, width, sheet_cells)
    row_index = ((distance + REACH) * slot_count + local_slot) * 6 + opposite
    picked = rows_table[row_index.reshape(-1)].reshape(layer_pack.shape)
    return jnp.where(tag_high, layer_pack, picked)


def on_device(
    fine_state,
    weight_in,
    weight_out,
    weight_coarse,
    cotangent,
    owner_count,
    neighbour,
    level_tag,
    octant,
):
    slot_count = fine_state.shape[0]
    width = fine_state.shape[1]
    half_cells = (EDGE // 2) ** 3
    rank_here = lax.axis_index("patch")
    devices = lax.axis_size("patch")
    device_rank = jnp.arange(owner_count.shape[0])
    first_pos = jnp.sum(jnp.where(device_rank < rank_here, owner_count, 0))
    live_count = jnp.sum(jnp.where(device_rank == rank_here, owner_count, 0))
    stop_pos = first_pos + live_count
    slot_ids = jnp.arange(slot_count)
    is_live = slot_ids < live_count
    position = first_pos + slot_ids
    live_mask = is_live[:, None, None]
    state_zero = jnp.where(live_mask, fine_state, jnp.zeros_like(fine_state))
    cotan_zero = jnp.where(live_mask, cotangent, jnp.zeros_like(cotangent))
    tag_high = (level_tag == 1)[:, :, None, None]
    lead_count = jnp.mod(-first_pos, 8)
    lead_child = is_live & (slot_ids < lead_count)
    lead_rows = jnp.where(lead_child, octant, 8)
    octant_ids = jnp.arange(8)
    slot_ones = jnp.ones((slot_count,), jnp.bfloat16)

    def trade(layer_pack):
        return exchange_faces(layer_pack, neighbour, tag_high, rank_here)

    first_parent = (first_pos + 7) // 8
    own_child = is_live & (slot_ids >= lead_count)
    own_rows = jnp.where(own_child, (position // 8 - first_parent) * 8 + octant, QSLOTS * 8)
    next_parent = jnp.where(stop_pos % 8 != 0, stop_pos // 8 - first_parent, QSLOTS)
    owned_parents = jnp.ones((QSLOTS,), jnp.bfloat16)

    def gather_parents(blocks):
        leading = (
            jnp.zeros((8, width, half_cells), jnp.bfloat16).at[lead_rows].set(blocks, mode="drop")
        )
        incoming = from_behind(leading, "patch", -1)
        rows_table = (
            jnp.zeros((QSLOTS * 8, width, half_cells), jnp.bfloat16)
            .at[own_rows]
            .set(blocks, mode="drop")
        )
        rows_table = rows_table.at[next_parent * 8 + octant_ids].add(incoming, mode="drop")
        return octants_to_cells(rows_table.reshape(QSLOTS, 8, width, half_cells))

    def return_children(cells_field):
        octant_rows = cells_to_octants(cells_field).reshape(QSLOTS * 8, width, half_cells)
        leaving = octant_rows[jnp.clip(next_parent, 0, QSLOTS - 1) * 8 + octant_ids]
        leaving = jnp.where(stop_pos % 8 != 0, leaving, jnp.zeros_like(leaving))
        arrived = from_behind(leaving, "patch", 1)
        rows_table = jnp.concatenate([octant_rows, arrived], axis=0)
        row_index = jnp.where(lead_child, QSLOTS * 8 + octant, jnp.where(own_child, own_rows, 0))
        return rows_table[row_index]

    ghosts_in = trade(all_layers(state_zero))
    pre_a = conv_forward(state_zero, ghosts_in, weight_in)
    hidden = jax.nn.silu(pre_a).astype(jnp.bfloat16)
    restricted = (restrict_sum(hidden) * 0.125).astype(jnp.bfloat16)
    coarse = gather_parents(restricted)
    coarse_ghosts = all_layers(coarse)
    pre_b = conv_forward(coarse, coarse_ghosts, weight_coarse)
    coarse_act = jax.nn.silu(pre_b).astype(jnp.bfloat16)
    upward = spread_block(return_children(coarse_act))
    upward = jnp.where(live_mask, upward, jnp.zeros_like(upward))
    merged = (hidden.astype(jnp.float32) + upward.astype(jnp.float32)).astype(jnp.bfloat16)
    ghosts_out = trade(all_layers(merged))
    post = conv_forward(merged, ghosts_out, weight_out)
    output = (state_zero.astype(jnp.float32) + post).astype(jnp.bfloat16)
    local_merged, ghost_out, dw_out = conv_backward(
        merged, ghosts_out, weight_out, cotan_zero, slot_ones
    )
    arrived_out = trade(ghost_out.astype(jnp.bfloat16))
    grad_merged = settle(local_merged, arrived_out).astype(jnp.bfloat16)
    grad_up = restrict_sum(grad_merged).astype(jnp.bfloat16)
    grad_act = gather_parents(grad_up)
    grad_pre_b = (grad_act.astype(jnp.float32) * silu_slope(pre_b)).astype(jnp.bfloat16)
    local_coarse, coarse_sheets, dw_coarse = conv_backward(
        coarse, coarse_ghosts, weight_coarse, grad_pre_b, owned_parents
    )
    grad_coarse_in = settle(local_coarse, coarse_sheets).astype(jnp.bfloat16)
    downward = spread_block(return_children(grad_coarse_in)).astype(jnp.float32) * 0.125
    downward = jnp.where(live_mask, downward, 0.0)
    grad_hidden = grad_merged.astype(jnp.float32) + downward
    grad_pre_a = (grad_hidden * silu_slope(pre_a)).astype(jnp.bfloat16)
    local_state, ghost_in, dw_in = conv_backward(
        state_zero, ghosts_in, weight_in, grad_pre_a, slot_ones
    )
    arrived_in = trade(ghost_in.astype(jnp.bfloat16))
    grad_state = settle(cotan_zero.astype(jnp.float32) + local_state, arrived_in).astype(
        jnp.bfloat16
    )
    summed_in, summed_out, summed_coarse = lax.psum((dw_in, dw_out, dw_coarse), "patch")
    scale = 1.0 / math.sqrt(float(devices * slot_count * EDGE**3))
    return (output, grad_state, summed_in * scale, summed_out * scale, summed_coarse * scale)


def solution(mesh):
    in_specs = (
        P("patch", None, None),
        P(),
        P(),
        P(),
        P("patch", None, None),
        P(),
        P("patch", None),
        P("patch", None),
        P("patch"),
    )
    out_specs = (P("patch", None, None), P("patch", None, None), P(), P(), P())
    return jax.shard_map(
        on_device, mesh=mesh, in_specs=in_specs, out_specs=out_specs, check_vma=False
    )
```

profile of v0, /device:TPU:0, one launch (start us, length us, event | category | flops | bytes accessed | tf_op | source)
XLA Modules:
  0.0 1143.8 jit_solution(1609294725987953873)
XLA Ops:
  16.8 6.5 fusion.161
  96.5 6.0 collective-permute-start.10
  160.7 4.9 bitcast_dynamic-update-slice_fusion.15
  176.9 4.9 bitcast_dynamic-update-slice_fusion.14
  195.6 15.3 %copy.489 = bf16[5,32,6,32,64]{4,3,2,1,0:T(8,128)(2,1)} copy(bf16[5,32,6,32,64]{3,4,1,2,0:T(8,128)(2,1)} %bitcast_dynamic-update-slice_fusion.13) | data formatting | bytes 7864320 | tf_op jit(solution)/shard_map/stack | solution.py:176
  210.9 5.3 gather_fusion
  245.9 15.3 %copy.575 = bf16[5,32,6,32,64]{4,3,2,1,0:T(8,128)(2,1)} copy(bf16[5,32,6,32,64]{3,4,1,2,0:T(8,128)(2,1)} %bitcast_dynamic-update-slice_fusion.4) | data formatting | bytes 7864320 | tf_op jit(solution)/shard_map/stack | solution.py:176
  268.1 6.8 broadcast_select_fusion.1
  331.8 5.8 fusion.49
  337.6 7.6 copy.508
  361.6 6.7 copy.577
  368.2 5.5 broadcast_in_dim.666
  373.7 6.3 copy.578
  380.0 5.1 broadcast_in_dim.667
  385.1 6.3 copy.579
  391.4 5.0 broadcast_in_dim.668
  396.4 6.2 copy.580
  407.1 6.3 copy.581
  417.8 6.2 copy.582
  424.1 11.3 fusion.34
  435.4 7.6 copy.583
  520.5 19.3 %collective-permute-start.5 = (bf16[8,32,64]{2,1,0:T(8,128)(2,1)S(1)}, bf16[8,32,64]{2,1,0:T(8,128)(2,1)S(1)}, u32[]{:S(2)}, u32[]{:S(2)}) collective-permute-start(bf16[8,32,64]{2,1,0:T(8,128)(2,1)S(1)} %broadcast_select_fusion.25), channel_id=1, source_target_pairs={{0,1},{1,2},{2,3},{3,4},{4,5},{5,6},{6,7},{7,8},{8,9},{9,10},{10,1... | collective-permute-start | bytes 98312 | tf_op jit(solution)/shard_map/ppermute | solution.py:16
  561.6 5.7 fusion.160
  579.2 5.8 collective-permute-start.6
  597.0 6.3 copy.606
  670.6 6.0 collective-permute-start.16
  676.7 5.8 convolution_bitcast_fusion.22
  725.5 4.9 bitcast_dynamic-update-slice_fusion.10
  741.7 4.9 bitcast_dynamic-update-slice_fusion.9
  760.4 15.2 %copy.550 = bf16[5,32,6,32,64]{4,3,2,1,0:T(8,128)(2,1)} copy(bf16[5,32,6,32,64]{3,4,1,2,0:T(8,128)(2,1)} %bitcast_dynamic-update-slice_fusion.8) | data formatting | bytes 7864320 | tf_op jit(solution)/shard_map/stack | solution.py:176
  775.7 5.2 gather_fusion.3
  810.5 15.3 %copy.621 = bf16[5,32,6,32,64]{4,3,2,1,0:T(8,128)(2,1)} copy(bf16[5,32,6,32,64]{3,4,1,2,0:T(8,128)(2,1)} %bitcast_dynamic-update-slice_fusion) | data formatting | bytes 7864320 | tf_op jit(solution)/shard_map/stack | solution.py:176
  832.8 6.8 broadcast_select_fusion
  844.1 4.9 copy.552
  896.4 5.8 convolution_bitcast_fusion.21
  911.0 6.3 copy.623
  917.3 5.6 broadcast_in_dim.692
  922.9 6.4 copy.624
  929.3 5.0 broadcast_in_dim.693
  934.2 6.3 copy.625
  940.5 5.1 broadcast_in_dim.694
  945.6 6.2 copy.626
  951.8 5.6 broadcast_in_dim.695
  957.4 6.3 copy.627
  968.2 6.3 copy.628
  974.6 11.4 %fusion.33 = bf16[32,32,512]{2,1,0:T(8,128)(2,1)} fusion(f32[32,32,512]{2,1,0:T(8,128)} %copy.628, f32[32,32,512]{2,1,0:T(8,128)} %copy.627, f32[32,32,512]{2,1,0:T(8,128)} %copy.626, f32[32,32,512]{2,1,0:T(8,128)} %copy.625, f32[32,32,512]{2,1,0:T(8,128)} %copy.624, f32[32,32,512]{2,1,0:T(8,128)} %copy.623, f32[32,32,511]{2,1,0:T(8,128)} %bitcast.773, ...), kind=kOutput, calls=%fused_computation.77 | convolution fusion | flops 48234496 | bytes 29335040 | tf_op jit(solution)/shard_map/io,soc->sic/dot_general | solution.py:81
  986.1 5.5 fusion.23
  991.6 140.5 %all-reduce.3.cloned.1.call-done = (f32[7,32,32]{2,1,0:T(8,128)}, f32[7,32,32]{2,1,0:T(8,128)}, f32[7,32,32]{2,1,0:T(8,128)}) async-done(((f32[7,32,32]{2,1,0:T(8,128)}, f32[7,32,32]{2,1,0:T(8,128)}, f32[7,32,32]{2,1,0:T(8,128)}), (f32[7,32,32]{2,1,0:T(8,128)}, f32[7,32,32]{2,1,0:T(8,128)}, f32[7,32,32]{2,1,0:T(8,128)})) %all-reduce.3.cloned.1.call-update) | async-done | bytes 86032 | tf_op jit(solution)/shard_map/psum | solution.py:283
  (547 shorter events, 645.6 us)
Async XLA Ops:
  7.2 1125.0 %all-reduce.3.cloned.1.call-start = ((), (), s32[]{:S(2)}) async-start(), calls=%async_computation | async-start | bytes 688128 | tf_op jit(solution)/shard_map/psum | solution.py:283
  11.7 104.6 %copy-start = (bf16[32,32,512]{2,1,0:T(8,128)(2,1)}, bf16[32,32,512]{2,1,0:T(8,128)(2,1)S(1)}, u32[]{:S(2)}) copy-start(bf16[32,32,512]{2,1,0:T(8,128)(2,1)S(1)} %get-tuple-element.27) | copy-start | bytes 3145732
  16.8 12.3 %copy-start.2 = (bf16[32,32,512]{2,1,0:T(8,128)(2,1)S(1)}, bf16[32,32,512]{2,1,0:T(8,128)(2,1)}, u32[]{:S(2)}) copy-start(bf16[32,32,512]{2,1,0:T(8,128)(2,1)} %param.17) | copy-start | bytes 3145732
  16.8 12.3 %copy-start.59 = (bf16[7,32,32]{2,1,0:T(8,128)(2,1)S(1)}, bf16[7,32,32]{2,1,0:T(8,128)(2,1)}, u32[]{:S(2)}) copy-start(bf16[7,32,32]{2,1,0:T(8,128)(2,1)} %param.15) | copy-start | bytes 43012
  23.4 303.7 %copy-start.64 = (pred[512]{0:T(512)(128)(4,1)}, pred[512]{0:T(512)(128)(4,1)S(1)}, u32[]{:S(2)}) copy-start(pred[512]{0:T(512)(128)(4,1)S(1)} %broadcast_compare_fusion.1) | copy-start | bytes 1540
  23.4 305.1 %copy-start.68 = (pred[512]{0:T(512)(128)(4,1)}, pred[512]{0:T(512)(128)(4,1)S(1)}, u32[]{:S(2)}) copy-start(pred[512]{0:T(512)(128)(4,1)S(1)} %fusion.148) | copy-start | bytes 1540
  23.4 306.9 %copy-start.72 = (pred[512]{0:T(512)(128)(4,1)}, pred[512]{0:T(512)(128)(4,1)S(1)}, u32[]{:S(2)}) copy-start(pred[512]{0:T(512)(128)(4,1)S(1)} %fusion.147) | copy-start | bytes 1540
  64.7 11.4 copy-start.17
  68.2 8.8 copy-start.29
  82.4 51.0 %collective-permute-start = (bf16[32,6,32,64]{3,2,1,0:T(8,128)(2,1)}, bf16[32,6,32,64]{3,2,1,0:T(8,128)(2,1)}, u32[]{:S(2)}, u32[]{:S(2)}) collective-permute-start(bf16[32,6,32,64]{3,2,1,0:T(8,128)(2,1)} %copy.481), channel_id=1, source_target_pairs={{0,2},{1,3},{2,4},{3,5},{4,6},{5,7},{6,8},{7,9},{8,10},{9,11},{10,... | collective-permute-start | bytes 2359304 | tf_op jit(solution)/shard_map/ppermute | solution.py:16
  87.1 54.1 %collective-permute-start.1 = (bf16[32,6,32,64]{3,2,1,0:T(8,128)(2,1)}, bf16[32,6,32,64]{3,2,1,0:T(8,128)(2,1)}, u32[]{:S(2)}, u32[]{:S(2)}) collective-permute-start(bf16[32,6,32,64]{3,2,1,0:T(8,128)(2,1)} %copy.481), channel_id=1, source_target_pairs={{0,1},{1,2},{2,3},{3,4},{4,5},{5,6},{6,7},{7,8},{8,9},{9,10},{10,1... | collective-permute-start | bytes 2359304 | tf_op jit(solution)/shard_map/ppermute | solution.py:16
  89.6 79.0 %collective-permute-start.2 = (bf16[32,6,32,64]{3,2,1,0:T(8,128)(2,1)}, bf16[32,6,32,64]{3,2,1,0:T(8,128)(2,1)}, u32[]{:S(2)}, u32[]{:S(2)}) collective-permute-start(bf16[32,6,32,64]{3,2,1,0:T(8,128)(2,1)} %copy.481), channel_id=1, source_target_pairs={{1,0},{2,1},{3,2},{4,3},{5,4},{6,5},{7,6},{8,7},{9,8},{10,9},{11,1... | collective-permute-start | bytes 2359304 | tf_op jit(solution)/shard_map/ppermute | solution.py:16
  90.9 81.8 %collective-permute-start.3 = (bf16[32,6,32,64]{3,2,1,0:T(8,128)(2,1)}, bf16[32,6,32,64]{3,2,1,0:T(8,128)(2,1)}, u32[]{:S(2)}, u32[]{:S(2)}) collective-permute-start(bf16[32,6,32,64]{3,2,1,0:T(8,128)(2,1)} %copy.481), channel_id=1, source_target_pairs={{2,0},{3,1},{4,2},{5,3},{6,4},{7,5},{8,6},{9,7},{10,8},{11,9},{12,... | collective-permute-start | bytes 2359304 | tf_op jit(solution)/shard_map/ppermute | solution.py:16
  96.5 58.2 %collective-permute-start.10 = (bf16[32,6,32,64]{3,2,1,0:T(8,128)(2,1)}, bf16[32,6,32,64]{3,2,1,0:T(8,128)(2,1)}, u32[]{:S(2)}, u32[]{:S(2)}) collective-permute-start(bf16[32,6,32,64]{3,2,1,0:T(8,128)(2,1)} %copy.567), channel_id=1, source_target_pairs={{0,2},{1,3},{2,4},{3,5},{4,6},{5,7},{6,8},{7,9},{8,10},{9,11},{10,... | collective-permute-start | bytes 2359304 | tf_op jit(solution)/shard_map/ppermute | solution.py:16
  110.9 157.2 %copy-start.77 = (pred[32,6]{0,1:T(8,128)(4,1)}, pred[32,6]{0,1:T(8,128)(4,1)S(1)}, u32[]{:S(2)}) copy-start(pred[32,6]{0,1:T(8,128)(4,1)S(1)} %broadcast_compare_fusion) | copy-start | bytes 580
  113.9 147.3 %copy-start.75 = (s32[1024]{0:T(1024)}, s32[1024]{0:T(1024)S(1)}, u32[]{:S(2)}) copy-start(s32[1024]{0:T(1024)S(1)} %get-tuple-element.142) | copy-start | bytes 12292
  133.4 51.4 %collective-permute-start.11 = (bf16[32,6,32,64]{3,2,1,0:T(8,128)(2,1)}, bf16[32,6,32,64]{3,2,1,0:T(8,128)(2,1)}, u32[]{:S(2)}, u32[]{:S(2)}) collective-permute-start(bf16[32,6,32,64]{3,2,1,0:T(8,128)(2,1)} %copy.567), channel_id=1, source_target_pairs={{0,1},{1,2},{2,3},{3,4},{4,5},{5,6},{6,7},{7,8},{8,9},{9,10},{10,1... | collective-permute-start | bytes 2359304 | tf_op jit(solution)/shard_map/ppermute | solution.py:16
  141.2 84.9 %collective-permute-start.12 = (bf16[32,6,32,64]{3,2,1,0:T(8,128)(2,1)}, bf16[32,6,32,64]{3,2,1,0:T(8,128)(2,1)}, u32[]{:S(2)}, u32[]{:S(2)}) collective-permute-start(bf16[32,6,32,64]{3,2,1,0:T(8,128)(2,1)} %copy.567), channel_id=1, source_target_pairs={{1,0},{2,1},{3,2},{4,3},{5,4},{6,5},{7,6},{8,7},{9,8},{10,9},{11,1... | collective-permute-start | bytes 2359304 | tf_op jit(solution)/shard_map/ppermute | solution.py:16
  154.7 82.2 %collective-permute-start.13 = (bf16[32,6,32,64]{3,2,1,0:T(8,128)(2,1)}, bf16[32,6,32,64]{3,2,1,0:T(8,128)(2,1)}, u32[]{:S(2)}, u32[]{:S(2)}) collective-permute-start(bf16[32,6,32,64]{3,2,1,0:T(8,128)(2,1)} %copy.567), channel_id=1, source_target_pairs={{2,0},{3,1},{4,2},{5,3},{6,4},{7,5},{8,6},{9,7},{10,8},{11,9},{12,... | collective-permute-start | bytes 2359304 | tf_op jit(solution)/shard_map/ppermute | solution.py:16
  352.1 102.4 %collective-permute-start.4 = (bf16[8,32,64]{2,1,0:T(8,128)(2,1)S(1)}, bf16[8,32,64]{2,1,0:T(8,128)(2,1)}, u32[]{:S(2)}, u32[]{:S(2)}) collective-permute-start(bf16[8,32,64]{2,1,0:T(8,128)(2,1)S(1)} %scatter_fusion.1), channel_id=1, source_target_pairs={{1,0},{2,1},{3,2},{4,3},{5,4},{6,5},{7,6},{8,7},{9,8},{10,9},{11,1... | collective-permute-start | bytes 98312 | tf_op jit(solution)/shard_map/ppermute | solution.py:16
  435.4 7.6 copy-start.4
  443.0 8.1 copy-start.87
  447.5 7.0 copy-start.85
  449.7 32.8 %collective-permute-start.14 = (bf16[8,32,64]{2,1,0:T(8,128)(2,1)S(1)}, bf16[8,32,64]{2,1,0:T(8,128)(2,1)}, u32[]{:S(2)}, u32[]{:S(2)}) collective-permute-start(bf16[8,32,64]{2,1,0:T(8,128)(2,1)S(1)} %scatter_fusion.4), channel_id=1, source_target_pairs={{1,0},{2,1},{3,2},{4,3},{5,4},{6,5},{7,6},{8,7},{9,8},{10,9},{11,1... | collective-permute-start | bytes 98312 | tf_op jit(solution)/shard_map/ppermute | solution.py:16
  469.1 9.1 copy-start.58
  471.0 8.3 copy-start.84
  473.4 7.4 copy-start.57
  474.3 7.5 copy-start.83
  474.3 8.2 copy-start.86
  484.7 8.5 copy-start.61
  486.0 9.7 copy-start.66
  488.1 8.5 copy-start.70
  489.2 7.6 copy-start.73
  520.5 24.1 %collective-permute-start.5 = (bf16[8,32,64]{2,1,0:T(8,128)(2,1)S(1)}, bf16[8,32,64]{2,1,0:T(8,128)(2,1)S(1)}, u32[]{:S(2)}, u32[]{:S(2)}) collective-permute-start(bf16[8,32,64]{2,1,0:T(8,128)(2,1)S(1)} %broadcast_select_fusion.25), channel_id=1, source_target_pairs={{0,1},{1,2},{2,3},{3,4},{4,5},{5,6},{6,7},{7,8},{8,9},{9,10},{10,1... | collective-permute-start | bytes 98312 | tf_op jit(solution)/shard_map/ppermute | solution.py:16
  540.8 50.1 %collective-permute-start.15 = (bf16[8,32,64]{2,1,0:T(8,128)(2,1)S(1)}, bf16[8,32,64]{2,1,0:T(8,128)(2,1)S(1)}, u32[]{:S(2)}, u32[]{:S(2)}) collective-permute-start(bf16[8,32,64]{2,1,0:T(8,128)(2,1)S(1)} %broadcast_select_fusion.24), channel_id=1, source_target_pairs={{0,1},{1,2},{2,3},{3,4},{4,5},{5,6},{6,7},{7,8},{8,9},{9,10},{10,1... | collective-permute-start | bytes 98312 | tf_op jit(solution)/shard_map/ppermute | solution.py:16
  579.2 118.8 %collective-permute-start.6 = (bf16[32,6,32,64]{3,2,1,0:T(8,128)(2,1)}, bf16[32,6,32,64]{3,2,1,0:T(8,128)(2,1)}, u32[]{:S(2)}, u32[]{:S(2)}) collective-permute-start(bf16[32,6,32,64]{3,2,1,0:T(8,128)(2,1)} %copy.542), channel_id=1, source_target_pairs={{0,2},{1,3},{2,4},{3,5},{4,6},{5,7},{6,8},{7,9},{8,10},{9,11},{10,... | collective-permute-start | bytes 2359304 | tf_op jit(solution)/shard_map/ppermute | solution.py:16
  585.0 121.7 %collective-permute-start.7 = (bf16[32,6,32,64]{3,2,1,0:T(8,128)(2,1)}, bf16[32,6,32,64]{3,2,1,0:T(8,128)(2,1)}, u32[]{:S(2)}, u32[]{:S(2)}) collective-permute-start(bf16[32,6,32,64]{3,2,1,0:T(8,128)(2,1)} %copy.542), channel_id=1, source_target_pairs={{0,1},{1,2},{2,3},{3,4},{4,5},{5,6},{6,7},{7,8},{8,9},{9,10},{10,1... | collective-permute-start | bytes 2359304 | tf_op jit(solution)/shard_map/ppermute | solution.py:16
  588.3 145.1 %collective-permute-start.8 = (bf16[32,6,32,64]{3,2,1,0:T(8,128)(2,1)}, bf16[32,6,32,64]{3,2,1,0:T(8,128)(2,1)}, u32[]{:S(2)}, u32[]{:S(2)}) collective-permute-start(bf16[32,6,32,64]{3,2,1,0:T(8,128)(2,1)} %copy.542), channel_id=1, source_target_pairs={{1,0},{2,1},{3,2},{4,3},{5,4},{6,5},{7,6},{8,7},{9,8},{10,9},{11,1... | collective-permute-start | bytes 2359304 | tf_op jit(solution)/shard_map/ppermute | solution.py:16
  589.6 147.9 %collective-permute-start.9 = (bf16[32,6,32,64]{3,2,1,0:T(8,128)(2,1)}, bf16[32,6,32,64]{3,2,1,0:T(8,128)(2,1)}, u32[]{:S(2)}, u32[]{:S(2)}) collective-permute-start(bf16[32,6,32,64]{3,2,1,0:T(8,128)(2,1)} %copy.542), channel_id=1, source_target_pairs={{2,0},{3,1},{4,2},{5,3},{6,4},{7,5},{8,6},{9,7},{10,8},{11,9},{12,... | collective-permute-start | bytes 2359304 | tf_op jit(solution)/shard_map/ppermute | solution.py:16
  658.5 6.9 copy-start.19
  670.6 12.7 %copy-start.15 = (f32[32,32,512]{2,1,0:T(8,128)S(1)}, f32[32,32,512]{2,1,0:T(8,128)}, u32[]{:S(2)}) copy-start(f32[32,32,512]{2,1,0:T(8,128)} %get-tuple-element.135) | copy-start | bytes 6291460
  670.6 49.4 %collective-permute-start.16 = (bf16[32,6,32,64]{3,2,1,0:T(8,128)(2,1)}, bf16[32,6,32,64]{3,2,1,0:T(8,128)(2,1)}, u32[]{:S(2)}, u32[]{:S(2)}) collective-permute-start(bf16[32,6,32,64]{3,2,1,0:T(8,128)(2,1)} %copy.613), channel_id=1, source_target_pairs={{0,2},{1,3},{2,4},{3,5},{4,6},{5,7},{6,8},{7,9},{8,10},{9,11},{10,... | collective-permute-start | bytes 2359304 | tf_op jit(solution)/shard_map/ppermute | solution.py:16
  698.0 51.6 %collective-permute-start.17 = (bf16[32,6,32,64]{3,2,1,0:T(8,128)(2,1)}, bf16[32,6,32,64]{3,2,1,0:T(8,128)(2,1)}, u32[]{:S(2)}, u32[]{:S(2)}) collective-permute-start(bf16[32,6,32,64]{3,2,1,0:T(8,128)(2,1)} %copy.613), channel_id=1, source_target_pairs={{0,1},{1,2},{2,3},{3,4},{4,5},{5,6},{6,7},{7,8},{8,9},{9,10},{10,1... | collective-permute-start | bytes 2359304 | tf_op jit(solution)/shard_map/ppermute | solution.py:16
  706.6 84.1 %collective-permute-start.18 = (bf16[32,6,32,64]{3,2,1,0:T(8,128)(2,1)}, bf16[32,6,32,64]{3,2,1,0:T(8,128)(2,1)}, u32[]{:S(2)}, u32[]{:S(2)}) collective-permute-start(bf16[32,6,32,64]{3,2,1,0:T(8,128)(2,1)} %copy.613), channel_id=1, source_target_pairs={{1,0},{2,1},{3,2},{4,3},{5,4},{6,5},{7,6},{8,7},{9,8},{10,9},{11,1... | collective-permute-start | bytes 2359304 | tf_op jit(solution)/shard_map/ppermute | solution.py:16
  720.0 81.6 %collective-permute-start.19 = (bf16[32,6,32,64]{3,2,1,0:T(8,128)(2,1)}, bf16[32,6,32,64]{3,2,1,0:T(8,128)(2,1)}, u32[]{:S(2)}, u32[]{:S(2)}) collective-permute-start(bf16[32,6,32,64]{3,2,1,0:T(8,128)(2,1)} %copy.613), channel_id=1, source_target_pairs={{2,0},{3,1},{4,2},{5,3},{6,4},{7,5},{8,6},{9,7},{10,8},{11,9},{12,... | collective-permute-start | bytes 2359304 | tf_op jit(solution)/shard_map/ppermute | solution.py:16
  760.4 15.2 %copy-start.76 = (s32[1024]{0:T(1024)S(1)}, s32[1024]{0:T(1024)}, u32[]{:S(2)}) copy-start(s32[1024]{0:T(1024)} %copy-done.75) | copy-start | bytes 12292
  974.6 11.5 %copy-start.1 = (bf16[32,32,512]{2,1,0:T(8,128)(2,1)S(1)}, bf16[32,32,512]{2,1,0:T(8,128)(2,1)}, u32[]{:S(2)}) copy-start(bf16[32,32,512]{2,1,0:T(8,128)(2,1)} %copy-done) | copy-start | bytes 3145732
  974.6 11.5 %copy-start.60 = (bf16[7,32,32]{2,1,0:T(8,128)(2,1)S(1)}, bf16[7,32,32]{2,1,0:T(8,128)(2,1)}, u32[]{:S(2)}) copy-start(bf16[7,32,32]{2,1,0:T(8,128)(2,1)} %param.15) | copy-start | bytes 43012
  (63 other events, 268.0 us)
Sparse Core Ops, SparseCore 0:
  974.7 157.4 all-reduce.2
where the time goes:
time: 1160 us; the launch traced here: 1140 us
  local copies, waits for them, and re-layouts  750 us (65%)
  waiting for transfers between devices  141 us (12%)
  other arithmetic  84 us (7%)
  matrix products  77.3 us (7%)
  starting transfers between devices  72.9 us (6%)
  between operations  19.1 us (2%)
    psum x1, waiting for transfers between devices, on_device(): lax.psum((dw_in, dw_out, dw_coarse), 'patch')  141 us
    reshape x36, local copies, waits for them, and re-layouts, spread_layer(): jnp.broadcast_to(square, lead_dims + (EDGE, EDGE, EDGE))  138 us
    unnamed x239, local copies, waits for them, and re-layouts  127 us
    broadcast_in_dim x44, local copies, waits for them, and re-layouts, spread_layer(): jnp.broadcast_to(square, lead_dims + (EDGE, EDGE, EDGE))  102 us
    another operation x8, local copies, waits for them, and re-layouts, exchange_faces(): rows_table = jnp.stack(gathered).reshape(-1, width, sheet_cells)  76.5 us
    ppermute x20, starting transfers between devices, from_behind(): return lax.ppermute(block, axis, route)  72.8 us
    ppermute x16, local copies, waits for them, and re-layouts, from_behind(): return lax.ppermute(block, axis, route)  67.7 us
    transpose x18, local copies, waits for them, and re-layouts, conv_backward(): jnp.einsum('io,soc->sic', weight[face_id + 1], cotan, preferred_element_t...  47.4 us
  transfers between devices with their start and end apart: 21, of which 2 were waited for; matrix products, arithmetic and copies ran while one was open for 44% of the time, Pallas kernels for 0%

commit v1 on v0

v1 whole, which is shorter than its diff:
```python
import functools
import math

import numpy as np
import jax
import jax.numpy as jnp
from jax import lax
from jax.experimental import pallas as pl
from jax.experimental.pallas import tpu as pltpu
from jax.sharding import PartitionSpec as P

BF = jnp.bfloat16
F32 = jnp.float32
EDGE = 8
CELLS = 512
SLOTS = 32
C = 32
PB = 8
STEPS = SLOTS // PB
NPAR = 5
STRIDES = (64, 8, 1)
MORTON = (3, 8, 16)
ROW0 = (24, 16, 0)
NEAR = 27
FAR = 8
BASE_A = 6 * SLOTS
BASE_B = BASE_A + NEAR
BASE_C = BASE_B + NEAR + FAR
ROWS = BASE_C + FAR
VMEM_LIMIT = 56 * 1024 * 1024


def cell_coords():
    ids = np.arange(CELLS)
    return [ids // 64, ids // 8 % 8, ids % 8]


def face_cells(face):
    coords = cell_coords()
    keep = coords[face // 2] == (EDGE - 1 if face % 2 else 0)
    return np.nonzero(keep)[0]


def constants():
    sel = np.zeros((3, 2, CELLS, 256), np.float32)
    spread = np.zeros((6, 128, 2 * CELLS), np.float32)
    for face in range(6):
        cells = face_cells(face)
        for j, cell in enumerate(cells):
            for kind in range(2):
                sel[face // 2, kind, cell, (face % 2) * 128 + kind * 64 + j] = 1
                spread[face, kind * 64 + j, kind * CELLS + cell] = 1
    c0, c1, c2 = cell_coords()
    group = (c0 // 2) * 16 + (c1 // 2) * 4 + c2 // 2
    rest = np.zeros((2, CELLS, 128), np.float32)
    up = np.zeros((128, 2 * CELLS), np.float32)
    for cell in range(CELLS):
        rest[0, cell, group[cell]] = 0.125
        rest[1, cell, 64 + group[cell]] = 1
        up[group[cell], cell] = 1
        up[64 + group[cell], CELLS + cell] = 1
    place = np.zeros((128, 2 * CELLS), np.float32)
    for a in range(64):
        cell = (a // 16) * 64 + (a // 4 % 4) * 8 + a % 4
        place[a, cell] = 1
        place[64 + a, CELLS + cell] = 1
    as_bf = lambda item: np.asarray(item, jnp.bfloat16)
    return (
        as_bf(sel.reshape(6, CELLS, 256)),
        as_bf(spread),
        as_bf(rest),
        as_bf(up),
        as_bf(place),
        as_bf(place.T),
    )


def dot(a, b):
    return jnp.dot(a, b, preferred_element_type=F32)


def dot_nt(a, b):
    return lax.dot_general(a, b, (((1,), (1,)), ((), ())), preferred_element_type=F32)


def inside(face, rows):
    lane = lax.broadcasted_iota(jnp.int32, (rows, CELLS), 1)
    stride = STRIDES[face // 2]
    coord = (lane // stride) % EDGE
    edge = EDGE - 1 if face % 2 else 0
    return jnp.where(coord == edge, 0.0, 1.0).astype(BF)


def toward(field, face):
    stride = STRIDES[face // 2]
    shift = CELLS - stride if face % 2 else stride
    return pltpu.roll(field, shift, 1)


def send_rows(side, count, v_ref, y_ref, sel_ref, v_rows, y_rows, out_ref):
    for dim in (2, 1, 0):
        depth = MORTON[dim]
        face = 2 * dim + side
        for i in range(depth):
            slot = jnp.clip(count - depth + i, 0, SLOTS - 1) if side else i
            v_rows[i] = v_ref[slot]
            y_rows[i] = y_ref[slot]
        cols = slice((face % 2) * 128, (face % 2) * 128 + 128)
        layers = dot(v_rows[:depth].reshape(depth * C, CELLS), sel_ref[2 * dim, :, cols])
        layers += dot(y_rows[:depth].reshape(depth * C, CELLS), sel_ref[2 * dim + 1, :, cols])
        layers = layers.astype(BF).reshape(depth, C, 128)
        if dim == 2 and side:
            out_ref[0:8] = layers[8:16]
            out_ref[8:16] = layers[0:8]
        else:
            out_ref[ROW0[dim] : ROW0[dim] + depth] = layers


def send_both(scal, v_ref, y_ref, sel_ref, v_rows, y_rows, inner_ref, outer_ref):
    count = scal[0]
    odd = scal[1]

    @pl.when(odd == 0)
    def _():
        send_rows(1, count, v_ref, y_ref, sel_ref, v_rows, y_rows, inner_ref)
        send_rows(0, count, v_ref, y_ref, sel_ref, v_rows, y_rows, outer_ref)

    @pl.when(odd == 1)
    def _():
        send_rows(0, count, v_ref, y_ref, sel_ref, v_rows, y_rows, inner_ref)
        send_rows(1, count, v_ref, y_ref, sel_ref, v_rows, y_rows, outer_ref)


def layers_kernel(scal, v_ref, y_ref, sel_ref, inner_ref, outer_ref, v_rows, y_rows):
    send_both(scal, v_ref, y_ref, sel_ref, v_rows, y_rows, inner_ref, outer_ref)


def fill_table(v_ref, y_ref, sel_ref, a_ref, b_ref, c_ref, table):
    for dim in range(3):
        layers = dot(v_ref[...].reshape(SLOTS * C, CELLS), sel_ref[2 * dim])
        layers += dot(y_ref[...].reshape(SLOTS * C, CELLS), sel_ref[2 * dim + 1])
        layers = layers.astype(BF)
        for high in range(2):
            face = 2 * dim + high
            table[face * SLOTS : (face + 1) * SLOTS] = layers[
                :, high * 128 : high * 128 + 128
            ].reshape(SLOTS, C, 128)
    table[BASE_A:BASE_B] = a_ref[...]
    table[BASE_B:BASE_C] = b_ref[...]
    table[BASE_C:ROWS] = c_ref[...]


def block_taps(start, idx, tag, v_ref, y_ref, spread_ref, table, picked, ta, tb):
    masks = [inside(face, C) for face in range(6)]
    for p in range(PB):
        ta[p, 0:C] = v_ref[start + p]
        tb[p, 0:C] = y_ref[start + p]
    for dim in range(3):
        spreads = []
        for face in (2 * dim, 2 * dim + 1):
            for p in range(PB):
                picked[p] = table[idx[(start + p) * 6 + face]]
            spreads.append(dot(picked[...].reshape(PB * C, 128), spread_ref[face]))
        low, high = 2 * dim, 2 * dim + 1
        for p in range(PB):
            field = v_ref[start + p]
            other = y_ref[start + p]
            rows = slice(p * C, (p + 1) * C)
            t_low = tag[(start + p) * 6 + low].astype(F32)
            t_high = tag[(start + p) * 6 + high].astype(F32)
            z_low = spreads[0][rows, CELLS:]
            z_high = spreads[1][rows, CELLS:]
            for k, face in enumerate((low, high)):
                ta[p, C * (face + 1) : C * (face + 2)] = (
                    toward(field, face) * masks[face] + spreads[k][rows, :CELLS].astype(BF)
                )
            tb[p, C * (high + 1) : C * (high + 2)] = toward(other, low) * masks[low] + (
                z_low * (1.0 - t_low) + z_high * t_high
            ).astype(BF)
            tb[p, C * (low + 1) : C * (low + 2)] = toward(other, high) * masks[high] + (
                z_high * (1.0 - t_high) + z_low * t_low
            ).astype(BF)


def fine_kernel(
    scal, idx, tag, dst, lead_dst, trail_dst,
    x_ref, z_ref, a_ref, b_ref, c_ref, wa_ref, wb_ref, sel_ref, spread_ref, rest_ref,
    ta_ref, tb_ref, hidden_ref, slope_ref, gm_ref, par_ref, inner_ref, outer_ref,
    xs, zs, table, picked, par, lead, trail,
):
    step = pl.program_id(0)

    @pl.when(step == 0)
    def _():
        for p in range(SLOTS):
            live = (p < scal[0]).astype(F32)
            xs[p] = (x_ref[p].astype(F32) * live).astype(BF)
            zs[p] = (z_ref[p].astype(F32) * live).astype(BF)
        fill_table(xs, zs, sel_ref, a_ref, b_ref, c_ref, table)
        par[...] = jnp.zeros_like(par)
        lead[...] = jnp.zeros_like(lead)
        trail[...] = jnp.zeros_like(trail)

    start = step * PB
    block_taps(start, idx, tag, xs, zs, spread_ref, table, picked, ta_ref, tb_ref)
    for p in range(PB):
        pre = dot(wa_ref[...], ta_ref[p])
        sigma = 1.0 / (1.0 + jnp.exp(-pre))
        hidden_ref[p] = (pre * sigma).astype(BF)
        slope_ref[p] = (sigma * (1.0 + pre * (1.0 - sigma))).astype(BF)
        gm_ref[p] = dot(wb_ref[...], tb_ref[p]).astype(BF)
    child = dot(hidden_ref[...].reshape(PB * C, CELLS), rest_ref[0])
    child += dot(gm_ref[...].reshape(PB * C, CELLS), rest_ref[1])
    child = child.astype(BF)
    for p in range(PB):
        row = child[p * C : (p + 1) * C]
        par[dst[start + p]] = row
        lead[lead_dst[start + p]] = row
        trail[trail_dst[start + p]] = row

    @pl.when(step == STEPS - 1)
    def _():
        par_ref[...] = par[: NPAR * 8]

        @pl.when(scal[1] == 0)
        def _():
            inner_ref[...] = trail[:8]
            outer_ref[...] = lead[:8]

        @pl.when(scal[1] == 1)
        def _():
            inner_ref[...] = lead[:8]
            outer_ref[...] = trail[:8]


def coarse_level(scal, par_ref, inner_ref, outer_ref, wa, wb, place_ref, unplace_ref, par, taps, up_rows, dw_ref):
    par[: NPAR * 8] = par_ref[...]
    par[NPAR * 8 :] = jnp.zeros((8, C, 128), BF)
    last = scal[2] * 8
    first_in = 1 - scal[1]

    def merge(start, got_ref):
        for o in range(8):
            par[start + o] = par[start + o] + got_ref[o]

    @pl.when(scal[1] == 0)
    def _():
        merge(0, outer_ref)
        merge(last, inner_ref)

    @pl.when(scal[1] == 1)
    def _():
        merge(0, inner_ref)
        merge(last, outer_ref)

    masks = [inside(face, C) for face in range(6)]
    shifts = [(o // 4) * 256 + (o // 2 % 2) * 32 + (o % 2) * 4 for o in range(8)]
    dw = jnp.zeros((C, 7 * C), F32)
    for q in range(NPAR):
        field = jnp.zeros((C, CELLS), F32)
        cotan = jnp.zeros((C, CELLS), F32)
        for o in range(8):
            put = dot(par[q * 8 + o], place_ref[...])
            one, two = put[:, :CELLS], put[:, CELLS:]
            if shifts[o]:
                one = pltpu.roll(one, shifts[o], 1)
                two = pltpu.roll(two, shifts[o], 1)
            field += one
            cotan += two
        field = field.astype(BF)
        taps[0:C] = field
        for face in range(6):
            taps[C * (face + 1) : C * (face + 2)] = toward(field, face) * masks[face] + field * (
                1 - masks[face]
            )
        pre = dot(wa, taps[...])
        sigma = 1.0 / (1.0 + jnp.exp(-pre))
        act = (pre * sigma).astype(BF)
        grad = (cotan * (sigma * (1.0 + pre * (1.0 - sigma)))).astype(BF)
        part = dot_nt(grad, taps[...])
        if q == 0:
            part = part * scal[3].astype(F32)
        dw += part
        taps[0:C] = grad
        for face in range(6):
            back = face ^ 1
            taps[C * (face + 1) : C * (face + 2)] = toward(grad, back) * masks[back] + grad * (
                1 - masks[face]
            )
        down = dot(wb, taps[...]).astype(BF)
        for o in range(8):
            one, two = act, down
            if shifts[o]:
                one = pltpu.roll(act, CELLS - shifts[o], 1)
                two = pltpu.roll(down, CELLS - shifts[o], 1)
            rows = dot(one, unplace_ref[:CELLS]) + dot(two, unplace_ref[CELLS:])
            up_rows[q * 8 + o] = rows.astype(BF)
    up_rows[NPAR * 8] = jnp.zeros((C, 128), BF)
    dw_ref[2 * C : 3 * C, 0 : 7 * C] = dw


def merge_kernel(
    scal, urow,
    ta_ref, tb_ref, hidden_ref, slope_ref, gm_ref, par_ref, pin_ref, pout_ref,
    wa_ref, wb_ref, place_ref, unplace_ref, up_ref, sel_ref,
    merged_ref, gpa_ref, dw_ref, inner_ref, outer_ref,
    par, taps, up_rows, picked, v_rows, y_rows,
):
    step = pl.program_id(0)

    @pl.when(step == 0)
    def _():
        dw_ref[...] = jnp.zeros_like(dw_ref)
        coarse_level(
            scal, par_ref, pin_ref, pout_ref, wa_ref[...], wb_ref[...],
            place_ref, unplace_ref, par, taps, up_rows, dw_ref,
        )

    start = step * PB
    for p in range(PB):
        picked[p] = up_rows[urow[start + p]]
    spread = dot(picked[...].reshape(PB * C, 128), up_ref[...])
    dw_in = jnp.zeros((C, 7 * C), F32)
    dw_out = jnp.zeros((C, 7 * C), F32)
    for p in range(PB):
        rows = slice(p * C, (p + 1) * C)
        merged = (hidden_ref[p].astype(F32) + spread[rows, :CELLS]).astype(BF)
        grad = gm_ref[p].astype(F32) + spread[rows, CELLS:] * 0.125
        gpa = (grad * slope_ref[p].astype(F32)).astype(BF)
        merged_ref[start + p] = merged
        gpa_ref[start + p] = gpa
        dw_in += dot_nt(gpa, ta_ref[p])
        dw_out += dot_nt(merged, tb_ref[p])
    dw_ref[0:C, 0 : 7 * C] += dw_in
    dw_ref[C : 2 * C, 0 : 7 * C] += dw_out

    @pl.when(step == STEPS - 1)
    def _():
        send_both(scal, merged_ref, gpa_ref, sel_ref, v_rows, y_rows, inner_ref, outer_ref)


def final_kernel(
    scal, idx, tag,
    v_ref, y_ref, x_ref, z_ref, a_ref, b_ref, c_ref, wa_ref, wb_ref, sel_ref, spread_ref,
    out_ref, gs_ref,
    table, picked, ta, tb,
):
    step = pl.program_id(0)

    @pl.when(step == 0)
    def _():
        fill_table(v_ref, y_ref, sel_ref, a_ref, b_ref, c_ref, table)

    start = step * PB
    block_taps(start, idx, tag, v_ref, y_ref, spread_ref, table, picked, ta, tb)
    for p in range(PB):
        live = (start + p < scal[0]).astype(F32)
        out_ref[p] = (x_ref[p].astype(F32) * live + dot(wa_ref[...], ta[p])).astype(BF)
        gs_ref[p] = (z_ref[p].astype(F32) * live + dot(wb_ref[...], tb[p])).astype(BF)


SMEM = functools.partial(pl.BlockSpec, memory_space=pltpu.SMEM)


def whole(shape):
    zeros = (0,) * len(shape)
    return pl.BlockSpec(shape, lambda i: zeros)


def blocked(shape):
    rest = (0,) * (len(shape) - 1)
    return pl.BlockSpec((PB,) + tuple(shape[1:]), lambda i: (i,) + rest)


def params():
    return pltpu.CompilerParams(
        dimension_semantics=("arbitrary",), vmem_limit_bytes=VMEM_LIMIT
    )


def shape_of(shape, dtype=BF):
    return jax.ShapeDtypeStruct(shape, dtype)


def pairs(kind, devices):
    if kind == "inner":
        links = [(2 * c, 2 * c + 1) for c in range(devices // 2)]
    else:
        links = [(2 * c + 1, 2 * c + 2) for c in range(devices // 2 - 1)]
    return links + [(b, a) for a, b in links]


def trade(block, kind):
    return lax.ppermute(block, "patch", pairs(kind, lax.axis_size("patch")))


def relay(inner, outer):
    got_a = trade(inner, "inner")
    got_b = trade(jnp.concatenate([outer, got_a[:FAR]], axis=0), "outer")
    got_c = trade(got_b[:FAR], "inner")
    return got_a, got_b, got_c


def sum_over_devices(block):
    devices = lax.axis_size("patch")
    for mask in (1, 2, 6, 8, 24, 32, 96):
        block = block + lax.ppermute(block, "patch", [(i, i ^ mask) for i in range(devices)])
    return block


def on_device(
    fine_state, weight_in, weight_out, weight_coarse, cotangent,
    owner_count, neighbour, level_tag, octant,
):
    rank = lax.axis_index("patch")
    devices = lax.axis_size("patch")
    sel, spread, rest, up, place, unplace = [jnp.asarray(item) for item in constants()]

    odd = rank % 2
    ranks = jnp.arange(devices)
    first = jnp.sum(jnp.where(ranks < rank, owner_count, 0))
    count = jnp.sum(jnp.where(ranks == rank, owner_count, 0))
    count_1 = jnp.sum(jnp.where(ranks == rank - 1, owner_count, 0))
    count_2 = jnp.sum(jnp.where(ranks == rank - 2, owner_count, 0))
    stop = first + count
    last = jnp.where(stop % 8 != 0, stop // 8 - first // 8, NPAR)
    scal = jnp.stack([count, odd, last, jnp.where(first % 8 == 0, 1, 0)]).astype(jnp.int32)

    slots = jnp.arange(SLOTS)
    live = slots < count
    dst = jnp.where(live, (first % 8 + slots) // 8 * 8 + octant, NPAR * 8)
    lead = live & (slots < (-first) % 8)
    trail = live & (slots >= count - stop % 8)
    lead_dst = jnp.where(lead, octant, 8)
    trail_dst = jnp.where(trail, octant, 8)

    face = jnp.arange(6)[None, :]
    dim = face // 2
    depth = jnp.where(dim == 0, MORTON[0], jnp.where(dim == 1, MORTON[1], MORTON[2]))
    row0 = jnp.where(dim == 0, ROW0[0], jnp.where(dim == 1, ROW0[1], ROW0[2]))
    away = neighbour // SLOTS - rank
    slot = neighbour % SLOTS
    opposite = face + 1 - 2 * (face % 2)
    here = opposite * SLOTS + slot
    from_left = slot - (count_1 - depth)
    near_left = jnp.where(dim == 2, (from_left + 8) % 16, row0 + from_left)
    far_left = slot - (count_2 - 8)
    near_right = row0 + slot
    far_right = slot
    inner_is_left = odd == 1
    near_base_left = jnp.where(inner_is_left, BASE_A, BASE_B)
    near_base_right = jnp.where(inner_is_left, BASE_B, BASE_A)
    far_base_left = jnp.where(inner_is_left, BASE_C, BASE_B + NEAR)
    far_base_right = jnp.where(inner_is_left, BASE_B + NEAR, BASE_C)
    index = jnp.where(away == 0, here, 0)
    index = jnp.where(away == -1, near_base_left + near_left, index)
    index = jnp.where(away == -2, far_base_left + far_left, index)
    index = jnp.where(away == 1, near_base_right + near_right, index)
    index = jnp.where(away == 2, far_base_right + far_right, index)
    index = jnp.where(level_tag == 1, face * SLOTS + slots[:, None], index)
    index = jnp.clip(index, 0, ROWS - 1).astype(jnp.int32).reshape(-1)
    tags = level_tag.reshape(-1)

    def forward_matrix(weight):
        return weight.transpose(2, 0, 1).reshape(C, 7 * C)

    def backward_matrix(weight):
        return weight.transpose(1, 0, 2).reshape(C, 7 * C)

    field = (SLOTS, C, CELLS)
    stack = (SLOTS, 7 * C, CELLS)
    near = (NEAR, C, 128)
    near_far = (NEAR + FAR, C, 128)
    far = (FAR, C, 128)
    mat = (C, 7 * C)
    rows_scratch = pltpu.VMEM((16, C, CELLS), BF)

    inner, outer = pl.pallas_call(
        layers_kernel,
        grid=(1,),
        in_specs=[SMEM(), whole(field), whole(field), whole(sel.shape)],
        out_specs=[whole(near), whole(near)],
        out_shape=[shape_of(near), shape_of(near)],
        scratch_shapes=[rows_scratch, rows_scratch],
        compiler_params=params(),
        name="face_rows",
    )(scal, fine_state, cotangent, sel)
    got_a, got_b, got_c = relay(inner, outer)

    taps_a, taps_b, hidden, slope, grad_merged, par, pin, pout = pl.pallas_call(
        fine_kernel,
        grid=(STEPS,),
        in_specs=[SMEM()] * 6
        + [whole(field), whole(field), whole(near), whole(near_far), whole(far)]
        + [whole(mat), whole(mat), whole(sel.shape), whole(spread.shape), whole(rest.shape)],
        out_specs=[blocked(stack), blocked(stack), blocked(field), blocked(field), blocked(field)]
        + [whole((NPAR * 8, C, 128)), whole(far), whole(far)],
        out_shape=[shape_of(stack), shape_of(stack), shape_of(field), shape_of(field)]
        + [shape_of(field), shape_of((NPAR * 8, C, 128)), shape_of(far), shape_of(far)],
        scratch_shapes=[
            pltpu.VMEM(field, BF),
            pltpu.VMEM(field, BF),
            pltpu.VMEM((ROWS, C, 128), BF),
            pltpu.VMEM((PB, C, 128), BF),
            pltpu.VMEM((NPAR * 8 + 8, C, 128), BF),
            pltpu.VMEM((16, C, 128), BF),
            pltpu.VMEM((16, C, 128), BF),
        ],
        compiler_params=params(),
        name="fine_level",
    )(
        scal, index, tags, dst.astype(jnp.int32), lead_dst.astype(jnp.int32),
        trail_dst.astype(jnp.int32), fine_state, cotangent, got_a, got_b, got_c,
        forward_matrix(weight_in), backward_matrix(weight_out), sel, spread, rest,
    )
    child_out = trade(pout, "outer")
    child_in = trade(pin, "inner")

    dw_shape = (3 * C, 256)
    merged, grad_pre, dw, inner, outer = pl.pallas_call(
        merge_kernel,
        grid=(STEPS,),
        in_specs=[SMEM()] * 2
        + [blocked(stack), blocked(stack), blocked(field), blocked(field), blocked(field)]
        + [whole((NPAR * 8, C, 128)), whole(far), whole(far), whole(mat), whole(mat)]
        + [whole(place.shape), whole(unplace.shape), whole(up.shape), whole(sel.shape)],
        out_specs=[whole(field), whole(field), whole(dw_shape), whole(near), whole(near)],
        out_shape=[shape_of(field), shape_of(field), shape_of(dw_shape, F32)]
        + [shape_of(near), shape_of(near)],
        scratch_shapes=[
            pltpu.VMEM((NPAR * 8 + 8, C, 128), BF),
            pltpu.VMEM((7 * C, CELLS), BF),
            pltpu.VMEM((NPAR * 8 + 8, C, 128), BF),
            pltpu.VMEM((PB, C, 128), BF),
            rows_scratch,
            rows_scratch,
        ],
        compiler_params=params(),
        name="coarse_and_merge",
    )(
        scal, dst.astype(jnp.int32), taps_a, taps_b, hidden, slope, grad_merged, par,
        child_in, child_out, forward_matrix(weight_coarse), backward_matrix(weight_coarse),
        place, unplace, up, sel,
    )
    got_a, got_b, got_c = relay(inner, outer)
    total = sum_over_devices(dw)

    output, grad_state = pl.pallas_call(
        final_kernel,
        grid=(STEPS,),
        in_specs=[SMEM()] * 3
        + [whole(field), whole(field), blocked(field), blocked(field)]
        + [whole(near), whole(near_far), whole(far), whole(mat), whole(mat)]
        + [whole(sel.shape), whole(spread.shape)],
        out_specs=[blocked(field), blocked(field)],
        out_shape=[shape_of(field), shape_of(field)],
        scratch_shapes=[
            pltpu.VMEM((ROWS, C, 128), BF),
            pltpu.VMEM((PB, C, 128), BF),
            pltpu.VMEM((PB, 7 * C, CELLS), BF),
            pltpu.VMEM((PB, 7 * C, CELLS), BF),
        ],
        compiler_params=params(),
        name="last_level",
    )(
        scal, index, tags, merged, grad_pre, fine_state, cotangent, got_a, got_b, got_c,
        forward_matrix(weight_out), backward_matrix(weight_in), sel, spread,
    )

    scale = 1.0 / math.sqrt(float(devices * SLOTS * CELLS))
    total = total[:, : 7 * C].reshape(3, C, 7, C) * scale
    return (
        output,
        grad_state,
        total[0].transpose(1, 2, 0),
        total[1].transpose(1, 0, 2),
        total[2].transpose(1, 2, 0),
    )


def solution(mesh):
    in_specs = (
        P("patch", None, None),
        P(),
        P(),
        P(),
        P("patch", None, None),
        P(),
        P("patch", None),
        P("patch", None),
        P("patch"),
    )
    out_specs = (P("patch", None, None), P("patch", None, None), P(), P(), P())
    return jax.shard_map(
        on_device, mesh=mesh, in_specs=in_specs, out_specs=out_specs, check_vma=False
    )
```

time: 1160 us -> 138 us (0.12); the launches traced: 1140 us -> 136 us
  local copies, waits for them, and re-layouts: 750 us -> 12.5 us
  waiting for transfers between devices: 141 us -> 16.7 us
  matrix products: 77.3 us -> 0 us
  other arithmetic: 84 us -> 8.96 us
  Pallas kernels: 0 us -> 53.5 us
  starting transfers between devices: 72.9 us -> 37.3 us
  between operations: 19.1 us -> 6.82 us
    reshape x42 -> x8, local copies, waits for them, and re-layouts: 157 us -> 6.37 us  [the longest x3 2.87 us: forward_matrix(): return weight.transpose(2, 0, 1).reshape(C, 7 * C)]
    psum x1 -> x0, waiting for transfers between devices: 141 us -> none  [on_device(): lax.psum((dw_in, dw_out, dw_coarse), 'patch')]
    unnamed x239 -> x26, local copies, waits for them, and re-layouts: 127 us -> 4.86 us
    broadcast_in_dim x46 -> x0, local copies, waits for them, and re-layouts: 109 us -> none  [the longest x44 102 us: spread_layer(): jnp.broadcast_to(square, lead_dims + (EDGE, EDGE, EDGE))]
    another operation x22 -> x0, local copies, waits for them, and re-layouts: 98.1 us -> none  [the longest x8 76.5 us: exchange_faces(): rows_table = jnp.stack(gathered).reshape(-1, width, sheet_cells)]
    dot_general x27 -> x0, matrix products: 77.3 us -> none  [the longest x18 26.8 us: conv_backward(): jnp.einsum('io,soc->sic', weight[face_id + 1], cotan, preferred_element_t...]
    ppermute x16 -> x0, local copies, waits for them, and re-layouts: 67.7 us -> none  [from_behind(): return lax.ppermute(block, axis, route)]
    slice x42 -> x5, local copies, waits for them, and re-layouts: 64.1 us -> 0.03 us  [the longest x2 0.01 us: relay(): got_c = trade(got_b[:FAR], 'inner')]
  transfers between devices with their start and end apart: 21 -> 15, of which waited for: 2 -> 6; matrix products, arithmetic and copies ran while one was open for 44% -> 10% of each run, Pallas kernels for 0% -> 10%
where the time goes in v1:
time: 138 us; the launch traced here: 136 us
  Pallas kernels  53.5 us (39%)
  starting transfers between devices  37.3 us (27%)
  waiting for transfers between devices  16.7 us (12%)
  local copies, waits for them, and re-layouts  12.5 us (9%)
  other arithmetic  8.96 us (6%)
  between operations  6.82 us (5%)
    ppermute x7, starting transfers between devices, sum_over_devices(): lax.ppermute(block, 'patch', [(i, i ^ mask) for i in range(devices)])  27.6 us
    pallas_call x1, Pallas kernels, on_device(): pl.pallas_call(merge_kernel, grid=(STEPS,), in_specs=[SMEM()] * 2 + [bloc...  19.4 us
    pallas_call x1, Pallas kernels, on_device(): pl.pallas_call(fine_kernel, grid=(STEPS,), in_specs=[SMEM()] * 6 + [whole...  16.8 us
    ppermute x7, waiting for transfers between devices, sum_over_devices(): lax.ppermute(block, 'patch', [(i, i ^ mask) for i in range(devices)])  16.7 us
    pallas_call x1, Pallas kernels, on_device(): pl.pallas_call(final_kernel, grid=(STEPS,), in_specs=[SMEM()] * 3 + [whol...  13.4 us
    ppermute x8, starting transfers between devices, trade(): return lax.ppermute(block, 'patch', pairs(kind, lax.axis_size('patch')))  9.72 us
    unnamed x26, local copies, waits for them, and re-layouts  4.86 us
    pallas_call x1, Pallas kernels, on_device(): pl.pallas_call(layers_kernel, grid=(1,), in_specs=[SMEM(), whole(field),...  3.91 us
  transfers between devices with their start and end apart: 15, of which 6 were waited for; matrix products, arithmetic and copies ran while one was open for 10% of the time, Pallas kernels for 10%

profile of v1, /device:TPU:0, one launch (start us, length us, event | category | flops | bytes accessed | tf_op | source)
XLA Modules:
  0.0 135.8 jit_solution(1266711447927651913)
XLA Ops:
  0.6 1.4 %fusion.19 = (s32[]{:T(128)}, s32[]{:T(128)}, s32[]{:T(128)}, s32[]{:T(128)}) fusion(s32[128]{0:T(128)} %param.20, s32[]{:T(128)S(6)} %sub.90, s32[]{:T(128)S(6)} %axis_index.12, s32[]{:T(128)S(6)} %sub.94), kind=kLoop, calls=%fused_computation.50 | loop fusion | flops 1532 | bytes 540 | tf_op jit(solution)/shard_map/reduce_sum | solution.py:424
  6.0 1.2 pad_add_fusion.scal
  7.2 3.9 %face_rows.1 = (bf16[27,32,128]{2,1,0:T(8,128)(2,1)}, bf16[27,32,128]{2,1,0:T(8,128)(2,1)}) custom-call(s32[4]{0:T(128)} %pad_add_fusion.scal, bf16[32,32,512]{2,1,0:T(8,128)(2,1)} %x_ref.3, bf16[32,32,512]{2,1,0:T(8,128)(2,1)} %z_ref.3, bf16[6,512,256]{2,1,0:T(8,128)(2,1)} %constant.176.clone.sel_ref), custom_call_target="tpu_custom_call" | custom-call | tf_op jit(solution)/shard_map/face_rows/pallas_call | solution.py:478
  13.1 0.6 fusion.16
  13.8 1.0 pad_maximum_fusion
  14.9 0.7 collective-permute-start.1
  15.6 0.8 fusion.10
  16.4 7.0 %collective-permute-start.2 = (bf16[8,32,128]{2,1,0:T(8,128)(2,1)S(1)}, bf16[8,32,128]{2,1,0:T(8,128)(2,1)S(1)}, u32[]{:S(2)}, u32[]{:S(2)}) collective-permute-start(bf16[8,32,128]{2,1,0:T(8,128)(2,1)S(1)} %slice.36), channel_id=1, source_target_pairs={{0,1},{2,3},{4,5},{6,7},{8,9},{10,11},{12,13},{14,15},{16,17},{18,... | collective-permute-start | bytes 196616 | tf_op jit(solution)/shard_map/ppermute | solution.py:394
  23.4 1.9 %and_select_fusion = (s32[32]{0:T(128)}, s32[32]{0:T(128)}, s32[32]{0:T(128)}) fusion(s32[32]{0:T(128)} %param.23, s32[]{:T(128)S(6)} %sub.101, s32[]{:T(128)} %get-tuple-element.46, s32[]{:T(128)S(6)} %select_n.194, s32[]{:T(128)S(6)} %select_n.220), kind=kLoop, calls=%fused_computation.25 | loop fusion | flops 832 | bytes 528 | tf_op jit(solution)/shard_map/jit(_where)/select_n | solution.py:435
  25.3 0.8 copy.30
  26.1 0.7 reshape.128.idx
  26.8 0.7 reshape.129.tag
  27.5 0.8 copy.32
  28.4 0.7 reshape.131.wb_ref
  29.1 1.5 %copy.40.wa_ref = bf16[32,224]{1,0:T(8,128)(2,1)} copy(bf16[32,224]{0,1:T(8,128)(2,1)} %bitcast.24) | data formatting | bytes 28672 | tf_op jit(solution)/shard_map/reshape | solution.py:465
  30.6 0.6 copy-done.10
  31.2 16.8 %fine_level.1 = (bf16[32,224,512]{2,1,0:T(8,128)(2,1)}, bf16[32,224,512]{2,1,0:T(8,128)(2,1)}, bf16[32,32,512]{2,1,0:T(8,128)(2,1)}, bf16[32,32,512]{2,1,0:T(8,1...) custom-call(s32[4]{0:T(128)} %pad_add_fusion.scal, ...), custom_call_target="tpu_custom_call" | custom-call | tf_op jit(solution)/shard_map/fine_level/pallas_call | solution.py:490
  48.0 0.1 collective-permute-start.3
  48.1 0.8 collective-permute-start.4
  49.0 0.7 reshape.133.wb_ref
  49.7 0.7 copy.41.wa_ref
  50.4 0.6 copy-done.7
  51.1 19.4 %coarse_and_merge.1 = (bf16[32,32,512]{2,1,0:T(8,128)(2,1)}, bf16[32,32,512]{2,1,0:T(8,128)(2,1)}, f32[96,256]{1,0:T(8,128)}, bf16[27,32,128]{2,1,0:T(8,128)(2,1)}, bf16[27,32,128]{2,1,0:T(8,128)(2,1)}) custom-call(s32[4]{0:T(128)} %pad_add_fusion.scal, s32[32]{0:T(128)} %get-tuple-element.52.dst.urow, bf16[32,224,512]{2,1,0:T(8,128)(2,1)} %get-tuple-element.24.ta_ref, ...), custom_call_target="tpu_custom_call" | custom-call | tf_op jit(solution)/shard_map/coarse_and_merge/pallas_call | solution.py:520
  70.5 4.0 %collective-permute-start.8 = (f32[96,256]{1,0:T(8,128)}, f32[96,256]{1,0:T(8,128)S(1)}, u32[]{:S(2)}, u32[]{:S(2)}) collective-permute-start(f32[96,256]{1,0:T(8,128)} %get-tuple-element.38), channel_id=1, source_target_pairs={{0,1},{1,0},{2,3},{3,2},{4,5},{5,4},{6,7},{7,6},{8,9},{9,8},{10,11... | collective-permute-start | bytes 294920 | tf_op jit(solution)/shard_map/ppermute | solution.py:407
  74.5 0.1 collective-permute-start.5
  74.6 1.1 collective-permute-done.8
  75.7 0.9 add.193
  76.6 1.7 %collective-permute-start.9 = (f32[96,256]{1,0:T(8,128)S(1)}, f32[96,256]{1,0:T(8,128)S(1)}, u32[]{:S(2)}, u32[]{:S(2)}) collective-permute-start(f32[96,256]{1,0:T(8,128)S(1)} %add.193), channel_id=1, source_target_pairs={{0,2},{1,3},{2,0},{3,1},{4,6},{5,7},{6,4},{7,5},{8,10},{9,11},{10,... | collective-permute-start | bytes 294920 | tf_op jit(solution)/shard_map/ppermute | solution.py:407
  78.2 3.5 %collective-permute-done.9 = f32[96,256]{1,0:T(8,128)S(1)} collective-permute-done((f32[96,256]{1,0:T(8,128)S(1)}, f32[96,256]{1,0:T(8,128)S(1)}, u32[]{:S(2)}, u32[]{:S(2)}) %collective-permute-start.9) | collective-permute-done | bytes 98336 | tf_op jit(solution)/shard_map/ppermute | solution.py:407
  81.7 7.1 %collective-permute-start.10 = (f32[96,256]{1,0:T(8,128)S(1)}, f32[96,256]{1,0:T(8,128)S(1)}, u32[]{:S(2)}, u32[]{:S(2)}) collective-permute-start(f32[96,256]{1,0:T(8,128)S(1)} %add.194), channel_id=1, source_target_pairs={{0,6},{1,7},{2,4},{3,5},{4,2},{5,3},{6,0},{7,1},{8,14},{9,15},{10,... | collective-permute-start | bytes 294920 | tf_op jit(solution)/shard_map/ppermute | solution.py:407
  88.9 2.6 %collective-permute-done.10 = f32[96,256]{1,0:T(8,128)S(1)} collective-permute-done((f32[96,256]{1,0:T(8,128)S(1)}, f32[96,256]{1,0:T(8,128)S(1)}, u32[]{:S(2)}, u32[]{:S(2)}) %collective-permute-start.10) | collective-permute-done | bytes 98336 | tf_op jit(solution)/shard_map/ppermute | solution.py:407
  91.5 1.8 %collective-permute-start.11 = (f32[96,256]{1,0:T(8,128)S(1)}, f32[96,256]{1,0:T(8,128)S(1)}, u32[]{:S(2)}, u32[]{:S(2)}) collective-permute-start(f32[96,256]{1,0:T(8,128)S(1)} %add.195), channel_id=1, source_target_pairs={{0,8},{1,9},{2,10},{3,11},{4,12},{5,13},{6,14},{7,15},{8,0},{9,1},... | collective-permute-start | bytes 294920 | tf_op jit(solution)/shard_map/ppermute | solution.py:407
  93.2 1.0 pad_maximum_fusion.1
  94.2 0.7 collective-permute-start.6
  94.9 1.3 collective-permute-done.11
  96.2 8.0 %collective-permute-start.12 = (f32[96,256]{1,0:T(8,128)S(1)}, f32[96,256]{1,0:T(8,128)S(1)}, u32[]{:S(2)}, u32[]{:S(2)}) collective-permute-start(f32[96,256]{1,0:T(8,128)S(1)} %add.196), channel_id=1, source_target_pairs={{0,24},{1,25},{2,26},{3,27},{4,28},{5,29},{6,30},{7,31},{8,16},{9,... | collective-permute-start | bytes 294920 | tf_op jit(solution)/shard_map/ppermute | solution.py:407
  104.2 5.7 %collective-permute-done.12 = f32[96,256]{1,0:T(8,128)S(1)} collective-permute-done((f32[96,256]{1,0:T(8,128)S(1)}, f32[96,256]{1,0:T(8,128)S(1)}, u32[]{:S(2)}, u32[]{:S(2)}) %collective-permute-start.12) | collective-permute-done | bytes 98336 | tf_op jit(solution)/shard_map/ppermute | solution.py:407
  109.9 2.7 %collective-permute-start.13 = (f32[96,256]{1,0:T(8,128)S(1)}, f32[96,256]{1,0:T(8,128)S(1)}, u32[]{:S(2)}, u32[]{:S(2)}) collective-permute-start(f32[96,256]{1,0:T(8,128)S(1)} %add.197), channel_id=1, source_target_pairs={{0,32},{1,33},{2,34},{3,35},{4,36},{5,37},{6,38},{7,39},{8,40},{9,... | collective-permute-start | bytes 294920 | tf_op jit(solution)/shard_map/ppermute | solution.py:407
  112.6 2.6 %collective-permute-done.13 = f32[96,256]{1,0:T(8,128)S(1)} collective-permute-done((f32[96,256]{1,0:T(8,128)S(1)}, f32[96,256]{1,0:T(8,128)S(1)}, u32[]{:S(2)}, u32[]{:S(2)}) %collective-permute-start.13) | collective-permute-done | bytes 98336 | tf_op jit(solution)/shard_map/ppermute | solution.py:407
  115.2 2.3 %collective-permute-start.14 = (f32[96,256]{1,0:T(8,128)S(1)}, f32[96,256]{1,0:T(8,128)S(1)}, u32[]{:S(2)}, u32[]{:S(2)}) collective-permute-start(f32[96,256]{1,0:T(8,128)S(1)} %add.198), channel_id=1, source_target_pairs={{0,96},{1,97},{2,98},{3,99},{4,100},{5,101},{6,102},{7,103},{8,104... | collective-permute-start | bytes 294920 | tf_op jit(solution)/shard_map/ppermute | solution.py:407
  117.5 0.3 collective-permute-start.7
  117.8 0.7 reshape.135.wb_ref
  118.6 0.7 copy.42.wa_ref
  119.3 0.6 copy-done.9
  119.9 13.4 %last_level.1 = (bf16[32,32,512]{2,1,0:T(8,128)(2,1)}, bf16[32,32,512]{2,1,0:T(8,128)(2,1)}) custom-call(s32[4]{0:T(128)} %pad_add_fusion.scal, s32[192]{0:T(256)} %reshape.128.idx, s32[192]{0:T(256)} %reshape.129.tag, bf16[32,32,512]{2,1,0:T(8,128)(2,1)} %get-tuple-element.32.v_ref, bf16[32,32,512]{2,1,0:T(8,128)(2,1)} %get-tuple-element.33.y_ref, ...), custom_call_target="tpu_custom_call" | custom-call | tf_op jit(solution)/shard_map/last_level/pallas_call | solution.py:548
  133.4 0.8 copy.37
  134.2 0.7 copy.38
  135.0 0.8 copy.39
  (48 shorter events, 0.6 us)
Async XLA Ops:
  0.6 48.4 %copy-start.4 = (bf16[7,32,32]{2,1,0:T(8,128)(2,1)S(1)}, bf16[7,32,32]{2,1,0:T(8,128)(2,1)}, u32[]{:S(2)}) copy-start(bf16[7,32,32]{2,1,0:T(8,128)(2,1)} %param.18) | copy-start | bytes 43012
  11.1 2.6 %collective-permute-start = (bf16[27,32,128]{2,1,0:T(8,128)(2,1)}, bf16[27,32,128]{2,1,0:T(8,128)(2,1)S(1)}, u32[]{:S(2)}, u32[]{:S(2)}) collective-permute-start(bf16[27,32,128]{2,1,0:T(8,128)(2,1)} %get-tuple-element.22), channel_id=1, source_target_pairs={{0,1},{2,3},{4,5},{6,7},{8,9},{10,11},{12,13},{14,15},{16,17},{18,... | collective-permute-start | bytes 663560 | tf_op jit(solution)/shard_map/ppermute | solution.py:394
  13.8 16.8 %copy-start.3 = (bf16[27,32,128]{2,1,0:T(8,128)(2,1)}, bf16[27,32,128]{2,1,0:T(8,128)(2,1)S(1)}, u32[]{:S(2)}) copy-start(bf16[27,32,128]{2,1,0:T(8,128)(2,1)S(1)} %collective-permute-done.a_ref) | copy-start | bytes 663556
  14.9 1.5 %collective-permute-start.1 = (bf16[35,32,128]{2,1,0:T(8,128)(2,1)S(1)}, bf16[35,32,128]{2,1,0:T(8,128)(2,1)S(1)}, u32[]{:S(2)}, u32[]{:S(2)}) collective-permute-start(bf16[35,32,128]{2,1,0:T(8,128)(2,1)S(1)} %pad_maximum_fusion), channel_id=1, source_target_pairs={{1,2},{3,4},{5,6},{7,8},{9,10},{11,12},{13,14},{15,16},{17,18},{19... | collective-permute-start | bytes 860168 | tf_op jit(solution)/shard_map/ppermute | solution.py:394
  16.4 14.2 %copy-start.1 = (bf16[35,32,128]{2,1,0:T(8,128)(2,1)}, bf16[35,32,128]{2,1,0:T(8,128)(2,1)S(1)}, u32[]{:S(2)}) copy-start(bf16[35,32,128]{2,1,0:T(8,128)(2,1)S(1)} %collective-permute-done.1.b_ref) | copy-start | bytes 860164
  16.4 14.2 %collective-permute-start.2 = (bf16[8,32,128]{2,1,0:T(8,128)(2,1)S(1)}, bf16[8,32,128]{2,1,0:T(8,128)(2,1)S(1)}, u32[]{:S(2)}, u32[]{:S(2)}) collective-permute-start(bf16[8,32,128]{2,1,0:T(8,128)(2,1)S(1)} %slice.36), channel_id=1, source_target_pairs={{0,1},{2,3},{4,5},{6,7},{8,9},{10,11},{12,13},{14,15},{16,17},{18,... | collective-permute-start | bytes 196616 | tf_op jit(solution)/shard_map/ppermute | solution.py:394
  30.6 0.6 copy-start.10
  48.0 2.4 %collective-permute-start.3 = (bf16[8,32,128]{2,1,0:T(8,128)(2,1)}, bf16[8,32,128]{2,1,0:T(8,128)(2,1)S(1)}, u32[]{:S(2)}, u32[]{:S(2)}) collective-permute-start(bf16[8,32,128]{2,1,0:T(8,128)(2,1)} %get-tuple-element.30), channel_id=1, source_target_pairs={{0,1},{2,3},{4,5},{6,7},{8,9},{10,11},{12,13},{14,15},{16,17},{18,... | collective-permute-start | bytes 196616 | tf_op jit(solution)/shard_map/ppermute | solution.py:394
  48.1 2.3 %collective-permute-start.4 = (bf16[8,32,128]{2,1,0:T(8,128)(2,1)}, bf16[8,32,128]{2,1,0:T(8,128)(2,1)S(1)}, u32[]{:S(2)}, u32[]{:S(2)}) collective-permute-start(bf16[8,32,128]{2,1,0:T(8,128)(2,1)} %get-tuple-element.31), channel_id=1, source_target_pairs={{1,2},{3,4},{5,6},{7,8},{9,10},{11,12},{13,14},{15,16},{17,18},{19... | collective-permute-start | bytes 196616 | tf_op jit(solution)/shard_map/ppermute | solution.py:394
  50.4 0.6 copy-start.7
  50.4 0.6 copy-start.8
  51.1 66.7 %copy-start.5 = (bf16[7,32,32]{2,1,0:T(8,128)(2,1)S(1)}, bf16[7,32,32]{2,1,0:T(8,128)(2,1)}, u32[]{:S(2)}) copy-start(bf16[7,32,32]{2,1,0:T(8,128)(2,1)} %param.16) | copy-start | bytes 43012
  51.1 67.5 %copy-start.6 = (bf16[7,32,32]{2,1,0:T(8,128)(2,1)S(1)}, bf16[7,32,32]{2,1,0:T(8,128)(2,1)}, u32[]{:S(2)}) copy-start(bf16[7,32,32]{2,1,0:T(8,128)(2,1)} %param.17) | copy-start | bytes 43012
  70.5 5.2 %collective-permute-start.8 = (f32[96,256]{1,0:T(8,128)}, f32[96,256]{1,0:T(8,128)S(1)}, u32[]{:S(2)}, u32[]{:S(2)}) collective-permute-start(f32[96,256]{1,0:T(8,128)} %get-tuple-element.38), channel_id=1, source_target_pairs={{0,1},{1,0},{2,3},{3,2},{4,5},{5,4},{6,7},{7,6},{8,9},{9,8},{10,11... | collective-permute-start | bytes 294920 | tf_op jit(solution)/shard_map/ppermute | solution.py:407
  74.5 14.4 %collective-permute-start.5 = (bf16[27,32,128]{2,1,0:T(8,128)(2,1)}, bf16[27,32,128]{2,1,0:T(8,128)(2,1)S(1)}, u32[]{:S(2)}, u32[]{:S(2)}) collective-permute-start(bf16[27,32,128]{2,1,0:T(8,128)(2,1)} %get-tuple-element.34), channel_id=1, source_target_pairs={{0,1},{2,3},{4,5},{6,7},{8,9},{10,11},{12,13},{14,15},{16,17},{18,... | collective-permute-start | bytes 663560 | tf_op jit(solution)/shard_map/ppermute | solution.py:394
  76.6 5.1 %collective-permute-start.9 = (f32[96,256]{1,0:T(8,128)S(1)}, f32[96,256]{1,0:T(8,128)S(1)}, u32[]{:S(2)}, u32[]{:S(2)}) collective-permute-start(f32[96,256]{1,0:T(8,128)S(1)} %add.193), channel_id=1, source_target_pairs={{0,2},{1,3},{2,0},{3,1},{4,6},{5,7},{6,4},{7,5},{8,10},{9,11},{10,... | collective-permute-start | bytes 294920 | tf_op jit(solution)/shard_map/ppermute | solution.py:407
  81.7 9.7 %collective-permute-start.10 = (f32[96,256]{1,0:T(8,128)S(1)}, f32[96,256]{1,0:T(8,128)S(1)}, u32[]{:S(2)}, u32[]{:S(2)}) collective-permute-start(f32[96,256]{1,0:T(8,128)S(1)} %add.194), channel_id=1, source_target_pairs={{0,6},{1,7},{2,4},{3,5},{4,2},{5,3},{6,0},{7,1},{8,14},{9,15},{10,... | collective-permute-start | bytes 294920 | tf_op jit(solution)/shard_map/ppermute | solution.py:407
  88.9 30.4 %copy-start.2 = (bf16[27,32,128]{2,1,0:T(8,128)(2,1)}, bf16[27,32,128]{2,1,0:T(8,128)(2,1)S(1)}, u32[]{:S(2)}) copy-start(bf16[27,32,128]{2,1,0:T(8,128)(2,1)S(1)} %collective-permute-done.5.a_ref) | copy-start | bytes 663556
  91.5 4.7 %collective-permute-start.11 = (f32[96,256]{1,0:T(8,128)S(1)}, f32[96,256]{1,0:T(8,128)S(1)}, u32[]{:S(2)}, u32[]{:S(2)}) collective-permute-start(f32[96,256]{1,0:T(8,128)S(1)} %add.195), channel_id=1, source_target_pairs={{0,8},{1,9},{2,10},{3,11},{4,12},{5,13},{6,14},{7,15},{8,0},{9,1},... | collective-permute-start | bytes 294920 | tf_op jit(solution)/shard_map/ppermute | solution.py:407
  94.2 23.3 %collective-permute-start.6 = (bf16[35,32,128]{2,1,0:T(8,128)(2,1)S(1)}, bf16[35,32,128]{2,1,0:T(8,128)(2,1)S(1)}, u32[]{:S(2)}, u32[]{:S(2)}) collective-permute-start(bf16[35,32,128]{2,1,0:T(8,128)(2,1)S(1)} %pad_maximum_fusion.1), channel_id=1, source_target_pairs={{1,2},{3,4},{5,6},{7,8},{9,10},{11,12},{13,14},{15,16},{17,18},{19... | collective-permute-start | bytes 860168 | tf_op jit(solution)/shard_map/ppermute | solution.py:394
  96.2 13.7 %collective-permute-start.12 = (f32[96,256]{1,0:T(8,128)S(1)}, f32[96,256]{1,0:T(8,128)S(1)}, u32[]{:S(2)}, u32[]{:S(2)}) collective-permute-start(f32[96,256]{1,0:T(8,128)S(1)} %add.196), channel_id=1, source_target_pairs={{0,24},{1,25},{2,26},{3,27},{4,28},{5,29},{6,30},{7,31},{8,16},{9,... | collective-permute-start | bytes 294920 | tf_op jit(solution)/shard_map/ppermute | solution.py:407
  109.9 5.3 %collective-permute-start.13 = (f32[96,256]{1,0:T(8,128)S(1)}, f32[96,256]{1,0:T(8,128)S(1)}, u32[]{:S(2)}, u32[]{:S(2)}) collective-permute-start(f32[96,256]{1,0:T(8,128)S(1)} %add.197), channel_id=1, source_target_pairs={{0,32},{1,33},{2,34},{3,35},{4,36},{5,37},{6,38},{7,39},{8,40},{9,... | collective-permute-start | bytes 294920 | tf_op jit(solution)/shard_map/ppermute | solution.py:407
  115.2 18.1 %collective-permute-start.14 = (f32[96,256]{1,0:T(8,128)S(1)}, f32[96,256]{1,0:T(8,128)S(1)}, u32[]{:S(2)}, u32[]{:S(2)}) collective-permute-start(f32[96,256]{1,0:T(8,128)S(1)} %add.198), channel_id=1, source_target_pairs={{0,96},{1,97},{2,98},{3,99},{4,100},{5,101},{6,102},{7,103},{8,104... | collective-permute-start | bytes 294920 | tf_op jit(solution)/shard_map/ppermute | solution.py:407
  117.5 1.8 %copy-start = (bf16[35,32,128]{2,1,0:T(8,128)(2,1)}, bf16[35,32,128]{2,1,0:T(8,128)(2,1)S(1)}, u32[]{:S(2)}) copy-start(bf16[35,32,128]{2,1,0:T(8,128)(2,1)S(1)} %collective-permute-done.6.b_ref) | copy-start | bytes 860164
  117.5 1.8 %collective-permute-start.7 = (bf16[8,32,128]{2,1,0:T(8,128)(2,1)S(1)}, bf16[8,32,128]{2,1,0:T(8,128)(2,1)S(1)}, u32[]{:S(2)}, u32[]{:S(2)}) collective-permute-start(bf16[8,32,128]{2,1,0:T(8,128)(2,1)S(1)} %slice.38), channel_id=1, source_target_pairs={{0,1},{2,3},{4,5},{6,7},{8,9},{10,11},{12,13},{14,15},{16,17},{18,... | collective-permute-start | bytes 196616 | tf_op jit(solution)/shard_map/ppermute | solution.py:394
  119.3 0.6 copy-start.9

commit v2 on v1

v2 whole, which is shorter than its diff:
```python
import functools
import math

import numpy as np
import jax
import jax.numpy as jnp
from jax import lax
from jax.experimental import pallas as pl
from jax.experimental.pallas import tpu as pltpu
from jax.sharding import PartitionSpec as P

BF = jnp.bfloat16
F32 = jnp.float32
EDGE = 8
CELLS = 512
SLOTS = 32
C = 32
PB = 8
STEPS = SLOTS // PB
NPAR = 5
STRIDES = (64, 8, 1)
MORTON = (3, 8, 16)
ROW0 = (24, 16, 0)
NEAR = 27
FAR = 8
BASE_A = 6 * SLOTS
BASE_B = BASE_A + NEAR
BASE_C = BASE_B + NEAR + FAR
ROWS = BASE_C + FAR
VMEM_LIMIT = 56 * 1024 * 1024
IDX, TAG, DST, LEAD, TRAIL, SCAL = 0, 192, 384, 416, 448, 480
N_COUNT, N_ODD, N_LAST, N_OWNED = SCAL, SCAL + 1, SCAL + 2, SCAL + 3
META = 512
IN_F, OUT_B, OUT_F, IN_B, CO_F, CO_B = range(6)


def cell_coords():
    ids = np.arange(CELLS)
    return [ids // 64, ids // 8 % 8, ids % 8]


def face_cells(face):
    coords = cell_coords()
    keep = coords[face // 2] == (EDGE - 1 if face % 2 else 0)
    return np.nonzero(keep)[0]


def constants():
    sel = np.zeros((3, 2, CELLS, 256), np.float32)
    spread = np.zeros((2, 256, 2 * CELLS), np.float32)
    for face in range(6):
        for j, cell in enumerate(face_cells(face)):
            for kind in range(2):
                col = (face % 2) * 128 + kind * 64 + j
                sel[face // 2, kind, cell, col] = 1
                if face >= 2:
                    spread[face // 2 - 1, col, kind * CELLS + cell] = 1
    c0, c1, c2 = cell_coords()
    group = (c0 // 2) * 16 + (c1 // 2) * 4 + c2 // 2
    rest = np.zeros((2, CELLS, 128), np.float32)
    up = np.zeros((128, 2 * CELLS), np.float32)
    for cell in range(CELLS):
        rest[0, cell, group[cell]] = 0.125
        rest[1, cell, 64 + group[cell]] = 1
        up[group[cell], cell] = 1
        up[64 + group[cell], CELLS + cell] = 1
    place = np.zeros((256, 2 * CELLS), np.float32)
    for o2 in range(2):
        for a in range(64):
            cell = (a // 16) * 64 + (a // 4 % 4) * 8 + a % 4 + 4 * o2
            place[128 * o2 + a, cell] = 1
            place[128 * o2 + 64 + a, CELLS + cell] = 1
    as_bf = lambda item: np.asarray(item, jnp.bfloat16)
    return (
        as_bf(sel.reshape(6, CELLS, 256)),
        as_bf(spread),
        as_bf(rest),
        as_bf(up),
        as_bf(place),
    )


def dot(a, b):
    return jnp.dot(a, b, preferred_element_type=F32)


def dot_nt(a, b):
    return lax.dot_general(a, b, (((1,), (1,)), ((), ())), preferred_element_type=F32)


def coord_of(dim):
    lane = lax.broadcasted_iota(jnp.int32, (16, CELLS), 1)
    return (lane // STRIDES[dim]) % EDGE


def on_face(face):
    edge = EDGE - 1 if face % 2 else 0
    return jnp.where(coord_of(face // 2) == edge, 1.0, 0.0)


def halves(field):
    return field.reshape(field.shape[0] // 16, 16, CELLS)


def times(field, mask):
    return (halves(field) * mask[None]).reshape(field.shape)


def toward(field, face):
    stride = STRIDES[face // 2]
    shift = CELLS - stride if face % 2 else stride
    return pltpu.roll(field, shift, 1)


def send_rows(count, odd, v_ref, y_ref, sel_ref, v_rows, y_rows, sides, inner_ref, outer_ref):
    for side in range(2):
        for dim in (2, 1, 0):
            depth = MORTON[dim]
            for i in range(depth):
                slot = jnp.clip(count - depth + i, 0, SLOTS - 1) if side else i
                v_rows[i] = v_ref[slot]
                y_rows[i] = y_ref[slot]
            cols = slice(side * 128, side * 128 + 128)
            layers = dot(v_rows[:depth].reshape(depth * C, CELLS), sel_ref[2 * dim, :, cols])
            layers += dot(y_rows[:depth].reshape(depth * C, CELLS), sel_ref[2 * dim + 1, :, cols])
            layers = layers.astype(BF).reshape(depth, C, 128)
            if dim == 2 and side:
                sides[side, 0:8] = layers[8:16]
                sides[side, 8:16] = layers[0:8]
            else:
                sides[side, ROW0[dim] : ROW0[dim] + depth] = layers
    inner_ref[...] = sides[1 - odd]
    outer_ref[...] = sides[odd]


def layers_kernel(counts, v_ref, y_ref, sel_ref, inner_ref, outer_ref, v_rows, y_rows, sides):
    rank = lax.axis_index("patch")
    send_rows(
        counts[rank], rank % 2, v_ref, y_ref, sel_ref, v_rows, y_rows, sides, inner_ref, outer_ref
    )


def fill_table(v_ref, y_ref, sel_ref, table):
    for dim in range(3):
        layers = dot(v_ref[...].reshape(SLOTS * C, CELLS), sel_ref[2 * dim])
        layers += dot(y_ref[...].reshape(SLOTS * C, CELLS), sel_ref[2 * dim + 1])
        layers = layers.astype(BF)
        for high in range(2):
            face = 2 * dim + high
            table[face * SLOTS : (face + 1) * SLOTS] = layers[
                :, high * 128 : high * 128 + 128
            ].reshape(SLOTS, C, 128)


def prepare_kernel(
    counts, neighbour, level_tag, octant,
    got_ref, x_ref, z_ref, sel_ref, w_in, w_out, w_co,
    meta, xs, zs, mats, table,
):
    rank = lax.axis_index("patch")
    odd = rank % 2

    def count_at(device):
        here = counts[jnp.clip(device, 0, counts.shape[0] - 1)]
        return jnp.where(device < 0, 0, here)

    first = lax.fori_loop(0, rank, lambda d, s: s + counts[d], jnp.int32(0))
    count = count_at(rank)
    count_1 = count_at(rank - 1)
    count_2 = count_at(rank - 2)
    stop = first + count
    meta[N_COUNT] = count
    meta[N_ODD] = odd
    meta[N_LAST] = jnp.where(stop % 8 != 0, stop // 8 - first // 8, NPAR)
    meta[N_OWNED] = jnp.where(first % 8 == 0, 1, 0)
    near_left = jnp.where(odd == 1, BASE_A, BASE_B)
    near_right = jnp.where(odd == 1, BASE_B, BASE_A)
    far_left = jnp.where(odd == 1, BASE_C, BASE_B + NEAR)
    far_right = jnp.where(odd == 1, BASE_B + NEAR, BASE_C)
    lead_count = (8 - first % 8) % 8

    def per_slot(p, carry):
        live = p < count
        parent = (first % 8 + p) // 8
        o = jnp.clip(octant[p], 0, 7)
        meta[DST + p] = jnp.where(live, parent * 8 + o, NPAR * 8)
        meta[LEAD + p] = jnp.where(live & (p < lead_count), o, 8)
        meta[TRAIL + p] = jnp.where(live & (p >= count - stop % 8), o, 8)
        for face in range(6):
            dim = face // 2
            depth = MORTON[dim]
            other = neighbour[face, p]
            tag = level_tag[face, p]
            away = other // SLOTS - rank
            slot = other % SLOTS
            if face % 2:
                near = near_right + ROW0[dim] + slot
                far = far_right + slot
            else:
                back = slot - (count_1 - depth)
                near = near_left + ((back + 8) % 16 if dim == 2 else ROW0[dim] + back)
                far = far_left + slot - (count_2 - 8)
            row = jnp.where(away == 0, (face ^ 1) * SLOTS + slot, near)
            row = jnp.where(jnp.abs(away) == 2, far, row)
            row = jnp.where(tag == 1, face * SLOTS + p, row)
            meta[IDX + face * SLOTS + p] = jnp.clip(row, 0, ROWS - 1)
            meta[TAG + face * SLOTS + p] = tag
        return carry

    lax.fori_loop(0, SLOTS, per_slot, 0)
    for k, (weight, turned) in enumerate(
        ((w_in, True), (w_out, False), (w_out, True), (w_in, False), (w_co, True), (w_co, False))
    ):
        for f in range(7):
            one = weight[f].astype(F32)
            mats[k, :, f * C : (f + 1) * C] = (one.T if turned else one).astype(BF)
    for p in range(SLOTS):
        live = (p < count).astype(F32)
        xs[p] = (x_ref[p].astype(F32) * live).astype(BF)
        zs[p] = (z_ref[p].astype(F32) * live).astype(BF)
    fill_table(xs, zs, sel_ref, table)
    table[BASE_A:BASE_B] = got_ref[...]


def table_kernel(v_ref, y_ref, sel_ref, table):
    fill_table(v_ref, y_ref, sel_ref, table)


def join_table(parts, coef, table):
    start = 0
    for part in parts:
        size = part.shape[0]
        table[start : start + size] = part[...]
        start += size
    for dim in range(3):
        low, high = on_face(2 * dim), on_face(2 * dim + 1)
        for t_low in range(2):
            for t_high in range(2):
                row = dim * 4 + t_low * 2 + t_high
                coef[row, 0] = (low * (1 - t_low) + high * t_high).astype(BF)
                coef[row, 1] = (high * (1 - t_high) + low * t_low).astype(BF)


def block_taps(start, meta, v_ref, y_ref, spread_ref, table, coef, picked, ta, tb):
    for dim in range(3):
        low, high = 2 * dim, 2 * dim + 1
        edges = [on_face(low), on_face(high)]
        inside = [(1.0 - edge).astype(BF) for edge in edges]
        edges = [edge.astype(BF) for edge in edges]
        if dim:
            for p in range(PB):
                picked[p, :, 0:128] = table[meta[IDX + low * SLOTS + start + p]]
                picked[p, :, 128:256] = table[meta[IDX + high * SLOTS + start + p]]
            spread = dot(picked[...].reshape(PB * C, 256), spread_ref[dim - 1]).astype(BF)
        for p in range(PB):
            if dim:
                rows = slice(p * C, (p + 1) * C)
                v_edge = spread[rows, :CELLS]
                y_edge = spread[rows, CELLS:]
            else:
                r_low = table[meta[IDX + low * SLOTS + start + p]]
                r_high = table[meta[IDX + high * SLOTS + start + p]]
                blank = jnp.zeros((C, 256), BF)
                v_edge = jnp.concatenate([r_low, blank, pltpu.roll(r_high, 64, 1)], axis=1)
                y_edge = jnp.concatenate([pltpu.roll(r_low, 64, 1), blank, r_high], axis=1)
            field = v_ref[p]
            other = y_ref[p]
            if dim == 0:
                ta[p, 0:C] = field
                tb[p, 0:C] = other
            row = (
                dim * 4
                + meta[TAG + low * SLOTS + start + p] * 2
                + meta[TAG + high * SLOTS + start + p]
            )
            for k, face in enumerate((low, high)):
                ta[p, C * (face + 1) : C * (face + 2)] = times(
                    toward(field, face), inside[k]
                ) + times(v_edge, edges[k])
                back = face ^ 1
                tb[p, C * (back + 1) : C * (back + 2)] = times(
                    toward(other, face), inside[k]
                ) + times(y_edge, coef[row, k])


def silu_pair(pre):
    sigma = 1.0 / (1.0 + jnp.exp(-pre))
    return pre * sigma, sigma * (1.0 + pre * (1.0 - sigma))


def fine_kernel(
    meta, xs, zs, t_ref, b_ref, c_ref, mats, spread_ref, rest_ref,
    ta_ref, tb_ref, hidden_ref, slope_ref, gm_ref, par_ref, inner_ref, outer_ref,
    table, coef, picked, par, ends,
):
    step = pl.program_id(0)

    @pl.when(step == 0)
    def _():
        join_table((t_ref, b_ref, c_ref), coef, table)
        par[...] = jnp.zeros_like(par)
        ends[...] = jnp.zeros_like(ends)

    start = step * PB
    block_taps(start, meta, xs, zs, spread_ref, table, coef, picked, ta_ref, tb_ref)
    for p in range(PB):
        hidden, slope = silu_pair(dot(mats[IN_F], ta_ref[p]))
        hidden_ref[p] = hidden.astype(BF)
        slope_ref[p] = slope.astype(BF)
        gm_ref[p] = dot(mats[OUT_B], tb_ref[p]).astype(BF)
    child = dot(hidden_ref[...].reshape(PB * C, CELLS), rest_ref[0])
    child += dot(gm_ref[...].reshape(PB * C, CELLS), rest_ref[1])
    child = child.astype(BF)
    for p in range(PB):
        row = child[p * C : (p + 1) * C]
        par[meta[DST + start + p]] = row
        ends[0, meta[LEAD + start + p]] = row
        ends[1, meta[TRAIL + start + p]] = row

    @pl.when(step == STEPS - 1)
    def _():
        par_ref[...] = par[: NPAR * 8]
        odd = meta[N_ODD]
        inner_ref[...] = ends[1 - odd, 0:8]
        outer_ref[...] = ends[odd, 0:8]


def coarse_level(meta, par_ref, inner_ref, outer_ref, wa, wb, place_ref, par, taps, up_rows, dw_ref):
    par[: NPAR * 8] = par_ref[...]
    par[NPAR * 8 :] = jnp.zeros((8, C, 128), BF)
    last = meta[N_LAST] * 8
    odd = meta[N_ODD]
    inner_at = jnp.where(odd == 1, 0, last)
    outer_at = jnp.where(odd == 1, last, 0)
    for o in range(8):
        par[inner_at + o] = par[inner_at + o] + inner_ref[o]
    for o in range(8):
        par[outer_at + o] = par[outer_at + o] + outer_ref[o]

    rows = NPAR * C
    both = jnp.zeros((rows, 2 * CELLS), BF)
    for o in range(0, 8, 2):
        lhs = jnp.concatenate(
            [
                jnp.concatenate([par[q * 8 + o], par[q * 8 + o + 1]], axis=1)
                for q in range(NPAR)
            ],
            axis=0,
        )
        put = dot(lhs, place_ref[...]).astype(BF)
        shift = (o // 4) * 256 + (o // 2 % 2) * 32
        if shift:
            put = jnp.concatenate(
                [
                    pltpu.roll(put[:, :CELLS], shift, 1),
                    pltpu.roll(put[:, CELLS:], shift, 1),
                ],
                axis=1,
            )
        both += put
    field = both[:, :CELLS]
    cotan = both[:, CELLS:].astype(F32)
    edges = [on_face(face).astype(BF) for face in range(6)]
    inside = [(1.0 - on_face(face)).astype(BF) for face in range(6)]

    def store(face, value):
        taps[:, C * face : C * (face + 1)] = value.reshape(NPAR, C, CELLS)

    store(0, field)
    for face in range(6):
        store(face + 1, times(toward(field, face), inside[face]) + times(field, edges[face]))
    pre = jnp.concatenate([dot(wa, taps[q]) for q in range(NPAR)], axis=0)
    act, slope = silu_pair(pre)
    act = act.astype(BF)
    grad = (cotan * slope).astype(BF)
    dw = jnp.zeros((7 * C, C), F32)
    for q in range(NPAR):
        part = dot_nt(taps[q], grad[q * C : (q + 1) * C])
        if q == 0:
            part = part * meta[N_OWNED].astype(F32)
        dw += part
    store(0, grad)
    for face in range(6):
        back = face ^ 1
        store(face + 1, times(toward(grad, back), inside[back]) + times(grad, edges[face]))
    down = jnp.concatenate([dot(wb, taps[q]) for q in range(NPAR)], axis=0).astype(BF)
    for o in range(0, 8, 2):
        one, two = act, down
        shift = (o // 4) * 256 + (o // 2 % 2) * 32
        if shift:
            one = pltpu.roll(act, CELLS - shift, 1)
            two = pltpu.roll(down, CELLS - shift, 1)
        got = dot_nt(one, place_ref[:, :CELLS]) + dot_nt(two, place_ref[:, CELLS:])
        got = got.astype(BF)
        for q in range(NPAR):
            up_rows[q * 8 + o] = got[q * C : (q + 1) * C, :128]
            up_rows[q * 8 + o + 1] = got[q * C : (q + 1) * C, 128:]
    up_rows[NPAR * 8] = jnp.zeros((C, 128), BF)
    dw_ref[:, 2 * C : 3 * C] = dw


def merge_kernel(
    meta,
    ta_ref, tb_ref, hidden_ref, slope_ref, gm_ref, par_ref, pin_ref, pout_ref,
    mats, place_ref, up_ref, sel_ref,
    merged_ref, gpa_ref, dw_ref, inner_ref, outer_ref,
    par, taps, up_rows, picked, v_rows, y_rows, sides,
):
    step = pl.program_id(0)

    @pl.when(step == 0)
    def _():
        dw_ref[...] = jnp.zeros_like(dw_ref)
        coarse_level(
            meta, par_ref, pin_ref, pout_ref, mats[CO_F], mats[CO_B],
            place_ref, par, taps, up_rows, dw_ref,
        )

    start = step * PB
    for p in range(PB):
        picked[p] = up_rows[meta[DST + start + p]]
    spread = dot(picked[...].reshape(PB * C, 128), up_ref[...])
    dw_in = jnp.zeros((7 * C, C), F32)
    dw_out = jnp.zeros((7 * C, C), F32)
    for p in range(PB):
        rows = slice(p * C, (p + 1) * C)
        merged = (hidden_ref[p].astype(F32) + spread[rows, :CELLS]).astype(BF)
        grad = gm_ref[p].astype(F32) + spread[rows, CELLS:] * 0.125
        gpa = (grad * slope_ref[p].astype(F32)).astype(BF)
        merged_ref[start + p] = merged
        gpa_ref[start + p] = gpa
        dw_in += dot_nt(ta_ref[p], gpa)
        dw_out += dot_nt(tb_ref[p], merged)
    dw_ref[:, 0:C] += dw_in
    dw_ref[:, C : 2 * C] += dw_out

    @pl.when(step == STEPS - 1)
    def _():
        send_rows(
            meta[N_COUNT], meta[N_ODD], merged_ref, gpa_ref, sel_ref,
            v_rows, y_rows, sides, inner_ref, outer_ref,
        )


def final_kernel(
    meta, v_ref, y_ref, xs, zs, t_ref, a_ref, b_ref, c_ref, mats, spread_ref,
    out_ref, gs_ref,
    table, coef, picked, ta, tb,
):
    step = pl.program_id(0)

    @pl.when(step == 0)
    def _():
        join_table((t_ref, a_ref, b_ref, c_ref), coef, table)

    start = step * PB
    block_taps(start, meta, v_ref, y_ref, spread_ref, table, coef, picked, ta, tb)
    for p in range(PB):
        out_ref[p] = (xs[p].astype(F32) + dot(mats[OUT_F], ta[p])).astype(BF)
        gs_ref[p] = (zs[p].astype(F32) + dot(mats[IN_B], tb[p])).astype(BF)


def weights_kernel(scale, parts_ref, in_ref, out_ref, co_ref):
    total = parts_ref[...] * scale
    for f in range(7):
        rows = slice(f * C, (f + 1) * C)
        in_ref[f] = total[rows, 0:C]
        out_ref[f] = total[rows, C : 2 * C].T
        co_ref[f] = total[rows, 2 * C : 3 * C]


SMEM = functools.partial(pl.BlockSpec, memory_space=pltpu.SMEM)


def whole(shape):
    zeros = (0,) * len(shape)
    return pl.BlockSpec(shape, lambda i: zeros)


def blocked(shape):
    rest = (0,) * (len(shape) - 1)
    return pl.BlockSpec((PB,) + tuple(shape[1:]), lambda i: (i,) + rest)


def params():
    return pltpu.CompilerParams(
        dimension_semantics=("arbitrary",), vmem_limit_bytes=VMEM_LIMIT
    )


def shape_of(shape, dtype=BF):
    return jax.ShapeDtypeStruct(shape, dtype)


def cost(micros):
    return pl.CostEstimate(
        flops=int(micros * 1e6), bytes_accessed=int(micros * 3.0e6), transcendentals=0
    )


def pairs(kind, devices):
    if kind == "inner":
        links = [(2 * c, 2 * c + 1) for c in range(devices // 2)]
    else:
        links = [(2 * c + 1, 2 * c + 2) for c in range(devices // 2 - 1)]
    return links + [(b, a) for a, b in links]


def trade(block, kind):
    return lax.ppermute(block, "patch", pairs(kind, lax.axis_size("patch")))


def relay_out(outer, got_a):
    return trade(jnp.concatenate([outer, got_a[:FAR]], axis=0), "outer")


def relay_in(got_b, first):
    got_b, first = lax.optimization_barrier((got_b, first))
    return trade(got_b[:FAR], "inner"), first


def sum_over_devices(block):
    devices = lax.axis_size("patch")
    for mask in (1, 2, 6, 8, 24, 32, 96):
        block = block + lax.ppermute(block, "patch", [(i, i ^ mask) for i in range(devices)])
    return block


def on_device(
    fine_state, weight_in, weight_out, weight_coarse, cotangent,
    owner_count, neighbour, level_tag, octant,
):
    devices = lax.axis_size("patch")
    sel, spread, rest, up, place = [jnp.asarray(item) for item in constants()]

    field = (SLOTS, C, CELLS)
    stack = (SLOTS, 7 * C, CELLS)
    near = (NEAR, C, 128)
    near_far = (NEAR + FAR, C, 128)
    far = (FAR, C, 128)
    mats_shape = (6, C, 7 * C)
    first_part = (BASE_B, C, 128)
    local_part = (BASE_A, C, 128)
    rows_scratch = [pltpu.VMEM((16, C, CELLS), BF)] * 2 + [pltpu.VMEM((2, NEAR, C, 128), BF)]
    tap_scratch = [
        pltpu.VMEM((ROWS, C, 128), BF),
        pltpu.VMEM((12, 2, 16, CELLS), BF),
        pltpu.VMEM((PB, C, 256), BF),
    ]

    inner, outer = pl.pallas_call(
        layers_kernel,
        grid=(1,),
        in_specs=[SMEM(), whole(field), whole(field), whole(sel.shape)],
        out_specs=[whole(near), whole(near)],
        out_shape=[shape_of(near), shape_of(near)],
        scratch_shapes=rows_scratch,
        compiler_params=params(),
        cost_estimate=cost(4),
        name="face_rows",
    )(owner_count, fine_state, cotangent, sel)
    got_a = trade(inner, "inner")
    got_b = relay_out(outer, got_a)

    meta, xs, zs, mats, table = pl.pallas_call(
        prepare_kernel,
        grid=(1,),
        in_specs=[SMEM()] * 4
        + [whole(near), whole(field), whole(field), whole(sel.shape)]
        + [whole(weight_in.shape)] * 3,
        out_specs=[SMEM(), whole(field), whole(field), whole(mats_shape), whole(first_part)],
        out_shape=[shape_of((META,), jnp.int32), shape_of(field), shape_of(field)]
        + [shape_of(mats_shape), shape_of(first_part)],
        compiler_params=params(),
        cost_estimate=cost(6),
        name="prepare",
    )(
        owner_count, neighbour.T, level_tag.T, octant, got_a, fine_state, cotangent, sel,
        weight_in, weight_out, weight_coarse,
    )
    got_c, meta = relay_in(got_b, meta)

    taps_a, taps_b, hidden, slope, grad_merged, par, pin, pout = pl.pallas_call(
        fine_kernel,
        grid=(STEPS,),
        in_specs=[SMEM(), blocked(field), blocked(field)]
        + [whole(first_part), whole(near_far), whole(far), whole(mats_shape)]
        + [whole(spread.shape), whole(rest.shape)],
        out_specs=[blocked(stack), blocked(stack), blocked(field), blocked(field), blocked(field)]
        + [whole((NPAR * 8, C, 128)), whole(far), whole(far)],
        out_shape=[shape_of(stack), shape_of(stack), shape_of(field), shape_of(field)]
        + [shape_of(field), shape_of((NPAR * 8, C, 128)), shape_of(far), shape_of(far)],
        scratch_shapes=tap_scratch
        + [pltpu.VMEM((NPAR * 8 + 8, C, 128), BF), pltpu.VMEM((2, 16, C, 128), BF)],
        compiler_params=params(),
        cost_estimate=cost(12),
        name="fine_level",
    )(meta, xs, zs, table, got_b, got_c, mats, spread, rest)
    child_out = trade(pout, "outer")
    child_in = trade(pin, "inner")

    dw_shape = (7 * C, 128)
    merged, grad_pre, dw, inner, outer = pl.pallas_call(
        merge_kernel,
        grid=(STEPS,),
        in_specs=[SMEM()]
        + [blocked(stack), blocked(stack), blocked(field), blocked(field), blocked(field)]
        + [whole((NPAR * 8, C, 128)), whole(far), whole(far), whole(mats_shape)]
        + [whole(place.shape), whole(up.shape), whole(sel.shape)],
        out_specs=[whole(field), whole(field), whole(dw_shape), whole(near), whole(near)],
        out_shape=[shape_of(field), shape_of(field), shape_of(dw_shape, F32)]
        + [shape_of(near), shape_of(near)],
        scratch_shapes=[
            pltpu.VMEM((NPAR * 8 + 8, C, 128), BF),
            pltpu.VMEM((NPAR, 7 * C, CELLS), BF),
            pltpu.VMEM((NPAR * 8 + 8, C, 128), BF),
            pltpu.VMEM((PB, C, 128), BF),
        ]
        + rows_scratch,
        compiler_params=params(),
        cost_estimate=cost(14),
        name="coarse_and_merge",
    )(
        meta, taps_a, taps_b, hidden, slope, grad_merged, par, child_in, child_out, mats,
        place, up, sel,
    )
    parts = sum_over_devices(dw)
    got_a = trade(inner, "inner")
    got_b = relay_out(outer, got_a)

    table = pl.pallas_call(
        table_kernel,
        grid=(1,),
        in_specs=[whole(field), whole(field), whole(sel.shape)],
        out_specs=whole(local_part),
        out_shape=shape_of(local_part),
        compiler_params=params(),
        cost_estimate=cost(3),
        name="face_table",
    )(merged, grad_pre, sel)
    got_c, table = relay_in(got_b, table)

    output, grad_state = pl.pallas_call(
        final_kernel,
        grid=(STEPS,),
        in_specs=[SMEM()]
        + [blocked(field)] * 4
        + [whole(local_part), whole(near), whole(near_far), whole(far), whole(mats_shape)]
        + [whole(spread.shape)],
        out_specs=[blocked(field), blocked(field)],
        out_shape=[shape_of(field), shape_of(field)],
        scratch_shapes=tap_scratch
        + [pltpu.VMEM((PB, 7 * C, CELLS), BF), pltpu.VMEM((PB, 7 * C, CELLS), BF)],
        compiler_params=params(),
        cost_estimate=cost(10),
        name="last_level",
    )(meta, merged, grad_pre, xs, zs, table, got_a, got_b, got_c, mats, spread)

    scale = 1.0 / math.sqrt(float(devices * SLOTS * CELLS))
    mat = shape_of((7, C, C), F32)
    grads = pl.pallas_call(
        functools.partial(weights_kernel, scale),
        out_shape=[mat, mat, mat],
        cost_estimate=cost(2),
        name="weight_sums",
    )(parts)
    return (output, grad_state, *grads)


def solution(mesh):
    in_specs = (
        P("patch", None, None),
        P(),
        P(),
        P(),
        P("patch", None, None),
        P(),
        P("patch", None),
        P("patch", None),
        P("patch"),
    )
    out_specs = (P("patch", None, None), P("patch", None, None), P(), P(), P())
    return jax.shard_map(
        on_device, mesh=mesh, in_specs=in_specs, out_specs=out_specs, check_vma=False
    )
```

time: 138 us -> 116 us (0.84)
  local copies, waits for them, and re-layouts: 12.5 us -> 1.93 us
  between operations: 6.82 us -> 0.78 us
  other arithmetic: 8.96 us -> 3.66 us
  waiting for transfers between devices: 16.7 us -> 18.7 us
    reshape x8 -> x0, local copies, waits for them, and re-layouts: 6.37 us -> none  [the longest x3 2.87 us: forward_matrix(): return weight.transpose(2, 0, 1).reshape(C, 7 * C)]
    ppermute x8, waiting for transfers between devices: 0.02 us -> 4.29 us  [trade(): return lax.ppermute(block, 'patch', pairs(kind, lax.axis_size('patch')))]
    ppermute x8, starting transfers between devices: 9.72 us -> 5.53 us  [trade(): return lax.ppermute(block, 'patch', pairs(kind, lax.axis_size('patch')))]
    ppermute x7, starting transfers between devices: 27.6 us -> 30.7 us  [sum_over_devices(): lax.ppermute(block, 'patch', [(i, i ^ mask) for i in range(devices)])]
    unnamed x26 -> x16, local copies, waits for them, and re-layouts: 4.86 us -> 1.91 us
    ppermute x7, waiting for transfers between devices: 16.7 us -> 14.4 us  [sum_over_devices(): lax.ppermute(block, 'patch', [(i, i ^ mask) for i in range(devices)])]
    select_n x2 -> x0, other arithmetic: 1.89 us -> none  [the longest x1 1.88 us: on_device(): trail_dst = jnp.where(trail, octant, 8)]
    reduce_sum x1 -> x0, other arithmetic: 1.41 us -> none  [on_device(): count_2 = jnp.sum(jnp.where(ranks == rank - 2, owner_count, 0))]
  transfers between devices with their start and end apart: 15 -> 15, of which waited for: 6 -> 10; matrix products, arithmetic and copies ran while one was open for 10% -> 1% of each run, Pallas kernels for 10% -> 19%
where the time goes in v2:
time: 116 us; the launch traced here: 115 us
  Pallas kernels  53.6 us (46%)
  starting transfers between devices  36.2 us (31%)
  waiting for transfers between devices  18.7 us (16%)
  other arithmetic  3.66 us (3%)
  local copies, waits for them, and re-layouts  1.93 us (2%)
    ppermute x7, starting transfers between devices, sum_over_devices(): lax.ppermute(block, 'patch', [(i, i ^ mask) for i in range(devices)])  30.7 us
    pallas_call x1, Pallas kernels, on_device(): pl.pallas_call(merge_kernel, grid=(STEPS,), in_specs=[SMEM()] + [blocked(...  15.4 us
    ppermute x7, waiting for transfers between devices, sum_over_devices(): lax.ppermute(block, 'patch', [(i, i ^ mask) for i in range(devices)])  14.4 us
    pallas_call x1, Pallas kernels, on_device(): pl.pallas_call(fine_kernel, grid=(STEPS,), in_specs=[SMEM(), blocked(fiel...  11 us
    pallas_call x1, Pallas kernels, on_device(): pl.pallas_call(prepare_kernel, grid=(1,), in_specs=[SMEM()] * 4 + [whole(...  8.22 us
    pallas_call x1, Pallas kernels, on_device(): pl.pallas_call(final_kernel, grid=(STEPS,), in_specs=[SMEM()] + [blocked(...  8.16 us
    ppermute x8, starting transfers between devices, trade(): return lax.ppermute(block, 'patch', pairs(kind, lax.axis_size('patch')))  5.53 us
    pallas_call x1, Pallas kernels, on_device(): pl.pallas_call(table_kernel, grid=(1,), in_specs=[whole(field), whole(fie...  5 us
  transfers between devices with their start and end apart: 15, of which 10 were waited for; matrix products, arithmetic and copies ran while one was open for 1% of the time, Pallas kernels for 19%

profile of v2, /device:TPU:0, one launch (start us, length us, event | category | flops | bytes accessed | tf_op | source)
XLA Modules:
  0.0 114.9 jit_solution(16892705105706312365)
XLA Ops:
  0.6 4.0 %face_rows.1 = (bf16[27,32,128]{2,1,0:T(8,128)(2,1)}, bf16[27,32,128]{2,1,0:T(8,128)(2,1)}) custom-call(s32[128]{0:T(128)} %counts.3, bf16[32,32,512]{2,1,0:T(8,128)(2,1)} %x_ref.1, bf16[32,32,512]{2,1,0:T(8,128)(2,1)} %z_ref.1, bf16[6,512,256]{2,1,0:T(8,128)(2,1)} %constant.10.clone.sel_ref), custom_call_target="tpu_custom_call" | custom-call | flops 4000000 | bytes 12000000 | tf_op jit(solution)/shard_map/face_rows/pallas_call | solution.py:551
  4.6 0.0 collective-permute-start
  4.6 1.7 %collective-permute-done.got_ref = bf16[27,32,128]{2,1,0:T(8,128)(2,1)S(1)} collective-permute-done((bf16[27,32,128]{2,1,0:T(8,128)(2,1)}, bf16[27,32,128]{2,1,0:T(8,128)(2,1)S(1)}, u32[]{:S(2)}, u32[]{:S(2)}) %collective-permute-start) | collective-permute-done | bytes 221216 | tf_op jit(solution)/shard_map/ppermute | solution.py:510
  6.3 1.0 pad_maximum_fusion
  7.4 0.7 collective-permute-start.1
  8.1 0.0 copy-done.3
  8.1 8.2 %prepare.1 = (s32[512]{0:T(512)}, bf16[32,32,512]{2,1,0:T(8,128)(2,1)}, bf16[32,32,512]{2,1,0:T(8,128)(2,1)}, bf16[6,32,224]{2,1,0:T(8,128)(2,1)}, bf16[219,32,128]{2,1,0:T(8,128)(2,1)}) custom-call(s32[128]{0:T(128)} %counts.3, s32[6,32]{1,0:T(8,128)} %bitcast.2, s32[6,32]{1,0:T(8,128)} %bitcast.3, s32[32]{0:T(128)} %octant.1, ...), custom_call_target="tpu_custom_call" | custom-call | flops 6000000 | bytes 18000000 | tf_op jit(solution)/shard_map/prepare/pallas_call | solution.py:565
  16.3 0.0 collective-permute-done.1.b_ref
  16.3 0.0 copy-start
  16.3 3.0 %collective-permute-start.2 = (bf16[8,32,128]{2,1,0:T(8,128)(2,1)S(1)}, bf16[8,32,128]{2,1,0:T(8,128)(2,1)S(1)}, u32[]{:S(2)}, u32[]{:S(2)}) collective-permute-start(bf16[8,32,128]{2,1,0:T(8,128)(2,1)S(1)} %slice.13), channel_id=1, source_target_pairs={{0,1},{2,3},{4,5},{6,7},{8,9},{10,11},{12,13},{14,15},{16,17},{18,... | collective-permute-start | bytes 196616 | tf_op jit(solution)/shard_map/ppermute | solution.py:510
  19.3 0.9 collective-permute-done.2.c_ref
  20.2 0.0 copy-done
  20.2 0.6 copy-done.6
  20.9 11.0 %fine_level.1 = (bf16[32,224,512]{2,1,0:T(8,128)(2,1)}, bf16[32,224,512]{2,1,0:T(8,128)(2,1)}, bf16[32,32,512]{2,1,0:T(8,128)(2,1)}, bf16[32,32,512]{2,1,0:T(8,1...) custom-call(s32[512]{0:T(512)} %get-tuple-element.37.meta, ...), custom_call_target="tpu_custom_call" | custom-call | flops 12000000 | bytes 36000000 | tf_op jit(solution)/shard_map/fine_level/pallas_call | solution.py:583
  31.8 0.4 collective-permute-start.3
  32.3 0.7 collective-permute-start.4
  32.9 0.5 collective-permute-done.3.pin_ref
  33.4 0.0 collective-permute-done.4.pout_ref
  33.4 0.6 copy-done.4
  34.0 0.0 copy-done.5
  34.0 15.4 %coarse_and_merge.1 = (bf16[32,32,512]{2,1,0:T(8,128)(2,1)}, bf16[32,32,512]{2,1,0:T(8,128)(2,1)}, f32[224,128]{1,0:T(8,128)}, bf16[27,32,128]{2,1,0:T(8,128)(2,1)}, bf16[27,32,128]{2,1,0:T(8,128)(2,1)}) custom-call(s32[512]{0:T(512)} %get-tuple-element.37.meta, bf16[32,224,512]{2,1,0:T(8,128)(2,1)} %get-tuple-element.43.ta_ref, ...), custom_call_target="tpu_custom_call" | custom-call | flops 14000000 | bytes 42000000 | tf_op jit(solution)/shard_map/coarse_and_merge/pallas_call | solution.py:603
  49.4 4.8 %collective-permute-start.8 = (f32[224,128]{1,0:T(8,128)}, f32[224,128]{1,0:T(8,128)S(1)}, u32[]{:S(2)}, u32[]{:S(2)}) collective-permute-start(f32[224,128]{1,0:T(8,128)} %get-tuple-element.59), channel_id=1, source_target_pairs={{0,1},{1,0},{2,3},{3,2},{4,5},{5,4},{6,7},{7,6},{8,9},{9,8},{10,11... | collective-permute-start | bytes 344072 | tf_op jit(solution)/shard_map/ppermute | solution.py:525
  54.3 1.2 %collective-permute-done.8 = f32[224,128]{1,0:T(8,128)S(1)} collective-permute-done((f32[224,128]{1,0:T(8,128)}, f32[224,128]{1,0:T(8,128)S(1)}, u32[]{:S(2)}, u32[]{:S(2)}) %collective-permute-start.8) | collective-permute-done | bytes 114720 | tf_op jit(solution)/shard_map/ppermute | solution.py:525
  55.4 0.9 add.21
  56.3 1.8 %collective-permute-start.9 = (f32[224,128]{1,0:T(8,128)S(1)}, f32[224,128]{1,0:T(8,128)S(1)}, u32[]{:S(2)}, u32[]{:S(2)}) collective-permute-start(f32[224,128]{1,0:T(8,128)S(1)} %add.21), channel_id=1, source_target_pairs={{0,2},{1,3},{2,0},{3,1},{4,6},{5,7},{6,4},{7,5},{8,10},{9,11},{10,... | collective-permute-start | bytes 344072 | tf_op jit(solution)/shard_map/ppermute | solution.py:525
  58.1 0.0 collective-permute-start.5
  58.1 3.7 %collective-permute-done.9 = f32[224,128]{1,0:T(8,128)S(1)} collective-permute-done((f32[224,128]{1,0:T(8,128)S(1)}, f32[224,128]{1,0:T(8,128)S(1)}, u32[]{:S(2)}, u32[]{:S(2)}) %collective-permute-start.9) | collective-permute-done | bytes 114720 | tf_op jit(solution)/shard_map/ppermute | solution.py:525
  61.9 5.0 %collective-permute-start.10 = (f32[224,128]{1,0:T(8,128)S(1)}, f32[224,128]{1,0:T(8,128)S(1)}, u32[]{:S(2)}, u32[]{:S(2)}) collective-permute-start(f32[224,128]{1,0:T(8,128)S(1)} %add.22), channel_id=1, source_target_pairs={{0,6},{1,7},{2,4},{3,5},{4,2},{5,3},{6,0},{7,1},{8,14},{9,15},{10,... | collective-permute-start | bytes 344072 | tf_op jit(solution)/shard_map/ppermute | solution.py:525
  66.8 0.0 collective-permute-done.5.a_ref
  66.8 2.8 %collective-permute-done.10 = f32[224,128]{1,0:T(8,128)S(1)} collective-permute-done((f32[224,128]{1,0:T(8,128)S(1)}, f32[224,128]{1,0:T(8,128)S(1)}, u32[]{:S(2)}, u32[]{:S(2)}) %collective-permute-start.10) | collective-permute-done | bytes 114720 | tf_op jit(solution)/shard_map/ppermute | solution.py:525
  69.7 3.0 %collective-permute-start.11 = (f32[224,128]{1,0:T(8,128)S(1)}, f32[224,128]{1,0:T(8,128)S(1)}, u32[]{:S(2)}, u32[]{:S(2)}) collective-permute-start(f32[224,128]{1,0:T(8,128)S(1)} %add.23), channel_id=1, source_target_pairs={{0,8},{1,9},{2,10},{3,11},{4,12},{5,13},{6,14},{7,15},{8,0},{9,1},... | collective-permute-start | bytes 344072 | tf_op jit(solution)/shard_map/ppermute | solution.py:525
  72.7 1.0 pad_maximum_fusion.1
  73.6 0.7 collective-permute-start.6
  74.3 1.1 collective-permute-done.11
  75.5 5.2 %collective-permute-start.12 = (f32[224,128]{1,0:T(8,128)S(1)}, f32[224,128]{1,0:T(8,128)S(1)}, u32[]{:S(2)}, u32[]{:S(2)}) collective-permute-start(f32[224,128]{1,0:T(8,128)S(1)} %add.24), channel_id=1, source_target_pairs={{0,24},{1,25},{2,26},{3,27},{4,28},{5,29},{6,30},{7,31},{8,16},{9,... | collective-permute-start | bytes 344072 | tf_op jit(solution)/shard_map/ppermute | solution.py:525
  80.7 2.8 %collective-permute-done.12 = f32[224,128]{1,0:T(8,128)S(1)} collective-permute-done((f32[224,128]{1,0:T(8,128)S(1)}, f32[224,128]{1,0:T(8,128)S(1)}, u32[]{:S(2)}, u32[]{:S(2)}) %collective-permute-start.12) | collective-permute-done | bytes 114720 | tf_op jit(solution)/shard_map/ppermute | solution.py:525
  83.5 8.1 %collective-permute-start.13 = (f32[224,128]{1,0:T(8,128)S(1)}, f32[224,128]{1,0:T(8,128)S(1)}, u32[]{:S(2)}, u32[]{:S(2)}) collective-permute-start(f32[224,128]{1,0:T(8,128)S(1)} %add.25), channel_id=1, source_target_pairs={{0,32},{1,33},{2,34},{3,35},{4,36},{5,37},{6,38},{7,39},{8,40},{9,... | collective-permute-start | bytes 344072 | tf_op jit(solution)/shard_map/ppermute | solution.py:525
  91.6 2.8 %collective-permute-done.13 = f32[224,128]{1,0:T(8,128)S(1)} collective-permute-done((f32[224,128]{1,0:T(8,128)S(1)}, f32[224,128]{1,0:T(8,128)S(1)}, u32[]{:S(2)}, u32[]{:S(2)}) %collective-permute-start.13) | collective-permute-done | bytes 114720 | tf_op jit(solution)/shard_map/ppermute | solution.py:525
  94.4 2.8 %collective-permute-start.14 = (f32[224,128]{1,0:T(8,128)S(1)}, f32[224,128]{1,0:T(8,128)S(1)}, u32[]{:S(2)}, u32[]{:S(2)}) collective-permute-start(f32[224,128]{1,0:T(8,128)S(1)} %add.26), channel_id=1, source_target_pairs={{0,96},{1,97},{2,98},{3,99},{4,100},{5,101},{6,102},{7,103},{8,104... | collective-permute-start | bytes 344072 | tf_op jit(solution)/shard_map/ppermute | solution.py:525
  97.2 5.0 %face_table.1.t_ref = bf16[192,32,128]{2,1,0:T(8,128)(2,1)} custom-call(bf16[32,32,512]{2,1,0:T(8,128)(2,1)} %get-tuple-element.51.v_ref, bf16[32,32,512]{2,1,0:T(8,128)(2,1)} %get-tuple-element.52.y_ref, bf16[6,512,256]{2,1,0:T(8,128)(2,1)} %constant.10.clone.sel_ref), custom_call_target="tpu_custom_call" | custom-call | flops 3000000 | bytes 9000000 | tf_op jit(solution)/shard_map/face_table/pallas_call | solution.py:631
  102.2 0.0 collective-permute-done.6.b_ref
  102.2 0.1 collective-permute-start.7
  102.3 1.2 %collective-permute-done.7.c_ref = bf16[8,32,128]{2,1,0:T(8,128)(2,1)S(1)} collective-permute-done((bf16[8,32,128]{2,1,0:T(8,128)(2,1)S(1)}, bf16[8,32,128]{2,1,0:T(8,128)(2,1)S(1)}, u32[]{:S(2)}, u32[]{:S(2)}) %collective-permute-start.7) | collective-permute-done | bytes 65568 | tf_op jit(solution)/shard_map/ppermute | solution.py:510
  103.5 0.6 copy-done.7
  104.2 8.2 %last_level.1 = (bf16[32,32,512]{2,1,0:T(8,128)(2,1)}, bf16[32,32,512]{2,1,0:T(8,128)(2,1)}) custom-call(s32[512]{0:T(512)} %get-tuple-element.37.meta, bf16[32,32,512]{2,1,0:T(8,128)(2,1)} %get-tuple-element.51.v_ref, bf16[32,32,512]{2,1,0:T(8,128)(2,1)} %get-tuple-element.52.y_ref, bf16[32,32,512]{2,1,0:T(8,128)(2,1)} %get-tuple-element.38.xs, ...), custom_call_target="tpu_custom_call" | custom-call | flops 10000000 | bytes 30000000 | tf_op jit(solution)/shard_map/last_level/pallas_call | solution.py:643
  112.3 0.0 collective-permute-done.14
  112.3 0.7 add.27.parts_ref
  113.0 1.9 %weight_sums.1 = (f32[7,32,32]{2,1,0:T(8,128)}, f32[7,32,32]{2,1,0:T(8,128)}, f32[7,32,32]{2,1,0:T(8,128)}) custom-call(f32[224,128]{1,0:T(8,128)} %add.27.parts_ref), custom_call_target="tpu_custom_call" | custom-call | flops 2000000 | bytes 6000000 | tf_op jit(solution)/shard_map/weight_sums/pallas_call | solution.py:661
  (18 shorter events, 0.1 us)
Async XLA Ops:
  4.6 1.7 %collective-permute-start = (bf16[27,32,128]{2,1,0:T(8,128)(2,1)}, bf16[27,32,128]{2,1,0:T(8,128)(2,1)S(1)}, u32[]{:S(2)}, u32[]{:S(2)}) collective-permute-start(bf16[27,32,128]{2,1,0:T(8,128)(2,1)} %get-tuple-element.35), channel_id=1, source_target_pairs={{0,1},{2,3},{4,5},{6,7},{8,9},{10,11},{12,13},{14,15},{16,17},{18,... | collective-permute-start | bytes 663560 | tf_op jit(solution)/shard_map/ppermute | solution.py:510
  6.3 1.7 %copy-start.3 = (bf16[27,32,128]{2,1,0:T(8,128)(2,1)}, bf16[27,32,128]{2,1,0:T(8,128)(2,1)S(1)}, u32[]{:S(2)}) copy-start(bf16[27,32,128]{2,1,0:T(8,128)(2,1)S(1)} %collective-permute-done.got_ref) | copy-start | bytes 663556
  7.4 8.9 %collective-permute-start.1 = (bf16[35,32,128]{2,1,0:T(8,128)(2,1)S(1)}, bf16[35,32,128]{2,1,0:T(8,128)(2,1)S(1)}, u32[]{:S(2)}, u32[]{:S(2)}) collective-permute-start(bf16[35,32,128]{2,1,0:T(8,128)(2,1)S(1)} %pad_maximum_fusion), channel_id=1, source_target_pairs={{1,2},{3,4},{5,6},{7,8},{9,10},{11,12},{13,14},{15,16},{17,18},{19... | collective-permute-start | bytes 860168 | tf_op jit(solution)/shard_map/ppermute | solution.py:510
  16.3 3.9 %copy-start = (bf16[35,32,128]{2,1,0:T(8,128)(2,1)}, bf16[35,32,128]{2,1,0:T(8,128)(2,1)S(1)}, u32[]{:S(2)}) copy-start(bf16[35,32,128]{2,1,0:T(8,128)(2,1)S(1)} %collective-permute-done.1.b_ref) | copy-start | bytes 860164
  16.3 3.9 %collective-permute-start.2 = (bf16[8,32,128]{2,1,0:T(8,128)(2,1)S(1)}, bf16[8,32,128]{2,1,0:T(8,128)(2,1)S(1)}, u32[]{:S(2)}, u32[]{:S(2)}) collective-permute-start(bf16[8,32,128]{2,1,0:T(8,128)(2,1)S(1)} %slice.13), channel_id=1, source_target_pairs={{0,1},{2,3},{4,5},{6,7},{8,9},{10,11},{12,13},{14,15},{16,17},{18,... | collective-permute-start | bytes 196616 | tf_op jit(solution)/shard_map/ppermute | solution.py:510
  20.2 0.6 copy-start.6
  31.8 1.5 %collective-permute-start.3 = (bf16[8,32,128]{2,1,0:T(8,128)(2,1)}, bf16[8,32,128]{2,1,0:T(8,128)(2,1)S(1)}, u32[]{:S(2)}, u32[]{:S(2)}) collective-permute-start(bf16[8,32,128]{2,1,0:T(8,128)(2,1)} %get-tuple-element.49), channel_id=1, source_target_pairs={{0,1},{2,3},{4,5},{6,7},{8,9},{10,11},{12,13},{14,15},{16,17},{18,... | collective-permute-start | bytes 196616 | tf_op jit(solution)/shard_map/ppermute | solution.py:510
  32.3 1.1 collective-permute-start.4
  33.4 0.6 copy-start.4
  33.4 0.6 copy-start.5
  49.4 6.0 %collective-permute-start.8 = (f32[224,128]{1,0:T(8,128)}, f32[224,128]{1,0:T(8,128)S(1)}, u32[]{:S(2)}, u32[]{:S(2)}) collective-permute-start(f32[224,128]{1,0:T(8,128)} %get-tuple-element.59), channel_id=1, source_target_pairs={{0,1},{1,0},{2,3},{3,2},{4,5},{5,4},{6,7},{7,6},{8,9},{9,8},{10,11... | collective-permute-start | bytes 344072 | tf_op jit(solution)/shard_map/ppermute | solution.py:525
  56.3 5.5 %collective-permute-start.9 = (f32[224,128]{1,0:T(8,128)S(1)}, f32[224,128]{1,0:T(8,128)S(1)}, u32[]{:S(2)}, u32[]{:S(2)}) collective-permute-start(f32[224,128]{1,0:T(8,128)S(1)} %add.21), channel_id=1, source_target_pairs={{0,2},{1,3},{2,0},{3,1},{4,6},{5,7},{6,4},{7,5},{8,10},{9,11},{10,... | collective-permute-start | bytes 344072 | tf_op jit(solution)/shard_map/ppermute | solution.py:525
  58.1 8.7 %collective-permute-start.5 = (bf16[27,32,128]{2,1,0:T(8,128)(2,1)}, bf16[27,32,128]{2,1,0:T(8,128)(2,1)S(1)}, u32[]{:S(2)}, u32[]{:S(2)}) collective-permute-start(bf16[27,32,128]{2,1,0:T(8,128)(2,1)} %get-tuple-element.54), channel_id=1, source_target_pairs={{0,1},{2,3},{4,5},{6,7},{8,9},{10,11},{12,13},{14,15},{16,17},{18,... | collective-permute-start | bytes 663560 | tf_op jit(solution)/shard_map/ppermute | solution.py:510
  61.9 7.8 %collective-permute-start.10 = (f32[224,128]{1,0:T(8,128)S(1)}, f32[224,128]{1,0:T(8,128)S(1)}, u32[]{:S(2)}, u32[]{:S(2)}) collective-permute-start(f32[224,128]{1,0:T(8,128)S(1)} %add.22), channel_id=1, source_target_pairs={{0,6},{1,7},{2,4},{3,5},{4,2},{5,3},{6,0},{7,1},{8,14},{9,15},{10,... | collective-permute-start | bytes 344072 | tf_op jit(solution)/shard_map/ppermute | solution.py:525
  66.8 35.4 %copy-start.2 = (bf16[27,32,128]{2,1,0:T(8,128)(2,1)}, bf16[27,32,128]{2,1,0:T(8,128)(2,1)S(1)}, u32[]{:S(2)}) copy-start(bf16[27,32,128]{2,1,0:T(8,128)(2,1)S(1)} %collective-permute-done.5.a_ref) | copy-start | bytes 663556
  69.7 5.8 %collective-permute-start.11 = (f32[224,128]{1,0:T(8,128)S(1)}, f32[224,128]{1,0:T(8,128)S(1)}, u32[]{:S(2)}, u32[]{:S(2)}) collective-permute-start(f32[224,128]{1,0:T(8,128)S(1)} %add.23), channel_id=1, source_target_pairs={{0,8},{1,9},{2,10},{3,11},{4,12},{5,13},{6,14},{7,15},{8,0},{9,1},... | collective-permute-start | bytes 344072 | tf_op jit(solution)/shard_map/ppermute | solution.py:525
  73.6 28.5 %collective-permute-start.6 = (bf16[35,32,128]{2,1,0:T(8,128)(2,1)S(1)}, bf16[35,32,128]{2,1,0:T(8,128)(2,1)S(1)}, u32[]{:S(2)}, u32[]{:S(2)}) collective-permute-start(bf16[35,32,128]{2,1,0:T(8,128)(2,1)S(1)} %pad_maximum_fusion.1), channel_id=1, source_target_pairs={{1,2},{3,4},{5,6},{7,8},{9,10},{11,12},{13,14},{15,16},{17,18},{19... | collective-permute-start | bytes 860168 | tf_op jit(solution)/shard_map/ppermute | solution.py:510
  75.5 8.0 %collective-permute-start.12 = (f32[224,128]{1,0:T(8,128)S(1)}, f32[224,128]{1,0:T(8,128)S(1)}, u32[]{:S(2)}, u32[]{:S(2)}) collective-permute-start(f32[224,128]{1,0:T(8,128)S(1)} %add.24), channel_id=1, source_target_pairs={{0,24},{1,25},{2,26},{3,27},{4,28},{5,29},{6,30},{7,31},{8,16},{9,... | collective-permute-start | bytes 344072 | tf_op jit(solution)/shard_map/ppermute | solution.py:525
  83.5 10.9 %collective-permute-start.13 = (f32[224,128]{1,0:T(8,128)S(1)}, f32[224,128]{1,0:T(8,128)S(1)}, u32[]{:S(2)}, u32[]{:S(2)}) collective-permute-start(f32[224,128]{1,0:T(8,128)S(1)} %add.25), channel_id=1, source_target_pairs={{0,32},{1,33},{2,34},{3,35},{4,36},{5,37},{6,38},{7,39},{8,40},{9,... | collective-permute-start | bytes 344072 | tf_op jit(solution)/shard_map/ppermute | solution.py:525
  94.4 17.9 %collective-permute-start.14 = (f32[224,128]{1,0:T(8,128)S(1)}, f32[224,128]{1,0:T(8,128)S(1)}, u32[]{:S(2)}, u32[]{:S(2)}) collective-permute-start(f32[224,128]{1,0:T(8,128)S(1)} %add.26), channel_id=1, source_target_pairs={{0,96},{1,97},{2,98},{3,99},{4,100},{5,101},{6,102},{7,103},{8,104... | collective-permute-start | bytes 344072 | tf_op jit(solution)/shard_map/ppermute | solution.py:525
  102.2 1.4 %copy-start.1 = (bf16[35,32,128]{2,1,0:T(8,128)(2,1)}, bf16[35,32,128]{2,1,0:T(8,128)(2,1)S(1)}, u32[]{:S(2)}) copy-start(bf16[35,32,128]{2,1,0:T(8,128)(2,1)S(1)} %collective-permute-done.6.b_ref) | copy-start | bytes 860164
  102.2 1.3 %collective-permute-start.7 = (bf16[8,32,128]{2,1,0:T(8,128)(2,1)S(1)}, bf16[8,32,128]{2,1,0:T(8,128)(2,1)S(1)}, u32[]{:S(2)}, u32[]{:S(2)}) collective-permute-start(bf16[8,32,128]{2,1,0:T(8,128)(2,1)S(1)} %slice.15), channel_id=1, source_target_pairs={{0,1},{2,3},{4,5},{6,7},{8,9},{10,11},{12,13},{14,15},{16,17},{18,... | collective-permute-start | bytes 196616 | tf_op jit(solution)/shard_map/ppermute | solution.py:510
  103.5 0.6 copy-start.7

commit v3 on v2

--- a/solution.py
+++ b/solution.py
@@ -27,7 +27,7 @@
 BASE_B = BASE_A + NEAR
 BASE_C = BASE_B + NEAR + FAR
 ROWS = BASE_C + FAR
-VMEM_LIMIT = 56 * 1024 * 1024
+VMEM_LIMIT = 14 * 1024 * 1024
 IDX, TAG, DST, LEAD, TRAIL, SCAL = 0, 192, 384, 416, 448, 480
 N_COUNT, N_ODD, N_LAST, N_OWNED = SCAL, SCAL + 1, SCAL + 2, SCAL + 3
 META = 512
@@ -293,36 +293,36 @@
     ta_ref, tb_ref, hidden_ref, slope_ref, gm_ref, par_ref, inner_ref, outer_ref,
     table, coef, picked, par, ends,
 ):
-    step = pl.program_id(0)
-
-    @pl.when(step == 0)
-    def _():
-        join_table((t_ref, b_ref, c_ref), coef, table)
-        par[...] = jnp.zeros_like(par)
-        ends[...] = jnp.zeros_like(ends)
-
-    start = step * PB
-    block_taps(start, meta, xs, zs, spread_ref, table, coef, picked, ta_ref, tb_ref)
-    for p in range(PB):
-        hidden, slope = silu_pair(dot(mats[IN_F], ta_ref[p]))
-        hidden_ref[p] = hidden.astype(BF)
-        slope_ref[p] = slope.astype(BF)
-        gm_ref[p] = dot(mats[OUT_B], tb_ref[p]).astype(BF)
-    child = dot(hidden_ref[...].reshape(PB * C, CELLS), rest_ref[0])
-    child += dot(gm_ref[...].reshape(PB * C, CELLS), rest_ref[1])
-    child = child.astype(BF)
-    for p in range(PB):
-        row = child[p * C : (p + 1) * C]
-        par[meta[DST + start + p]] = row
-        ends[0, meta[LEAD + start + p]] = row
-        ends[1, meta[TRAIL + start + p]] = row
-
-    @pl.when(step == STEPS - 1)
-    def _():
-        par_ref[...] = par[: NPAR * 8]
-        odd = meta[N_ODD]
-        inner_ref[...] = ends[1 - odd, 0:8]
-        outer_ref[...] = ends[odd, 0:8]
+    join_table((t_ref, b_ref, c_ref), coef, table)
+    par[...] = jnp.zeros_like(par)
+    ends[...] = jnp.zeros_like(ends)
+
+    @pl.loop(0, STEPS)
+    def _(step):
+        start = step * PB
+        x_at, z_at, ta, tb, hidden_at, slope_at, gm_at = [
+            item.at[pl.ds(start, PB)]
+            for item in (xs, zs, ta_ref, tb_ref, hidden_ref, slope_ref, gm_ref)
+        ]
+        block_taps(start, meta, x_at, z_at, spread_ref, table, coef, picked, ta, tb)
+        for p in range(PB):
+            hidden, slope = silu_pair(dot(mats[IN_F], ta[p]))
+            hidden_at[p] = hidden.astype(BF)
+            slope_at[p] = slope.astype(BF)
+            gm_at[p] = dot(mats[OUT_B], tb[p]).astype(BF)
+        child = dot(hidden_at[...].reshape(PB * C, CELLS), rest_ref[0])
+        child += dot(gm_at[...].reshape(PB * C, CELLS), rest_ref[1])
+        child = child.astype(BF)
+        for p in range(PB):
+            row = child[p * C : (p + 1) * C]
+            par[meta[DST + start + p]] = row
+            ends[0, meta[LEAD + start + p]] = row
+            ends[1, meta[TRAIL + start + p]] = row
+
+    par_ref[...] = par[: NPAR * 8]
+    odd = meta[N_ODD]
+    inner_ref[...] = ends[1 - odd, 0:8]
+    outer_ref[...] = ends[odd, 0:8]
 
 
 def coarse_level(meta, par_ref, inner_ref, outer_ref, wa, wb, place_ref, par, taps, up_rows, dw_ref):
@@ -406,40 +406,37 @@
     merged_ref, gpa_ref, dw_ref, inner_ref, outer_ref,
     par, taps, up_rows, picked, v_rows, y_rows, sides,
 ):
-    step = pl.program_id(0)
-
-    @pl.when(step == 0)
-    def _():
-        dw_ref[...] = jnp.zeros_like(dw_ref)
-        coarse_level(
-            meta, par_ref, pin_ref, pout_ref, mats[CO_F], mats[CO_B],
-            place_ref, par, taps, up_rows, dw_ref,
-        )
-
-    start = step * PB
-    for p in range(PB):
-        picked[p] = up_rows[meta[DST + start + p]]
-    spread = dot(picked[...].reshape(PB * C, 128), up_ref[...])
-    dw_in = jnp.zeros((7 * C, C), F32)
-    dw_out = jnp.zeros((7 * C, C), F32)
-    for p in range(PB):
-        rows = slice(p * C, (p + 1) * C)
-        merged = (hidden_ref[p].astype(F32) + spread[rows, :CELLS]).astype(BF)
-        grad = gm_ref[p].astype(F32) + spread[rows, CELLS:] * 0.125
-        gpa = (grad * slope_ref[p].astype(F32)).astype(BF)
-        merged_ref[start + p] = merged
-        gpa_ref[start + p] = gpa
-        dw_in += dot_nt(ta_ref[p], gpa)
-        dw_out += dot_nt(tb_ref[p], merged)
-    dw_ref[:, 0:C] += dw_in
-    dw_ref[:, C : 2 * C] += dw_out
-
-    @pl.when(step == STEPS - 1)
-    def _():
-        send_rows(
-            meta[N_COUNT], meta[N_ODD], merged_ref, gpa_ref, sel_ref,
-            v_rows, y_rows, sides, inner_ref, outer_ref,
-        )
+    dw_ref[...] = jnp.zeros_like(dw_ref)
+    coarse_level(
+        meta, par_ref, pin_ref, pout_ref, mats[CO_F], mats[CO_B],
+        place_ref, par, taps, up_rows, dw_ref,
+    )
+
+    @pl.loop(0, STEPS)
+    def _(step):
+        start = step * PB
+        for p in range(PB):
+            picked[p] = up_rows[meta[DST + start + p]]
+        spread = dot(picked[...].reshape(PB * C, 128), up_ref[...])
+        dw_in = jnp.zeros((7 * C, C), F32)
+        dw_out = jnp.zeros((7 * C, C), F32)
+        for p in range(PB):
+            rows = slice(p * C, (p + 1) * C)
+            here = start + p
+            merged = (hidden_ref[here].astype(F32) + spread[rows, :CELLS]).astype(BF)
+            grad = gm_ref[here].astype(F32) + spread[rows, CELLS:] * 0.125
+            gpa = (grad * slope_ref[here].astype(F32)).astype(BF)
+            merged_ref[here] = merged
+            gpa_ref[here] = gpa
+            dw_in += dot_nt(ta_ref[here], gpa)
+            dw_out += dot_nt(tb_ref[here], merged)
+        dw_ref[:, 0:C] += dw_in
+        dw_ref[:, C : 2 * C] += dw_out
+
+    send_rows(
+        meta[N_COUNT], meta[N_ODD], merged_ref, gpa_ref, sel_ref,
+        v_rows, y_rows, sides, inner_ref, outer_ref,
+    )
 
 
 def final_kernel(
@@ -447,17 +444,17 @@
     out_ref, gs_ref,
     table, coef, picked, ta, tb,
 ):
-    step = pl.program_id(0)
-
-    @pl.when(step == 0)
-    def _():
-        join_table((t_ref, a_ref, b_ref, c_ref), coef, table)
-
-    start = step * PB
-    block_taps(start, meta, v_ref, y_ref, spread_ref, table, coef, picked, ta, tb)
-    for p in range(PB):
-        out_ref[p] = (xs[p].astype(F32) + dot(mats[OUT_F], ta[p])).astype(BF)
-        gs_ref[p] = (zs[p].astype(F32) + dot(mats[IN_B], tb[p])).astype(BF)
+    join_table((t_ref, a_ref, b_ref, c_ref), coef, table)
+
+    @pl.loop(0, STEPS)
+    def _(step):
+        start = step * PB
+        v_at, y_at = v_ref.at[pl.ds(start, PB)], y_ref.at[pl.ds(start, PB)]
+        block_taps(start, meta, v_at, y_at, spread_ref, table, coef, picked, ta, tb)
+        for p in range(PB):
+            here = start + p
+            out_ref[here] = (xs[here].astype(F32) + dot(mats[OUT_F], ta[p])).astype(BF)
+            gs_ref[here] = (zs[here].astype(F32) + dot(mats[IN_B], tb[p])).astype(BF)
 
 
 def weights_kernel(scale, parts_ref, in_ref, out_ref, co_ref):
@@ -472,20 +469,11 @@
 SMEM = functools.partial(pl.BlockSpec, memory_space=pltpu.SMEM)
 
 
-def whole(shape):
-    zeros = (0,) * len(shape)
-    return pl.BlockSpec(shape, lambda i: zeros)
-
-
-def blocked(shape):
-    rest = (0,) * (len(shape) - 1)
-    return pl.BlockSpec((PB,) + tuple(shape[1:]), lambda i: (i,) + rest)
+VMEM = functools.partial(pl.BlockSpec, memory_space=pltpu.VMEM)
 
 
 def params():
-    return pltpu.CompilerParams(
-        dimension_semantics=("arbitrary",), vmem_limit_bytes=VMEM_LIMIT
-    )
+    return pltpu.CompilerParams(vmem_limit_bytes=VMEM_LIMIT)
 
 
 def shape_of(shape, dtype=BF):
@@ -550,9 +538,8 @@
 
     inner, outer = pl.pallas_call(
         layers_kernel,
-        grid=(1,),
-        in_specs=[SMEM(), whole(field), whole(field), whole(sel.shape)],
-        out_specs=[whole(near), whole(near)],
+        in_specs=[SMEM(), VMEM(), VMEM(), VMEM()],
+        out_specs=[VMEM(), VMEM()],
         out_shape=[shape_of(near), shape_of(near)],
         scratch_shapes=rows_scratch,
         compiler_params=params(),
@@ -564,11 +551,10 @@
 
     meta, xs, zs, mats, table = pl.pallas_call(
         prepare_kernel,
-        grid=(1,),
         in_specs=[SMEM()] * 4
-        + [whole(near), whole(field), whole(field), whole(sel.shape)]
-        + [whole(weight_in.shape)] * 3,
-        out_specs=[SMEM(), whole(field), whole(field), whole(mats_shape), whole(first_part)],
+        + [VMEM(), VMEM(), VMEM(), VMEM()]
+        + [VMEM()] * 3,
+        out_specs=[SMEM(), VMEM(), VMEM(), VMEM(), VMEM()],
         out_shape=[shape_of((META,), jnp.int32), shape_of(field), shape_of(field)]
         + [shape_of(mats_shape), shape_of(first_part)],
         compiler_params=params(),
@@ -582,12 +568,11 @@
 
     taps_a, taps_b, hidden, slope, grad_merged, par, pin, pout = pl.pallas_call(
         fine_kernel,
-        grid=(STEPS,),
-        in_specs=[SMEM(), blocked(field), blocked(field)]
-        + [whole(first_part), whole(near_far), whole(far), whole(mats_shape)]
-        + [whole(spread.shape), whole(rest.shape)],
-        out_specs=[blocked(stack), blocked(stack), blocked(field), blocked(field), blocked(field)]
-        + [whole((NPAR * 8, C, 128)), whole(far), whole(far)],
+        in_specs=[SMEM(), VMEM(), VMEM()]
+        + [VMEM(), VMEM(), VMEM(), VMEM()]
+        + [VMEM(), VMEM()],
+        out_specs=[VMEM(), VMEM(), VMEM(), VMEM(), VMEM()]
+        + [VMEM(), VMEM(), VMEM()],
         out_shape=[shape_of(stack), shape_of(stack), shape_of(field), shape_of(field)]
         + [shape_of(field), shape_of((NPAR * 8, C, 128)), shape_of(far), shape_of(far)],
         scratch_shapes=tap_scratch
@@ -602,12 +587,11 @@
     dw_shape = (7 * C, 128)
     merged, grad_pre, dw, inner, outer = pl.pallas_call(
         merge_kernel,
-        grid=(STEPS,),
         in_specs=[SMEM()]
-        + [blocked(stack), blocked(stack), blocked(field), blocked(field), blocked(field)]
-        + [whole((NPAR * 8, C, 128)), whole(far), whole(far), whole(mats_shape)]
-        + [whole(place.shape), whole(up.shape), whole(sel.shape)],
-        out_specs=[whole(field), whole(field), whole(dw_shape), whole(near), whole(near)],
+        + [VMEM(), VMEM(), VMEM(), VMEM(), VMEM()]
+        + [VMEM(), VMEM(), VMEM(), VMEM()]
+        + [VMEM(), VMEM(), VMEM()],
+        out_specs=[VMEM(), VMEM(), VMEM(), VMEM(), VMEM()],
         out_shape=[shape_of(field), shape_of(field), shape_of(dw_shape, F32)]
         + [shape_of(near), shape_of(near)],
         scratch_shapes=[
@@ -630,9 +614,8 @@
 
     table = pl.pallas_call(
         table_kernel,
-        grid=(1,),
-        in_specs=[whole(field), whole(field), whole(sel.shape)],
-        out_specs=whole(local_part),
+        in_specs=[VMEM(), VMEM(), VMEM()],
+        out_specs=VMEM(),
         out_shape=shape_of(local_part),
         compiler_params=params(),
         cost_estimate=cost(3),
@@ -642,12 +625,11 @@
 
     output, grad_state = pl.pallas_call(
         final_kernel,
-        grid=(STEPS,),
         in_specs=[SMEM()]
-        + [blocked(field)] * 4
-        + [whole(local_part), whole(near), whole(near_far), whole(far), whole(mats_shape)]
-        + [whole(spread.shape)],
-        out_specs=[blocked(field), blocked(field)],
+        + [VMEM()] * 4
+        + [VMEM(), VMEM(), VMEM(), VMEM(), VMEM()]
+        + [VMEM()],
+        out_specs=[VMEM(), VMEM()],
         out_shape=[shape_of(field), shape_of(field)],
         scratch_shapes=tap_scratch
         + [pltpu.VMEM((PB, 7 * C, CELLS), BF), pltpu.VMEM((PB, 7 * C, CELLS), BF)],
@@ -660,6 +642,9 @@
     mat = shape_of((7, C, C), F32)
     grads = pl.pallas_call(
         functools.partial(weights_kernel, scale),
+        in_specs=[VMEM()],
+        out_specs=[VMEM()] * 3,
+        compiler_params=params(),
         out_shape=[mat, mat, mat],
         cost_estimate=cost(2),
         name="weight_sums",

time: 116 us -> 97 us (0.84)
  Pallas kernels: 53.6 us -> 34.7 us
  other arithmetic: 3.66 us -> 0.16 us
  local copies, waits for them, and re-layouts: 1.93 us -> 4.58 us
    pallas_call x7, Pallas kernels: 53.6 us -> 34.7 us  [the longest x1 9.78 us: on_device(): pl.pallas_call(merge_kernel, in_specs=[SMEM()] + [VMEM(), VMEM(), VMEM(),...]
    unnamed x16 -> x30, local copies, waits for them, and re-layouts: 1.91 us -> 4.56 us
    concatenate x2, other arithmetic: 2.01 us -> 0.05 us  [relay_out(): return trade(jnp.concatenate([outer, got_a[:FAR]], axis=0), 'outer')]
    add x7, other arithmetic: 1.65 us -> 0.1 us  [sum_over_devices(): block + lax.ppermute(block, 'patch', [(i, i ^ mask) for i in range(device...]
  transfers between devices with their start and end apart: 15 -> 15, of which waited for: 10 -> 10; matrix products, arithmetic and copies ran while one was open for 1% -> 0% of each run, Pallas kernels for 19% -> 15%
where the time goes in v3:
time: 97 us; the launch traced here: 95.7 us
  starting transfers between devices  36.4 us (38%)
  Pallas kernels  34.7 us (36%)
  waiting for transfers between devices  19 us (20%)
  local copies, waits for them, and re-layouts  4.58 us (5%)
    ppermute x7, starting transfers between devices, sum_over_devices(): lax.ppermute(block, 'patch', [(i, i ^ mask) for i in range(devices)])  30.7 us
    ppermute x7, waiting for transfers between devices, sum_over_devices(): lax.ppermute(block, 'patch', [(i, i ^ mask) for i in range(devices)])  15.1 us
    pallas_call x1, Pallas kernels, on_device(): pl.pallas_call(merge_kernel, in_specs=[SMEM()] + [VMEM(), VMEM(), VMEM(),...  9.78 us
    pallas_call x1, Pallas kernels, on_device(): pl.pallas_call(fine_kernel, in_specs=[SMEM(), VMEM(), VMEM()] + [VMEM(),...  7.44 us
    pallas_call x1, Pallas kernels, on_device(): pl.pallas_call(final_kernel, in_specs=[SMEM()] + [VMEM()] * 4 + [VMEM(),...  6.93 us
    pallas_call x1, Pallas kernels, on_device(): pl.pallas_call(prepare_kernel, in_specs=[SMEM()] * 4 + [VMEM(), VMEM(), V...  6.07 us
    ppermute x8, starting transfers between devices, trade(): return lax.ppermute(block, 'patch', pairs(kind, lax.axis_size('patch')))  5.62 us
    unnamed x30, local copies, waits for them, and re-layouts  4.56 us
  transfers between devices with their start and end apart: 15, of which 10 were waited for; matrix products, arithmetic and copies ran while one was open for 0% of the time, Pallas kernels for 15%

profile of v3, /device:TPU:0, one launch (start us, length us, event | category | flops | bytes accessed | tf_op | source)
XLA Modules:
  0.0 95.7 jit_solution(16285987104908015570)
XLA Ops:
  0.6 0.0 copy-start
  0.6 1.4 %copy-done = bf16[6,512,256]{2,1,0:T(8,128)(2,1)S(1)} copy-done((bf16[6,512,256]{2,1,0:T(8,128)(2,1)S(1)}, bf16[6,512,256]{2,1,0:T(8,128)(2,1)}, u32[]{:S(2)}) %copy-start) | copy-done | bytes 1572888
  2.0 1.2 %copy-done.2 = bf16[32,32,512]{2,1,0:T(8,128)(2,1)S(1)} copy-done((bf16[32,32,512]{2,1,0:T(8,128)(2,1)S(1)}, bf16[32,32,512]{2,1,0:T(8,128)(2,1)}, u32[]{:S(2)}) %copy-start.2) | copy-done | bytes 1048600
  3.3 1.2 %copy-done.3 = bf16[32,32,512]{2,1,0:T(8,128)(2,1)S(1)} copy-done((bf16[32,32,512]{2,1,0:T(8,128)(2,1)S(1)}, bf16[32,32,512]{2,1,0:T(8,128)(2,1)}, u32[]{:S(2)}) %copy-start.3) | copy-done | bytes 1048600
  4.5 0.7 copy-done.13
  5.2 0.0 copy-start.12
  5.2 0.0 copy-start.14
  5.2 1.7 %face_rows.1 = (bf16[27,32,128]{2,1,0:T(8,128)(2,1)S(1)}, bf16[27,32,128]{2,1,0:T(8,128)(2,1)S(1)}) custom-call(s32[128]{0:T(128)S(1)} %copy-done.13, bf16[32,32,512]{2,1,0:T(8,128)(2,1)S(1)} %copy-done.2, bf16[32,32,512]{2,1,0:T(8,128)(2,1)S(1)} %copy-done.3, bf16[6,512,256]{2,1,0:T(8,128)(2,1)S(1)} %copy-done), custom_call_target="tpu_custom_call" | custom-call | flops 4000000 | bytes 12000000 | tf_op jit(solution)/shard_map/face_rows/pallas_call | solution.py:539
  6.9 0.1 collective-permute-start
  7.0 1.5 %collective-permute-done.got_ref = bf16[27,32,128]{2,1,0:T(8,128)(2,1)S(1)} collective-permute-done((bf16[27,32,128]{2,1,0:T(8,128)(2,1)S(1)}, bf16[27,32,128]{2,1,0:T(8,128)(2,1)S(1)}, u32[]{:S(2)}, u32[]{:S(2)}) %collective-permute-start) | collective-permute-done | bytes 221216 | tf_op jit(solution)/shard_map/ppermute | solution.py:498
  8.5 0.7 collective-permute-start.1
  9.2 0.0 copy-done.8
  9.2 0.0 copy-start.4
  9.3 0.0 copy-start.7
  9.3 6.1 %prepare.1 = (s32[512]{0:T(512)S(1)}, bf16[32,32,512]{2,1,0:T(8,128)(2,1)S(1)}, bf16[32,32,512]{2,1,0:T(8,128)(2,1)S(1)}, bf16[6,32,224]{2,1,0:T(8,128)(2,1)S(1)}, bf16[219,32,128]{2,1,0:T(8,128)(2,1)S(1)}) custom-call(s32[128]{0:T(128)S(1)} %copy-done.13, s32[6,32]{1,0:T(8,128)S(1)} %bitcast.2, s32[6,32]{1,0:T(8,128)S(1)} %bitcast.3, s32[32]{0:T(128)S(1)} %copy-done.14, ...), custom_call_target="tpu_custom_call" | custom-call | flops 6000000 | bytes 18000000 | tf_op jit(solution)/shard_map/prepare/pallas_call | solution.py:552
  15.3 0.0 collective-permute-done.1.b_ref
  15.4 3.0 %collective-permute-start.2 = (bf16[8,32,128]{2,1,0:T(8,128)(2,1)S(1)}, bf16[8,32,128]{2,1,0:T(8,128)(2,1)S(1)}, u32[]{:S(2)}, u32[]{:S(2)}) collective-permute-start(bf16[8,32,128]{2,1,0:T(8,128)(2,1)S(1)} %slice.13), channel_id=1, source_target_pairs={{0,1},{2,3},{4,5},{6,7},{8,9},{10,11},{12,13},{14,15},{16,17},{18,... | collective-permute-start | bytes 196616 | tf_op jit(solution)/shard_map/ppermute | solution.py:498
  18.4 0.9 collective-permute-done.2.c_ref
  19.3 0.0 copy-start.6
  19.3 7.4 %fine_level.1 = (bf16[32,224,512]{2,1,0:T(8,128)(2,1)S(1)}, bf16[32,224,512]{2,1,0:T(8,128)(2,1)S(1)}, bf16[32,32,512]{2,1,0:T(8,128)(2,1)S(1)}, bf16[32,32,512]...) custom-call(s32[512]{0:T(512)S(1)} %get-tuple-element.37.meta, ...), custom_call_target="tpu_custom_call" | custom-call | flops 12000000 | bytes 36000000 | tf_op jit(solution)/shard_map/fine_level/pallas_call | solution.py:569
  26.8 0.4 collective-permute-start.3
  27.2 0.7 collective-permute-start.4
  27.8 0.2 collective-permute-done.3.pin_ref
  28.1 0.0 collective-permute-done.4.pout_ref
  28.1 9.8 %coarse_and_merge.1 = (bf16[32,32,512]{2,1,0:T(8,128)(2,1)S(1)}, bf16[32,32,512]{2,1,0:T(8,128)(2,1)S(1)}, f32[224,128]{1,0:T(8,128)S(1)}, bf16[27,32,128]{2,1,0:T(8,128)(2,1)S(1)}, bf16[27,32,128]{2,1,0:T(8,128)(2,1)S(1)}) custom-call(s32[512]{0:T(512)S(1)} %get-tuple-element.37.meta, bf16[32,224,512]{2,1,0:T(8,128)(2,1)S(1)} %get-tuple-element.43.ta_ref, ...), custom_call_target="tpu_custom_call" | custom-call | flops 14000000 | bytes 42000000 | tf_op jit(solution)/shard_map/coarse_and_merge/pallas_call | solution.py:588
  37.9 4.9 %collective-permute-start.8 = (f32[224,128]{1,0:T(8,128)S(1)}, f32[224,128]{1,0:T(8,128)S(1)}, u32[]{:S(2)}, u32[]{:S(2)}) collective-permute-start(f32[224,128]{1,0:T(8,128)S(1)} %get-tuple-element.59), channel_id=1, source_target_pairs={{0,1},{1,0},{2,3},{3,2},{4,5},{5,4},{6,7},{7,6},{8,9},{9,8},{10,11... | collective-permute-start | bytes 344072 | tf_op jit(solution)/shard_map/ppermute | solution.py:513
  42.8 1.0 %collective-permute-done.8 = f32[224,128]{1,0:T(8,128)S(1)} collective-permute-done((f32[224,128]{1,0:T(8,128)S(1)}, f32[224,128]{1,0:T(8,128)S(1)}, u32[]{:S(2)}, u32[]{:S(2)}) %collective-permute-start.8) | collective-permute-done | bytes 114720 | tf_op jit(solution)/shard_map/ppermute | solution.py:513
  43.8 1.8 %collective-permute-start.9 = (f32[224,128]{1,0:T(8,128)S(1)}, f32[224,128]{1,0:T(8,128)S(1)}, u32[]{:S(2)}, u32[]{:S(2)}) collective-permute-start(f32[224,128]{1,0:T(8,128)S(1)} %add.21), channel_id=1, source_target_pairs={{0,2},{1,3},{2,0},{3,1},{4,6},{5,7},{6,4},{7,5},{8,10},{9,11},{10,... | collective-permute-start | bytes 344072 | tf_op jit(solution)/shard_map/ppermute | solution.py:513
  45.6 0.0 collective-permute-start.5
  45.6 3.7 %collective-permute-done.9 = f32[224,128]{1,0:T(8,128)S(1)} collective-permute-done((f32[224,128]{1,0:T(8,128)S(1)}, f32[224,128]{1,0:T(8,128)S(1)}, u32[]{:S(2)}, u32[]{:S(2)}) %collective-permute-start.9) | collective-permute-done | bytes 114720 | tf_op jit(solution)/shard_map/ppermute | solution.py:513
  49.3 5.3 %collective-permute-start.10 = (f32[224,128]{1,0:T(8,128)S(1)}, f32[224,128]{1,0:T(8,128)S(1)}, u32[]{:S(2)}, u32[]{:S(2)}) collective-permute-start(f32[224,128]{1,0:T(8,128)S(1)} %add.22), channel_id=1, source_target_pairs={{0,6},{1,7},{2,4},{3,5},{4,2},{5,3},{6,0},{7,1},{8,14},{9,15},{10,... | collective-permute-start | bytes 344072 | tf_op jit(solution)/shard_map/ppermute | solution.py:513
  54.6 0.0 collective-permute-done.5.a_ref
  54.6 2.8 %collective-permute-done.10 = f32[224,128]{1,0:T(8,128)S(1)} collective-permute-done((f32[224,128]{1,0:T(8,128)S(1)}, f32[224,128]{1,0:T(8,128)S(1)}, u32[]{:S(2)}, u32[]{:S(2)}) %collective-permute-start.10) | collective-permute-done | bytes 114720 | tf_op jit(solution)/shard_map/ppermute | solution.py:513
  57.5 2.6 %collective-permute-start.11 = (f32[224,128]{1,0:T(8,128)S(1)}, f32[224,128]{1,0:T(8,128)S(1)}, u32[]{:S(2)}, u32[]{:S(2)}) collective-permute-start(f32[224,128]{1,0:T(8,128)S(1)} %add.23), channel_id=1, source_target_pairs={{0,8},{1,9},{2,10},{3,11},{4,12},{5,13},{6,14},{7,15},{8,0},{9,1},... | collective-permute-start | bytes 344072 | tf_op jit(solution)/shard_map/ppermute | solution.py:513
  60.1 0.7 collective-permute-start.6
  60.8 2.1 %collective-permute-done.11 = f32[224,128]{1,0:T(8,128)S(1)} collective-permute-done((f32[224,128]{1,0:T(8,128)S(1)}, f32[224,128]{1,0:T(8,128)S(1)}, u32[]{:S(2)}, u32[]{:S(2)}) %collective-permute-start.11) | collective-permute-done | bytes 114720 | tf_op jit(solution)/shard_map/ppermute | solution.py:513
  62.9 6.8 %collective-permute-start.12 = (f32[224,128]{1,0:T(8,128)S(1)}, f32[224,128]{1,0:T(8,128)S(1)}, u32[]{:S(2)}, u32[]{:S(2)}) collective-permute-start(f32[224,128]{1,0:T(8,128)S(1)} %add.24), channel_id=1, source_target_pairs={{0,24},{1,25},{2,26},{3,27},{4,28},{5,29},{6,30},{7,31},{8,16},{9,... | collective-permute-start | bytes 344072 | tf_op jit(solution)/shard_map/ppermute | solution.py:513
  69.7 2.8 %collective-permute-done.12 = f32[224,128]{1,0:T(8,128)S(1)} collective-permute-done((f32[224,128]{1,0:T(8,128)S(1)}, f32[224,128]{1,0:T(8,128)S(1)}, u32[]{:S(2)}, u32[]{:S(2)}) %collective-permute-start.12) | collective-permute-done | bytes 114720 | tf_op jit(solution)/shard_map/ppermute | solution.py:513
  72.5 6.3 %collective-permute-start.13 = (f32[224,128]{1,0:T(8,128)S(1)}, f32[224,128]{1,0:T(8,128)S(1)}, u32[]{:S(2)}, u32[]{:S(2)}) collective-permute-start(f32[224,128]{1,0:T(8,128)S(1)} %add.25), channel_id=1, source_target_pairs={{0,32},{1,33},{2,34},{3,35},{4,36},{5,37},{6,38},{7,39},{8,40},{9,... | collective-permute-start | bytes 344072 | tf_op jit(solution)/shard_map/ppermute | solution.py:513
  78.9 2.8 %collective-permute-done.13 = f32[224,128]{1,0:T(8,128)S(1)} collective-permute-done((f32[224,128]{1,0:T(8,128)S(1)}, f32[224,128]{1,0:T(8,128)S(1)}, u32[]{:S(2)}, u32[]{:S(2)}) %collective-permute-start.13) | collective-permute-done | bytes 114720 | tf_op jit(solution)/shard_map/ppermute | solution.py:513
  81.6 2.9 %collective-permute-start.14 = (f32[224,128]{1,0:T(8,128)S(1)}, f32[224,128]{1,0:T(8,128)S(1)}, u32[]{:S(2)}, u32[]{:S(2)}) collective-permute-start(f32[224,128]{1,0:T(8,128)S(1)} %add.26), channel_id=1, source_target_pairs={{0,96},{1,97},{2,98},{3,99},{4,100},{5,101},{6,102},{7,103},{8,104... | collective-permute-start | bytes 344072 | tf_op jit(solution)/shard_map/ppermute | solution.py:513
  84.6 1.8 %face_table.1.t_ref = bf16[192,32,128]{2,1,0:T(8,128)(2,1)S(1)} custom-call(bf16[32,32,512]{2,1,0:T(8,128)(2,1)S(1)} %get-tuple-element.51.v_ref, bf16[32,32,512]{2,1,0:T(8,128)(2,1)S(1)} %get-tuple-element.52.y_ref, bf16[6,512,256]{2,1,0:T(8,128)(2,1)S(1)} %copy-done.1), custom_call_target="tpu_custom_call" | custom-call | flops 3000000 | bytes 9000000 | tf_op jit(solution)/shard_map/face_table/pallas_call | solution.py:615
  86.4 0.0 collective-permute-done.6.b_ref
  86.4 0.1 collective-permute-start.7
  86.5 1.2 %collective-permute-done.7.c_ref = bf16[8,32,128]{2,1,0:T(8,128)(2,1)S(1)} collective-permute-done((bf16[8,32,128]{2,1,0:T(8,128)(2,1)S(1)}, bf16[8,32,128]{2,1,0:T(8,128)(2,1)S(1)}, u32[]{:S(2)}, u32[]{:S(2)}) %collective-permute-start.7) | collective-permute-done | bytes 65568 | tf_op jit(solution)/shard_map/ppermute | solution.py:498
  87.7 6.9 %last_level.1 = (bf16[32,32,512]{2,1,0:T(8,128)(2,1)}, bf16[32,32,512]{2,1,0:T(8,128)(2,1)}) custom-call(s32[512]{0:T(512)S(1)} %get-tuple-element.37.meta, bf16[32,32,512]{2,1,0:T(8,128)(2,1)S(1)} %get-tuple-element.51.v_ref, bf16[32,32,512]{2,1,0:T(8,128)(2,1)S(1)} %get-tuple-element.52.y_ref, bf16[32,32,512]{2,1,0:T(8,128)(2,1)S(1)} %get-tuple-element.38.xs, ...), custom_call_target="tpu_custom_call" | custom-call | flops 10000000 | bytes 30000000 | tf_op jit(solution)/shard_map/last_level/pallas_call | solution.py:626
  94.7 0.0 collective-permute-done.14
  94.7 1.0 %weight_sums.1 = (f32[7,32,32]{2,1,0:T(8,128)}, f32[7,32,32]{2,1,0:T(8,128)}, f32[7,32,32]{2,1,0:T(8,128)}) custom-call(f32[224,128]{1,0:T(8,128)S(1)} %add.27.parts_ref), custom_call_target="tpu_custom_call" | custom-call | flops 2000000 | bytes 6000000 | tf_op jit(solution)/shard_map/weight_sums/pallas_call | solution.py:643
  (32 shorter events, 0.2 us)
Async XLA Ops:
  0.6 1.4 %copy-start = (bf16[6,512,256]{2,1,0:T(8,128)(2,1)S(1)}, bf16[6,512,256]{2,1,0:T(8,128)(2,1)}, u32[]{:S(2)}) copy-start(bf16[6,512,256]{2,1,0:T(8,128)(2,1)} %constant.10.clone.sel_ref) | copy-start | bytes 4718596
  2.0 1.2 %copy-start.2 = (bf16[32,32,512]{2,1,0:T(8,128)(2,1)S(1)}, bf16[32,32,512]{2,1,0:T(8,128)(2,1)}, u32[]{:S(2)}) copy-start(bf16[32,32,512]{2,1,0:T(8,128)(2,1)} %x_ref.1) | copy-start | bytes 3145732
  3.3 1.2 %copy-start.3 = (bf16[32,32,512]{2,1,0:T(8,128)(2,1)S(1)}, bf16[32,32,512]{2,1,0:T(8,128)(2,1)}, u32[]{:S(2)}) copy-start(bf16[32,32,512]{2,1,0:T(8,128)(2,1)} %z_ref.1) | copy-start | bytes 3145732
  4.5 0.7 copy-start.13
  5.2 4.0 %copy-start.8 = (bf16[7,32,32]{2,1,0:T(8,128)(2,1)S(1)}, bf16[7,32,32]{2,1,0:T(8,128)(2,1)}, u32[]{:S(2)}) copy-start(bf16[7,32,32]{2,1,0:T(8,128)(2,1)} %w_in.1) | copy-start | bytes 43012
  5.2 4.0 %copy-start.9 = (bf16[7,32,32]{2,1,0:T(8,128)(2,1)S(1)}, bf16[7,32,32]{2,1,0:T(8,128)(2,1)}, u32[]{:S(2)}) copy-start(bf16[7,32,32]{2,1,0:T(8,128)(2,1)} %w_out.1) | copy-start | bytes 43012
  5.2 4.1 %copy-start.10 = (bf16[7,32,32]{2,1,0:T(8,128)(2,1)S(1)}, bf16[7,32,32]{2,1,0:T(8,128)(2,1)}, u32[]{:S(2)}) copy-start(bf16[7,32,32]{2,1,0:T(8,128)(2,1)} %w_co.1) | copy-start | bytes 43012
  5.2 4.1 %copy-start.11 = (s32[32,6]{0,1:T(8,128)S(1)}, s32[32,6]{0,1:T(8,128)}, u32[]{:S(2)}) copy-start(s32[32,6]{0,1:T(8,128)} %param.20) | copy-start | bytes 2308
  5.2 4.1 %copy-start.12 = (s32[32,6]{0,1:T(8,128)S(1)}, s32[32,6]{0,1:T(8,128)}, u32[]{:S(2)}) copy-start(s32[32,6]{0,1:T(8,128)} %param.21) | copy-start | bytes 2308
  5.2 4.1 %copy-start.14 = (s32[32]{0:T(128)S(1)}, s32[32]{0:T(128)}, u32[]{:S(2)}) copy-start(s32[32]{0:T(128)} %octant.1) | copy-start | bytes 388
  6.9 1.6 %collective-permute-start = (bf16[27,32,128]{2,1,0:T(8,128)(2,1)S(1)}, bf16[27,32,128]{2,1,0:T(8,128)(2,1)S(1)}, u32[]{:S(2)}, u32[]{:S(2)}) collective-permute-start(bf16[27,32,128]{2,1,0:T(8,128)(2,1)S(1)} %get-tuple-element.35), channel_id=1, source_target_pairs={{0,1},{2,3},{4,5},{6,7},{8,9},{10,11},{12,13},{14,15},{16,17},{18,... | collective-permute-start | bytes 663560 | tf_op jit(solution)/shard_map/ppermute | solution.py:498
  8.5 6.8 %collective-permute-start.1 = (bf16[35,32,128]{2,1,0:T(8,128)(2,1)S(1)}, bf16[35,32,128]{2,1,0:T(8,128)(2,1)S(1)}, u32[]{:S(2)}, u32[]{:S(2)}) collective-permute-start(bf16[35,32,128]{2,1,0:T(8,128)(2,1)S(1)} %pad_maximum_fusion), channel_id=1, source_target_pairs={{1,2},{3,4},{5,6},{7,8},{9,10},{11,12},{13,14},{15,16},{17,18},{19... | collective-permute-start | bytes 860168 | tf_op jit(solution)/shard_map/ppermute | solution.py:498
  9.2 10.0 %copy-start.4 = (bf16[2,256,1024]{2,1,0:T(8,128)(2,1)S(1)}, bf16[2,256,1024]{2,1,0:T(8,128)(2,1)}, u32[]{:S(2)}) copy-start(bf16[2,256,1024]{2,1,0:T(8,128)(2,1)} %constant.11.clone.spread_ref) | copy-start | bytes 3145732
  9.3 10.0 %copy-start.7 = (bf16[2,512,128]{2,1,0:T(8,128)(2,1)S(1)}, bf16[2,512,128]{2,1,0:T(8,128)(2,1)}, u32[]{:S(2)}) copy-start(bf16[2,512,128]{2,1,0:T(8,128)(2,1)} %constant.12.clone.rest_ref) | copy-start | bytes 786436
  15.4 3.9 %collective-permute-start.2 = (bf16[8,32,128]{2,1,0:T(8,128)(2,1)S(1)}, bf16[8,32,128]{2,1,0:T(8,128)(2,1)S(1)}, u32[]{:S(2)}, u32[]{:S(2)}) collective-permute-start(bf16[8,32,128]{2,1,0:T(8,128)(2,1)S(1)} %slice.13), channel_id=1, source_target_pairs={{0,1},{2,3},{4,5},{6,7},{8,9},{10,11},{12,13},{14,15},{16,17},{18,... | collective-permute-start | bytes 196616 | tf_op jit(solution)/shard_map/ppermute | solution.py:498
  19.3 8.8 %copy-start.1 = (bf16[6,512,256]{2,1,0:T(8,128)(2,1)S(1)}, bf16[6,512,256]{2,1,0:T(8,128)(2,1)}, u32[]{:S(2)}) copy-start(bf16[6,512,256]{2,1,0:T(8,128)(2,1)} %constant.10.clone.sel_ref) | copy-start | bytes 4718596
  19.3 8.8 %copy-start.5 = (bf16[256,1024]{1,0:T(8,128)(2,1)S(1)}, bf16[256,1024]{1,0:T(8,128)(2,1)}, u32[]{:S(2)}) copy-start(bf16[256,1024]{1,0:T(8,128)(2,1)} %constant.14.clone.place_ref) | copy-start | bytes 1572868
  19.3 8.8 %copy-start.6 = (bf16[128,1024]{1,0:T(8,128)(2,1)S(1)}, bf16[128,1024]{1,0:T(8,128)(2,1)}, u32[]{:S(2)}) copy-start(bf16[128,1024]{1,0:T(8,128)(2,1)} %constant.13.clone.up_ref) | copy-start | bytes 786436
  26.8 1.3 %collective-permute-start.3 = (bf16[8,32,128]{2,1,0:T(8,128)(2,1)S(1)}, bf16[8,32,128]{2,1,0:T(8,128)(2,1)S(1)}, u32[]{:S(2)}, u32[]{:S(2)}) collective-permute-start(bf16[8,32,128]{2,1,0:T(8,128)(2,1)S(1)} %get-tuple-element.49), channel_id=1, source_target_pairs={{0,1},{2,3},{4,5},{6,7},{8,9},{10,11},{12,13},{14,15},{16,17},{18,... | collective-permute-start | bytes 196616 | tf_op jit(solution)/shard_map/ppermute | solution.py:498
  27.2 0.9 collective-permute-start.4
  37.9 5.9 %collective-permute-start.8 = (f32[224,128]{1,0:T(8,128)S(1)}, f32[224,128]{1,0:T(8,128)S(1)}, u32[]{:S(2)}, u32[]{:S(2)}) collective-permute-start(f32[224,128]{1,0:T(8,128)S(1)} %get-tuple-element.59), channel_id=1, source_target_pairs={{0,1},{1,0},{2,3},{3,2},{4,5},{5,4},{6,7},{7,6},{8,9},{9,8},{10,11... | collective-permute-start | bytes 344072 | tf_op jit(solution)/shard_map/ppermute | solution.py:513
  43.8 5.5 %collective-permute-start.9 = (f32[224,128]{1,0:T(8,128)S(1)}, f32[224,128]{1,0:T(8,128)S(1)}, u32[]{:S(2)}, u32[]{:S(2)}) collective-permute-start(f32[224,128]{1,0:T(8,128)S(1)} %add.21), channel_id=1, source_target_pairs={{0,2},{1,3},{2,0},{3,1},{4,6},{5,7},{6,4},{7,5},{8,10},{9,11},{10,... | collective-permute-start | bytes 344072 | tf_op jit(solution)/shard_map/ppermute | solution.py:513
  45.6 9.1 %collective-permute-start.5 = (bf16[27,32,128]{2,1,0:T(8,128)(2,1)S(1)}, bf16[27,32,128]{2,1,0:T(8,128)(2,1)S(1)}, u32[]{:S(2)}, u32[]{:S(2)}) collective-permute-start(bf16[27,32,128]{2,1,0:T(8,128)(2,1)S(1)} %get-tuple-element.54), channel_id=1, source_target_pairs={{0,1},{2,3},{4,5},{6,7},{8,9},{10,11},{12,13},{14,15},{16,17},{18,... | collective-permute-start | bytes 663560 | tf_op jit(solution)/shard_map/ppermute | solution.py:498
  49.3 8.2 %collective-permute-start.10 = (f32[224,128]{1,0:T(8,128)S(1)}, f32[224,128]{1,0:T(8,128)S(1)}, u32[]{:S(2)}, u32[]{:S(2)}) collective-permute-start(f32[224,128]{1,0:T(8,128)S(1)} %add.22), channel_id=1, source_target_pairs={{0,6},{1,7},{2,4},{3,5},{4,2},{5,3},{6,0},{7,1},{8,14},{9,15},{10,... | collective-permute-start | bytes 344072 | tf_op jit(solution)/shard_map/ppermute | solution.py:513
  57.5 5.4 %collective-permute-start.11 = (f32[224,128]{1,0:T(8,128)S(1)}, f32[224,128]{1,0:T(8,128)S(1)}, u32[]{:S(2)}, u32[]{:S(2)}) collective-permute-start(f32[224,128]{1,0:T(8,128)S(1)} %add.23), channel_id=1, source_target_pairs={{0,8},{1,9},{2,10},{3,11},{4,12},{5,13},{6,14},{7,15},{8,0},{9,1},... | collective-permute-start | bytes 344072 | tf_op jit(solution)/shard_map/ppermute | solution.py:513
  60.1 26.2 %collective-permute-start.6 = (bf16[35,32,128]{2,1,0:T(8,128)(2,1)S(1)}, bf16[35,32,128]{2,1,0:T(8,128)(2,1)S(1)}, u32[]{:S(2)}, u32[]{:S(2)}) collective-permute-start(bf16[35,32,128]{2,1,0:T(8,128)(2,1)S(1)} %pad_maximum_fusion.1), channel_id=1, source_target_pairs={{1,2},{3,4},{5,6},{7,8},{9,10},{11,12},{13,14},{15,16},{17,18},{19... | collective-permute-start | bytes 860168 | tf_op jit(solution)/shard_map/ppermute | solution.py:498
  62.9 9.6 %collective-permute-start.12 = (f32[224,128]{1,0:T(8,128)S(1)}, f32[224,128]{1,0:T(8,128)S(1)}, u32[]{:S(2)}, u32[]{:S(2)}) collective-permute-start(f32[224,128]{1,0:T(8,128)S(1)} %add.24), channel_id=1, source_target_pairs={{0,24},{1,25},{2,26},{3,27},{4,28},{5,29},{6,30},{7,31},{8,16},{9,... | collective-permute-start | bytes 344072 | tf_op jit(solution)/shard_map/ppermute | solution.py:513
  72.5 9.1 %collective-permute-start.13 = (f32[224,128]{1,0:T(8,128)S(1)}, f32[224,128]{1,0:T(8,128)S(1)}, u32[]{:S(2)}, u32[]{:S(2)}) collective-permute-start(f32[224,128]{1,0:T(8,128)S(1)} %add.25), channel_id=1, source_target_pairs={{0,32},{1,33},{2,34},{3,35},{4,36},{5,37},{6,38},{7,39},{8,40},{9,... | collective-permute-start | bytes 344072 | tf_op jit(solution)/shard_map/ppermute | solution.py:513
  81.6 13.0 %collective-permute-start.14 = (f32[224,128]{1,0:T(8,128)S(1)}, f32[224,128]{1,0:T(8,128)S(1)}, u32[]{:S(2)}, u32[]{:S(2)}) collective-permute-start(f32[224,128]{1,0:T(8,128)S(1)} %add.26), channel_id=1, source_target_pairs={{0,96},{1,97},{2,98},{3,99},{4,100},{5,101},{6,102},{7,103},{8,104... | collective-permute-start | bytes 344072 | tf_op jit(solution)/shard_map/ppermute | solution.py:513
  86.4 1.3 %collective-permute-start.7 = (bf16[8,32,128]{2,1,0:T(8,128)(2,1)S(1)}, bf16[8,32,128]{2,1,0:T(8,128)(2,1)S(1)}, u32[]{:S(2)}, u32[]{:S(2)}) collective-permute-start(bf16[8,32,128]{2,1,0:T(8,128)(2,1)S(1)} %slice.15), channel_id=1, source_target_pairs={{0,1},{2,3},{4,5},{6,7},{8,9},{10,11},{12,13},{14,15},{16,17},{18,... | collective-permute-start | bytes 196616 | tf_op jit(solution)/shard_map/ppermute | solution.py:498

commit v4 on v3

--- a/solution.py
+++ b/solution.py
@@ -28,10 +28,14 @@
 BASE_C = BASE_B + NEAR + FAR
 ROWS = BASE_C + FAR
 VMEM_LIMIT = 14 * 1024 * 1024
-IDX, TAG, DST, LEAD, TRAIL, SCAL = 0, 192, 384, 416, 448, 480
+FULL_LIMIT = 60 * 1024 * 1024
+DST, LEAD, TRAIL, SCAL = 0, 32, 64, 96
 N_COUNT, N_ODD, N_LAST, N_OWNED = SCAL, SCAL + 1, SCAL + 2, SCAL + 3
-META = 512
-IN_F, OUT_B, OUT_F, IN_B, CO_F, CO_B = range(6)
+META = 128
+IN_F, OUT_B = range(2)
+OUT_F, IN_B, CO_F, CO_B = range(4)
+CHUNKS = 8
+DWR = 7
 
 
 def cell_coords():
@@ -133,10 +137,42 @@
     outer_ref[...] = sides[odd]
 
 
-def layers_kernel(counts, v_ref, y_ref, sel_ref, inner_ref, outer_ref, v_rows, y_rows, sides):
+def make_selection(sel_ref):
+    cell = lax.broadcasted_iota(jnp.int32, (CELLS, 256), 0)
+    lane = lax.broadcasted_iota(jnp.int32, (CELLS, 256), 1)
+    at = lane % 64
+    edge = jnp.where(lane < 128, 0, EDGE - 1)
+    first_half = lane % 128 < 64
+    for dim in range(3):
+        if dim == 0:
+            want = edge * 64 + at
+        elif dim == 1:
+            want = at // 8 * 64 + edge * 8 + at % 8
+        else:
+            want = at * 8 + edge
+        hit = cell == want
+        sel_ref[2 * dim] = jnp.where(hit & first_half, 1.0, 0.0).astype(BF)
+        sel_ref[2 * dim + 1] = jnp.where(hit & ~first_half, 1.0, 0.0).astype(BF)
+
+
+def layers_kernel(
+    counts_hbm, x_hbm, z_hbm, inner_ref, outer_ref,
+    v_rows, y_rows, sides, x_ref, z_ref, sel_ref, counts, sems, counts_sem,
+):
     rank = lax.axis_index("patch")
+    size = SLOTS // CHUNKS
+    copies = [pltpu.make_async_copy(counts_hbm, counts, counts_sem)]
+    for k in range(CHUNKS):
+        part = pl.ds(k * size, size)
+        copies.append(pltpu.make_async_copy(x_hbm.at[part], x_ref.at[part], sems.at[0, k]))
+        copies.append(pltpu.make_async_copy(z_hbm.at[part], z_ref.at[part], sems.at[1, k]))
+    for copy in copies:
+        copy.start()
+    make_selection(sel_ref)
+    for copy in copies:
+        copy.wait()
     send_rows(
-        counts[rank], rank % 2, v_ref, y_ref, sel_ref, v_rows, y_rows, sides, inner_ref, outer_ref
+        counts[rank], rank % 2, x_ref, z_ref, sel_ref, v_rows, y_rows, sides, inner_ref, outer_ref
     )
 
 
@@ -152,10 +188,17 @@
             ].reshape(SLOTS, C, 128)
 
 
+def fill_mats(mats, weights):
+    for k, (weight, turned) in enumerate(weights):
+        for f in range(7):
+            one = weight[f].astype(F32)
+            mats[k, :, f * C : (f + 1) * C] = (one.T if turned else one).astype(BF)
+
+
 def prepare_kernel(
-    counts, neighbour, level_tag, octant,
-    got_ref, x_ref, z_ref, sel_ref, w_in, w_out, w_co,
-    meta, xs, zs, mats, table,
+    counts, octant, neighbour, level_tag,
+    got_ref, x_ref, z_ref, sel_ref, w_in, w_out,
+    meta, index, xs, zs, mats, table,
 ):
     rank = lax.axis_index("patch")
     odd = rank % 2
@@ -173,53 +216,58 @@
     meta[N_ODD] = odd
     meta[N_LAST] = jnp.where(stop % 8 != 0, stop // 8 - first // 8, NPAR)
     meta[N_OWNED] = jnp.where(first % 8 == 0, 1, 0)
-    near_left = jnp.where(odd == 1, BASE_A, BASE_B)
-    near_right = jnp.where(odd == 1, BASE_B, BASE_A)
-    far_left = jnp.where(odd == 1, BASE_C, BASE_B + NEAR)
-    far_right = jnp.where(odd == 1, BASE_B + NEAR, BASE_C)
     lead_count = (8 - first % 8) % 8
-
-    def per_slot(p, carry):
+    for p in range(SLOTS):
         live = p < count
         parent = (first % 8 + p) // 8
         o = jnp.clip(octant[p], 0, 7)
         meta[DST + p] = jnp.where(live, parent * 8 + o, NPAR * 8)
         meta[LEAD + p] = jnp.where(live & (p < lead_count), o, 8)
         meta[TRAIL + p] = jnp.where(live & (p >= count - stop % 8), o, 8)
-        for face in range(6):
-            dim = face // 2
-            depth = MORTON[dim]
-            other = neighbour[face, p]
-            tag = level_tag[face, p]
-            away = other // SLOTS - rank
-            slot = other % SLOTS
-            if face % 2:
-                near = near_right + ROW0[dim] + slot
-                far = far_right + slot
-            else:
-                back = slot - (count_1 - depth)
-                near = near_left + ((back + 8) % 16 if dim == 2 else ROW0[dim] + back)
-                far = far_left + slot - (count_2 - 8)
-            row = jnp.where(away == 0, (face ^ 1) * SLOTS + slot, near)
-            row = jnp.where(jnp.abs(away) == 2, far, row)
-            row = jnp.where(tag == 1, face * SLOTS + p, row)
-            meta[IDX + face * SLOTS + p] = jnp.clip(row, 0, ROWS - 1)
-            meta[TAG + face * SLOTS + p] = tag
-        return carry
-
-    lax.fori_loop(0, SLOTS, per_slot, 0)
-    for k, (weight, turned) in enumerate(
-        ((w_in, True), (w_out, False), (w_out, True), (w_in, False), (w_co, True), (w_co, False))
-    ):
-        for f in range(7):
-            one = weight[f].astype(F32)
-            mats[k, :, f * C : (f + 1) * C] = (one.T if turned else one).astype(BF)
+
+    near_left = jnp.where(odd == 1, BASE_A, BASE_B)
+    near_right = jnp.where(odd == 1, BASE_B, BASE_A)
+    far_left = jnp.where(odd == 1, BASE_C, BASE_B + NEAR)
+    far_right = jnp.where(odd == 1, BASE_B + NEAR, BASE_C)
+    face = lax.broadcasted_iota(jnp.int32, (6, SLOTS), 0)
+    own = lax.broadcasted_iota(jnp.int32, (6, SLOTS), 1)
+    depth = jnp.where(face < 2, MORTON[0], jnp.where(face < 4, MORTON[1], MORTON[2]))
+    row0 = jnp.where(face < 2, ROW0[0], jnp.where(face < 4, ROW0[1], ROW0[2]))
+    high = (face & 1) == 1
+    other = neighbour[...]
+    away = (other >> 5) - rank
+    slot = other & 31
+    back = slot - (count_1 - depth)
+    left = jnp.where(face >= 4, (back + 8) & 15, row0 + back) + near_left
+    near = jnp.where(high, near_right + row0 + slot, left)
+    far = jnp.where(high, far_right + slot, far_left + slot - (count_2 - 8))
+    row = jnp.where(away == 0, (face ^ 1) * SLOTS + slot, near)
+    row = jnp.where((away == 2) | (away == -2), far, row)
+    row = jnp.where(level_tag[...] == 1, face * SLOTS + own, row)
+    index[0:6] = jnp.clip(row, 0, ROWS - 1)
+    index[6:12] = level_tag[...]
+
+    fill_mats(mats, ((w_in, True), (w_out, False)))
     for p in range(SLOTS):
         live = (p < count).astype(F32)
         xs[p] = (x_ref[p].astype(F32) * live).astype(BF)
         zs[p] = (z_ref[p].astype(F32) * live).astype(BF)
     fill_table(xs, zs, sel_ref, table)
     table[BASE_A:BASE_B] = got_ref[...]
+
+
+def window_kernel(hidden_ref, tb_ref, rest_ref, w_in, w_out, w_co, mats, dw_ref, means_ref):
+    fill_mats(mats, ((w_out, True), (w_in, False), (w_co, True), (w_co, False)))
+    dw_ref[...] = jnp.zeros_like(dw_ref)
+
+    @pl.loop(0, STEPS)
+    def _(step):
+        dw = jnp.zeros((7 * C, C), F32)
+        for p in range(PB):
+            here = step * PB + p
+            dw += dot_nt(tb_ref[here], hidden_ref[here])
+            means_ref[here] = dot(tb_ref[here], rest_ref[0]).astype(BF)
+        dw_ref[...] += dw
 
 
 def table_kernel(v_ref, y_ref, sel_ref, table):
@@ -241,7 +289,7 @@
                 coef[row, 1] = (high * (1 - t_high) + low * t_low).astype(BF)
 
 
-def block_taps(start, meta, v_ref, y_ref, spread_ref, table, coef, picked, ta, tb):
+def block_taps(start, index, v_ref, y_ref, spread_ref, table, coef, picked, ta, tb):
     for dim in range(3):
         low, high = 2 * dim, 2 * dim + 1
         edges = [on_face(low), on_face(high)]
@@ -249,8 +297,8 @@
         edges = [edge.astype(BF) for edge in edges]
         if dim:
             for p in range(PB):
-                picked[p, :, 0:128] = table[meta[IDX + low * SLOTS + start + p]]
-                picked[p, :, 128:256] = table[meta[IDX + high * SLOTS + start + p]]
+                picked[p, :, 0:128] = table[index[low, start + p]]
+                picked[p, :, 128:256] = table[index[high, start + p]]
             spread = dot(picked[...].reshape(PB * C, 256), spread_ref[dim - 1]).astype(BF)
         for p in range(PB):
             if dim:
@@ -258,8 +306,8 @@
                 v_edge = spread[rows, :CELLS]
                 y_edge = spread[rows, CELLS:]
             else:
-                r_low = table[meta[IDX + low * SLOTS + start + p]]
-                r_high = table[meta[IDX + high * SLOTS + start + p]]
+                r_low = table[index[low, start + p]]
+                r_high = table[index[high, start + p]]
                 blank = jnp.zeros((C, 256), BF)
                 v_edge = jnp.concatenate([r_low, blank, pltpu.roll(r_high, 64, 1)], axis=1)
                 y_edge = jnp.concatenate([pltpu.roll(r_low, 64, 1), blank, r_high], axis=1)
@@ -270,8 +318,8 @@
                 tb[p, 0:C] = other
             row = (
                 dim * 4
-                + meta[TAG + low * SLOTS + start + p] * 2
-                + meta[TAG + high * SLOTS + start + p]
+                + index[6 + low, start + p] * 2
+                + index[6 + high, start + p]
             )
             for k, face in enumerate((low, high)):
                 ta[p, C * (face + 1) : C * (face + 2)] = times(
@@ -289,7 +337,7 @@
 
 
 def fine_kernel(
-    meta, xs, zs, t_ref, b_ref, c_ref, mats, spread_ref, rest_ref,
+    meta, index, xs, zs, t_ref, b_ref, c_ref, mats, spread_ref, rest_ref,
     ta_ref, tb_ref, hidden_ref, slope_ref, gm_ref, par_ref, inner_ref, outer_ref,
     table, coef, picked, par, ends,
 ):
@@ -304,7 +352,7 @@
             item.at[pl.ds(start, PB)]
             for item in (xs, zs, ta_ref, tb_ref, hidden_ref, slope_ref, gm_ref)
         ]
-        block_taps(start, meta, x_at, z_at, spread_ref, table, coef, picked, ta, tb)
+        block_taps(start, index, x_at, z_at, spread_ref, table, coef, picked, ta, tb)
         for p in range(PB):
             hidden, slope = silu_pair(dot(mats[IN_F], ta[p]))
             hidden_at[p] = hidden.astype(BF)
@@ -401,12 +449,13 @@
 
 def merge_kernel(
     meta,
-    ta_ref, tb_ref, hidden_ref, slope_ref, gm_ref, par_ref, pin_ref, pout_ref,
+    ta_ref, means_ref, dw0_ref, hidden_ref, slope_ref, gm_ref, par_ref, pin_ref, pout_ref,
     mats, place_ref, up_ref, sel_ref,
-    merged_ref, gpa_ref, dw_ref, inner_ref, outer_ref,
-    par, taps, up_rows, picked, v_rows, y_rows, sides,
+    merged_ref, gpa_ref, sum_ref, inner_ref, outer_ref,
+    par, taps, up_rows, picked, v_rows, y_rows, sides, dw_ref,
 ):
     dw_ref[...] = jnp.zeros_like(dw_ref)
+    dw_ref[:, C : 2 * C] = dw0_ref[...]
     coarse_level(
         meta, par_ref, pin_ref, pout_ref, mats[CO_F], mats[CO_B],
         place_ref, par, taps, up_rows, dw_ref,
@@ -429,51 +478,78 @@
             merged_ref[here] = merged
             gpa_ref[here] = gpa
             dw_in += dot_nt(ta_ref[here], gpa)
-            dw_out += dot_nt(tb_ref[here], merged)
+            dw_out += dot_nt(means_ref[here], picked[p])
         dw_ref[:, 0:C] += dw_in
-        dw_ref[:, C : 2 * C] += dw_out
+        dw_ref[:, C : 2 * C] += dw_out * 8.0
 
     send_rows(
         meta[N_COUNT], meta[N_ODD], merged_ref, gpa_ref, sel_ref,
-        v_rows, y_rows, sides, inner_ref, outer_ref,
-    )
-
-
-def final_kernel(
-    meta, v_ref, y_ref, xs, zs, t_ref, a_ref, b_ref, c_ref, mats, spread_ref,
-    out_ref, gs_ref,
-    table, coef, picked, ta, tb,
+        v_rows, y_rows, sides, inner_ref.at[0:NEAR], outer_ref,
+    )
+    rounded = dw_ref[...].astype(BF).reshape(DWR, C, 128)
+    sum_ref[...] = rounded
+    inner_ref[NEAR : NEAR + DWR] = rounded
+
+
+def second_table_kernel(v_ref, y_ref, sel_ref, got_ref, table):
+    fill_table(v_ref, y_ref, sel_ref, table)
+    table[BASE_A:BASE_B] = got_ref[0:NEAR]
+
+
+def final_body(step, index, v_ref, y_ref, xs, zs, mats, spread_ref, table, coef, out_hbm, gs_hbm,
+               picked, ta, tb, out_ref, gs_ref, sems):
+    start = step * PB
+    part = pl.ds(start, PB)
+    block_taps(
+        start, index, v_ref.at[part], y_ref.at[part], spread_ref, table, coef, picked, ta, tb
+    )
+    for p in range(PB):
+        out_ref[p] = (xs[start + p].astype(F32) + dot(mats[OUT_F], ta[p])).astype(BF)
+        gs_ref[p] = (zs[start + p].astype(F32) + dot(mats[IN_B], tb[p])).astype(BF)
+    copies = [
+        pltpu.make_async_copy(out_ref, out_hbm.at[part], sems.at[0]),
+        pltpu.make_async_copy(gs_ref, gs_hbm.at[part], sems.at[1]),
+    ]
+    for copy in copies:
+        copy.start()
+    for copy in copies:
+        copy.wait()
+
+
+def first_final_kernel(
+    index, v_ref, y_ref, xs, zs, mats, spread_ref, t_ref, b_ref, c_ref,
+    table, coef, out_hbm, gs_hbm, *scratch,
 ):
-    join_table((t_ref, a_ref, b_ref, c_ref), coef, table)
-
-    @pl.loop(0, STEPS)
-    def _(step):
-        start = step * PB
-        v_at, y_at = v_ref.at[pl.ds(start, PB)], y_ref.at[pl.ds(start, PB)]
-        block_taps(start, meta, v_at, y_at, spread_ref, table, coef, picked, ta, tb)
-        for p in range(PB):
-            here = start + p
-            out_ref[here] = (xs[here].astype(F32) + dot(mats[OUT_F], ta[p])).astype(BF)
-            gs_ref[here] = (zs[here].astype(F32) + dot(mats[IN_B], tb[p])).astype(BF)
-
-
-def weights_kernel(scale, parts_ref, in_ref, out_ref, co_ref):
-    total = parts_ref[...] * scale
+    join_table((t_ref, b_ref, c_ref), coef, table)
+    final_body(0, index, v_ref, y_ref, xs, zs, mats, spread_ref, table, coef, out_hbm, gs_hbm,
+               *scratch)
+
+
+def next_final_kernel(
+    step, index, v_ref, y_ref, xs, zs, mats, spread_ref, table, coef, out_in, gs_in,
+    out_hbm, gs_hbm, *scratch,
+):
+    final_body(step, index, v_ref, y_ref, xs, zs, mats, spread_ref, table, coef, out_hbm, gs_hbm,
+               *scratch)
+
+
+def weights_kernel(scale, one_ref, two_ref, in_ref, out_ref, co_ref):
     for f in range(7):
-        rows = slice(f * C, (f + 1) * C)
-        in_ref[f] = total[rows, 0:C]
-        out_ref[f] = total[rows, C : 2 * C].T
-        co_ref[f] = total[rows, 2 * C : 3 * C]
+        total = (one_ref[f].astype(F32) + two_ref[f].astype(F32)) * scale
+        in_ref[f] = total[:, 0:C]
+        out_ref[f] = total[:, C : 2 * C].T
+        co_ref[f] = total[:, 2 * C : 3 * C]
 
 
 SMEM = functools.partial(pl.BlockSpec, memory_space=pltpu.SMEM)
 
 
 VMEM = functools.partial(pl.BlockSpec, memory_space=pltpu.VMEM)
-
-
-def params():
-    return pltpu.CompilerParams(vmem_limit_bytes=VMEM_LIMIT)
+HBM = functools.partial(pl.BlockSpec, memory_space=pltpu.HBM)
+
+
+def params(limit=VMEM_LIMIT):
+    return pltpu.CompilerParams(vmem_limit_bytes=limit)
 
 
 def shape_of(shape, dtype=BF):
@@ -507,11 +583,13 @@
     return trade(got_b[:FAR], "inner"), first
 
 
-def sum_over_devices(block):
+def add(one, two):
+    return (one.astype(F32) + two.astype(F32)).astype(BF)
+
+
+def swap(block, mask):
     devices = lax.axis_size("patch")
-    for mask in (1, 2, 6, 8, 24, 32, 96):
-        block = block + lax.ppermute(block, "patch", [(i, i ^ mask) for i in range(devices)])
-    return block
+    return lax.ppermute(block, "patch", [(i, i ^ mask) for i in range(devices)])
 
 
 def on_device(
@@ -524,131 +602,167 @@
     field = (SLOTS, C, CELLS)
     stack = (SLOTS, 7 * C, CELLS)
     near = (NEAR, C, 128)
-    near_far = (NEAR + FAR, C, 128)
     far = (FAR, C, 128)
-    mats_shape = (6, C, 7 * C)
-    first_part = (BASE_B, C, 128)
-    local_part = (BASE_A, C, 128)
+    par_rows = (NPAR * 8, C, 128)
+    sel_shape = (6, CELLS, 256)
     rows_scratch = [pltpu.VMEM((16, C, CELLS), BF)] * 2 + [pltpu.VMEM((2, NEAR, C, 128), BF)]
-    tap_scratch = [
-        pltpu.VMEM((ROWS, C, 128), BF),
-        pltpu.VMEM((12, 2, 16, CELLS), BF),
-        pltpu.VMEM((PB, C, 256), BF),
-    ]
+    table_shape = (ROWS, C, 128)
+    coef_shape = (12, 2, 16, CELLS)
+    picked_scratch = pltpu.VMEM((PB, C, 256), BF)
 
     inner, outer = pl.pallas_call(
         layers_kernel,
-        in_specs=[SMEM(), VMEM(), VMEM(), VMEM()],
-        out_specs=[VMEM(), VMEM()],
+        in_specs=[HBM()] * 3,
+        out_specs=[VMEM()] * 2,
         out_shape=[shape_of(near), shape_of(near)],
-        scratch_shapes=rows_scratch,
+        scratch_shapes=rows_scratch
+        + [pltpu.VMEM(field, BF), pltpu.VMEM(field, BF), pltpu.VMEM(sel_shape, BF)]
+        + [pltpu.SMEM(owner_count.shape, jnp.int32)]
+        + [pltpu.SemaphoreType.DMA((2, CHUNKS)), pltpu.SemaphoreType.DMA],
         compiler_params=params(),
         cost_estimate=cost(4),
         name="face_rows",
-    )(owner_count, fine_state, cotangent, sel)
+    )(
+        pltpu.with_memory_space_constraint(owner_count, pltpu.HBM),
+        pltpu.with_memory_space_constraint(fine_state, pltpu.HBM),
+        pltpu.with_memory_space_constraint(cotangent, pltpu.HBM),
+    )
     got_a = trade(inner, "inner")
     got_b = relay_out(outer, got_a)
 
-    meta, xs, zs, mats, table = pl.pallas_call(
+    meta, index, xs, zs, mats, table = pl.pallas_call(
         prepare_kernel,
-        in_specs=[SMEM()] * 4
-        + [VMEM(), VMEM(), VMEM(), VMEM()]
-        + [VMEM()] * 3,
-        out_specs=[SMEM(), VMEM(), VMEM(), VMEM(), VMEM()],
-        out_shape=[shape_of((META,), jnp.int32), shape_of(field), shape_of(field)]
-        + [shape_of(mats_shape), shape_of(first_part)],
+        in_specs=[SMEM()] * 2 + [VMEM()] * 8,
+        out_specs=[SMEM()] + [VMEM()] * 5,
+        out_shape=[shape_of((META,), jnp.int32), shape_of((12, SLOTS), jnp.int32)]
+        + [shape_of(field), shape_of(field), shape_of((2, C, 7 * C)), shape_of((BASE_B, C, 128))],
         compiler_params=params(),
-        cost_estimate=cost(6),
+        cost_estimate=cost(4),
         name="prepare",
     )(
-        owner_count, neighbour.T, level_tag.T, octant, got_a, fine_state, cotangent, sel,
-        weight_in, weight_out, weight_coarse,
+        owner_count, octant, neighbour.T, level_tag.T, got_a, fine_state, cotangent, sel,
+        weight_in, weight_out,
     )
     got_c, meta = relay_in(got_b, meta)
 
     taps_a, taps_b, hidden, slope, grad_merged, par, pin, pout = pl.pallas_call(
         fine_kernel,
-        in_specs=[SMEM(), VMEM(), VMEM()]
-        + [VMEM(), VMEM(), VMEM(), VMEM()]
-        + [VMEM(), VMEM()],
-        out_specs=[VMEM(), VMEM(), VMEM(), VMEM(), VMEM()]
-        + [VMEM(), VMEM(), VMEM()],
+        in_specs=[SMEM()] * 2 + [VMEM()] * 8,
+        out_specs=[VMEM()] * 8,
         out_shape=[shape_of(stack), shape_of(stack), shape_of(field), shape_of(field)]
-        + [shape_of(field), shape_of((NPAR * 8, C, 128)), shape_of(far), shape_of(far)],
-        scratch_shapes=tap_scratch
-        + [pltpu.VMEM((NPAR * 8 + 8, C, 128), BF), pltpu.VMEM((2, 16, C, 128), BF)],
+        + [shape_of(field), shape_of(par_rows), shape_of(far), shape_of(far)],
+        scratch_shapes=[
+            pltpu.VMEM(table_shape, BF),
+            pltpu.VMEM(coef_shape, BF),
+            picked_scratch,
+            pltpu.VMEM((NPAR * 8 + 8, C, 128), BF),
+            pltpu.VMEM((2, 16, C, 128), BF),
+        ],
         compiler_params=params(),
-        cost_estimate=cost(12),
+        cost_estimate=cost(8),
         name="fine_level",
-    )(meta, xs, zs, table, got_b, got_c, mats, spread, rest)
+    )(meta, index, xs, zs, table, got_b, got_c, mats, spread, rest)
     child_out = trade(pout, "outer")
     child_in = trade(pin, "inner")
 
-    dw_shape = (7 * C, 128)
-    merged, grad_pre, dw, inner, outer = pl.pallas_call(
+    mats, dw_part, means = pl.pallas_call(
+        window_kernel,
+        in_specs=[VMEM()] * 6,
+        out_specs=[VMEM()] * 3,
+        out_shape=[shape_of((4, C, 7 * C)), shape_of((7 * C, C), F32)]
+        + [shape_of((SLOTS, 7 * C, 128))],
+        compiler_params=params(),
+        cost_estimate=cost(3),
+        name="window",
+    )(hidden, taps_b, rest, weight_in, weight_out, weight_coarse)
+
+    merged, grad_pre, sums, inner, outer = pl.pallas_call(
         merge_kernel,
-        in_specs=[SMEM()]
-        + [VMEM(), VMEM(), VMEM(), VMEM(), VMEM()]
-        + [VMEM(), VMEM(), VMEM(), VMEM()]
-        + [VMEM(), VMEM(), VMEM()],
-        out_specs=[VMEM(), VMEM(), VMEM(), VMEM(), VMEM()],
-        out_shape=[shape_of(field), shape_of(field), shape_of(dw_shape, F32)]
-        + [shape_of(near), shape_of(near)],
+        in_specs=[SMEM()] + [VMEM()] * 13,
+        out_specs=[VMEM()] * 5,
+        out_shape=[shape_of(field), shape_of(field), shape_of((DWR, C, 128))]
+        + [shape_of((NEAR + DWR, C, 128)), shape_of(near)],
         scratch_shapes=[
             pltpu.VMEM((NPAR * 8 + 8, C, 128), BF),
             pltpu.VMEM((NPAR, 7 * C, CELLS), BF),
             pltpu.VMEM((NPAR * 8 + 8, C, 128), BF),
             pltpu.VMEM((PB, C, 128), BF),
         ]
-        + rows_scratch,
+        + rows_scratch
+        + [pltpu.VMEM((7 * C, 128), F32)],
         compiler_params=params(),
-        cost_estimate=cost(14),
+        cost_estimate=cost(9),
         name="coarse_and_merge",
     )(
-        meta, taps_a, taps_b, hidden, slope, grad_merged, par, child_in, child_out, mats,
+        meta, taps_a, means, dw_part, hidden, slope, grad_merged, par, child_in, child_out, mats,
         place, up, sel,
     )
-    parts = sum_over_devices(dw)
     got_a = trade(inner, "inner")
     got_b = relay_out(outer, got_a)
+    sums = add(sums, got_a[NEAR:])
+    sums = add(sums, swap(sums, 2))
 
     table = pl.pallas_call(
-        table_kernel,
-        in_specs=[VMEM(), VMEM(), VMEM()],
+        second_table_kernel,
+        in_specs=[VMEM()] * 4,
         out_specs=VMEM(),
-        out_shape=shape_of(local_part),
+        out_shape=shape_of((BASE_B, C, 128)),
         compiler_params=params(),
-        cost_estimate=cost(3),
+        cost_estimate=cost(2),
         name="face_table",
-    )(merged, grad_pre, sel)
+    )(merged, grad_pre, sel, got_a)
     got_c, table = relay_in(got_b, table)
 
-    output, grad_state = pl.pallas_call(
-        final_kernel,
-        in_specs=[SMEM()]
-        + [VMEM()] * 4
-        + [VMEM(), VMEM(), VMEM(), VMEM(), VMEM()]
-        + [VMEM()],
-        out_specs=[VMEM(), VMEM()],
-        out_shape=[shape_of(field), shape_of(field)],
-        scratch_shapes=tap_scratch
-        + [pltpu.VMEM((PB, 7 * C, CELLS), BF), pltpu.VMEM((PB, 7 * C, CELLS), BF)],
+    last_scratch = [
+        picked_scratch,
+        pltpu.VMEM((PB, 7 * C, CELLS), BF),
+        pltpu.VMEM((PB, 7 * C, CELLS), BF),
+        pltpu.VMEM((PB, C, CELLS), BF),
+        pltpu.VMEM((PB, C, CELLS), BF),
+        pltpu.SemaphoreType.DMA((2,)),
+    ]
+    fixed = (index, merged, grad_pre, xs, zs, mats, spread)
+    partner = swap(sums, 6)
+    table, coef, output, grad_state = pl.pallas_call(
+        first_final_kernel,
+        in_specs=[SMEM()] + [VMEM()] * 9,
+        out_specs=[VMEM(), VMEM(), HBM(), HBM()],
+        out_shape=[shape_of(table_shape), shape_of(coef_shape), shape_of(field), shape_of(field)],
+        scratch_shapes=last_scratch,
         compiler_params=params(),
-        cost_estimate=cost(10),
+        cost_estimate=cost(2),
         name="last_level",
-    )(meta, merged, grad_pre, xs, zs, table, got_a, got_b, got_c, mats, spread)
+    )(*fixed, table, got_b, got_c)
+    sums = add(sums, partner)
+    for step, mask in ((1, 8), (2, 24), (3, 32)):
+        sums, coef = lax.optimization_barrier((sums, coef))
+        partner = swap(sums, mask)
+        output, grad_state = pl.pallas_call(
+            functools.partial(next_final_kernel, step),
+            in_specs=[SMEM()] + [VMEM()] * 8 + [HBM(), HBM()],
+            out_specs=[HBM(), HBM()],
+            out_shape=[shape_of(field), shape_of(field)],
+            input_output_aliases={9: 0, 10: 1},
+            scratch_shapes=last_scratch,
+            compiler_params=params(),
+            cost_estimate=cost(2),
+            name="last_level",
+        )(*fixed, table, coef, output, grad_state)
+        sums = add(sums, partner)
+        sums, output = lax.optimization_barrier((sums, output))
+    partner = swap(sums, 96)
 
     scale = 1.0 / math.sqrt(float(devices * SLOTS * CELLS))
     mat = shape_of((7, C, C), F32)
     grads = pl.pallas_call(
         functools.partial(weights_kernel, scale),
-        in_specs=[VMEM()],
+        in_specs=[VMEM()] * 2,
         out_specs=[VMEM()] * 3,
         compiler_params=params(),
         out_shape=[mat, mat, mat],
-        cost_estimate=cost(2),
+        cost_estimate=cost(1),
         name="weight_sums",
-    )(parts)
+    )(sums, partner)
     return (output, grad_state, *grads)
 
 

time: 97 us -> 86.3 us (0.89); the launches traced: 95.7 us -> 86.1 us
  waiting for transfers between devices: 19 us -> 8.63 us
  Pallas kernels: 34.7 us -> 39.7 us
  local copies, waits for them, and re-layouts: 4.58 us -> 1.3 us
  starting transfers between devices: 36.4 us -> 35.2 us
    ppermute x7 -> x6, waiting for transfers between devices: 15.1 us -> 4.63 us  [swap(): return lax.ppermute(block, 'patch', [(i, i ^ mask) for i in range(devices)])]
    pallas_call x6 -> x10, Pallas kernels: 33.7 us -> 38.8 us  [the longest x1 8.17 us: on_device(): pl.pallas_call(merge_kernel, in_specs=[SMEM()] + [VMEM()] * 13, out_specs...]
    ppermute x7 -> x6, starting transfers between devices: 30.7 us -> 26.1 us  [swap(): return lax.ppermute(block, 'patch', [(i, i ^ mask) for i in range(devices)])]
    ppermute x8, starting transfers between devices: 5.62 us -> 9.08 us  [trade(): return lax.ppermute(block, 'patch', pairs(kind, lax.axis_size('patch')))]
    unnamed x30 -> x28, local copies, waits for them, and re-layouts: 4.56 us -> 1.28 us
  transfers between devices with their start and end apart: 15 -> 14, of which waited for: 10 -> 7; matrix products, arithmetic and copies ran while one was open for 0% -> 0% of each run, Pallas kernels for 15% -> 20%
where the time goes in v4:
time: 86.3 us; the launch traced here: 86.1 us
  Pallas kernels  39.7 us (46%)
  starting transfers between devices  35.2 us (41%)
  waiting for transfers between devices  8.63 us (10%)
  local copies, waits for them, and re-layouts  1.3 us (2%)
  between operations  1.04 us (1%)
    ppermute x6, starting transfers between devices, swap(): return lax.ppermute(block, 'patch', [(i, i ^ mask) for i in range(devices)])  26.1 us
    ppermute x8, starting transfers between devices, trade(): return lax.ppermute(block, 'patch', pairs(kind, lax.axis_size('patch')))  9.08 us
    pallas_call x1, Pallas kernels, on_device(): pl.pallas_call(merge_kernel, in_specs=[SMEM()] + [VMEM()] * 13, out_specs...  8.17 us
    pallas_call x3, Pallas kernels, on_device(): pl.pallas_call(functools.partial(next_final_kernel, step), in_specs=[SMEM...  8 us
    pallas_call x1, Pallas kernels, on_device(): pl.pallas_call(fine_kernel, in_specs=[SMEM()] * 2 + [VMEM()] * 8, out_spe...  7.4 us
    pallas_call x1, Pallas kernels, on_device(): pl.pallas_call(window_kernel, in_specs=[VMEM()] * 6, out_specs=[VMEM()] *...  4.67 us
    ppermute x6, waiting for transfers between devices, swap(): return lax.ppermute(block, 'patch', [(i, i ^ mask) for i in range(devices)])  4.63 us
    ppermute x8, waiting for transfers between devices, trade(): return lax.ppermute(block, 'patch', pairs(kind, lax.axis_size('patch')))  4 us
  transfers between devices with their start and end apart: 14, of which 7 were waited for; matrix products, arithmetic and copies ran while one was open for 0% of the time, Pallas kernels for 20%

profile of v4, /device:TPU:0, one launch (start us, length us, event | category | flops | bytes accessed | tf_op | source)
XLA Modules:
  0.0 86.1 jit_solution(3441890008170387268)
XLA Ops:
  0.6 0.0 copy-start.1
  0.6 0.0 copy-start.12
  0.7 3.1 %face_rows.1 = (bf16[27,32,128]{2,1,0:T(8,128)(2,1)S(1)}, bf16[27,32,128]{2,1,0:T(8,128)(2,1)S(1)}) custom-call(s32[128]{0:T(128)} %counts.1, bf16[32,32,512]{2,1,0:T(8,128)(2,1)} %x_ref.1, bf16[32,32,512]{2,1,0:T(8,128)(2,1)} %z_ref.1), custom_call_target="tpu_custom_call" | custom-call | flops 4000000 | bytes 12000000 | tf_op jit(solution)/shard_map/face_rows/pallas_call | solution.py:613
  3.8 0.1 collective-permute-start
  3.9 1.5 %collective-permute-done.got_ref = bf16[27,32,128]{2,1,0:T(8,128)(2,1)S(1)} collective-permute-done((bf16[27,32,128]{2,1,0:T(8,128)(2,1)S(1)}, bf16[27,32,128]{2,1,0:T(8,128)(2,1)S(1)}, u32[]{:S(2)}, u32[]{:S(2)}) %collective-permute-start) | collective-permute-done | bytes 221216 | tf_op jit(solution)/shard_map/ppermute | solution.py:574
  5.4 0.7 collective-permute-start.1
  6.1 0.0 copy-start.3
  6.2 1.2 %copy-done.3 = bf16[32,32,512]{2,1,0:T(8,128)(2,1)S(1)} copy-done((bf16[32,32,512]{2,1,0:T(8,128)(2,1)S(1)}, bf16[32,32,512]{2,1,0:T(8,128)(2,1)}, u32[]{:S(2)}) %copy-start.3) | copy-done | bytes 1048600
  7.4 2.9 %prepare.1 = (s32[128]{0:T(128)S(1)}, s32[12,32]{1,0:T(8,128)S(1)}, bf16[32,32,512]{2,1,0:T(8,128)(2,1)S(1)}, bf16[32,32,512]{2,1,0:T(8,128)(2,1)S(1)}, bf16[2,3...) custom-call(s32[128]{0:T(128)S(1)} %copy-done.12, s32[32]{0:T(128)S(1)} %copy-done.13, s32[6,32]{1,0:T(8,128)S(1)} %bitcast.2, ...), custom_call_target="tpu_custom_call" | custom-call | flops 4000000 | bytes 12000000 | tf_op jit(solution)/shard_map/prepare/pallas_call | solution.py:633
  10.3 0.0 collective-permute-done.1.b_ref
  10.3 3.2 %collective-permute-start.2 = (bf16[8,32,128]{2,1,0:T(8,128)(2,1)S(1)}, bf16[8,32,128]{2,1,0:T(8,128)(2,1)S(1)}, u32[]{:S(2)}, u32[]{:S(2)}) collective-permute-start(bf16[8,32,128]{2,1,0:T(8,128)(2,1)S(1)} %slice.16), channel_id=1, source_target_pairs={{0,1},{2,3},{4,5},{6,7},{8,9},{10,11},{12,13},{14,15},{16,17},{18,... | collective-permute-start | bytes 196616 | tf_op jit(solution)/shard_map/ppermute | solution.py:574
  13.5 0.9 %collective-permute-done.2.c_ref = bf16[8,32,128]{2,1,0:T(8,128)(2,1)S(1)} collective-permute-done((bf16[8,32,128]{2,1,0:T(8,128)(2,1)S(1)}, bf16[8,32,128]{2,1,0:T(8,128)(2,1)S(1)}, u32[]{:S(2)}, u32[]{:S(2)}) %collective-permute-start.2) | collective-permute-done | bytes 65568 | tf_op jit(solution)/shard_map/ppermute | solution.py:574
  14.4 7.4 %fine_level.1 = (bf16[32,224,512]{2,1,0:T(8,128)(2,1)S(1)}, bf16[32,224,512]{2,1,0:T(8,128)(2,1)S(1)}, bf16[32,32,512]{2,1,0:T(8,128)(2,1)S(1)}, bf16[32,32,512]...) custom-call(s32[128]{0:T(128)S(1)} %get-tuple-element.61.meta, ...), custom_call_target="tpu_custom_call" | custom-call | flops 8000000 | bytes 24000000 | tf_op jit(solution)/shard_map/fine_level/pallas_call | solution.py:648
  21.8 0.4 collective-permute-start.3
  22.2 0.7 collective-permute-start.4
  22.9 0.0 copy-done.9
  22.9 0.0 copy-start.5
  22.9 0.0 copy-start.6
  22.9 4.7 %window.1 = (bf16[4,32,224]{2,1,0:T(8,128)(2,1)S(1)}, f32[224,32]{1,0:T(8,128)S(1)}, bf16[32,224,128]{2,1,0:T(8,128)(2,1)S(1)}) custom-call(bf16[32,32,512]{2,1,0:T(8,128)(2,1)S(1)} %get-tuple-element.69.hidden_ref, bf16[32,224,512]{2,1,0:T(8,128)(2,1)S(1)} %get-tuple-element.70.tb_ref, bf16[2,512,128]{2,1,0:T(8,128)(2,1)S(1)} %copy-done.4, ...), custom_call_target="tpu_custom_call" | custom-call | flops 3000000 | bytes 9000000 | tf_op jit(solution)/shard_map/window/pallas_call | solution.py:668
  27.6 0.0 collective-permute-done.3.pin_ref
  27.6 0.0 collective-permute-done.4.pout_ref
  27.6 0.0 copy-done.5
  27.6 0.0 copy-done.6
  27.6 8.2 %coarse_and_merge.1 = (bf16[32,32,512]{2,1,0:T(8,128)(2,1)S(1)}, bf16[32,32,512]{2,1,0:T(8,128)(2,1)S(1)}, bf16[7,32,128]{2,1,0:T(8,128)(2,1)S(1)}, bf16[34,32,1...) custom-call(s32[128]{0:T(128)S(1)} %get-tuple-element.61.meta, bf16[32,224,512]{2,1,0:T(8,128)(2,1)S(1)} %get-tuple-element.68.ta_ref, ...), custom_call_target="tpu_custom_call" | custom-call | flops 9000000 | bytes 27000000 | tf_op jit(solution)/shard_map/coarse_and_merge/pallas_call | solution.py:679
  35.8 3.1 %collective-permute-start.5 = (bf16[34,32,128]{2,1,0:T(8,128)(2,1)S(1)}, bf16[34,32,128]{2,1,0:T(8,128)(2,1)S(1)}, u32[]{:S(2)}, u32[]{:S(2)}) collective-permute-start(bf16[34,32,128]{2,1,0:T(8,128)(2,1)S(1)} %get-tuple-element.80), channel_id=1, source_target_pairs={{0,1},{2,3},{4,5},{6,7},{8,9},{10,11},{12,13},{14,15},{16,17},{18,... | collective-permute-start | bytes 835592 | tf_op jit(solution)/shard_map/ppermute | solution.py:574
  38.9 1.2 %collective-permute-done.5.got_ref = bf16[34,32,128]{2,1,0:T(8,128)(2,1)S(1)} collective-permute-done((bf16[34,32,128]{2,1,0:T(8,128)(2,1)S(1)}, bf16[34,32,128]{2,1,0:T(8,128)(2,1)S(1)}, u32[]{:S(2)}, u32[]{:S(2)}) %collective-permute-start.5) | collective-permute-done | bytes 278560 | tf_op jit(solution)/shard_map/ppermute | solution.py:574
  40.1 1.6 %collective-permute-start.6 = (bf16[7,32,128]{2,1,0:T(8,128)(2,1)S(1)}, bf16[7,32,128]{2,1,0:T(8,128)(2,1)S(1)}, u32[]{:S(2)}, u32[]{:S(2)}) collective-permute-start(bf16[7,32,128]{2,1,0:T(8,128)(2,1)S(1)} %add_convert_fusion.5), channel_id=1, source_target_pairs={{0,2},{1,3},{2,0},{3,1},{4,6},{5,7},{6,4},{7,5},{8,10},{9,11},{10,... | collective-permute-start | bytes 172040 | tf_op jit(solution)/shard_map/ppermute | solution.py:592
  41.7 0.7 collective-permute-start.8
  42.4 2.0 %collective-permute-done.6 = bf16[7,32,128]{2,1,0:T(8,128)(2,1)S(1)} collective-permute-done((bf16[7,32,128]{2,1,0:T(8,128)(2,1)S(1)}, bf16[7,32,128]{2,1,0:T(8,128)(2,1)S(1)}, u32[]{:S(2)}, u32[]{:S(2)}) %collective-permute-start.6) | collective-permute-done | bytes 57376 | tf_op jit(solution)/shard_map/ppermute | solution.py:592
  44.4 5.1 %collective-permute-start.7 = (bf16[7,32,128]{2,1,0:T(8,128)(2,1)S(1)}, bf16[7,32,128]{2,1,0:T(8,128)(2,1)S(1)}, u32[]{:S(2)}, u32[]{:S(2)}) collective-permute-start(bf16[7,32,128]{2,1,0:T(8,128)(2,1)S(1)} %add_convert_fusion.4), channel_id=1, source_target_pairs={{0,6},{1,7},{2,4},{3,5},{4,2},{5,3},{6,0},{7,1},{8,14},{9,15},{10,... | collective-permute-start | bytes 172040 | tf_op jit(solution)/shard_map/ppermute | solution.py:592
  49.5 1.8 %face_table.1.t_ref = bf16[219,32,128]{2,1,0:T(8,128)(2,1)S(1)} custom-call(bf16[32,32,512]{2,1,0:T(8,128)(2,1)S(1)} %get-tuple-element.81.v_ref, bf16[32,32,512]{2,1,0:T(8,128)(2,1)S(1)} %get-tuple-element.82.y_ref, bf16[6,512,256]{2,1,0:T(8,128)(2,1)S(1)} %copy-done.1, bf16[34,32,128]{2,1,0:T(8,128)(2,1)S(1)} %collective-permute-done.5.got_ref), custom_call_target="tpu_custom_call" | custom-call | flops 2000000 | bytes 6000000 | tf_op jit(solution)/shard_map/face_table/pallas_call | solution.py:705
  51.3 0.0 collective-permute-done.8.b_ref
  51.3 0.4 collective-permute-start.9
  51.6 0.5 collective-permute-done.7
  52.2 0.4 collective-permute-done.9.c_ref
  52.6 2.8 %last_level.4 = (bf16[262,32,128]{2,1,0:T(8,128)(2,1)S(1)}, bf16[12,2,16,512]{3,2,1,0:T(8,128)(2,1)S(1)}, bf16[32,32,512]{2,1,0:T(8,128)(2,1)}, bf16[32,32,512]{2,1,0:T(8,128)(2,1)}) custom-call(s32[12,32]{1,0:T(8,128)S(1)} %get-tuple-element.62.index, bf16[32,32,512]{2,1,0:T(8,128)(2,1)S(1)} %get-tuple-element.81.v_ref, ...), custom_call_target="tpu_custom_call" | custom-call | flops 2000000 | bytes 6000000 | tf_op jit(solution)/shard_map/last_level/pallas_call | solution.py:726
  55.4 4.4 %collective-permute-start.10 = (bf16[7,32,128]{2,1,0:T(8,128)(2,1)S(1)}, bf16[7,32,128]{2,1,0:T(8,128)(2,1)S(1)}, u32[]{:S(2)}, u32[]{:S(2)}) collective-permute-start(bf16[7,32,128]{2,1,0:T(8,128)(2,1)S(1)} %add_convert_fusion.3), channel_id=1, source_target_pairs={{0,8},{1,9},{2,10},{3,11},{4,12},{5,13},{6,14},{7,15},{8,0},{9,1},... | collective-permute-start | bytes 172040 | tf_op jit(solution)/shard_map/ppermute | solution.py:592
  59.8 2.7 %last_level.5 = (bf16[32,32,512]{2,1,0:T(8,128)(2,1)}, bf16[32,32,512]{2,1,0:T(8,128)(2,1)}) custom-call(s32[12,32]{1,0:T(8,128)S(1)} %get-tuple-element.62.index, bf16[32,32,512]{2,1,0:T(8,128)(2,1)S(1)} %get-tuple-element.81.v_ref, bf16[32,32,512]{2,1,0:T(8,128)(2,1)S(1)} %get-tuple-element.82.y_ref, ...), custom_call_target="tpu_custom_call", output_to_operand_aliasing={{0}: (9, {}), {1}: (10, {})} | custom-call | flops 2000000 | bytes 6000000 | tf_op jit(solution)/shard_map/last_level/pallas_call | solution.py:740
  62.5 0.0 collective-permute-done.10
  62.5 4.4 %collective-permute-start.11 = (bf16[7,32,128]{2,1,0:T(8,128)(2,1)S(1)}, bf16[7,32,128]{2,1,0:T(8,128)(2,1)S(1)}, u32[]{:S(2)}, u32[]{:S(2)}) collective-permute-start(bf16[7,32,128]{2,1,0:T(8,128)(2,1)S(1)} %add_convert_fusion.2), channel_id=1, source_target_pairs={{0,24},{1,25},{2,26},{3,27},{4,28},{5,29},{6,30},{7,31},{8,16},{9,... | collective-permute-start | bytes 172040 | tf_op jit(solution)/shard_map/ppermute | solution.py:592
  67.0 2.7 %last_level.6 = (bf16[32,32,512]{2,1,0:T(8,128)(2,1)}, bf16[32,32,512]{2,1,0:T(8,128)(2,1)}) custom-call(s32[12,32]{1,0:T(8,128)S(1)} %get-tuple-element.62.index, bf16[32,32,512]{2,1,0:T(8,128)(2,1)S(1)} %get-tuple-element.81.v_ref, bf16[32,32,512]{2,1,0:T(8,128)(2,1)S(1)} %get-tuple-element.82.y_ref, ...), custom_call_target="tpu_custom_call", output_to_operand_aliasing={{0}: (9, {}), {1}: (10, {})} | custom-call | flops 2000000 | bytes 6000000 | tf_op jit(solution)/shard_map/last_level/pallas_call | solution.py:740
  69.6 0.0 collective-permute-done.11
  69.7 6.6 %collective-permute-start.12 = (bf16[7,32,128]{2,1,0:T(8,128)(2,1)S(1)}, bf16[7,32,128]{2,1,0:T(8,128)(2,1)S(1)}, u32[]{:S(2)}, u32[]{:S(2)}) collective-permute-start(bf16[7,32,128]{2,1,0:T(8,128)(2,1)S(1)} %add_convert_fusion.1), channel_id=1, source_target_pairs={{0,32},{1,33},{2,34},{3,35},{4,36},{5,37},{6,38},{7,39},{8,40},{9,... | collective-permute-start | bytes 172040 | tf_op jit(solution)/shard_map/ppermute | solution.py:592
  76.3 2.7 %last_level.7 = (bf16[32,32,512]{2,1,0:T(8,128)(2,1)}, bf16[32,32,512]{2,1,0:T(8,128)(2,1)}) custom-call(s32[12,32]{1,0:T(8,128)S(1)} %get-tuple-element.62.index, bf16[32,32,512]{2,1,0:T(8,128)(2,1)S(1)} %get-tuple-element.81.v_ref, bf16[32,32,512]{2,1,0:T(8,128)(2,1)S(1)} %get-tuple-element.82.y_ref, ...), custom_call_target="tpu_custom_call", output_to_operand_aliasing={{0}: (9, {}), {1}: (10, {})} | custom-call | flops 2000000 | bytes 6000000 | tf_op jit(solution)/shard_map/last_level/pallas_call | solution.py:740
  78.9 0.0 collective-permute-done.12
  79.0 4.0 %collective-permute-start.13 = (bf16[7,32,128]{2,1,0:T(8,128)(2,1)S(1)}, bf16[7,32,128]{2,1,0:T(8,128)(2,1)S(1)}, u32[]{:S(2)}, u32[]{:S(2)}) collective-permute-start(bf16[7,32,128]{2,1,0:T(8,128)(2,1)S(1)} %add_convert_fusion.one_ref), channel_id=1, source_target_pairs={{0,96},{1,97},{2,98},{3,99},{4,100},{5,101},{6,102},{7,103},{8,104... | collective-permute-start | bytes 172040 | tf_op jit(solution)/shard_map/ppermute | solution.py:592
  83.0 2.2 %collective-permute-done.13.two_ref = bf16[7,32,128]{2,1,0:T(8,128)(2,1)S(1)} collective-permute-done((bf16[7,32,128]{2,1,0:T(8,128)(2,1)S(1)}, bf16[7,32,128]{2,1,0:T(8,128)(2,1)S(1)}, u32[]{:S(2)}, u32[]{:S(2)}) %collective-permute-start.13) | collective-permute-done | bytes 57376 | tf_op jit(solution)/shard_map/ppermute | solution.py:592
  85.1 1.0 %weight_sums.1 = (f32[7,32,32]{2,1,0:T(8,128)}, f32[7,32,32]{2,1,0:T(8,128)}, f32[7,32,32]{2,1,0:T(8,128)}) custom-call(bf16[7,32,128]{2,1,0:T(8,128)(2,1)S(1)} %add_convert_fusion.one_ref, bf16[7,32,128]{2,1,0:T(8,128)(2,1)S(1)} %collective-permute-done.13.two_ref), custom_call_target="tpu_custom_call" | custom-call | flops 1000000 | bytes 3000000 | tf_op jit(solution)/shard_map/weight_sums/pallas_call | solution.py:757
  (31 shorter events, 0.2 us)
Async XLA Ops:
  0.6 5.4 %copy-start.1 = (bf16[6,512,256]{2,1,0:T(8,128)(2,1)S(1)}, bf16[6,512,256]{2,1,0:T(8,128)(2,1)}, u32[]{:S(2)}) copy-start(bf16[6,512,256]{2,1,0:T(8,128)(2,1)} %constant.10.clone.sel_ref) | copy-start | bytes 4718596
  0.6 5.4 %copy-start.12 = (s32[128]{0:T(128)S(1)}, s32[128]{0:T(128)}, u32[]{:S(2)}) copy-start(s32[128]{0:T(128)} %counts.1) | copy-start | bytes 1540
  0.7 5.4 %copy-start.2 = (bf16[32,32,512]{2,1,0:T(8,128)(2,1)S(1)}, bf16[32,32,512]{2,1,0:T(8,128)(2,1)}, u32[]{:S(2)}) copy-start(bf16[32,32,512]{2,1,0:T(8,128)(2,1)} %x_ref.1) | copy-start | bytes 3145732
  0.7 5.4 %copy-start.8 = (bf16[7,32,32]{2,1,0:T(8,128)(2,1)S(1)}, bf16[7,32,32]{2,1,0:T(8,128)(2,1)}, u32[]{:S(2)}) copy-start(bf16[7,32,32]{2,1,0:T(8,128)(2,1)} %w_out.3) | copy-start | bytes 43012
  0.7 5.4 %copy-start.7 = (bf16[7,32,32]{2,1,0:T(8,128)(2,1)S(1)}, bf16[7,32,32]{2,1,0:T(8,128)(2,1)}, u32[]{:S(2)}) copy-start(bf16[7,32,32]{2,1,0:T(8,128)(2,1)} %w_in.3) | copy-start | bytes 43012
  0.7 5.4 %copy-start.13 = (s32[32]{0:T(128)S(1)}, s32[32]{0:T(128)}, u32[]{:S(2)}) copy-start(s32[32]{0:T(128)} %octant.1) | copy-start | bytes 388
  0.7 5.4 %copy-start.11 = (s32[32,6]{0,1:T(8,128)S(1)}, s32[32,6]{0,1:T(8,128)}, u32[]{:S(2)}) copy-start(s32[32,6]{0,1:T(8,128)} %param.21) | copy-start | bytes 2308
  0.7 5.4 %copy-start.10 = (s32[32,6]{0,1:T(8,128)S(1)}, s32[32,6]{0,1:T(8,128)}, u32[]{:S(2)}) copy-start(s32[32,6]{0,1:T(8,128)} %param.20) | copy-start | bytes 2308
  3.8 1.6 %collective-permute-start = (bf16[27,32,128]{2,1,0:T(8,128)(2,1)S(1)}, bf16[27,32,128]{2,1,0:T(8,128)(2,1)S(1)}, u32[]{:S(2)}, u32[]{:S(2)}) collective-permute-start(bf16[27,32,128]{2,1,0:T(8,128)(2,1)S(1)} %get-tuple-element.59), channel_id=1, source_target_pairs={{0,1},{2,3},{4,5},{6,7},{8,9},{10,11},{12,13},{14,15},{16,17},{18,... | collective-permute-start | bytes 663560 | tf_op jit(solution)/shard_map/ppermute | solution.py:574
  5.4 4.9 %collective-permute-start.1 = (bf16[35,32,128]{2,1,0:T(8,128)(2,1)S(1)}, bf16[35,32,128]{2,1,0:T(8,128)(2,1)S(1)}, u32[]{:S(2)}, u32[]{:S(2)}) collective-permute-start(bf16[35,32,128]{2,1,0:T(8,128)(2,1)S(1)} %pad_maximum_fusion), channel_id=1, source_target_pairs={{1,2},{3,4},{5,6},{7,8},{9,10},{11,12},{13,14},{15,16},{17,18},{19... | collective-permute-start | bytes 860168 | tf_op jit(solution)/shard_map/ppermute | solution.py:574
  6.1 1.2 %copy-start.3 = (bf16[32,32,512]{2,1,0:T(8,128)(2,1)S(1)}, bf16[32,32,512]{2,1,0:T(8,128)(2,1)}, u32[]{:S(2)}) copy-start(bf16[32,32,512]{2,1,0:T(8,128)(2,1)} %z_ref.1) | copy-start | bytes 3145732
  7.4 7.0 %copy-start = (bf16[2,256,1024]{2,1,0:T(8,128)(2,1)S(1)}, bf16[2,256,1024]{2,1,0:T(8,128)(2,1)}, u32[]{:S(2)}) copy-start(bf16[2,256,1024]{2,1,0:T(8,128)(2,1)} %constant.11.clone.spread_ref) | copy-start | bytes 3145732
  7.4 7.0 %copy-start.4 = (bf16[2,512,128]{2,1,0:T(8,128)(2,1)S(1)}, bf16[2,512,128]{2,1,0:T(8,128)(2,1)}, u32[]{:S(2)}) copy-start(bf16[2,512,128]{2,1,0:T(8,128)(2,1)} %constant.12.clone.rest_ref) | copy-start | bytes 786436
  10.3 4.1 %collective-permute-start.2 = (bf16[8,32,128]{2,1,0:T(8,128)(2,1)S(1)}, bf16[8,32,128]{2,1,0:T(8,128)(2,1)S(1)}, u32[]{:S(2)}, u32[]{:S(2)}) collective-permute-start(bf16[8,32,128]{2,1,0:T(8,128)(2,1)S(1)} %slice.16), channel_id=1, source_target_pairs={{0,1},{2,3},{4,5},{6,7},{8,9},{10,11},{12,13},{14,15},{16,17},{18,... | collective-permute-start | bytes 196616 | tf_op jit(solution)/shard_map/ppermute | solution.py:574
  14.4 8.5 %copy-start.9 = (bf16[7,32,32]{2,1,0:T(8,128)(2,1)S(1)}, bf16[7,32,32]{2,1,0:T(8,128)(2,1)}, u32[]{:S(2)}) copy-start(bf16[7,32,32]{2,1,0:T(8,128)(2,1)} %w_co.1) | copy-start | bytes 43012
  21.8 5.8 %collective-permute-start.3 = (bf16[8,32,128]{2,1,0:T(8,128)(2,1)S(1)}, bf16[8,32,128]{2,1,0:T(8,128)(2,1)S(1)}, u32[]{:S(2)}, u32[]{:S(2)}) collective-permute-start(bf16[8,32,128]{2,1,0:T(8,128)(2,1)S(1)} %get-tuple-element.76), channel_id=1, source_target_pairs={{0,1},{2,3},{4,5},{6,7},{8,9},{10,11},{12,13},{14,15},{16,17},{18,... | collective-permute-start | bytes 196616 | tf_op jit(solution)/shard_map/ppermute | solution.py:574
  22.2 5.4 %collective-permute-start.4 = (bf16[8,32,128]{2,1,0:T(8,128)(2,1)S(1)}, bf16[8,32,128]{2,1,0:T(8,128)(2,1)S(1)}, u32[]{:S(2)}, u32[]{:S(2)}) collective-permute-start(bf16[8,32,128]{2,1,0:T(8,128)(2,1)S(1)} %get-tuple-element.77), channel_id=1, source_target_pairs={{1,2},{3,4},{5,6},{7,8},{9,10},{11,12},{13,14},{15,16},{17,18},{19... | collective-permute-start | bytes 196616 | tf_op jit(solution)/shard_map/ppermute | solution.py:574
  22.9 4.7 %copy-start.5 = (bf16[256,1024]{1,0:T(8,128)(2,1)S(1)}, bf16[256,1024]{1,0:T(8,128)(2,1)}, u32[]{:S(2)}) copy-start(bf16[256,1024]{1,0:T(8,128)(2,1)} %constant.14.clone.place_ref) | copy-start | bytes 1572868
  22.9 4.7 %copy-start.6 = (bf16[128,1024]{1,0:T(8,128)(2,1)S(1)}, bf16[128,1024]{1,0:T(8,128)(2,1)}, u32[]{:S(2)}) copy-start(bf16[128,1024]{1,0:T(8,128)(2,1)} %constant.13.clone.up_ref) | copy-start | bytes 786436
  35.8 4.2 %collective-permute-start.5 = (bf16[34,32,128]{2,1,0:T(8,128)(2,1)S(1)}, bf16[34,32,128]{2,1,0:T(8,128)(2,1)S(1)}, u32[]{:S(2)}, u32[]{:S(2)}) collective-permute-start(bf16[34,32,128]{2,1,0:T(8,128)(2,1)S(1)} %get-tuple-element.80), channel_id=1, source_target_pairs={{0,1},{2,3},{4,5},{6,7},{8,9},{10,11},{12,13},{14,15},{16,17},{18,... | collective-permute-start | bytes 835592 | tf_op jit(solution)/shard_map/ppermute | solution.py:574
  40.1 4.3 %collective-permute-start.6 = (bf16[7,32,128]{2,1,0:T(8,128)(2,1)S(1)}, bf16[7,32,128]{2,1,0:T(8,128)(2,1)S(1)}, u32[]{:S(2)}, u32[]{:S(2)}) collective-permute-start(bf16[7,32,128]{2,1,0:T(8,128)(2,1)S(1)} %add_convert_fusion.5), channel_id=1, source_target_pairs={{0,2},{1,3},{2,0},{3,1},{4,6},{5,7},{6,4},{7,5},{8,10},{9,11},{10,... | collective-permute-start | bytes 172040 | tf_op jit(solution)/shard_map/ppermute | solution.py:592
  41.7 9.6 %collective-permute-start.8 = (bf16[35,32,128]{2,1,0:T(8,128)(2,1)S(1)}, bf16[35,32,128]{2,1,0:T(8,128)(2,1)S(1)}, u32[]{:S(2)}, u32[]{:S(2)}) collective-permute-start(bf16[35,32,128]{2,1,0:T(8,128)(2,1)S(1)} %pad_maximum_fusion.1), channel_id=1, source_target_pairs={{1,2},{3,4},{5,6},{7,8},{9,10},{11,12},{13,14},{15,16},{17,18},{19... | collective-permute-start | bytes 860168 | tf_op jit(solution)/shard_map/ppermute | solution.py:574
  44.4 7.8 %collective-permute-start.7 = (bf16[7,32,128]{2,1,0:T(8,128)(2,1)S(1)}, bf16[7,32,128]{2,1,0:T(8,128)(2,1)S(1)}, u32[]{:S(2)}, u32[]{:S(2)}) collective-permute-start(bf16[7,32,128]{2,1,0:T(8,128)(2,1)S(1)} %add_convert_fusion.4), channel_id=1, source_target_pairs={{0,6},{1,7},{2,4},{3,5},{4,2},{5,3},{6,0},{7,1},{8,14},{9,15},{10,... | collective-permute-start | bytes 172040 | tf_op jit(solution)/shard_map/ppermute | solution.py:592
  51.3 1.3 %collective-permute-start.9 = (bf16[8,32,128]{2,1,0:T(8,128)(2,1)S(1)}, bf16[8,32,128]{2,1,0:T(8,128)(2,1)S(1)}, u32[]{:S(2)}, u32[]{:S(2)}) collective-permute-start(bf16[8,32,128]{2,1,0:T(8,128)(2,1)S(1)} %slice.19), channel_id=1, source_target_pairs={{0,1},{2,3},{4,5},{6,7},{8,9},{10,11},{12,13},{14,15},{16,17},{18,... | collective-permute-start | bytes 196616 | tf_op jit(solution)/shard_map/ppermute | solution.py:574
  55.4 7.1 %collective-permute-start.10 = (bf16[7,32,128]{2,1,0:T(8,128)(2,1)S(1)}, bf16[7,32,128]{2,1,0:T(8,128)(2,1)S(1)}, u32[]{:S(2)}, u32[]{:S(2)}) collective-permute-start(bf16[7,32,128]{2,1,0:T(8,128)(2,1)S(1)} %add_convert_fusion.3), channel_id=1, source_target_pairs={{0,8},{1,9},{2,10},{3,11},{4,12},{5,13},{6,14},{7,15},{8,0},{9,1},... | collective-permute-start | bytes 172040 | tf_op jit(solution)/shard_map/ppermute | solution.py:592
  62.5 7.1 %collective-permute-start.11 = (bf16[7,32,128]{2,1,0:T(8,128)(2,1)S(1)}, bf16[7,32,128]{2,1,0:T(8,128)(2,1)S(1)}, u32[]{:S(2)}, u32[]{:S(2)}) collective-permute-start(bf16[7,32,128]{2,1,0:T(8,128)(2,1)S(1)} %add_convert_fusion.2), channel_id=1, source_target_pairs={{0,24},{1,25},{2,26},{3,27},{4,28},{5,29},{6,30},{7,31},{8,16},{9,... | collective-permute-start | bytes 172040 | tf_op jit(solution)/shard_map/ppermute | solution.py:592
  69.7 9.3 %collective-permute-start.12 = (bf16[7,32,128]{2,1,0:T(8,128)(2,1)S(1)}, bf16[7,32,128]{2,1,0:T(8,128)(2,1)S(1)}, u32[]{:S(2)}, u32[]{:S(2)}) collective-permute-start(bf16[7,32,128]{2,1,0:T(8,128)(2,1)S(1)} %add_convert_fusion.1), channel_id=1, source_target_pairs={{0,32},{1,33},{2,34},{3,35},{4,36},{5,37},{6,38},{7,39},{8,40},{9,... | collective-permute-start | bytes 172040 | tf_op jit(solution)/shard_map/ppermute | solution.py:592
  79.0 6.1 %collective-permute-start.13 = (bf16[7,32,128]{2,1,0:T(8,128)(2,1)S(1)}, bf16[7,32,128]{2,1,0:T(8,128)(2,1)S(1)}, u32[]{:S(2)}, u32[]{:S(2)}) collective-permute-start(bf16[7,32,128]{2,1,0:T(8,128)(2,1)S(1)} %add_convert_fusion.one_ref), channel_id=1, source_target_pairs={{0,96},{1,97},{2,98},{3,99},{4,100},{5,101},{6,102},{7,103},{8,104... | collective-permute-start | bytes 172040 | tf_op jit(solution)/shard_map/ppermute | solution.py:592

commit v5 on v4

--- a/solution.py
+++ b/solution.py
@@ -322,9 +322,9 @@
                 + index[6 + high, start + p]
             )
             for k, face in enumerate((low, high)):
-                ta[p, C * (face + 1) : C * (face + 2)] = times(
-                    toward(field, face), inside[k]
-                ) + times(v_edge, edges[k])
+                ta[p, C * (face + 1) : C * (face + 2)] = jnp.where(
+                    edges[k][None] > 0, halves(v_edge), halves(toward(field, face))
+                ).reshape(C, CELLS)
                 back = face ^ 1
                 tb[p, C * (back + 1) : C * (back + 2)] = times(
                     toward(other, face), inside[k]
@@ -722,7 +722,8 @@
         pltpu.SemaphoreType.DMA((2,)),
     ]
     fixed = (index, merged, grad_pre, xs, zs, mats, spread)
-    partner = swap(sums, 6)
+    sums, got_c = lax.optimization_barrier((add(sums, swap(sums, 6)), got_c))
+    partner = swap(sums, 8)
     table, coef, output, grad_state = pl.pallas_call(
         first_final_kernel,
         in_specs=[SMEM()] + [VMEM()] * 9,
@@ -733,9 +734,8 @@
         cost_estimate=cost(2),
         name="last_level",
     )(*fixed, table, got_b, got_c)
-    sums = add(sums, partner)
-    for step, mask in ((1, 8), (2, 24), (3, 32)):
-        sums, coef = lax.optimization_barrier((sums, coef))
+    for step, mask in ((1, 24), (2, 32), (3, 96)):
+        sums, coef, output = lax.optimization_barrier((add(sums, partner), coef, output))
         partner = swap(sums, mask)
         output, grad_state = pl.pallas_call(
             functools.partial(next_final_kernel, step),
@@ -748,9 +748,6 @@
             cost_estimate=cost(2),
             name="last_level",
         )(*fixed, table, coef, output, grad_state)
-        sums = add(sums, partner)
-        sums, output = lax.optimization_barrier((sums, output))
-    partner = swap(sums, 96)
 
     scale = 1.0 / math.sqrt(float(devices * SLOTS * CELLS))
     mat = shape_of((7, C, C), F32)

time: 86.3 us -> 83.7 us (0.970)
  waiting for transfers between devices: 8.63 us -> 6.49 us
    ppermute x6, waiting for transfers between devices: 4.63 us -> 2.49 us  [swap(): return lax.ppermute(block, 'patch', [(i, i ^ mask) for i in range(devices)])]
  transfers between devices with their start and end apart: 14 -> 14, of which waited for: 7 -> 6; matrix products, arithmetic and copies ran while one was open for 0% -> 0% of each run, Pallas kernels for 20% -> 24%
where the time goes in v5:
time: 83.7 us; the launch traced here: 83.5 us
  Pallas kernels  39.4 us (47%)
  starting transfers between devices  35.1 us (42%)
  waiting for transfers between devices  6.49 us (8%)
  local copies, waits for them, and re-layouts  1.3 us (2%)
  between operations  1.05 us (1%)
    ppermute x6, starting transfers between devices, swap(): return lax.ppermute(block, 'patch', [(i, i ^ mask) for i in range(devices)])  26 us
    ppermute x8, starting transfers between devices, trade(): return lax.ppermute(block, 'patch', pairs(kind, lax.axis_size('patch')))  9.07 us
    pallas_call x1, Pallas kernels, on_device(): pl.pallas_call(merge_kernel, in_specs=[SMEM()] + [VMEM()] * 13, out_specs...  8.16 us
    pallas_call x3, Pallas kernels, on_device(): pl.pallas_call(functools.partial(next_final_kernel, step), in_specs=[SMEM...  7.93 us
    pallas_call x1, Pallas kernels, on_device(): pl.pallas_call(fine_kernel, in_specs=[SMEM()] * 2 + [VMEM()] * 8, out_spe...  7.12 us
    pallas_call x1, Pallas kernels, on_device(): pl.pallas_call(window_kernel, in_specs=[VMEM()] * 6, out_specs=[VMEM()] *...  4.69 us
    ppermute x8, waiting for transfers between devices, trade(): return lax.ppermute(block, 'patch', pairs(kind, lax.axis_size('patch')))  4 us
    pallas_call x1, Pallas kernels, on_device(): pl.pallas_call(layers_kernel, in_specs=[HBM()] * 3, out_specs=[VMEM()] *...  3.06 us
  transfers between devices with their start and end apart: 14, of which 6 were waited for; matrix products, arithmetic and copies ran while one was open for 0% of the time, Pallas kernels for 24%

profile of v5, /device:TPU:0, one launch (start us, length us, event | category | flops | bytes accessed | tf_op | source)
XLA Modules:
  0.0 83.5 jit_solution(4570993161226218320)
XLA Ops:
  0.6 0.0 copy-start.1
  0.6 0.0 copy-start.12
  0.7 3.1 %face_rows.1 = (bf16[27,32,128]{2,1,0:T(8,128)(2,1)S(1)}, bf16[27,32,128]{2,1,0:T(8,128)(2,1)S(1)}) custom-call(s32[128]{0:T(128)} %counts.1, bf16[32,32,512]{2,1,0:T(8,128)(2,1)} %x_ref.1, bf16[32,32,512]{2,1,0:T(8,128)(2,1)} %z_ref.1), custom_call_target="tpu_custom_call" | custom-call | flops 4000000 | bytes 12000000 | tf_op jit(solution)/shard_map/face_rows/pallas_call | solution.py:613
  3.8 0.1 collective-permute-start
  3.9 1.5 %collective-permute-done.got_ref = bf16[27,32,128]{2,1,0:T(8,128)(2,1)S(1)} collective-permute-done((bf16[27,32,128]{2,1,0:T(8,128)(2,1)S(1)}, bf16[27,32,128]{2,1,0:T(8,128)(2,1)S(1)}, u32[]{:S(2)}, u32[]{:S(2)}) %collective-permute-start) | collective-permute-done | bytes 221216 | tf_op jit(solution)/shard_map/ppermute | solution.py:574
  5.4 0.7 collective-permute-start.1
  6.1 0.0 copy-start.3
  6.2 1.2 %copy-done.3 = bf16[32,32,512]{2,1,0:T(8,128)(2,1)S(1)} copy-done((bf16[32,32,512]{2,1,0:T(8,128)(2,1)S(1)}, bf16[32,32,512]{2,1,0:T(8,128)(2,1)}, u32[]{:S(2)}) %copy-start.3) | copy-done | bytes 1048600
  7.4 2.9 %prepare.1 = (s32[128]{0:T(128)S(1)}, s32[12,32]{1,0:T(8,128)S(1)}, bf16[32,32,512]{2,1,0:T(8,128)(2,1)S(1)}, bf16[32,32,512]{2,1,0:T(8,128)(2,1)S(1)}, bf16[2,3...) custom-call(s32[128]{0:T(128)S(1)} %copy-done.12, s32[32]{0:T(128)S(1)} %copy-done.13, s32[6,32]{1,0:T(8,128)S(1)} %bitcast.2, ...), custom_call_target="tpu_custom_call" | custom-call | flops 4000000 | bytes 12000000 | tf_op jit(solution)/shard_map/prepare/pallas_call | solution.py:633
  10.3 0.0 collective-permute-done.1.b_ref
  10.3 3.2 %collective-permute-start.2 = (bf16[8,32,128]{2,1,0:T(8,128)(2,1)S(1)}, bf16[8,32,128]{2,1,0:T(8,128)(2,1)S(1)}, u32[]{:S(2)}, u32[]{:S(2)}) collective-permute-start(bf16[8,32,128]{2,1,0:T(8,128)(2,1)S(1)} %slice.16), channel_id=1, source_target_pairs={{0,1},{2,3},{4,5},{6,7},{8,9},{10,11},{12,13},{14,15},{16,17},{18,... | collective-permute-start | bytes 196616 | tf_op jit(solution)/shard_map/ppermute | solution.py:574
  13.5 0.9 %collective-permute-done.2.c_ref = bf16[8,32,128]{2,1,0:T(8,128)(2,1)S(1)} collective-permute-done((bf16[8,32,128]{2,1,0:T(8,128)(2,1)S(1)}, bf16[8,32,128]{2,1,0:T(8,128)(2,1)S(1)}, u32[]{:S(2)}, u32[]{:S(2)}) %collective-permute-start.2) | collective-permute-done | bytes 65568 | tf_op jit(solution)/shard_map/ppermute | solution.py:574
  14.4 0.0 copy-done
  14.4 7.1 %fine_level.1 = (bf16[32,224,512]{2,1,0:T(8,128)(2,1)S(1)}, bf16[32,224,512]{2,1,0:T(8,128)(2,1)S(1)}, bf16[32,32,512]{2,1,0:T(8,128)(2,1)S(1)}, bf16[32,32,512]...) custom-call(s32[128]{0:T(128)S(1)} %get-tuple-element.61.meta, ...), custom_call_target="tpu_custom_call" | custom-call | flops 8000000 | bytes 24000000 | tf_op jit(solution)/shard_map/fine_level/pallas_call | solution.py:648
  21.5 0.4 collective-permute-start.3
  22.0 0.7 collective-permute-start.4
  22.6 0.0 copy-start.5
  22.6 0.0 copy-start.6
  22.6 4.7 %window.1 = (bf16[4,32,224]{2,1,0:T(8,128)(2,1)S(1)}, f32[224,32]{1,0:T(8,128)S(1)}, bf16[32,224,128]{2,1,0:T(8,128)(2,1)S(1)}) custom-call(bf16[32,32,512]{2,1,0:T(8,128)(2,1)S(1)} %get-tuple-element.68.hidden_ref, bf16[32,224,512]{2,1,0:T(8,128)(2,1)S(1)} %get-tuple-element.69.tb_ref, bf16[2,512,128]{2,1,0:T(8,128)(2,1)S(1)} %copy-done.4, ...), custom_call_target="tpu_custom_call" | custom-call | flops 3000000 | bytes 9000000 | tf_op jit(solution)/shard_map/window/pallas_call | solution.py:668
  27.3 0.0 collective-permute-done.3.pin_ref
  27.4 0.0 collective-permute-done.4.pout_ref
  27.4 0.0 copy-done.5
  27.4 0.0 copy-done.6
  27.4 8.2 %coarse_and_merge.1 = (bf16[32,32,512]{2,1,0:T(8,128)(2,1)S(1)}, bf16[32,32,512]{2,1,0:T(8,128)(2,1)S(1)}, bf16[7,32,128]{2,1,0:T(8,128)(2,1)S(1)}, bf16[34,32,1...) custom-call(s32[128]{0:T(128)S(1)} %get-tuple-element.61.meta, bf16[32,224,512]{2,1,0:T(8,128)(2,1)S(1)} %get-tuple-element.67.ta_ref, ...), custom_call_target="tpu_custom_call" | custom-call | flops 9000000 | bytes 27000000 | tf_op jit(solution)/shard_map/coarse_and_merge/pallas_call | solution.py:679
  35.6 3.0 %collective-permute-start.5 = (bf16[34,32,128]{2,1,0:T(8,128)(2,1)S(1)}, bf16[34,32,128]{2,1,0:T(8,128)(2,1)S(1)}, u32[]{:S(2)}, u32[]{:S(2)}) collective-permute-start(bf16[34,32,128]{2,1,0:T(8,128)(2,1)S(1)} %get-tuple-element.81), channel_id=1, source_target_pairs={{0,1},{2,3},{4,5},{6,7},{8,9},{10,11},{12,13},{14,15},{16,17},{18,... | collective-permute-start | bytes 835592 | tf_op jit(solution)/shard_map/ppermute | solution.py:574
  38.6 1.2 %collective-permute-done.5.got_ref = bf16[34,32,128]{2,1,0:T(8,128)(2,1)S(1)} collective-permute-done((bf16[34,32,128]{2,1,0:T(8,128)(2,1)S(1)}, bf16[34,32,128]{2,1,0:T(8,128)(2,1)S(1)}, u32[]{:S(2)}, u32[]{:S(2)}) %collective-permute-start.5) | collective-permute-done | bytes 278560 | tf_op jit(solution)/shard_map/ppermute | solution.py:574
  39.8 1.6 %collective-permute-start.7 = (bf16[7,32,128]{2,1,0:T(8,128)(2,1)S(1)}, bf16[7,32,128]{2,1,0:T(8,128)(2,1)S(1)}, u32[]{:S(2)}, u32[]{:S(2)}) collective-permute-start(bf16[7,32,128]{2,1,0:T(8,128)(2,1)S(1)} %add_convert_fusion.5), channel_id=1, source_target_pairs={{0,2},{1,3},{2,0},{3,1},{4,6},{5,7},{6,4},{7,5},{8,10},{9,11},{10,... | collective-permute-start | bytes 172040 | tf_op jit(solution)/shard_map/ppermute | solution.py:592
  41.4 0.7 collective-permute-start.6
  42.1 2.0 %collective-permute-done.7 = bf16[7,32,128]{2,1,0:T(8,128)(2,1)S(1)} collective-permute-done((bf16[7,32,128]{2,1,0:T(8,128)(2,1)S(1)}, bf16[7,32,128]{2,1,0:T(8,128)(2,1)S(1)}, u32[]{:S(2)}, u32[]{:S(2)}) %collective-permute-start.7) | collective-permute-done | bytes 57376 | tf_op jit(solution)/shard_map/ppermute | solution.py:592
  44.1 5.1 %collective-permute-start.8 = (bf16[7,32,128]{2,1,0:T(8,128)(2,1)S(1)}, bf16[7,32,128]{2,1,0:T(8,128)(2,1)S(1)}, u32[]{:S(2)}, u32[]{:S(2)}) collective-permute-start(bf16[7,32,128]{2,1,0:T(8,128)(2,1)S(1)} %add_convert_fusion.4), channel_id=1, source_target_pairs={{0,6},{1,7},{2,4},{3,5},{4,2},{5,3},{6,0},{7,1},{8,14},{9,15},{10,... | collective-permute-start | bytes 172040 | tf_op jit(solution)/shard_map/ppermute | solution.py:592
  49.2 1.8 %face_table.1.t_ref = bf16[219,32,128]{2,1,0:T(8,128)(2,1)S(1)} custom-call(bf16[32,32,512]{2,1,0:T(8,128)(2,1)S(1)} %get-tuple-element.78.v_ref, bf16[32,32,512]{2,1,0:T(8,128)(2,1)S(1)} %get-tuple-element.79.y_ref, bf16[6,512,256]{2,1,0:T(8,128)(2,1)S(1)} %copy-done.1, bf16[34,32,128]{2,1,0:T(8,128)(2,1)S(1)} %collective-permute-done.5.got_ref), custom_call_target="tpu_custom_call" | custom-call | flops 2000000 | bytes 6000000 | tf_op jit(solution)/shard_map/face_table/pallas_call | solution.py:705
  51.0 0.0 collective-permute-done.6.b_ref
  51.0 0.4 collective-permute-start.9
  51.4 0.5 collective-permute-done.8
  51.9 0.4 collective-permute-done.9.c_ref
  52.4 4.3 %collective-permute-start.10 = (bf16[7,32,128]{2,1,0:T(8,128)(2,1)S(1)}, bf16[7,32,128]{2,1,0:T(8,128)(2,1)S(1)}, u32[]{:S(2)}, u32[]{:S(2)}) collective-permute-start(bf16[7,32,128]{2,1,0:T(8,128)(2,1)S(1)} %add_convert_fusion.3), channel_id=1, source_target_pairs={{0,8},{1,9},{2,10},{3,11},{4,12},{5,13},{6,14},{7,15},{8,0},{9,1},... | collective-permute-start | bytes 172040 | tf_op jit(solution)/shard_map/ppermute | solution.py:592
  56.7 2.8 %last_level.4 = (bf16[262,32,128]{2,1,0:T(8,128)(2,1)S(1)}, bf16[12,2,16,512]{3,2,1,0:T(8,128)(2,1)S(1)}, bf16[32,32,512]{2,1,0:T(8,128)(2,1)}, bf16[32,32,512]{2,1,0:T(8,128)(2,1)}) custom-call(s32[12,32]{1,0:T(8,128)S(1)} %get-tuple-element.58.index, bf16[32,32,512]{2,1,0:T(8,128)(2,1)S(1)} %get-tuple-element.78.v_ref, ...), custom_call_target="tpu_custom_call" | custom-call | flops 2000000 | bytes 6000000 | tf_op jit(solution)/shard_map/last_level/pallas_call | solution.py:727
  59.5 0.0 collective-permute-done.10
  59.5 4.3 %collective-permute-start.11 = (bf16[7,32,128]{2,1,0:T(8,128)(2,1)S(1)}, bf16[7,32,128]{2,1,0:T(8,128)(2,1)S(1)}, u32[]{:S(2)}, u32[]{:S(2)}) collective-permute-start(bf16[7,32,128]{2,1,0:T(8,128)(2,1)S(1)} %add_convert_fusion.2), channel_id=1, source_target_pairs={{0,24},{1,25},{2,26},{3,27},{4,28},{5,29},{6,30},{7,31},{8,16},{9,... | collective-permute-start | bytes 172040 | tf_op jit(solution)/shard_map/ppermute | solution.py:592
  63.8 2.6 %last_level.5 = (bf16[32,32,512]{2,1,0:T(8,128)(2,1)}, bf16[32,32,512]{2,1,0:T(8,128)(2,1)}) custom-call(s32[12,32]{1,0:T(8,128)S(1)} %get-tuple-element.58.index, bf16[32,32,512]{2,1,0:T(8,128)(2,1)S(1)} %get-tuple-element.78.v_ref, bf16[32,32,512]{2,1,0:T(8,128)(2,1)S(1)} %get-tuple-element.79.y_ref, ...), custom_call_target="tpu_custom_call", output_to_operand_aliasing={{0}: (9, {}), {1}: (10, {})} | custom-call | flops 2000000 | bytes 6000000 | tf_op jit(solution)/shard_map/last_level/pallas_call | solution.py:740
  66.5 0.0 collective-permute-done.11
  66.5 6.6 %collective-permute-start.12 = (bf16[7,32,128]{2,1,0:T(8,128)(2,1)S(1)}, bf16[7,32,128]{2,1,0:T(8,128)(2,1)S(1)}, u32[]{:S(2)}, u32[]{:S(2)}) collective-permute-start(bf16[7,32,128]{2,1,0:T(8,128)(2,1)S(1)} %add_convert_fusion.1), channel_id=1, source_target_pairs={{0,32},{1,33},{2,34},{3,35},{4,36},{5,37},{6,38},{7,39},{8,40},{9,... | collective-permute-start | bytes 172040 | tf_op jit(solution)/shard_map/ppermute | solution.py:592
  73.1 2.6 %last_level.6 = (bf16[32,32,512]{2,1,0:T(8,128)(2,1)}, bf16[32,32,512]{2,1,0:T(8,128)(2,1)}) custom-call(s32[12,32]{1,0:T(8,128)S(1)} %get-tuple-element.58.index, bf16[32,32,512]{2,1,0:T(8,128)(2,1)S(1)} %get-tuple-element.78.v_ref, bf16[32,32,512]{2,1,0:T(8,128)(2,1)S(1)} %get-tuple-element.79.y_ref, ...), custom_call_target="tpu_custom_call", output_to_operand_aliasing={{0}: (9, {}), {1}: (10, {})} | custom-call | flops 2000000 | bytes 6000000 | tf_op jit(solution)/shard_map/last_level/pallas_call | solution.py:740
  75.8 0.0 collective-permute-done.12
  75.8 4.0 %collective-permute-start.13 = (bf16[7,32,128]{2,1,0:T(8,128)(2,1)S(1)}, bf16[7,32,128]{2,1,0:T(8,128)(2,1)S(1)}, u32[]{:S(2)}, u32[]{:S(2)}) collective-permute-start(bf16[7,32,128]{2,1,0:T(8,128)(2,1)S(1)} %add_convert_fusion.one_ref), channel_id=1, source_target_pairs={{0,96},{1,97},{2,98},{3,99},{4,100},{5,101},{6,102},{7,103},{8,104... | collective-permute-start | bytes 172040 | tf_op jit(solution)/shard_map/ppermute | solution.py:592
  79.8 2.6 %last_level.7 = (bf16[32,32,512]{2,1,0:T(8,128)(2,1)}, bf16[32,32,512]{2,1,0:T(8,128)(2,1)}) custom-call(s32[12,32]{1,0:T(8,128)S(1)} %get-tuple-element.58.index, bf16[32,32,512]{2,1,0:T(8,128)(2,1)S(1)} %get-tuple-element.78.v_ref, bf16[32,32,512]{2,1,0:T(8,128)(2,1)S(1)} %get-tuple-element.79.y_ref, ...), custom_call_target="tpu_custom_call", output_to_operand_aliasing={{0}: (9, {}), {1}: (10, {})} | custom-call | flops 2000000 | bytes 6000000 | tf_op jit(solution)/shard_map/last_level/pallas_call | solution.py:740
  82.5 0.0 collective-permute-done.13.two_ref
  82.5 1.0 %weight_sums.1 = (f32[7,32,32]{2,1,0:T(8,128)}, f32[7,32,32]{2,1,0:T(8,128)}, f32[7,32,32]{2,1,0:T(8,128)}) custom-call(bf16[7,32,128]{2,1,0:T(8,128)(2,1)S(1)} %add_convert_fusion.one_ref, bf16[7,32,128]{2,1,0:T(8,128)(2,1)S(1)} %collective-permute-done.13.two_ref), custom_call_target="tpu_custom_call" | custom-call | flops 1000000 | bytes 3000000 | tf_op jit(solution)/shard_map/weight_sums/pallas_call | solution.py:754
  (31 shorter events, 0.2 us)
Async XLA Ops:
  0.6 5.4 %copy-start.1 = (bf16[6,512,256]{2,1,0:T(8,128)(2,1)S(1)}, bf16[6,512,256]{2,1,0:T(8,128)(2,1)}, u32[]{:S(2)}) copy-start(bf16[6,512,256]{2,1,0:T(8,128)(2,1)} %constant.10.clone.sel_ref) | copy-start | bytes 4718596
  0.6 5.4 %copy-start.12 = (s32[128]{0:T(128)S(1)}, s32[128]{0:T(128)}, u32[]{:S(2)}) copy-start(s32[128]{0:T(128)} %counts.1) | copy-start | bytes 1540
  0.7 5.4 %copy-start.2 = (bf16[32,32,512]{2,1,0:T(8,128)(2,1)S(1)}, bf16[32,32,512]{2,1,0:T(8,128)(2,1)}, u32[]{:S(2)}) copy-start(bf16[32,32,512]{2,1,0:T(8,128)(2,1)} %x_ref.1) | copy-start | bytes 3145732
  0.7 5.4 %copy-start.8 = (bf16[7,32,32]{2,1,0:T(8,128)(2,1)S(1)}, bf16[7,32,32]{2,1,0:T(8,128)(2,1)}, u32[]{:S(2)}) copy-start(bf16[7,32,32]{2,1,0:T(8,128)(2,1)} %w_out.3) | copy-start | bytes 43012
  0.7 5.4 %copy-start.7 = (bf16[7,32,32]{2,1,0:T(8,128)(2,1)S(1)}, bf16[7,32,32]{2,1,0:T(8,128)(2,1)}, u32[]{:S(2)}) copy-start(bf16[7,32,32]{2,1,0:T(8,128)(2,1)} %w_in.3) | copy-start | bytes 43012
  0.7 5.4 %copy-start.13 = (s32[32]{0:T(128)S(1)}, s32[32]{0:T(128)}, u32[]{:S(2)}) copy-start(s32[32]{0:T(128)} %octant.1) | copy-start | bytes 388
  0.7 5.4 %copy-start.11 = (s32[32,6]{0,1:T(8,128)S(1)}, s32[32,6]{0,1:T(8,128)}, u32[]{:S(2)}) copy-start(s32[32,6]{0,1:T(8,128)} %param.21) | copy-start | bytes 2308
  0.7 5.4 %copy-start.10 = (s32[32,6]{0,1:T(8,128)S(1)}, s32[32,6]{0,1:T(8,128)}, u32[]{:S(2)}) copy-start(s32[32,6]{0,1:T(8,128)} %param.20) | copy-start | bytes 2308
  3.8 1.6 %collective-permute-start = (bf16[27,32,128]{2,1,0:T(8,128)(2,1)S(1)}, bf16[27,32,128]{2,1,0:T(8,128)(2,1)S(1)}, u32[]{:S(2)}, u32[]{:S(2)}) collective-permute-start(bf16[27,32,128]{2,1,0:T(8,128)(2,1)S(1)} %get-tuple-element.57), channel_id=1, source_target_pairs={{0,1},{2,3},{4,5},{6,7},{8,9},{10,11},{12,13},{14,15},{16,17},{18,... | collective-permute-start | bytes 663560 | tf_op jit(solution)/shard_map/ppermute | solution.py:574
  5.4 4.9 %collective-permute-start.1 = (bf16[35,32,128]{2,1,0:T(8,128)(2,1)S(1)}, bf16[35,32,128]{2,1,0:T(8,128)(2,1)S(1)}, u32[]{:S(2)}, u32[]{:S(2)}) collective-permute-start(bf16[35,32,128]{2,1,0:T(8,128)(2,1)S(1)} %pad_maximum_fusion), channel_id=1, source_target_pairs={{1,2},{3,4},{5,6},{7,8},{9,10},{11,12},{13,14},{15,16},{17,18},{19... | collective-permute-start | bytes 860168 | tf_op jit(solution)/shard_map/ppermute | solution.py:574
  6.1 1.2 %copy-start.3 = (bf16[32,32,512]{2,1,0:T(8,128)(2,1)S(1)}, bf16[32,32,512]{2,1,0:T(8,128)(2,1)}, u32[]{:S(2)}) copy-start(bf16[32,32,512]{2,1,0:T(8,128)(2,1)} %z_ref.1) | copy-start | bytes 3145732
  7.4 7.0 %copy-start = (bf16[2,256,1024]{2,1,0:T(8,128)(2,1)S(1)}, bf16[2,256,1024]{2,1,0:T(8,128)(2,1)}, u32[]{:S(2)}) copy-start(bf16[2,256,1024]{2,1,0:T(8,128)(2,1)} %constant.11.clone.spread_ref) | copy-start | bytes 3145732
  7.4 7.0 %copy-start.4 = (bf16[2,512,128]{2,1,0:T(8,128)(2,1)S(1)}, bf16[2,512,128]{2,1,0:T(8,128)(2,1)}, u32[]{:S(2)}) copy-start(bf16[2,512,128]{2,1,0:T(8,128)(2,1)} %constant.12.clone.rest_ref) | copy-start | bytes 786436
  10.3 4.1 %collective-permute-start.2 = (bf16[8,32,128]{2,1,0:T(8,128)(2,1)S(1)}, bf16[8,32,128]{2,1,0:T(8,128)(2,1)S(1)}, u32[]{:S(2)}, u32[]{:S(2)}) collective-permute-start(bf16[8,32,128]{2,1,0:T(8,128)(2,1)S(1)} %slice.16), channel_id=1, source_target_pairs={{0,1},{2,3},{4,5},{6,7},{8,9},{10,11},{12,13},{14,15},{16,17},{18,... | collective-permute-start | bytes 196616 | tf_op jit(solution)/shard_map/ppermute | solution.py:574
  14.4 8.2 %copy-start.9 = (bf16[7,32,32]{2,1,0:T(8,128)(2,1)S(1)}, bf16[7,32,32]{2,1,0:T(8,128)(2,1)}, u32[]{:S(2)}) copy-start(bf16[7,32,32]{2,1,0:T(8,128)(2,1)} %w_co.1) | copy-start | bytes 43012
  21.5 5.8 %collective-permute-start.3 = (bf16[8,32,128]{2,1,0:T(8,128)(2,1)S(1)}, bf16[8,32,128]{2,1,0:T(8,128)(2,1)S(1)}, u32[]{:S(2)}, u32[]{:S(2)}) collective-permute-start(bf16[8,32,128]{2,1,0:T(8,128)(2,1)S(1)} %get-tuple-element.75), channel_id=1, source_target_pairs={{0,1},{2,3},{4,5},{6,7},{8,9},{10,11},{12,13},{14,15},{16,17},{18,... | collective-permute-start | bytes 196616 | tf_op jit(solution)/shard_map/ppermute | solution.py:574
  22.0 5.4 %collective-permute-start.4 = (bf16[8,32,128]{2,1,0:T(8,128)(2,1)S(1)}, bf16[8,32,128]{2,1,0:T(8,128)(2,1)S(1)}, u32[]{:S(2)}, u32[]{:S(2)}) collective-permute-start(bf16[8,32,128]{2,1,0:T(8,128)(2,1)S(1)} %get-tuple-element.76), channel_id=1, source_target_pairs={{1,2},{3,4},{5,6},{7,8},{9,10},{11,12},{13,14},{15,16},{17,18},{19... | collective-permute-start | bytes 196616 | tf_op jit(solution)/shard_map/ppermute | solution.py:574
  22.6 4.7 %copy-start.5 = (bf16[256,1024]{1,0:T(8,128)(2,1)S(1)}, bf16[256,1024]{1,0:T(8,128)(2,1)}, u32[]{:S(2)}) copy-start(bf16[256,1024]{1,0:T(8,128)(2,1)} %constant.14.clone.place_ref) | copy-start | bytes 1572868
  22.6 4.7 %copy-start.6 = (bf16[128,1024]{1,0:T(8,128)(2,1)S(1)}, bf16[128,1024]{1,0:T(8,128)(2,1)}, u32[]{:S(2)}) copy-start(bf16[128,1024]{1,0:T(8,128)(2,1)} %constant.13.clone.up_ref) | copy-start | bytes 786436
  35.6 4.2 %collective-permute-start.5 = (bf16[34,32,128]{2,1,0:T(8,128)(2,1)S(1)}, bf16[34,32,128]{2,1,0:T(8,128)(2,1)S(1)}, u32[]{:S(2)}, u32[]{:S(2)}) collective-permute-start(bf16[34,32,128]{2,1,0:T(8,128)(2,1)S(1)} %get-tuple-element.81), channel_id=1, source_target_pairs={{0,1},{2,3},{4,5},{6,7},{8,9},{10,11},{12,13},{14,15},{16,17},{18,... | collective-permute-start | bytes 835592 | tf_op jit(solution)/shard_map/ppermute | solution.py:574
  39.8 4.3 %collective-permute-start.7 = (bf16[7,32,128]{2,1,0:T(8,128)(2,1)S(1)}, bf16[7,32,128]{2,1,0:T(8,128)(2,1)S(1)}, u32[]{:S(2)}, u32[]{:S(2)}) collective-permute-start(bf16[7,32,128]{2,1,0:T(8,128)(2,1)S(1)} %add_convert_fusion.5), channel_id=1, source_target_pairs={{0,2},{1,3},{2,0},{3,1},{4,6},{5,7},{6,4},{7,5},{8,10},{9,11},{10,... | collective-permute-start | bytes 172040 | tf_op jit(solution)/shard_map/ppermute | solution.py:592
  41.4 9.6 %collective-permute-start.6 = (bf16[35,32,128]{2,1,0:T(8,128)(2,1)S(1)}, bf16[35,32,128]{2,1,0:T(8,128)(2,1)S(1)}, u32[]{:S(2)}, u32[]{:S(2)}) collective-permute-start(bf16[35,32,128]{2,1,0:T(8,128)(2,1)S(1)} %pad_maximum_fusion.1), channel_id=1, source_target_pairs={{1,2},{3,4},{5,6},{7,8},{9,10},{11,12},{13,14},{15,16},{17,18},{19... | collective-permute-start | bytes 860168 | tf_op jit(solution)/shard_map/ppermute | solution.py:574
  44.1 7.8 %collective-permute-start.8 = (bf16[7,32,128]{2,1,0:T(8,128)(2,1)S(1)}, bf16[7,32,128]{2,1,0:T(8,128)(2,1)S(1)}, u32[]{:S(2)}, u32[]{:S(2)}) collective-permute-start(bf16[7,32,128]{2,1,0:T(8,128)(2,1)S(1)} %add_convert_fusion.4), channel_id=1, source_target_pairs={{0,6},{1,7},{2,4},{3,5},{4,2},{5,3},{6,0},{7,1},{8,14},{9,15},{10,... | collective-permute-start | bytes 172040 | tf_op jit(solution)/shard_map/ppermute | solution.py:592
  51.0 1.3 %collective-permute-start.9 = (bf16[8,32,128]{2,1,0:T(8,128)(2,1)S(1)}, bf16[8,32,128]{2,1,0:T(8,128)(2,1)S(1)}, u32[]{:S(2)}, u32[]{:S(2)}) collective-permute-start(bf16[8,32,128]{2,1,0:T(8,128)(2,1)S(1)} %slice.19), channel_id=1, source_target_pairs={{0,1},{2,3},{4,5},{6,7},{8,9},{10,11},{12,13},{14,15},{16,17},{18,... | collective-permute-start | bytes 196616 | tf_op jit(solution)/shard_map/ppermute | solution.py:574
  52.4 7.1 %collective-permute-start.10 = (bf16[7,32,128]{2,1,0:T(8,128)(2,1)S(1)}, bf16[7,32,128]{2,1,0:T(8,128)(2,1)S(1)}, u32[]{:S(2)}, u32[]{:S(2)}) collective-permute-start(bf16[7,32,128]{2,1,0:T(8,128)(2,1)S(1)} %add_convert_fusion.3), channel_id=1, source_target_pairs={{0,8},{1,9},{2,10},{3,11},{4,12},{5,13},{6,14},{7,15},{8,0},{9,1},... | collective-permute-start | bytes 172040 | tf_op jit(solution)/shard_map/ppermute | solution.py:592
  59.5 7.0 %collective-permute-start.11 = (bf16[7,32,128]{2,1,0:T(8,128)(2,1)S(1)}, bf16[7,32,128]{2,1,0:T(8,128)(2,1)S(1)}, u32[]{:S(2)}, u32[]{:S(2)}) collective-permute-start(bf16[7,32,128]{2,1,0:T(8,128)(2,1)S(1)} %add_convert_fusion.2), channel_id=1, source_target_pairs={{0,24},{1,25},{2,26},{3,27},{4,28},{5,29},{6,30},{7,31},{8,16},{9,... | collective-permute-start | bytes 172040 | tf_op jit(solution)/shard_map/ppermute | solution.py:592
  66.5 9.3 %collective-permute-start.12 = (bf16[7,32,128]{2,1,0:T(8,128)(2,1)S(1)}, bf16[7,32,128]{2,1,0:T(8,128)(2,1)S(1)}, u32[]{:S(2)}, u32[]{:S(2)}) collective-permute-start(bf16[7,32,128]{2,1,0:T(8,128)(2,1)S(1)} %add_convert_fusion.1), channel_id=1, source_target_pairs={{0,32},{1,33},{2,34},{3,35},{4,36},{5,37},{6,38},{7,39},{8,40},{9,... | collective-permute-start | bytes 172040 | tf_op jit(solution)/shard_map/ppermute | solution.py:592
  75.8 6.7 %collective-permute-start.13 = (bf16[7,32,128]{2,1,0:T(8,128)(2,1)S(1)}, bf16[7,32,128]{2,1,0:T(8,128)(2,1)S(1)}, u32[]{:S(2)}, u32[]{:S(2)}) collective-permute-start(bf16[7,32,128]{2,1,0:T(8,128)(2,1)S(1)} %add_convert_fusion.one_ref), channel_id=1, source_target_pairs={{0,96},{1,97},{2,98},{3,99},{4,100},{5,101},{6,102},{7,103},{8,104... | collective-permute-start | bytes 172040 | tf_op jit(solution)/shard_map/ppermute | solution.py:592

commit v6 on v5

--- a/solution.py
+++ b/solution.py
@@ -17,6 +17,8 @@
 C = 32
 PB = 8
 STEPS = SLOTS // PB
+BIG = 32
+BIG_STEPS = SLOTS // BIG
 NPAR = 5
 STRIDES = (64, 8, 1)
 MORTON = (3, 8, 16)
@@ -28,7 +30,6 @@
 BASE_C = BASE_B + NEAR + FAR
 ROWS = BASE_C + FAR
 VMEM_LIMIT = 14 * 1024 * 1024
-FULL_LIMIT = 60 * 1024 * 1024
 DST, LEAD, TRAIL, SCAL = 0, 32, 64, 96
 N_COUNT, N_ODD, N_LAST, N_OWNED = SCAL, SCAL + 1, SCAL + 2, SCAL + 3
 META = 128
@@ -50,13 +51,11 @@
 
 
 def constants():
-    sel = np.zeros((3, 2, CELLS, 256), np.float32)
     spread = np.zeros((2, 256, 2 * CELLS), np.float32)
     for face in range(6):
         for j, cell in enumerate(face_cells(face)):
             for kind in range(2):
                 col = (face % 2) * 128 + kind * 64 + j
-                sel[face // 2, kind, cell, col] = 1
                 if face >= 2:
                     spread[face // 2 - 1, col, kind * CELLS + cell] = 1
     c0, c1, c2 = cell_coords()
@@ -76,7 +75,6 @@
             place[128 * o2 + 64 + a, CELLS + cell] = 1
     as_bf = lambda item: np.asarray(item, jnp.bfloat16)
     return (
-        as_bf(sel.reshape(6, CELLS, 256)),
         as_bf(spread),
         as_bf(rest),
         as_bf(up),
@@ -116,8 +114,12 @@
     return pltpu.roll(field, shift, 1)
 
 
-def send_rows(count, odd, v_ref, y_ref, sel_ref, v_rows, y_rows, sides, inner_ref, outer_ref):
+def send_rows(
+    count, odd, v_ref, y_ref, sel_ref, v_rows, y_rows, sides, inner_ref, outer_ref, waits=((), ())
+):
     for side in range(2):
+        for copy in waits[side]:
+            copy.wait()
         for dim in (2, 1, 0):
             depth = MORTON[dim]
             for i in range(depth):
@@ -156,12 +158,14 @@
 
 
 def layers_kernel(
-    counts_hbm, x_hbm, z_hbm, inner_ref, outer_ref,
-    v_rows, y_rows, sides, x_ref, z_ref, sel_ref, counts, sems, counts_sem,
+    counts_hbm, x_hbm, z_hbm, inner_ref, outer_ref, sel_ref,
+    v_rows, y_rows, sides, x_ref, z_ref, counts, sems, counts_sem,
 ):
     rank = lax.axis_index("patch")
     size = SLOTS // CHUNKS
-    copies = [pltpu.make_async_copy(counts_hbm, counts, counts_sem)]
+    count_copy = pltpu.make_async_copy(counts_hbm, counts, counts_sem)
+    count_copy.start()
+    copies = []
     for k in range(CHUNKS):
         part = pl.ds(k * size, size)
         copies.append(pltpu.make_async_copy(x_hbm.at[part], x_ref.at[part], sems.at[0, k]))
@@ -169,10 +173,10 @@
     for copy in copies:
         copy.start()
     make_selection(sel_ref)
-    for copy in copies:
-        copy.wait()
+    count_copy.wait()
     send_rows(
-        counts[rank], rank % 2, x_ref, z_ref, sel_ref, v_rows, y_rows, sides, inner_ref, outer_ref
+        counts[rank], rank % 2, x_ref, z_ref, sel_ref, v_rows, y_rows, sides, inner_ref, outer_ref,
+        waits=(copies[:CHUNKS], copies[CHUNKS:]),
     )
 
 
@@ -260,11 +264,11 @@
     fill_mats(mats, ((w_out, True), (w_in, False), (w_co, True), (w_co, False)))
     dw_ref[...] = jnp.zeros_like(dw_ref)
 
-    @pl.loop(0, STEPS)
+    @pl.loop(0, BIG_STEPS)
     def _(step):
         dw = jnp.zeros((7 * C, C), F32)
-        for p in range(PB):
-            here = step * PB + p
+        for p in range(BIG):
+            here = step * BIG + p
             dw += dot_nt(tb_ref[here], hidden_ref[here])
             means_ref[here] = dot(tb_ref[here], rest_ref[0]).astype(BF)
         dw_ref[...] += dw
@@ -290,17 +294,17 @@
 
 
 def block_taps(start, index, v_ref, y_ref, spread_ref, table, coef, picked, ta, tb):
+    size = v_ref.shape[0]
     for dim in range(3):
         low, high = 2 * dim, 2 * dim + 1
         edges = [on_face(low), on_face(high)]
-        inside = [(1.0 - edge).astype(BF) for edge in edges]
         edges = [edge.astype(BF) for edge in edges]
         if dim:
-            for p in range(PB):
+            for p in range(size):
                 picked[p, :, 0:128] = table[index[low, start + p]]
                 picked[p, :, 128:256] = table[index[high, start + p]]
-            spread = dot(picked[...].reshape(PB * C, 256), spread_ref[dim - 1]).astype(BF)
-        for p in range(PB):
+            spread = dot(picked[...].reshape(size * C, 256), spread_ref[dim - 1]).astype(BF)
+        for p in range(size):
             if dim:
                 rows = slice(p * C, (p + 1) * C)
                 v_edge = spread[rows, :CELLS]
@@ -326,9 +330,10 @@
                     edges[k][None] > 0, halves(v_edge), halves(toward(field, face))
                 ).reshape(C, CELLS)
                 back = face ^ 1
-                tb[p, C * (back + 1) : C * (back + 2)] = times(
-                    toward(other, face), inside[k]
-                ) + times(y_edge, coef[row, k])
+                kept = jnp.where(edges[k][None] > 0, 0.0, halves(toward(other, face)))
+                tb[p, C * (back + 1) : C * (back + 2)] = (
+                    kept + halves(y_edge) * coef[row, k][None]
+                ).reshape(C, CELLS)
 
 
 def silu_pair(pre):
@@ -345,23 +350,23 @@
     par[...] = jnp.zeros_like(par)
     ends[...] = jnp.zeros_like(ends)
 
-    @pl.loop(0, STEPS)
+    @pl.loop(0, BIG_STEPS)
     def _(step):
-        start = step * PB
+        start = step * BIG
         x_at, z_at, ta, tb, hidden_at, slope_at, gm_at = [
-            item.at[pl.ds(start, PB)]
+            item.at[pl.ds(start, BIG)]
             for item in (xs, zs, ta_ref, tb_ref, hidden_ref, slope_ref, gm_ref)
         ]
         block_taps(start, index, x_at, z_at, spread_ref, table, coef, picked, ta, tb)
-        for p in range(PB):
+        for p in range(BIG):
             hidden, slope = silu_pair(dot(mats[IN_F], ta[p]))
             hidden_at[p] = hidden.astype(BF)
             slope_at[p] = slope.astype(BF)
             gm_at[p] = dot(mats[OUT_B], tb[p]).astype(BF)
-        child = dot(hidden_at[...].reshape(PB * C, CELLS), rest_ref[0])
-        child += dot(gm_at[...].reshape(PB * C, CELLS), rest_ref[1])
+        child = dot(hidden_at[...].reshape(BIG * C, CELLS), rest_ref[0])
+        child += dot(gm_at[...].reshape(BIG * C, CELLS), rest_ref[1])
         child = child.astype(BF)
-        for p in range(PB):
+        for p in range(BIG):
             row = child[p * C : (p + 1) * C]
             par[meta[DST + start + p]] = row
             ends[0, meta[LEAD + start + p]] = row
@@ -461,15 +466,15 @@
         place_ref, par, taps, up_rows, dw_ref,
     )
 
-    @pl.loop(0, STEPS)
+    @pl.loop(0, BIG_STEPS)
     def _(step):
-        start = step * PB
-        for p in range(PB):
+        start = step * BIG
+        for p in range(BIG):
             picked[p] = up_rows[meta[DST + start + p]]
-        spread = dot(picked[...].reshape(PB * C, 128), up_ref[...])
+        spread = dot(picked[...].reshape(BIG * C, 128), up_ref[...])
         dw_in = jnp.zeros((7 * C, C), F32)
         dw_out = jnp.zeros((7 * C, C), F32)
-        for p in range(PB):
+        for p in range(BIG):
             rows = slice(p * C, (p + 1) * C)
             here = start + p
             merged = (hidden_ref[here].astype(F32) + spread[rows, :CELLS]).astype(BF)
@@ -503,15 +508,20 @@
     block_taps(
         start, index, v_ref.at[part], y_ref.at[part], spread_ref, table, coef, picked, ta, tb
     )
-    for p in range(PB):
-        out_ref[p] = (xs[start + p].astype(F32) + dot(mats[OUT_F], ta[p])).astype(BF)
-        gs_ref[p] = (zs[start + p].astype(F32) + dot(mats[IN_B], tb[p])).astype(BF)
-    copies = [
-        pltpu.make_async_copy(out_ref, out_hbm.at[part], sems.at[0]),
-        pltpu.make_async_copy(gs_ref, gs_hbm.at[part], sems.at[1]),
-    ]
-    for copy in copies:
-        copy.start()
+    half = PB // 2
+    copies = []
+    for k in range(2):
+        for p in range(k * half, (k + 1) * half):
+            out_ref[p] = (xs[start + p].astype(F32) + dot(mats[OUT_F], ta[p])).astype(BF)
+            gs_ref[p] = (zs[start + p].astype(F32) + dot(mats[IN_B], tb[p])).astype(BF)
+        here, there = pl.ds(k * half, half), pl.ds(start + k * half, half)
+        new = [
+            pltpu.make_async_copy(out_ref.at[here], out_hbm.at[there], sems.at[k, 0]),
+            pltpu.make_async_copy(gs_ref.at[here], gs_hbm.at[there], sems.at[k, 1]),
+        ]
+        for copy in new:
+            copy.start()
+        copies += new
     for copy in copies:
         copy.wait()
 
@@ -597,7 +607,7 @@
     owner_count, neighbour, level_tag, octant,
 ):
     devices = lax.axis_size("patch")
-    sel, spread, rest, up, place = [jnp.asarray(item) for item in constants()]
+    spread, rest, up, place = [jnp.asarray(item) for item in constants()]
 
     field = (SLOTS, C, CELLS)
     stack = (SLOTS, 7 * C, CELLS)
@@ -610,13 +620,13 @@
     coef_shape = (12, 2, 16, CELLS)
     picked_scratch = pltpu.VMEM((PB, C, 256), BF)
 
-    inner, outer = pl.pallas_call(
+    inner, outer, sel = pl.pallas_call(
         layers_kernel,
         in_specs=[HBM()] * 3,
-        out_specs=[VMEM()] * 2,
-        out_shape=[shape_of(near), shape_of(near)],
+        out_specs=[VMEM()] * 3,
+        out_shape=[shape_of(near), shape_of(near), shape_of(sel_shape)],
         scratch_shapes=rows_scratch
-        + [pltpu.VMEM(field, BF), pltpu.VMEM(field, BF), pltpu.VMEM(sel_shape, BF)]
+        + [pltpu.VMEM(field, BF), pltpu.VMEM(field, BF)]
         + [pltpu.SMEM(owner_count.shape, jnp.int32)]
         + [pltpu.SemaphoreType.DMA((2, CHUNKS)), pltpu.SemaphoreType.DMA],
         compiler_params=params(),
@@ -654,7 +664,7 @@
         scratch_shapes=[
             pltpu.VMEM(table_shape, BF),
             pltpu.VMEM(coef_shape, BF),
-            picked_scratch,
+            pltpu.VMEM((BIG, C, 256), BF),
             pltpu.VMEM((NPAR * 8 + 8, C, 128), BF),
             pltpu.VMEM((2, 16, C, 128), BF),
         ],
@@ -686,7 +696,7 @@
             pltpu.VMEM((NPAR * 8 + 8, C, 128), BF),
             pltpu.VMEM((NPAR, 7 * C, CELLS), BF),
             pltpu.VMEM((NPAR * 8 + 8, C, 128), BF),
-            pltpu.VMEM((PB, C, 128), BF),
+            pltpu.VMEM((BIG, C, 128), BF),
         ]
         + rows_scratch
         + [pltpu.VMEM((7 * C, 128), F32)],
@@ -719,7 +729,7 @@
         pltpu.VMEM((PB, 7 * C, CELLS), BF),
         pltpu.VMEM((PB, C, CELLS), BF),
         pltpu.VMEM((PB, C, CELLS), BF),
-        pltpu.SemaphoreType.DMA((2,)),
+        pltpu.SemaphoreType.DMA((2, 2)),
     ]
     fixed = (index, merged, grad_pre, xs, zs, mats, spread)
     sums, got_c = lax.optimization_barrier((add(sums, swap(sums, 6)), got_c))

time: 83.7 us -> 81.7 us (0.976)
  Pallas kernels: 39.4 us -> 37.1 us
  starting transfers between devices: 35.1 us -> 36.6 us
  local copies, waits for them, and re-layouts: 1.3 us -> 0.09 us
    ppermute x8, starting transfers between devices: 9.07 us -> 10.5 us  [trade(): return lax.ppermute(block, 'patch', pairs(kind, lax.axis_size('patch')))]
    unnamed x28 -> x26, local copies, waits for them, and re-layouts: 1.28 us -> 0.06 us
    pallas_call x1, Pallas kernels: 8.16 us -> 7.13 us  [on_device(): pl.pallas_call(merge_kernel, in_specs=[SMEM()] + [VMEM()] * 13, out_specs...]
where the time goes in v6:
time: 81.7 us; the launch traced here: 81.5 us
  Pallas kernels  37.1 us (45%)
  starting transfers between devices  36.6 us (45%)
  waiting for transfers between devices  6.47 us (8%)
  between operations  1.05 us (1%)
    ppermute x6, starting transfers between devices, swap(): return lax.ppermute(block, 'patch', [(i, i ^ mask) for i in range(devices)])  26.2 us
    ppermute x8, starting transfers between devices, trade(): return lax.ppermute(block, 'patch', pairs(kind, lax.axis_size('patch')))  10.5 us
    pallas_call x3, Pallas kernels, on_device(): pl.pallas_call(functools.partial(next_final_kernel, step), in_specs=[SMEM...  7.71 us
    pallas_call x1, Pallas kernels, on_device(): pl.pallas_call(merge_kernel, in_specs=[SMEM()] + [VMEM()] * 13, out_specs...  7.13 us
    pallas_call x1, Pallas kernels, on_device(): pl.pallas_call(fine_kernel, in_specs=[SMEM()] * 2 + [VMEM()] * 8, out_spe...  6.71 us
    pallas_call x1, Pallas kernels, on_device(): pl.pallas_call(window_kernel, in_specs=[VMEM()] * 6, out_specs=[VMEM()] *...  4.02 us
    ppermute x8, waiting for transfers between devices, trade(): return lax.ppermute(block, 'patch', pairs(kind, lax.axis_size('patch')))  3.99 us
    pallas_call x1, Pallas kernels, on_device(): pl.pallas_call(layers_kernel, in_specs=[HBM()] * 3, out_specs=[VMEM()] *...  3.09 us
  transfers between devices with their start and end apart: 14, of which 6 were waited for; matrix products, arithmetic and copies ran while one was open for 0% of the time, Pallas kernels for 24%

profile of v6, /device:TPU:0, one launch (start us, length us, event | category | flops | bytes accessed | tf_op | source)
XLA Modules:
  0.0 81.5 jit_solution(7427306408673104800)
XLA Ops:
  0.6 0.0 copy-start.11
  0.6 0.0 copy-start.2
  0.7 0.0 copy-start.1
  0.7 0.0 copy-start.7
  0.7 0.0 copy-start.6
  0.7 3.1 %face_rows.1 = (bf16[27,32,128]{2,1,0:T(8,128)(2,1)S(1)}, bf16[27,32,128]{2,1,0:T(8,128)(2,1)S(1)}, bf16[6,512,256]{2,1,0:T(8,128)(2,1)S(1)}) custom-call(s32[128]{0:T(128)} %counts.1, bf16[32,32,512]{2,1,0:T(8,128)(2,1)} %x_ref.1, bf16[32,32,512]{2,1,0:T(8,128)(2,1)} %z_ref.1), custom_call_target="tpu_custom_call" | custom-call | flops 4000000 | bytes 12000000 | tf_op jit(solution)/shard_map/face_rows/pallas_call | solution.py:623
  3.8 0.1 collective-permute-start
  3.9 1.5 %collective-permute-done.got_ref = bf16[27,32,128]{2,1,0:T(8,128)(2,1)S(1)} collective-permute-done((bf16[27,32,128]{2,1,0:T(8,128)(2,1)S(1)}, bf16[27,32,128]{2,1,0:T(8,128)(2,1)S(1)}, u32[]{:S(2)}, u32[]{:S(2)}) %collective-permute-start) | collective-permute-done | bytes 221216 | tf_op jit(solution)/shard_map/ppermute | solution.py:584
  5.4 0.7 collective-permute-start.1
  6.2 0.0 copy-start
  6.2 0.0 copy-start.3
  6.2 2.9 %prepare.1 = (s32[128]{0:T(128)S(1)}, s32[12,32]{1,0:T(8,128)S(1)}, bf16[32,32,512]{2,1,0:T(8,128)(2,1)S(1)}, bf16[32,32,512]{2,1,0:T(8,128)(2,1)S(1)}, bf16[2,3...) custom-call(s32[128]{0:T(128)S(1)} %copy-done.11, s32[32]{0:T(128)S(1)} %copy-done.12, s32[6,32]{1,0:T(8,128)S(1)} %bitcast.2, ...), custom_call_target="tpu_custom_call" | custom-call | flops 4000000 | bytes 12000000 | tf_op jit(solution)/shard_map/prepare/pallas_call | solution.py:643
  9.1 0.0 collective-permute-done.1.b_ref
  9.1 4.4 %collective-permute-start.2 = (bf16[8,32,128]{2,1,0:T(8,128)(2,1)S(1)}, bf16[8,32,128]{2,1,0:T(8,128)(2,1)S(1)}, u32[]{:S(2)}, u32[]{:S(2)}) collective-permute-start(bf16[8,32,128]{2,1,0:T(8,128)(2,1)S(1)} %slice.16), channel_id=1, source_target_pairs={{0,1},{2,3},{4,5},{6,7},{8,9},{10,11},{12,13},{14,15},{16,17},{18,... | collective-permute-start | bytes 196616 | tf_op jit(solution)/shard_map/ppermute | solution.py:584
  13.5 0.9 %collective-permute-done.2.c_ref = bf16[8,32,128]{2,1,0:T(8,128)(2,1)S(1)} collective-permute-done((bf16[8,32,128]{2,1,0:T(8,128)(2,1)S(1)}, bf16[8,32,128]{2,1,0:T(8,128)(2,1)S(1)}, u32[]{:S(2)}, u32[]{:S(2)}) %collective-permute-start.2) | collective-permute-done | bytes 65568 | tf_op jit(solution)/shard_map/ppermute | solution.py:584
  14.4 6.7 %fine_level.1 = (bf16[32,224,512]{2,1,0:T(8,128)(2,1)S(1)}, bf16[32,224,512]{2,1,0:T(8,128)(2,1)S(1)}, bf16[32,32,512]{2,1,0:T(8,128)(2,1)S(1)}, bf16[32,32,512]...) custom-call(s32[128]{0:T(128)S(1)} %get-tuple-element.63.meta, ...), custom_call_target="tpu_custom_call" | custom-call | flops 8000000 | bytes 24000000 | tf_op jit(solution)/shard_map/fine_level/pallas_call | solution.py:658
  21.1 0.4 collective-permute-start.3
  21.6 0.8 %collective-permute-start.4 = (bf16[8,32,128]{2,1,0:T(8,128)(2,1)S(1)}, bf16[8,32,128]{2,1,0:T(8,128)(2,1)S(1)}, u32[]{:S(2)}, u32[]{:S(2)}) collective-permute-start(bf16[8,32,128]{2,1,0:T(8,128)(2,1)S(1)} %get-tuple-element.78), channel_id=1, source_target_pairs={{1,2},{3,4},{5,6},{7,8},{9,10},{11,12},{13,14},{15,16},{17,18},{19... | collective-permute-start | bytes 196616 | tf_op jit(solution)/shard_map/ppermute | solution.py:584
  22.4 0.0 copy-start.4
  22.4 0.0 copy-start.5
  22.4 4.0 %window.1 = (bf16[4,32,224]{2,1,0:T(8,128)(2,1)S(1)}, f32[224,32]{1,0:T(8,128)S(1)}, bf16[32,224,128]{2,1,0:T(8,128)(2,1)S(1)}) custom-call(bf16[32,32,512]{2,1,0:T(8,128)(2,1)S(1)} %get-tuple-element.70.hidden_ref, bf16[32,224,512]{2,1,0:T(8,128)(2,1)S(1)} %get-tuple-element.71.tb_ref, bf16[2,512,128]{2,1,0:T(8,128)(2,1)S(1)} %copy-done.3, ...), custom_call_target="tpu_custom_call" | custom-call | flops 3000000 | bytes 9000000 | tf_op jit(solution)/shard_map/window/pallas_call | solution.py:678
  26.5 0.0 collective-permute-done.3.pin_ref
  26.5 0.0 collective-permute-done.4.pout_ref
  26.5 7.1 %coarse_and_merge.1 = (bf16[32,32,512]{2,1,0:T(8,128)(2,1)S(1)}, bf16[32,32,512]{2,1,0:T(8,128)(2,1)S(1)}, bf16[7,32,128]{2,1,0:T(8,128)(2,1)S(1)}, bf16[34,32,1...) custom-call(s32[128]{0:T(128)S(1)} %get-tuple-element.63.meta, bf16[32,224,512]{2,1,0:T(8,128)(2,1)S(1)} %get-tuple-element.69.ta_ref, ...), custom_call_target="tpu_custom_call" | custom-call | flops 9000000 | bytes 27000000 | tf_op jit(solution)/shard_map/coarse_and_merge/pallas_call | solution.py:689
  33.7 3.0 %collective-permute-start.5 = (bf16[34,32,128]{2,1,0:T(8,128)(2,1)S(1)}, bf16[34,32,128]{2,1,0:T(8,128)(2,1)S(1)}, u32[]{:S(2)}, u32[]{:S(2)}) collective-permute-start(bf16[34,32,128]{2,1,0:T(8,128)(2,1)S(1)} %get-tuple-element.83), channel_id=1, source_target_pairs={{0,1},{2,3},{4,5},{6,7},{8,9},{10,11},{12,13},{14,15},{16,17},{18,... | collective-permute-start | bytes 835592 | tf_op jit(solution)/shard_map/ppermute | solution.py:584
  36.7 1.2 %collective-permute-done.5.got_ref = bf16[34,32,128]{2,1,0:T(8,128)(2,1)S(1)} collective-permute-done((bf16[34,32,128]{2,1,0:T(8,128)(2,1)S(1)}, bf16[34,32,128]{2,1,0:T(8,128)(2,1)S(1)}, u32[]{:S(2)}, u32[]{:S(2)}) %collective-permute-start.5) | collective-permute-done | bytes 278560 | tf_op jit(solution)/shard_map/ppermute | solution.py:584
  37.9 1.6 %collective-permute-start.7 = (bf16[7,32,128]{2,1,0:T(8,128)(2,1)S(1)}, bf16[7,32,128]{2,1,0:T(8,128)(2,1)S(1)}, u32[]{:S(2)}, u32[]{:S(2)}) collective-permute-start(bf16[7,32,128]{2,1,0:T(8,128)(2,1)S(1)} %add_convert_fusion.5), channel_id=1, source_target_pairs={{0,2},{1,3},{2,0},{3,1},{4,6},{5,7},{6,4},{7,5},{8,10},{9,11},{10,... | collective-permute-start | bytes 172040 | tf_op jit(solution)/shard_map/ppermute | solution.py:602
  39.5 0.7 collective-permute-start.6
  40.2 2.0 %collective-permute-done.7 = bf16[7,32,128]{2,1,0:T(8,128)(2,1)S(1)} collective-permute-done((bf16[7,32,128]{2,1,0:T(8,128)(2,1)S(1)}, bf16[7,32,128]{2,1,0:T(8,128)(2,1)S(1)}, u32[]{:S(2)}, u32[]{:S(2)}) %collective-permute-start.7) | collective-permute-done | bytes 57376 | tf_op jit(solution)/shard_map/ppermute | solution.py:602
  42.2 5.2 %collective-permute-start.8 = (bf16[7,32,128]{2,1,0:T(8,128)(2,1)S(1)}, bf16[7,32,128]{2,1,0:T(8,128)(2,1)S(1)}, u32[]{:S(2)}, u32[]{:S(2)}) collective-permute-start(bf16[7,32,128]{2,1,0:T(8,128)(2,1)S(1)} %add_convert_fusion.4), channel_id=1, source_target_pairs={{0,6},{1,7},{2,4},{3,5},{4,2},{5,3},{6,0},{7,1},{8,14},{9,15},{10,... | collective-permute-start | bytes 172040 | tf_op jit(solution)/shard_map/ppermute | solution.py:602
  47.4 1.8 %face_table.1.t_ref = bf16[219,32,128]{2,1,0:T(8,128)(2,1)S(1)} custom-call(bf16[32,32,512]{2,1,0:T(8,128)(2,1)S(1)} %get-tuple-element.80.v_ref, bf16[32,32,512]{2,1,0:T(8,128)(2,1)S(1)} %get-tuple-element.81.y_ref, bf16[6,512,256]{2,1,0:T(8,128)(2,1)S(1)} %get-tuple-element.59.sel_ref, bf16[34,32,128]{2,1,0:T(8,128)(2,1)S(1)} %collective-permute-done.5.got_ref), custom_call_target="tpu_custom_call" | custom-call | flops 2000000 | bytes 6000000 | tf_op jit(solution)/shard_map/face_table/pallas_call | solution.py:715
  49.2 0.0 collective-permute-done.6.b_ref
  49.2 0.4 collective-permute-start.9
  49.6 0.5 collective-permute-done.8
  50.1 0.4 collective-permute-done.9.c_ref
  50.5 4.3 %collective-permute-start.10 = (bf16[7,32,128]{2,1,0:T(8,128)(2,1)S(1)}, bf16[7,32,128]{2,1,0:T(8,128)(2,1)S(1)}, u32[]{:S(2)}, u32[]{:S(2)}) collective-permute-start(bf16[7,32,128]{2,1,0:T(8,128)(2,1)S(1)} %add_convert_fusion.3), channel_id=1, source_target_pairs={{0,8},{1,9},{2,10},{3,11},{4,12},{5,13},{6,14},{7,15},{8,0},{9,1},... | collective-permute-start | bytes 172040 | tf_op jit(solution)/shard_map/ppermute | solution.py:602
  54.8 2.7 %last_level.4 = (bf16[262,32,128]{2,1,0:T(8,128)(2,1)S(1)}, bf16[12,2,16,512]{3,2,1,0:T(8,128)(2,1)S(1)}, bf16[32,32,512]{2,1,0:T(8,128)(2,1)}, bf16[32,32,512]{2,1,0:T(8,128)(2,1)}) custom-call(s32[12,32]{1,0:T(8,128)S(1)} %get-tuple-element.60.index, bf16[32,32,512]{2,1,0:T(8,128)(2,1)S(1)} %get-tuple-element.80.v_ref, ...), custom_call_target="tpu_custom_call" | custom-call | flops 2000000 | bytes 6000000 | tf_op jit(solution)/shard_map/last_level/pallas_call | solution.py:737
  57.6 0.0 collective-permute-done.10
  57.6 4.4 %collective-permute-start.11 = (bf16[7,32,128]{2,1,0:T(8,128)(2,1)S(1)}, bf16[7,32,128]{2,1,0:T(8,128)(2,1)S(1)}, u32[]{:S(2)}, u32[]{:S(2)}) collective-permute-start(bf16[7,32,128]{2,1,0:T(8,128)(2,1)S(1)} %add_convert_fusion.2), channel_id=1, source_target_pairs={{0,24},{1,25},{2,26},{3,27},{4,28},{5,29},{6,30},{7,31},{8,16},{9,... | collective-permute-start | bytes 172040 | tf_op jit(solution)/shard_map/ppermute | solution.py:602
  62.0 2.6 %last_level.5 = (bf16[32,32,512]{2,1,0:T(8,128)(2,1)}, bf16[32,32,512]{2,1,0:T(8,128)(2,1)}) custom-call(s32[12,32]{1,0:T(8,128)S(1)} %get-tuple-element.60.index, bf16[32,32,512]{2,1,0:T(8,128)(2,1)S(1)} %get-tuple-element.80.v_ref, bf16[32,32,512]{2,1,0:T(8,128)(2,1)S(1)} %get-tuple-element.81.y_ref, ...), custom_call_target="tpu_custom_call", output_to_operand_aliasing={{0}: (9, {}), {1}: (10, {})} | custom-call | flops 2000000 | bytes 6000000 | tf_op jit(solution)/shard_map/last_level/pallas_call | solution.py:750
  64.6 0.0 collective-permute-done.11
  64.7 6.6 %collective-permute-start.12 = (bf16[7,32,128]{2,1,0:T(8,128)(2,1)S(1)}, bf16[7,32,128]{2,1,0:T(8,128)(2,1)S(1)}, u32[]{:S(2)}, u32[]{:S(2)}) collective-permute-start(bf16[7,32,128]{2,1,0:T(8,128)(2,1)S(1)} %add_convert_fusion.1), channel_id=1, source_target_pairs={{0,32},{1,33},{2,34},{3,35},{4,36},{5,37},{6,38},{7,39},{8,40},{9,... | collective-permute-start | bytes 172040 | tf_op jit(solution)/shard_map/ppermute | solution.py:602
  71.3 2.6 %last_level.6 = (bf16[32,32,512]{2,1,0:T(8,128)(2,1)}, bf16[32,32,512]{2,1,0:T(8,128)(2,1)}) custom-call(s32[12,32]{1,0:T(8,128)S(1)} %get-tuple-element.60.index, bf16[32,32,512]{2,1,0:T(8,128)(2,1)S(1)} %get-tuple-element.80.v_ref, bf16[32,32,512]{2,1,0:T(8,128)(2,1)S(1)} %get-tuple-element.81.y_ref, ...), custom_call_target="tpu_custom_call", output_to_operand_aliasing={{0}: (9, {}), {1}: (10, {})} | custom-call | flops 2000000 | bytes 6000000 | tf_op jit(solution)/shard_map/last_level/pallas_call | solution.py:750
  73.8 0.0 collective-permute-done.12
  73.9 4.1 %collective-permute-start.13 = (bf16[7,32,128]{2,1,0:T(8,128)(2,1)S(1)}, bf16[7,32,128]{2,1,0:T(8,128)(2,1)S(1)}, u32[]{:S(2)}, u32[]{:S(2)}) collective-permute-start(bf16[7,32,128]{2,1,0:T(8,128)(2,1)S(1)} %add_convert_fusion.one_ref), channel_id=1, source_target_pairs={{0,96},{1,97},{2,98},{3,99},{4,100},{5,101},{6,102},{7,103},{8,104... | collective-permute-start | bytes 172040 | tf_op jit(solution)/shard_map/ppermute | solution.py:602
  78.0 2.6 %last_level.7 = (bf16[32,32,512]{2,1,0:T(8,128)(2,1)}, bf16[32,32,512]{2,1,0:T(8,128)(2,1)}) custom-call(s32[12,32]{1,0:T(8,128)S(1)} %get-tuple-element.60.index, bf16[32,32,512]{2,1,0:T(8,128)(2,1)S(1)} %get-tuple-element.80.v_ref, bf16[32,32,512]{2,1,0:T(8,128)(2,1)S(1)} %get-tuple-element.81.y_ref, ...), custom_call_target="tpu_custom_call", output_to_operand_aliasing={{0}: (9, {}), {1}: (10, {})} | custom-call | flops 2000000 | bytes 6000000 | tf_op jit(solution)/shard_map/last_level/pallas_call | solution.py:750
  80.5 0.0 collective-permute-done.13.two_ref
  80.5 1.0 %weight_sums.1 = (f32[7,32,32]{2,1,0:T(8,128)}, f32[7,32,32]{2,1,0:T(8,128)}, f32[7,32,32]{2,1,0:T(8,128)}) custom-call(bf16[7,32,128]{2,1,0:T(8,128)(2,1)S(1)} %add_convert_fusion.one_ref, bf16[7,32,128]{2,1,0:T(8,128)(2,1)S(1)} %collective-permute-done.13.two_ref), custom_call_target="tpu_custom_call" | custom-call | flops 1000000 | bytes 3000000 | tf_op jit(solution)/shard_map/weight_sums/pallas_call | solution.py:764
  (29 shorter events, 0.2 us)
Async XLA Ops:
  0.6 5.5 %copy-start.11 = (s32[128]{0:T(128)S(1)}, s32[128]{0:T(128)}, u32[]{:S(2)}) copy-start(s32[128]{0:T(128)} %counts.1) | copy-start | bytes 1540
  0.6 5.5 %copy-start.2 = (bf16[32,32,512]{2,1,0:T(8,128)(2,1)S(1)}, bf16[32,32,512]{2,1,0:T(8,128)(2,1)}, u32[]{:S(2)}) copy-start(bf16[32,32,512]{2,1,0:T(8,128)(2,1)} %z_ref.1) | copy-start | bytes 3145732
  0.7 5.5 %copy-start.1 = (bf16[32,32,512]{2,1,0:T(8,128)(2,1)S(1)}, bf16[32,32,512]{2,1,0:T(8,128)(2,1)}, u32[]{:S(2)}) copy-start(bf16[32,32,512]{2,1,0:T(8,128)(2,1)} %x_ref.1) | copy-start | bytes 3145732
  0.7 5.5 %copy-start.7 = (bf16[7,32,32]{2,1,0:T(8,128)(2,1)S(1)}, bf16[7,32,32]{2,1,0:T(8,128)(2,1)}, u32[]{:S(2)}) copy-start(bf16[7,32,32]{2,1,0:T(8,128)(2,1)} %w_out.3) | copy-start | bytes 43012
  0.7 5.5 %copy-start.6 = (bf16[7,32,32]{2,1,0:T(8,128)(2,1)S(1)}, bf16[7,32,32]{2,1,0:T(8,128)(2,1)}, u32[]{:S(2)}) copy-start(bf16[7,32,32]{2,1,0:T(8,128)(2,1)} %w_in.3) | copy-start | bytes 43012
  0.7 5.5 %copy-start.12 = (s32[32]{0:T(128)S(1)}, s32[32]{0:T(128)}, u32[]{:S(2)}) copy-start(s32[32]{0:T(128)} %octant.1) | copy-start | bytes 388
  0.7 5.5 %copy-start.10 = (s32[32,6]{0,1:T(8,128)S(1)}, s32[32,6]{0,1:T(8,128)}, u32[]{:S(2)}) copy-start(s32[32,6]{0,1:T(8,128)} %param.20) | copy-start | bytes 2308
  0.7 5.5 %copy-start.9 = (s32[32,6]{0,1:T(8,128)S(1)}, s32[32,6]{0,1:T(8,128)}, u32[]{:S(2)}) copy-start(s32[32,6]{0,1:T(8,128)} %param.19) | copy-start | bytes 2308
  3.8 1.6 %collective-permute-start = (bf16[27,32,128]{2,1,0:T(8,128)(2,1)S(1)}, bf16[27,32,128]{2,1,0:T(8,128)(2,1)S(1)}, u32[]{:S(2)}, u32[]{:S(2)}) collective-permute-start(bf16[27,32,128]{2,1,0:T(8,128)(2,1)S(1)} %get-tuple-element.58), channel_id=1, source_target_pairs={{0,1},{2,3},{4,5},{6,7},{8,9},{10,11},{12,13},{14,15},{16,17},{18,... | collective-permute-start | bytes 663560 | tf_op jit(solution)/shard_map/ppermute | solution.py:584
  5.4 3.7 %collective-permute-start.1 = (bf16[35,32,128]{2,1,0:T(8,128)(2,1)S(1)}, bf16[35,32,128]{2,1,0:T(8,128)(2,1)S(1)}, u32[]{:S(2)}, u32[]{:S(2)}) collective-permute-start(bf16[35,32,128]{2,1,0:T(8,128)(2,1)S(1)} %pad_maximum_fusion), channel_id=1, source_target_pairs={{1,2},{3,4},{5,6},{7,8},{9,10},{11,12},{13,14},{15,16},{17,18},{19... | collective-permute-start | bytes 860168 | tf_op jit(solution)/shard_map/ppermute | solution.py:584
  6.2 8.2 %copy-start = (bf16[2,256,1024]{2,1,0:T(8,128)(2,1)S(1)}, bf16[2,256,1024]{2,1,0:T(8,128)(2,1)}, u32[]{:S(2)}) copy-start(bf16[2,256,1024]{2,1,0:T(8,128)(2,1)} %constant.8.clone.spread_ref) | copy-start | bytes 3145732
  6.2 8.2 %copy-start.3 = (bf16[2,512,128]{2,1,0:T(8,128)(2,1)S(1)}, bf16[2,512,128]{2,1,0:T(8,128)(2,1)}, u32[]{:S(2)}) copy-start(bf16[2,512,128]{2,1,0:T(8,128)(2,1)} %constant.9.clone.rest_ref) | copy-start | bytes 786436
  9.1 5.3 %collective-permute-start.2 = (bf16[8,32,128]{2,1,0:T(8,128)(2,1)S(1)}, bf16[8,32,128]{2,1,0:T(8,128)(2,1)S(1)}, u32[]{:S(2)}, u32[]{:S(2)}) collective-permute-start(bf16[8,32,128]{2,1,0:T(8,128)(2,1)S(1)} %slice.16), channel_id=1, source_target_pairs={{0,1},{2,3},{4,5},{6,7},{8,9},{10,11},{12,13},{14,15},{16,17},{18,... | collective-permute-start | bytes 196616 | tf_op jit(solution)/shard_map/ppermute | solution.py:584
  14.4 8.0 %copy-start.8 = (bf16[7,32,32]{2,1,0:T(8,128)(2,1)S(1)}, bf16[7,32,32]{2,1,0:T(8,128)(2,1)}, u32[]{:S(2)}) copy-start(bf16[7,32,32]{2,1,0:T(8,128)(2,1)} %w_co.1) | copy-start | bytes 43012
  21.1 5.4 %collective-permute-start.3 = (bf16[8,32,128]{2,1,0:T(8,128)(2,1)S(1)}, bf16[8,32,128]{2,1,0:T(8,128)(2,1)S(1)}, u32[]{:S(2)}, u32[]{:S(2)}) collective-permute-start(bf16[8,32,128]{2,1,0:T(8,128)(2,1)S(1)} %get-tuple-element.77), channel_id=1, source_target_pairs={{0,1},{2,3},{4,5},{6,7},{8,9},{10,11},{12,13},{14,15},{16,17},{18,... | collective-permute-start | bytes 196616 | tf_op jit(solution)/shard_map/ppermute | solution.py:584
  21.6 4.9 %collective-permute-start.4 = (bf16[8,32,128]{2,1,0:T(8,128)(2,1)S(1)}, bf16[8,32,128]{2,1,0:T(8,128)(2,1)S(1)}, u32[]{:S(2)}, u32[]{:S(2)}) collective-permute-start(bf16[8,32,128]{2,1,0:T(8,128)(2,1)S(1)} %get-tuple-element.78), channel_id=1, source_target_pairs={{1,2},{3,4},{5,6},{7,8},{9,10},{11,12},{13,14},{15,16},{17,18},{19... | collective-permute-start | bytes 196616 | tf_op jit(solution)/shard_map/ppermute | solution.py:584
  22.4 4.1 %copy-start.4 = (bf16[256,1024]{1,0:T(8,128)(2,1)S(1)}, bf16[256,1024]{1,0:T(8,128)(2,1)}, u32[]{:S(2)}) copy-start(bf16[256,1024]{1,0:T(8,128)(2,1)} %constant.11.clone.place_ref) | copy-start | bytes 1572868
  22.4 4.1 %copy-start.5 = (bf16[128,1024]{1,0:T(8,128)(2,1)S(1)}, bf16[128,1024]{1,0:T(8,128)(2,1)}, u32[]{:S(2)}) copy-start(bf16[128,1024]{1,0:T(8,128)(2,1)} %constant.10.clone.up_ref) | copy-start | bytes 786436
  33.7 4.2 %collective-permute-start.5 = (bf16[34,32,128]{2,1,0:T(8,128)(2,1)S(1)}, bf16[34,32,128]{2,1,0:T(8,128)(2,1)S(1)}, u32[]{:S(2)}, u32[]{:S(2)}) collective-permute-start(bf16[34,32,128]{2,1,0:T(8,128)(2,1)S(1)} %get-tuple-element.83), channel_id=1, source_target_pairs={{0,1},{2,3},{4,5},{6,7},{8,9},{10,11},{12,13},{14,15},{16,17},{18,... | collective-permute-start | bytes 835592 | tf_op jit(solution)/shard_map/ppermute | solution.py:584
  37.9 4.3 %collective-permute-start.7 = (bf16[7,32,128]{2,1,0:T(8,128)(2,1)S(1)}, bf16[7,32,128]{2,1,0:T(8,128)(2,1)S(1)}, u32[]{:S(2)}, u32[]{:S(2)}) collective-permute-start(bf16[7,32,128]{2,1,0:T(8,128)(2,1)S(1)} %add_convert_fusion.5), channel_id=1, source_target_pairs={{0,2},{1,3},{2,0},{3,1},{4,6},{5,7},{6,4},{7,5},{8,10},{9,11},{10,... | collective-permute-start | bytes 172040 | tf_op jit(solution)/shard_map/ppermute | solution.py:602
  39.5 9.6 %collective-permute-start.6 = (bf16[35,32,128]{2,1,0:T(8,128)(2,1)S(1)}, bf16[35,32,128]{2,1,0:T(8,128)(2,1)S(1)}, u32[]{:S(2)}, u32[]{:S(2)}) collective-permute-start(bf16[35,32,128]{2,1,0:T(8,128)(2,1)S(1)} %pad_maximum_fusion.1), channel_id=1, source_target_pairs={{1,2},{3,4},{5,6},{7,8},{9,10},{11,12},{13,14},{15,16},{17,18},{19... | collective-permute-start | bytes 860168 | tf_op jit(solution)/shard_map/ppermute | solution.py:584
  42.2 7.9 %collective-permute-start.8 = (bf16[7,32,128]{2,1,0:T(8,128)(2,1)S(1)}, bf16[7,32,128]{2,1,0:T(8,128)(2,1)S(1)}, u32[]{:S(2)}, u32[]{:S(2)}) collective-permute-start(bf16[7,32,128]{2,1,0:T(8,128)(2,1)S(1)} %add_convert_fusion.4), channel_id=1, source_target_pairs={{0,6},{1,7},{2,4},{3,5},{4,2},{5,3},{6,0},{7,1},{8,14},{9,15},{10,... | collective-permute-start | bytes 172040 | tf_op jit(solution)/shard_map/ppermute | solution.py:602
  49.2 1.3 %collective-permute-start.9 = (bf16[8,32,128]{2,1,0:T(8,128)(2,1)S(1)}, bf16[8,32,128]{2,1,0:T(8,128)(2,1)S(1)}, u32[]{:S(2)}, u32[]{:S(2)}) collective-permute-start(bf16[8,32,128]{2,1,0:T(8,128)(2,1)S(1)} %slice.19), channel_id=1, source_target_pairs={{0,1},{2,3},{4,5},{6,7},{8,9},{10,11},{12,13},{14,15},{16,17},{18,... | collective-permute-start | bytes 196616 | tf_op jit(solution)/shard_map/ppermute | solution.py:584
  50.5 7.1 %collective-permute-start.10 = (bf16[7,32,128]{2,1,0:T(8,128)(2,1)S(1)}, bf16[7,32,128]{2,1,0:T(8,128)(2,1)S(1)}, u32[]{:S(2)}, u32[]{:S(2)}) collective-permute-start(bf16[7,32,128]{2,1,0:T(8,128)(2,1)S(1)} %add_convert_fusion.3), channel_id=1, source_target_pairs={{0,8},{1,9},{2,10},{3,11},{4,12},{5,13},{6,14},{7,15},{8,0},{9,1},... | collective-permute-start | bytes 172040 | tf_op jit(solution)/shard_map/ppermute | solution.py:602
  57.6 7.0 %collective-permute-start.11 = (bf16[7,32,128]{2,1,0:T(8,128)(2,1)S(1)}, bf16[7,32,128]{2,1,0:T(8,128)(2,1)S(1)}, u32[]{:S(2)}, u32[]{:S(2)}) collective-permute-start(bf16[7,32,128]{2,1,0:T(8,128)(2,1)S(1)} %add_convert_fusion.2), channel_id=1, source_target_pairs={{0,24},{1,25},{2,26},{3,27},{4,28},{5,29},{6,30},{7,31},{8,16},{9,... | collective-permute-start | bytes 172040 | tf_op jit(solution)/shard_map/ppermute | solution.py:602
  64.7 9.2 %collective-permute-start.12 = (bf16[7,32,128]{2,1,0:T(8,128)(2,1)S(1)}, bf16[7,32,128]{2,1,0:T(8,128)(2,1)S(1)}, u32[]{:S(2)}, u32[]{:S(2)}) collective-permute-start(bf16[7,32,128]{2,1,0:T(8,128)(2,1)S(1)} %add_convert_fusion.1), channel_id=1, source_target_pairs={{0,32},{1,33},{2,34},{3,35},{4,36},{5,37},{6,38},{7,39},{8,40},{9,... | collective-permute-start | bytes 172040 | tf_op jit(solution)/shard_map/ppermute | solution.py:602
  73.9 6.7 %collective-permute-start.13 = (bf16[7,32,128]{2,1,0:T(8,128)(2,1)S(1)}, bf16[7,32,128]{2,1,0:T(8,128)(2,1)S(1)}, u32[]{:S(2)}, u32[]{:S(2)}) collective-permute-start(bf16[7,32,128]{2,1,0:T(8,128)(2,1)S(1)} %add_convert_fusion.one_ref), channel_id=1, source_target_pairs={{0,96},{1,97},{2,98},{3,99},{4,100},{5,101},{6,102},{7,103},{8,104... | collective-permute-start | bytes 172040 | tf_op jit(solution)/shard_map/ppermute | solution.py:602

commit v7 on v6

--- a/solution.py
+++ b/solution.py
@@ -44,29 +44,13 @@
     return [ids // 64, ids // 8 % 8, ids % 8]
 
 
-def face_cells(face):
-    coords = cell_coords()
-    keep = coords[face // 2] == (EDGE - 1 if face % 2 else 0)
-    return np.nonzero(keep)[0]
-
-
 def constants():
-    spread = np.zeros((2, 256, 2 * CELLS), np.float32)
-    for face in range(6):
-        for j, cell in enumerate(face_cells(face)):
-            for kind in range(2):
-                col = (face % 2) * 128 + kind * 64 + j
-                if face >= 2:
-                    spread[face // 2 - 1, col, kind * CELLS + cell] = 1
     c0, c1, c2 = cell_coords()
     group = (c0 // 2) * 16 + (c1 // 2) * 4 + c2 // 2
     rest = np.zeros((2, CELLS, 128), np.float32)
-    up = np.zeros((128, 2 * CELLS), np.float32)
     for cell in range(CELLS):
         rest[0, cell, group[cell]] = 0.125
         rest[1, cell, 64 + group[cell]] = 1
-        up[group[cell], cell] = 1
-        up[64 + group[cell], CELLS + cell] = 1
     place = np.zeros((256, 2 * CELLS), np.float32)
     for o2 in range(2):
         for a in range(64):
@@ -75,9 +59,7 @@
             place[128 * o2 + 64 + a, CELLS + cell] = 1
     as_bf = lambda item: np.asarray(item, jnp.bfloat16)
     return (
-        as_bf(spread),
         as_bf(rest),
-        as_bf(up),
         as_bf(place),
     )
 
@@ -120,15 +102,18 @@
     for side in range(2):
         for copy in waits[side]:
             copy.wait()
+        if side:
+            for i in range(16):
+                slot = jnp.clip(count - 16 + i, 0, SLOTS - 1)
+                v_rows[i] = v_ref[slot]
+                y_rows[i] = y_ref[slot]
         for dim in (2, 1, 0):
             depth = MORTON[dim]
-            for i in range(depth):
-                slot = jnp.clip(count - depth + i, 0, SLOTS - 1) if side else i
-                v_rows[i] = v_ref[slot]
-                y_rows[i] = y_ref[slot]
+            v_part = v_rows[16 - depth : 16] if side else v_ref[0:depth]
+            y_part = y_rows[16 - depth : 16] if side else y_ref[0:depth]
             cols = slice(side * 128, side * 128 + 128)
-            layers = dot(v_rows[:depth].reshape(depth * C, CELLS), sel_ref[2 * dim, :, cols])
-            layers += dot(y_rows[:depth].reshape(depth * C, CELLS), sel_ref[2 * dim + 1, :, cols])
+            layers = dot(v_part.reshape(depth * C, CELLS), sel_ref[2 * dim, :, cols])
+            layers += dot(y_part.reshape(depth * C, CELLS), sel_ref[2 * dim + 1, :, cols])
             layers = layers.astype(BF).reshape(depth, C, 128)
             if dim == 2 and side:
                 sides[side, 0:8] = layers[8:16]
@@ -293,7 +278,7 @@
                 coef[row, 1] = (high * (1 - t_high) + low * t_low).astype(BF)
 
 
-def block_taps(start, index, v_ref, y_ref, spread_ref, table, coef, picked, ta, tb):
+def block_taps(start, index, v_ref, y_ref, sel_ref, table, coef, picked, ta, tb):
     size = v_ref.shape[0]
     for dim in range(3):
         low, high = 2 * dim, 2 * dim + 1
@@ -303,12 +288,14 @@
             for p in range(size):
                 picked[p, :, 0:128] = table[index[low, start + p]]
                 picked[p, :, 128:256] = table[index[high, start + p]]
-            spread = dot(picked[...].reshape(size * C, 256), spread_ref[dim - 1]).astype(BF)
+            rows_in = picked[...].reshape(size * C, 256)
+            v_spread = dot_nt(rows_in, sel_ref[2 * dim]).astype(BF)
+            y_spread = dot_nt(rows_in, sel_ref[2 * dim + 1]).astype(BF)
         for p in range(size):
             if dim:
                 rows = slice(p * C, (p + 1) * C)
-                v_edge = spread[rows, :CELLS]
-                y_edge = spread[rows, CELLS:]
+                v_edge = v_spread[rows]
+                y_edge = y_spread[rows]
             else:
                 r_low = table[index[low, start + p]]
                 r_high = table[index[high, start + p]]
@@ -342,7 +329,7 @@
 
 
 def fine_kernel(
-    meta, index, xs, zs, t_ref, b_ref, c_ref, mats, spread_ref, rest_ref,
+    meta, index, xs, zs, t_ref, b_ref, c_ref, mats, sel_ref, rest_ref,
     ta_ref, tb_ref, hidden_ref, slope_ref, gm_ref, par_ref, inner_ref, outer_ref,
     table, coef, picked, par, ends,
 ):
@@ -357,7 +344,7 @@
             item.at[pl.ds(start, BIG)]
             for item in (xs, zs, ta_ref, tb_ref, hidden_ref, slope_ref, gm_ref)
         ]
-        block_taps(start, index, x_at, z_at, spread_ref, table, coef, picked, ta, tb)
+        block_taps(start, index, x_at, z_at, sel_ref, table, coef, picked, ta, tb)
         for p in range(BIG):
             hidden, slope = silu_pair(dot(mats[IN_F], ta[p]))
             hidden_at[p] = hidden.astype(BF)
@@ -455,7 +442,7 @@
 def merge_kernel(
     meta,
     ta_ref, means_ref, dw0_ref, hidden_ref, slope_ref, gm_ref, par_ref, pin_ref, pout_ref,
-    mats, place_ref, up_ref, sel_ref,
+    mats, place_ref, rest_ref, sel_ref,
     merged_ref, gpa_ref, sum_ref, inner_ref, outer_ref,
     par, taps, up_rows, picked, v_rows, y_rows, sides, dw_ref,
 ):
@@ -471,14 +458,16 @@
         start = step * BIG
         for p in range(BIG):
             picked[p] = up_rows[meta[DST + start + p]]
-        spread = dot(picked[...].reshape(BIG * C, 128), up_ref[...])
+        rows_in = picked[...].reshape(BIG * C, 128)
+        up = dot_nt(rows_in, rest_ref[0]) * 8.0
+        down = dot_nt(rows_in, rest_ref[1]) * 0.125
         dw_in = jnp.zeros((7 * C, C), F32)
         dw_out = jnp.zeros((7 * C, C), F32)
         for p in range(BIG):
             rows = slice(p * C, (p + 1) * C)
             here = start + p
-            merged = (hidden_ref[here].astype(F32) + spread[rows, :CELLS]).astype(BF)
-            grad = gm_ref[here].astype(F32) + spread[rows, CELLS:] * 0.125
+            merged = (hidden_ref[here].astype(F32) + up[rows]).astype(BF)
+            grad = gm_ref[here].astype(F32) + down[rows]
             gpa = (grad * slope_ref[here].astype(F32)).astype(BF)
             merged_ref[here] = merged
             gpa_ref[here] = gpa
@@ -501,12 +490,12 @@
     table[BASE_A:BASE_B] = got_ref[0:NEAR]
 
 
-def final_body(step, index, v_ref, y_ref, xs, zs, mats, spread_ref, table, coef, out_hbm, gs_hbm,
+def final_body(step, index, v_ref, y_ref, xs, zs, mats, sel_ref, table, coef, out_hbm, gs_hbm,
                picked, ta, tb, out_ref, gs_ref, sems):
     start = step * PB
     part = pl.ds(start, PB)
     block_taps(
-        start, index, v_ref.at[part], y_ref.at[part], spread_ref, table, coef, picked, ta, tb
+        start, index, v_ref.at[part], y_ref.at[part], sel_ref, table, coef, picked, ta, tb
     )
     half = PB // 2
     copies = []
@@ -527,19 +516,19 @@
 
 
 def first_final_kernel(
-    index, v_ref, y_ref, xs, zs, mats, spread_ref, t_ref, b_ref, c_ref,
+    index, v_ref, y_ref, xs, zs, mats, sel_ref, t_ref, b_ref, c_ref,
     table, coef, out_hbm, gs_hbm, *scratch,
 ):
     join_table((t_ref, b_ref, c_ref), coef, table)
-    final_body(0, index, v_ref, y_ref, xs, zs, mats, spread_ref, table, coef, out_hbm, gs_hbm,
+    final_body(0, index, v_ref, y_ref, xs, zs, mats, sel_ref, table, coef, out_hbm, gs_hbm,
                *scratch)
 
 
 def next_final_kernel(
-    step, index, v_ref, y_ref, xs, zs, mats, spread_ref, table, coef, out_in, gs_in,
+    step, index, v_ref, y_ref, xs, zs, mats, sel_ref, table, coef, out_in, gs_in,
     out_hbm, gs_hbm, *scratch,
 ):
-    final_body(step, index, v_ref, y_ref, xs, zs, mats, spread_ref, table, coef, out_hbm, gs_hbm,
+    final_body(step, index, v_ref, y_ref, xs, zs, mats, sel_ref, table, coef, out_hbm, gs_hbm,
                *scratch)
 
 
@@ -607,7 +596,7 @@
     owner_count, neighbour, level_tag, octant,
 ):
     devices = lax.axis_size("patch")
-    spread, rest, up, place = [jnp.asarray(item) for item in constants()]
+    rest, place = [jnp.asarray(item) for item in constants()]
 
     field = (SLOTS, C, CELLS)
     stack = (SLOTS, 7 * C, CELLS)
@@ -671,7 +660,7 @@
         compiler_params=params(),
         cost_estimate=cost(8),
         name="fine_level",
-    )(meta, index, xs, zs, table, got_b, got_c, mats, spread, rest)
+    )(meta, index, xs, zs, table, got_b, got_c, mats, sel, rest)
     child_out = trade(pout, "outer")
     child_in = trade(pin, "inner")
 
@@ -705,7 +694,7 @@
         name="coarse_and_merge",
     )(
         meta, taps_a, means, dw_part, hidden, slope, grad_merged, par, child_in, child_out, mats,
-        place, up, sel,
+        place, rest, sel,
     )
     got_a = trade(inner, "inner")
     got_b = relay_out(outer, got_a)
@@ -731,7 +720,7 @@
         pltpu.VMEM((PB, C, CELLS), BF),
         pltpu.SemaphoreType.DMA((2, 2)),
     ]
-    fixed = (index, merged, grad_pre, xs, zs, mats, spread)
+    fixed = (index, merged, grad_pre, xs, zs, mats, sel)
     sums, got_c = lax.optimization_barrier((add(sums, swap(sums, 6)), got_c))
     partner = swap(sums, 8)
     table, coef, output, grad_state = pl.pallas_call(

time: 81.7 us -> 81.6 us (level)
  no operation moved by 1% of the time
where the time goes in v7:
time: 81.6 us; the launch traced here: 81.5 us
  Pallas kernels  37.1 us (45%)
  starting transfers between devices  36.5 us (45%)
  waiting for transfers between devices  6.53 us (8%)
  between operations  1.03 us (1%)
    ppermute x6, starting transfers between devices, swap(): return lax.ppermute(block, 'patch', [(i, i ^ mask) for i in range(devices)])  26.1 us
    ppermute x8, starting transfers between devices, trade(): return lax.ppermute(block, 'patch', pairs(kind, lax.axis_size('patch')))  10.4 us
    pallas_call x3, Pallas kernels, on_device(): pl.pallas_call(functools.partial(next_final_kernel, step), in_specs=[SMEM...  7.85 us
    pallas_call x1, Pallas kernels, on_device(): pl.pallas_call(merge_kernel, in_specs=[SMEM()] + [VMEM()] * 13, out_specs...  7.14 us
    pallas_call x1, Pallas kernels, on_device(): pl.pallas_call(fine_kernel, in_specs=[SMEM()] * 2 + [VMEM()] * 8, out_spe...  6.63 us
    pallas_call x1, Pallas kernels, on_device(): pl.pallas_call(window_kernel, in_specs=[VMEM()] * 6, out_specs=[VMEM()] *...  4.02 us
    ppermute x8, waiting for transfers between devices, trade(): return lax.ppermute(block, 'patch', pairs(kind, lax.axis_size('patch')))  3.99 us
    pallas_call x1, Pallas kernels, on_device(): pl.pallas_call(layers_kernel, in_specs=[HBM()] * 3, out_specs=[VMEM()] *...  3.09 us
  transfers between devices with their start and end apart: 14, of which 6 were waited for; matrix products, arithmetic and copies ran while one was open for 0% of the time, Pallas kernels for 24%

profile of v7, /device:TPU:0, one launch (start us, length us, event | category | flops | bytes accessed | tf_op | source)
XLA Modules:
  0.0 81.5 jit_solution(8048588948262853075)
XLA Ops:
  0.6 0.0 copy-start.9
  0.6 0.0 copy-start.1
  0.7 0.0 copy-start
  0.7 0.0 copy-start.5
  0.7 0.0 copy-start.4
  0.7 0.0 copy-start.10
  0.7 0.0 copy-start.8
  0.7 3.1 %face_rows.1 = (bf16[27,32,128]{2,1,0:T(8,128)(2,1)S(1)}, bf16[27,32,128]{2,1,0:T(8,128)(2,1)S(1)}, bf16[6,512,256]{2,1,0:T(8,128)(2,1)S(1)}) custom-call(s32[128]{0:T(128)} %counts.1, bf16[32,32,512]{2,1,0:T(8,128)(2,1)} %x_ref.1, bf16[32,32,512]{2,1,0:T(8,128)(2,1)} %z_ref.1), custom_call_target="tpu_custom_call" | custom-call | flops 4000000 | bytes 12000000 | tf_op jit(solution)/shard_map/face_rows/pallas_call | solution.py:612
  3.8 0.1 collective-permute-start
  3.9 1.5 %collective-permute-done.got_ref = bf16[27,32,128]{2,1,0:T(8,128)(2,1)S(1)} collective-permute-done((bf16[27,32,128]{2,1,0:T(8,128)(2,1)S(1)}, bf16[27,32,128]{2,1,0:T(8,128)(2,1)S(1)}, u32[]{:S(2)}, u32[]{:S(2)}) %collective-permute-start) | collective-permute-done | bytes 221216 | tf_op jit(solution)/shard_map/ppermute | solution.py:573
  5.4 0.7 collective-permute-start.1
  6.2 0.0 copy-start.2
  6.2 2.9 %prepare.1 = (s32[128]{0:T(128)S(1)}, s32[12,32]{1,0:T(8,128)S(1)}, bf16[32,32,512]{2,1,0:T(8,128)(2,1)S(1)}, bf16[32,32,512]{2,1,0:T(8,128)(2,1)S(1)}, bf16[2,3...) custom-call(s32[128]{0:T(128)S(1)} %copy-done.9, s32[32]{0:T(128)S(1)} %copy-done.10, s32[6,32]{1,0:T(8,128)S(1)} %bitcast.2, ...), custom_call_target="tpu_custom_call" | custom-call | flops 4000000 | bytes 12000000 | tf_op jit(solution)/shard_map/prepare/pallas_call | solution.py:632
  9.1 0.0 collective-permute-done.1.b_ref
  9.1 4.4 %collective-permute-start.2 = (bf16[8,32,128]{2,1,0:T(8,128)(2,1)S(1)}, bf16[8,32,128]{2,1,0:T(8,128)(2,1)S(1)}, u32[]{:S(2)}, u32[]{:S(2)}) collective-permute-start(bf16[8,32,128]{2,1,0:T(8,128)(2,1)S(1)} %slice.16), channel_id=1, source_target_pairs={{0,1},{2,3},{4,5},{6,7},{8,9},{10,11},{12,13},{14,15},{16,17},{18,... | collective-permute-start | bytes 196616 | tf_op jit(solution)/shard_map/ppermute | solution.py:573
  13.5 0.9 %collective-permute-done.2.c_ref = bf16[8,32,128]{2,1,0:T(8,128)(2,1)S(1)} collective-permute-done((bf16[8,32,128]{2,1,0:T(8,128)(2,1)S(1)}, bf16[8,32,128]{2,1,0:T(8,128)(2,1)S(1)}, u32[]{:S(2)}, u32[]{:S(2)}) %collective-permute-start.2) | collective-permute-done | bytes 65568 | tf_op jit(solution)/shard_map/ppermute | solution.py:573
  14.4 6.6 %fine_level.1 = (bf16[32,224,512]{2,1,0:T(8,128)(2,1)S(1)}, bf16[32,224,512]{2,1,0:T(8,128)(2,1)S(1)}, bf16[32,32,512]{2,1,0:T(8,128)(2,1)S(1)}, bf16[32,32,512]...) custom-call(s32[128]{0:T(128)S(1)} %get-tuple-element.63.meta, ...), custom_call_target="tpu_custom_call" | custom-call | flops 8000000 | bytes 24000000 | tf_op jit(solution)/shard_map/fine_level/pallas_call | solution.py:647
  21.0 0.4 collective-permute-start.3
  21.5 0.8 %collective-permute-start.4 = (bf16[8,32,128]{2,1,0:T(8,128)(2,1)S(1)}, bf16[8,32,128]{2,1,0:T(8,128)(2,1)S(1)}, u32[]{:S(2)}, u32[]{:S(2)}) collective-permute-start(bf16[8,32,128]{2,1,0:T(8,128)(2,1)S(1)} %get-tuple-element.78), channel_id=1, source_target_pairs={{1,2},{3,4},{5,6},{7,8},{9,10},{11,12},{13,14},{15,16},{17,18},{19... | collective-permute-start | bytes 196616 | tf_op jit(solution)/shard_map/ppermute | solution.py:573
  22.3 0.0 copy-start.3
  22.3 4.0 %window.1 = (bf16[4,32,224]{2,1,0:T(8,128)(2,1)S(1)}, f32[224,32]{1,0:T(8,128)S(1)}, bf16[32,224,128]{2,1,0:T(8,128)(2,1)S(1)}) custom-call(bf16[32,32,512]{2,1,0:T(8,128)(2,1)S(1)} %get-tuple-element.70.hidden_ref, bf16[32,224,512]{2,1,0:T(8,128)(2,1)S(1)} %get-tuple-element.71.tb_ref, bf16[2,512,128]{2,1,0:T(8,128)(2,1)S(1)} %copy-done.2, ...), custom_call_target="tpu_custom_call" | custom-call | flops 3000000 | bytes 9000000 | tf_op jit(solution)/shard_map/window/pallas_call | solution.py:667
  26.4 0.0 collective-permute-done.3.pin_ref
  26.4 0.0 collective-permute-done.4.pout_ref
  26.4 7.1 %coarse_and_merge.1 = (bf16[32,32,512]{2,1,0:T(8,128)(2,1)S(1)}, bf16[32,32,512]{2,1,0:T(8,128)(2,1)S(1)}, bf16[7,32,128]{2,1,0:T(8,128)(2,1)S(1)}, bf16[34,32,1...) custom-call(s32[128]{0:T(128)S(1)} %get-tuple-element.63.meta, bf16[32,224,512]{2,1,0:T(8,128)(2,1)S(1)} %get-tuple-element.69.ta_ref, ...), custom_call_target="tpu_custom_call" | custom-call | flops 9000000 | bytes 27000000 | tf_op jit(solution)/shard_map/coarse_and_merge/pallas_call | solution.py:678
  33.6 3.0 %collective-permute-start.5 = (bf16[34,32,128]{2,1,0:T(8,128)(2,1)S(1)}, bf16[34,32,128]{2,1,0:T(8,128)(2,1)S(1)}, u32[]{:S(2)}, u32[]{:S(2)}) collective-permute-start(bf16[34,32,128]{2,1,0:T(8,128)(2,1)S(1)} %get-tuple-element.83), channel_id=1, source_target_pairs={{0,1},{2,3},{4,5},{6,7},{8,9},{10,11},{12,13},{14,15},{16,17},{18,... | collective-permute-start | bytes 835592 | tf_op jit(solution)/shard_map/ppermute | solution.py:573
  36.6 1.2 %collective-permute-done.5.got_ref = bf16[34,32,128]{2,1,0:T(8,128)(2,1)S(1)} collective-permute-done((bf16[34,32,128]{2,1,0:T(8,128)(2,1)S(1)}, bf16[34,32,128]{2,1,0:T(8,128)(2,1)S(1)}, u32[]{:S(2)}, u32[]{:S(2)}) %collective-permute-start.5) | collective-permute-done | bytes 278560 | tf_op jit(solution)/shard_map/ppermute | solution.py:573
  37.8 1.6 %collective-permute-start.7 = (bf16[7,32,128]{2,1,0:T(8,128)(2,1)S(1)}, bf16[7,32,128]{2,1,0:T(8,128)(2,1)S(1)}, u32[]{:S(2)}, u32[]{:S(2)}) collective-permute-start(bf16[7,32,128]{2,1,0:T(8,128)(2,1)S(1)} %add_convert_fusion.5), channel_id=1, source_target_pairs={{0,2},{1,3},{2,0},{3,1},{4,6},{5,7},{6,4},{7,5},{8,10},{9,11},{10,... | collective-permute-start | bytes 172040 | tf_op jit(solution)/shard_map/ppermute | solution.py:591
  39.4 0.7 collective-permute-start.6
  40.1 2.0 %collective-permute-done.7 = bf16[7,32,128]{2,1,0:T(8,128)(2,1)S(1)} collective-permute-done((bf16[7,32,128]{2,1,0:T(8,128)(2,1)S(1)}, bf16[7,32,128]{2,1,0:T(8,128)(2,1)S(1)}, u32[]{:S(2)}, u32[]{:S(2)}) %collective-permute-start.7) | collective-permute-done | bytes 57376 | tf_op jit(solution)/shard_map/ppermute | solution.py:591
  42.1 5.2 %collective-permute-start.8 = (bf16[7,32,128]{2,1,0:T(8,128)(2,1)S(1)}, bf16[7,32,128]{2,1,0:T(8,128)(2,1)S(1)}, u32[]{:S(2)}, u32[]{:S(2)}) collective-permute-start(bf16[7,32,128]{2,1,0:T(8,128)(2,1)S(1)} %add_convert_fusion.4), channel_id=1, source_target_pairs={{0,6},{1,7},{2,4},{3,5},{4,2},{5,3},{6,0},{7,1},{8,14},{9,15},{10,... | collective-permute-start | bytes 172040 | tf_op jit(solution)/shard_map/ppermute | solution.py:591
  47.3 1.8 %face_table.1.t_ref = bf16[219,32,128]{2,1,0:T(8,128)(2,1)S(1)} custom-call(bf16[32,32,512]{2,1,0:T(8,128)(2,1)S(1)} %get-tuple-element.80.v_ref, bf16[32,32,512]{2,1,0:T(8,128)(2,1)S(1)} %get-tuple-element.81.y_ref, bf16[6,512,256]{2,1,0:T(8,128)(2,1)S(1)} %get-tuple-element.59.sel_ref, bf16[34,32,128]{2,1,0:T(8,128)(2,1)S(1)} %collective-permute-done.5.got_ref), custom_call_target="tpu_custom_call" | custom-call | flops 2000000 | bytes 6000000 | tf_op jit(solution)/shard_map/face_table/pallas_call | solution.py:704
  49.1 0.0 collective-permute-done.6.b_ref
  49.1 0.3 collective-permute-start.9
  49.4 0.6 collective-permute-done.8
  50.0 0.4 collective-permute-done.9.c_ref
  50.5 4.3 %collective-permute-start.10 = (bf16[7,32,128]{2,1,0:T(8,128)(2,1)S(1)}, bf16[7,32,128]{2,1,0:T(8,128)(2,1)S(1)}, u32[]{:S(2)}, u32[]{:S(2)}) collective-permute-start(bf16[7,32,128]{2,1,0:T(8,128)(2,1)S(1)} %add_convert_fusion.3), channel_id=1, source_target_pairs={{0,8},{1,9},{2,10},{3,11},{4,12},{5,13},{6,14},{7,15},{8,0},{9,1},... | collective-permute-start | bytes 172040 | tf_op jit(solution)/shard_map/ppermute | solution.py:591
  54.7 2.7 %last_level.4 = (bf16[262,32,128]{2,1,0:T(8,128)(2,1)S(1)}, bf16[12,2,16,512]{3,2,1,0:T(8,128)(2,1)S(1)}, bf16[32,32,512]{2,1,0:T(8,128)(2,1)}, bf16[32,32,512]{2,1,0:T(8,128)(2,1)}) custom-call(s32[12,32]{1,0:T(8,128)S(1)} %get-tuple-element.60.index, bf16[32,32,512]{2,1,0:T(8,128)(2,1)S(1)} %get-tuple-element.80.v_ref, ...), custom_call_target="tpu_custom_call" | custom-call | flops 2000000 | bytes 6000000 | tf_op jit(solution)/shard_map/last_level/pallas_call | solution.py:726
  57.5 0.0 collective-permute-done.10
  57.5 4.4 %collective-permute-start.11 = (bf16[7,32,128]{2,1,0:T(8,128)(2,1)S(1)}, bf16[7,32,128]{2,1,0:T(8,128)(2,1)S(1)}, u32[]{:S(2)}, u32[]{:S(2)}) collective-permute-start(bf16[7,32,128]{2,1,0:T(8,128)(2,1)S(1)} %add_convert_fusion.2), channel_id=1, source_target_pairs={{0,24},{1,25},{2,26},{3,27},{4,28},{5,29},{6,30},{7,31},{8,16},{9,... | collective-permute-start | bytes 172040 | tf_op jit(solution)/shard_map/ppermute | solution.py:591
  62.0 2.6 %last_level.5 = (bf16[32,32,512]{2,1,0:T(8,128)(2,1)}, bf16[32,32,512]{2,1,0:T(8,128)(2,1)}) custom-call(s32[12,32]{1,0:T(8,128)S(1)} %get-tuple-element.60.index, bf16[32,32,512]{2,1,0:T(8,128)(2,1)S(1)} %get-tuple-element.80.v_ref, bf16[32,32,512]{2,1,0:T(8,128)(2,1)S(1)} %get-tuple-element.81.y_ref, ...), custom_call_target="tpu_custom_call", output_to_operand_aliasing={{0}: (9, {}), {1}: (10, {})} | custom-call | flops 2000000 | bytes 6000000 | tf_op jit(solution)/shard_map/last_level/pallas_call | solution.py:739
  64.6 0.0 collective-permute-done.11
  64.6 6.5 %collective-permute-start.12 = (bf16[7,32,128]{2,1,0:T(8,128)(2,1)S(1)}, bf16[7,32,128]{2,1,0:T(8,128)(2,1)S(1)}, u32[]{:S(2)}, u32[]{:S(2)}) collective-permute-start(bf16[7,32,128]{2,1,0:T(8,128)(2,1)S(1)} %add_convert_fusion.1), channel_id=1, source_target_pairs={{0,32},{1,33},{2,34},{3,35},{4,36},{5,37},{6,38},{7,39},{8,40},{9,... | collective-permute-start | bytes 172040 | tf_op jit(solution)/shard_map/ppermute | solution.py:591
  71.2 2.6 %last_level.6 = (bf16[32,32,512]{2,1,0:T(8,128)(2,1)}, bf16[32,32,512]{2,1,0:T(8,128)(2,1)}) custom-call(s32[12,32]{1,0:T(8,128)S(1)} %get-tuple-element.60.index, bf16[32,32,512]{2,1,0:T(8,128)(2,1)S(1)} %get-tuple-element.80.v_ref, bf16[32,32,512]{2,1,0:T(8,128)(2,1)S(1)} %get-tuple-element.81.y_ref, ...), custom_call_target="tpu_custom_call", output_to_operand_aliasing={{0}: (9, {}), {1}: (10, {})} | custom-call | flops 2000000 | bytes 6000000 | tf_op jit(solution)/shard_map/last_level/pallas_call | solution.py:739
  73.8 0.0 collective-permute-done.12
  73.8 4.0 %collective-permute-start.13 = (bf16[7,32,128]{2,1,0:T(8,128)(2,1)S(1)}, bf16[7,32,128]{2,1,0:T(8,128)(2,1)S(1)}, u32[]{:S(2)}, u32[]{:S(2)}) collective-permute-start(bf16[7,32,128]{2,1,0:T(8,128)(2,1)S(1)} %add_convert_fusion.one_ref), channel_id=1, source_target_pairs={{0,96},{1,97},{2,98},{3,99},{4,100},{5,101},{6,102},{7,103},{8,104... | collective-permute-start | bytes 172040 | tf_op jit(solution)/shard_map/ppermute | solution.py:591
  77.9 2.6 %last_level.7 = (bf16[32,32,512]{2,1,0:T(8,128)(2,1)}, bf16[32,32,512]{2,1,0:T(8,128)(2,1)}) custom-call(s32[12,32]{1,0:T(8,128)S(1)} %get-tuple-element.60.index, bf16[32,32,512]{2,1,0:T(8,128)(2,1)S(1)} %get-tuple-element.80.v_ref, bf16[32,32,512]{2,1,0:T(8,128)(2,1)S(1)} %get-tuple-element.81.y_ref, ...), custom_call_target="tpu_custom_call", output_to_operand_aliasing={{0}: (9, {}), {1}: (10, {})} | custom-call | flops 2000000 | bytes 6000000 | tf_op jit(solution)/shard_map/last_level/pallas_call | solution.py:739
  80.5 0.0 collective-permute-done.13.two_ref
  80.5 1.0 %weight_sums.1 = (f32[7,32,32]{2,1,0:T(8,128)}, f32[7,32,32]{2,1,0:T(8,128)}, f32[7,32,32]{2,1,0:T(8,128)}) custom-call(bf16[7,32,128]{2,1,0:T(8,128)(2,1)S(1)} %add_convert_fusion.one_ref, bf16[7,32,128]{2,1,0:T(8,128)(2,1)S(1)} %collective-permute-done.13.two_ref), custom_call_target="tpu_custom_call" | custom-call | flops 1000000 | bytes 3000000 | tf_op jit(solution)/shard_map/weight_sums/pallas_call | solution.py:753
  (25 shorter events, 0.2 us)
Async XLA Ops:
  0.6 5.5 %copy-start.9 = (s32[128]{0:T(128)S(1)}, s32[128]{0:T(128)}, u32[]{:S(2)}) copy-start(s32[128]{0:T(128)} %counts.1) | copy-start | bytes 1540
  0.6 5.5 %copy-start.1 = (bf16[32,32,512]{2,1,0:T(8,128)(2,1)S(1)}, bf16[32,32,512]{2,1,0:T(8,128)(2,1)}, u32[]{:S(2)}) copy-start(bf16[32,32,512]{2,1,0:T(8,128)(2,1)} %z_ref.1) | copy-start | bytes 3145732
  0.7 5.5 %copy-start = (bf16[32,32,512]{2,1,0:T(8,128)(2,1)S(1)}, bf16[32,32,512]{2,1,0:T(8,128)(2,1)}, u32[]{:S(2)}) copy-start(bf16[32,32,512]{2,1,0:T(8,128)(2,1)} %x_ref.1) | copy-start | bytes 3145732
  0.7 5.5 %copy-start.5 = (bf16[7,32,32]{2,1,0:T(8,128)(2,1)S(1)}, bf16[7,32,32]{2,1,0:T(8,128)(2,1)}, u32[]{:S(2)}) copy-start(bf16[7,32,32]{2,1,0:T(8,128)(2,1)} %w_out.3) | copy-start | bytes 43012
  0.7 5.5 %copy-start.4 = (bf16[7,32,32]{2,1,0:T(8,128)(2,1)S(1)}, bf16[7,32,32]{2,1,0:T(8,128)(2,1)}, u32[]{:S(2)}) copy-start(bf16[7,32,32]{2,1,0:T(8,128)(2,1)} %w_in.3) | copy-start | bytes 43012
  0.7 5.5 %copy-start.10 = (s32[32]{0:T(128)S(1)}, s32[32]{0:T(128)}, u32[]{:S(2)}) copy-start(s32[32]{0:T(128)} %octant.1) | copy-start | bytes 388
  0.7 5.5 %copy-start.8 = (s32[32,6]{0,1:T(8,128)S(1)}, s32[32,6]{0,1:T(8,128)}, u32[]{:S(2)}) copy-start(s32[32,6]{0,1:T(8,128)} %param.18) | copy-start | bytes 2308
  0.7 5.5 %copy-start.7 = (s32[32,6]{0,1:T(8,128)S(1)}, s32[32,6]{0,1:T(8,128)}, u32[]{:S(2)}) copy-start(s32[32,6]{0,1:T(8,128)} %param.17) | copy-start | bytes 2308
  3.8 1.6 %collective-permute-start = (bf16[27,32,128]{2,1,0:T(8,128)(2,1)S(1)}, bf16[27,32,128]{2,1,0:T(8,128)(2,1)S(1)}, u32[]{:S(2)}, u32[]{:S(2)}) collective-permute-start(bf16[27,32,128]{2,1,0:T(8,128)(2,1)S(1)} %get-tuple-element.58), channel_id=1, source_target_pairs={{0,1},{2,3},{4,5},{6,7},{8,9},{10,11},{12,13},{14,15},{16,17},{18,... | collective-permute-start | bytes 663560 | tf_op jit(solution)/shard_map/ppermute | solution.py:573
  5.4 3.7 %collective-permute-start.1 = (bf16[35,32,128]{2,1,0:T(8,128)(2,1)S(1)}, bf16[35,32,128]{2,1,0:T(8,128)(2,1)S(1)}, u32[]{:S(2)}, u32[]{:S(2)}) collective-permute-start(bf16[35,32,128]{2,1,0:T(8,128)(2,1)S(1)} %pad_maximum_fusion), channel_id=1, source_target_pairs={{1,2},{3,4},{5,6},{7,8},{9,10},{11,12},{13,14},{15,16},{17,18},{19... | collective-permute-start | bytes 860168 | tf_op jit(solution)/shard_map/ppermute | solution.py:573
  6.2 8.2 %copy-start.2 = (bf16[2,512,128]{2,1,0:T(8,128)(2,1)S(1)}, bf16[2,512,128]{2,1,0:T(8,128)(2,1)}, u32[]{:S(2)}) copy-start(bf16[2,512,128]{2,1,0:T(8,128)(2,1)} %constant.4.clone.rest_ref) | copy-start | bytes 786436
  9.1 5.3 %collective-permute-start.2 = (bf16[8,32,128]{2,1,0:T(8,128)(2,1)S(1)}, bf16[8,32,128]{2,1,0:T(8,128)(2,1)S(1)}, u32[]{:S(2)}, u32[]{:S(2)}) collective-permute-start(bf16[8,32,128]{2,1,0:T(8,128)(2,1)S(1)} %slice.16), channel_id=1, source_target_pairs={{0,1},{2,3},{4,5},{6,7},{8,9},{10,11},{12,13},{14,15},{16,17},{18,... | collective-permute-start | bytes 196616 | tf_op jit(solution)/shard_map/ppermute | solution.py:573
  14.4 7.9 %copy-start.6 = (bf16[7,32,32]{2,1,0:T(8,128)(2,1)S(1)}, bf16[7,32,32]{2,1,0:T(8,128)(2,1)}, u32[]{:S(2)}) copy-start(bf16[7,32,32]{2,1,0:T(8,128)(2,1)} %w_co.1) | copy-start | bytes 43012
  21.0 5.3 %collective-permute-start.3 = (bf16[8,32,128]{2,1,0:T(8,128)(2,1)S(1)}, bf16[8,32,128]{2,1,0:T(8,128)(2,1)S(1)}, u32[]{:S(2)}, u32[]{:S(2)}) collective-permute-start(bf16[8,32,128]{2,1,0:T(8,128)(2,1)S(1)} %get-tuple-element.77), channel_id=1, source_target_pairs={{0,1},{2,3},{4,5},{6,7},{8,9},{10,11},{12,13},{14,15},{16,17},{18,... | collective-permute-start | bytes 196616 | tf_op jit(solution)/shard_map/ppermute | solution.py:573
  21.5 4.9 %collective-permute-start.4 = (bf16[8,32,128]{2,1,0:T(8,128)(2,1)S(1)}, bf16[8,32,128]{2,1,0:T(8,128)(2,1)S(1)}, u32[]{:S(2)}, u32[]{:S(2)}) collective-permute-start(bf16[8,32,128]{2,1,0:T(8,128)(2,1)S(1)} %get-tuple-element.78), channel_id=1, source_target_pairs={{1,2},{3,4},{5,6},{7,8},{9,10},{11,12},{13,14},{15,16},{17,18},{19... | collective-permute-start | bytes 196616 | tf_op jit(solution)/shard_map/ppermute | solution.py:573
  22.3 4.1 %copy-start.3 = (bf16[256,1024]{1,0:T(8,128)(2,1)S(1)}, bf16[256,1024]{1,0:T(8,128)(2,1)}, u32[]{:S(2)}) copy-start(bf16[256,1024]{1,0:T(8,128)(2,1)} %constant.5.clone.place_ref) | copy-start | bytes 1572868
  33.6 4.2 %collective-permute-start.5 = (bf16[34,32,128]{2,1,0:T(8,128)(2,1)S(1)}, bf16[34,32,128]{2,1,0:T(8,128)(2,1)S(1)}, u32[]{:S(2)}, u32[]{:S(2)}) collective-permute-start(bf16[34,32,128]{2,1,0:T(8,128)(2,1)S(1)} %get-tuple-element.83), channel_id=1, source_target_pairs={{0,1},{2,3},{4,5},{6,7},{8,9},{10,11},{12,13},{14,15},{16,17},{18,... | collective-permute-start | bytes 835592 | tf_op jit(solution)/shard_map/ppermute | solution.py:573
  37.8 4.3 %collective-permute-start.7 = (bf16[7,32,128]{2,1,0:T(8,128)(2,1)S(1)}, bf16[7,32,128]{2,1,0:T(8,128)(2,1)S(1)}, u32[]{:S(2)}, u32[]{:S(2)}) collective-permute-start(bf16[7,32,128]{2,1,0:T(8,128)(2,1)S(1)} %add_convert_fusion.5), channel_id=1, source_target_pairs={{0,2},{1,3},{2,0},{3,1},{4,6},{5,7},{6,4},{7,5},{8,10},{9,11},{10,... | collective-permute-start | bytes 172040 | tf_op jit(solution)/shard_map/ppermute | solution.py:591
  39.4 9.7 %collective-permute-start.6 = (bf16[35,32,128]{2,1,0:T(8,128)(2,1)S(1)}, bf16[35,32,128]{2,1,0:T(8,128)(2,1)S(1)}, u32[]{:S(2)}, u32[]{:S(2)}) collective-permute-start(bf16[35,32,128]{2,1,0:T(8,128)(2,1)S(1)} %pad_maximum_fusion.1), channel_id=1, source_target_pairs={{1,2},{3,4},{5,6},{7,8},{9,10},{11,12},{13,14},{15,16},{17,18},{19... | collective-permute-start | bytes 860168 | tf_op jit(solution)/shard_map/ppermute | solution.py:573
  42.1 7.9 %collective-permute-start.8 = (bf16[7,32,128]{2,1,0:T(8,128)(2,1)S(1)}, bf16[7,32,128]{2,1,0:T(8,128)(2,1)S(1)}, u32[]{:S(2)}, u32[]{:S(2)}) collective-permute-start(bf16[7,32,128]{2,1,0:T(8,128)(2,1)S(1)} %add_convert_fusion.4), channel_id=1, source_target_pairs={{0,6},{1,7},{2,4},{3,5},{4,2},{5,3},{6,0},{7,1},{8,14},{9,15},{10,... | collective-permute-start | bytes 172040 | tf_op jit(solution)/shard_map/ppermute | solution.py:591
  49.1 1.3 %collective-permute-start.9 = (bf16[8,32,128]{2,1,0:T(8,128)(2,1)S(1)}, bf16[8,32,128]{2,1,0:T(8,128)(2,1)S(1)}, u32[]{:S(2)}, u32[]{:S(2)}) collective-permute-start(bf16[8,32,128]{2,1,0:T(8,128)(2,1)S(1)} %slice.19), channel_id=1, source_target_pairs={{0,1},{2,3},{4,5},{6,7},{8,9},{10,11},{12,13},{14,15},{16,17},{18,... | collective-permute-start | bytes 196616 | tf_op jit(solution)/shard_map/ppermute | solution.py:573
  50.5 7.0 %collective-permute-start.10 = (bf16[7,32,128]{2,1,0:T(8,128)(2,1)S(1)}, bf16[7,32,128]{2,1,0:T(8,128)(2,1)S(1)}, u32[]{:S(2)}, u32[]{:S(2)}) collective-permute-start(bf16[7,32,128]{2,1,0:T(8,128)(2,1)S(1)} %add_convert_fusion.3), channel_id=1, source_target_pairs={{0,8},{1,9},{2,10},{3,11},{4,12},{5,13},{6,14},{7,15},{8,0},{9,1},... | collective-permute-start | bytes 172040 | tf_op jit(solution)/shard_map/ppermute | solution.py:591
  57.5 7.1 %collective-permute-start.11 = (bf16[7,32,128]{2,1,0:T(8,128)(2,1)S(1)}, bf16[7,32,128]{2,1,0:T(8,128)(2,1)S(1)}, u32[]{:S(2)}, u32[]{:S(2)}) collective-permute-start(bf16[7,32,128]{2,1,0:T(8,128)(2,1)S(1)} %add_convert_fusion.2), channel_id=1, source_target_pairs={{0,24},{1,25},{2,26},{3,27},{4,28},{5,29},{6,30},{7,31},{8,16},{9,... | collective-permute-start | bytes 172040 | tf_op jit(solution)/shard_map/ppermute | solution.py:591
  64.6 9.2 %collective-permute-start.12 = (bf16[7,32,128]{2,1,0:T(8,128)(2,1)S(1)}, bf16[7,32,128]{2,1,0:T(8,128)(2,1)S(1)}, u32[]{:S(2)}, u32[]{:S(2)}) collective-permute-start(bf16[7,32,128]{2,1,0:T(8,128)(2,1)S(1)} %add_convert_fusion.1), channel_id=1, source_target_pairs={{0,32},{1,33},{2,34},{3,35},{4,36},{5,37},{6,38},{7,39},{8,40},{9,... | collective-permute-start | bytes 172040 | tf_op jit(solution)/shard_map/ppermute | solution.py:591
  73.8 6.7 %collective-permute-start.13 = (bf16[7,32,128]{2,1,0:T(8,128)(2,1)S(1)}, bf16[7,32,128]{2,1,0:T(8,128)(2,1)S(1)}, u32[]{:S(2)}, u32[]{:S(2)}) collective-permute-start(bf16[7,32,128]{2,1,0:T(8,128)(2,1)S(1)} %add_convert_fusion.one_ref), channel_id=1, source_target_pairs={{0,96},{1,97},{2,98},{3,99},{4,100},{5,101},{6,102},{7,103},{8,104... | collective-permute-start | bytes 172040 | tf_op jit(solution)/shard_map/ppermute | solution.py:591

commit v8 on v7

--- a/solution.py
+++ b/solution.py
@@ -187,7 +187,7 @@
 def prepare_kernel(
     counts, octant, neighbour, level_tag,
     got_ref, x_ref, z_ref, sel_ref, w_in, w_out,
-    meta, index, xs, zs, mats, table,
+    meta, index, xs, zs, mats, table, coef,
 ):
     rank = lax.axis_index("patch")
     odd = rank % 2
@@ -237,6 +237,7 @@
     index[6:12] = level_tag[...]
 
     fill_mats(mats, ((w_in, True), (w_out, False)))
+    fill_coef(coef)
     for p in range(SLOTS):
         live = (p < count).astype(F32)
         xs[p] = (x_ref[p].astype(F32) * live).astype(BF)
@@ -263,12 +264,15 @@
     fill_table(v_ref, y_ref, sel_ref, table)
 
 
-def join_table(parts, coef, table):
+def join_table(parts, table):
     start = 0
     for part in parts:
         size = part.shape[0]
         table[start : start + size] = part[...]
         start += size
+
+
+def fill_coef(coef):
     for dim in range(3):
         low, high = on_face(2 * dim), on_face(2 * dim + 1)
         for t_low in range(2):
@@ -329,11 +333,11 @@
 
 
 def fine_kernel(
-    meta, index, xs, zs, t_ref, b_ref, c_ref, mats, sel_ref, rest_ref,
+    meta, index, xs, zs, t_ref, b_ref, c_ref, coef, mats, sel_ref, rest_ref,
     ta_ref, tb_ref, hidden_ref, slope_ref, gm_ref, par_ref, inner_ref, outer_ref,
-    table, coef, picked, par, ends,
+    table, picked, par, ends,
 ):
-    join_table((t_ref, b_ref, c_ref), coef, table)
+    join_table((t_ref, b_ref, c_ref), table)
     par[...] = jnp.zeros_like(par)
     ends[...] = jnp.zeros_like(ends)
 
@@ -516,10 +520,10 @@
 
 
 def first_final_kernel(
-    index, v_ref, y_ref, xs, zs, mats, sel_ref, t_ref, b_ref, c_ref,
-    table, coef, out_hbm, gs_hbm, *scratch,
+    index, v_ref, y_ref, xs, zs, mats, sel_ref, t_ref, b_ref, c_ref, coef,
+    table, out_hbm, gs_hbm, *scratch,
 ):
-    join_table((t_ref, b_ref, c_ref), coef, table)
+    join_table((t_ref, b_ref, c_ref), table)
     final_body(0, index, v_ref, y_ref, xs, zs, mats, sel_ref, table, coef, out_hbm, gs_hbm,
                *scratch)
 
@@ -629,12 +633,13 @@
     got_a = trade(inner, "inner")
     got_b = relay_out(outer, got_a)
 
-    meta, index, xs, zs, mats, table = pl.pallas_call(
+    meta, index, xs, zs, mats, table, coef = pl.pallas_call(
         prepare_kernel,
         in_specs=[SMEM()] * 2 + [VMEM()] * 8,
-        out_specs=[SMEM()] + [VMEM()] * 5,
+        out_specs=[SMEM()] + [VMEM()] * 6,
         out_shape=[shape_of((META,), jnp.int32), shape_of((12, SLOTS), jnp.int32)]
-        + [shape_of(field), shape_of(field), shape_of((2, C, 7 * C)), shape_of((BASE_B, C, 128))],
+        + [shape_of(field), shape_of(field), shape_of((2, C, 7 * C)), shape_of((BASE_B, C, 128))]
+        + [shape_of(coef_shape)],
         compiler_params=params(),
         cost_estimate=cost(4),
         name="prepare",
@@ -646,13 +651,12 @@
 
     taps_a, taps_b, hidden, slope, grad_merged, par, pin, pout = pl.pallas_call(
         fine_kernel,
-        in_specs=[SMEM()] * 2 + [VMEM()] * 8,
+        in_specs=[SMEM()] * 2 + [VMEM()] * 9,
         out_specs=[VMEM()] * 8,
         out_shape=[shape_of(stack), shape_of(stack), shape_of(field), shape_of(field)]
         + [shape_of(field), shape_of(par_rows), shape_of(far), shape_of(far)],
         scratch_shapes=[
             pltpu.VMEM(table_shape, BF),
-            pltpu.VMEM(coef_shape, BF),
             pltpu.VMEM((BIG, C, 256), BF),
             pltpu.VMEM((NPAR * 8 + 8, C, 128), BF),
             pltpu.VMEM((2, 16, C, 128), BF),
@@ -660,7 +664,7 @@
         compiler_params=params(),
         cost_estimate=cost(8),
         name="fine_level",
-    )(meta, index, xs, zs, table, got_b, got_c, mats, sel, rest)
+    )(meta, index, xs, zs, table, got_b, got_c, coef, mats, sel, rest)
     child_out = trade(pout, "outer")
     child_in = trade(pin, "inner")
 
@@ -723,18 +727,18 @@
     fixed = (index, merged, grad_pre, xs, zs, mats, sel)
     sums, got_c = lax.optimization_barrier((add(sums, swap(sums, 6)), got_c))
     partner = swap(sums, 8)
-    table, coef, output, grad_state = pl.pallas_call(
+    table, output, grad_state = pl.pallas_call(
         first_final_kernel,
-        in_specs=[SMEM()] + [VMEM()] * 9,
-        out_specs=[VMEM(), VMEM(), HBM(), HBM()],
-        out_shape=[shape_of(table_shape), shape_of(coef_shape), shape_of(field), shape_of(field)],
+        in_specs=[SMEM()] + [VMEM()] * 10,
+        out_specs=[VMEM(), HBM(), HBM()],
+        out_shape=[shape_of(table_shape), shape_of(field), shape_of(field)],
         scratch_shapes=last_scratch,
         compiler_params=params(),
         cost_estimate=cost(2),
         name="last_level",
-    )(*fixed, table, got_b, got_c)
+    )(*fixed, table, got_b, got_c, coef)
     for step, mask in ((1, 24), (2, 32), (3, 96)):
-        sums, coef, output = lax.optimization_barrier((add(sums, partner), coef, output))
+        sums, output = lax.optimization_barrier((add(sums, partner), output))
         partner = swap(sums, mask)
         output, grad_state = pl.pallas_call(
             functools.partial(next_final_kernel, step),

time: 81.6 us -> 81.7 us (level)
  no operation moved by 1% of the time
where the time goes in v8:
time: 81.7 us; the launch traced here: 81.5 us
  Pallas kernels  37.3 us (46%)
  starting transfers between devices  36.4 us (45%)
  waiting for transfers between devices  6.52 us (8%)
  between operations  1.03 us (1%)
    ppermute x6, starting transfers between devices, swap(): return lax.ppermute(block, 'patch', [(i, i ^ mask) for i in range(devices)])  26.1 us
    ppermute x8, starting transfers between devices, trade(): return lax.ppermute(block, 'patch', pairs(kind, lax.axis_size('patch')))  10.4 us
    pallas_call x3, Pallas kernels, on_device(): pl.pallas_call(functools.partial(next_final_kernel, step), in_specs=[SMEM...  7.89 us
    pallas_call x1, Pallas kernels, on_device(): pl.pallas_call(merge_kernel, in_specs=[SMEM()] + [VMEM()] * 13, out_specs...  7.14 us
    pallas_call x1, Pallas kernels, on_device(): pl.pallas_call(fine_kernel, in_specs=[SMEM()] * 2 + [VMEM()] * 9, out_spe...  6.7 us
    pallas_call x1, Pallas kernels, on_device(): pl.pallas_call(window_kernel, in_specs=[VMEM()] * 6, out_specs=[VMEM()] *...  4.03 us
    ppermute x8, waiting for transfers between devices, trade(): return lax.ppermute(block, 'patch', pairs(kind, lax.axis_size('patch')))  3.99 us
    pallas_call x1, Pallas kernels, on_device(): pl.pallas_call(layers_kernel, in_specs=[HBM()] * 3, out_specs=[VMEM()] *...  3.09 us
  transfers between devices with their start and end apart: 14, of which 6 were waited for; matrix products, arithmetic and copies ran while one was open for 0% of the time, Pallas kernels for 24%

profile of v8, /device:TPU:0, one launch (start us, length us, event | category | flops | bytes accessed | tf_op | source)
XLA Modules:
  0.0 81.5 jit_solution(1418397167497535118)
XLA Ops:
  0.7 3.1 %face_rows.1 = (bf16[27,32,128]{2,1,0:T(8,128)(2,1)S(1)}, bf16[27,32,128]{2,1,0:T(8,128)(2,1)S(1)}, bf16[6,512,256]{2,1,0:T(8,128)(2,1)S(1)}) custom-call(s32[128]{0:T(128)} %counts.1, bf16[32,32,512]{2,1,0:T(8,128)(2,1)} %x_ref.1, bf16[32,32,512]{2,1,0:T(8,128)(2,1)} %z_ref.1), custom_call_target="tpu_custom_call" | custom-call | flops 4000000 | bytes 12000000 | tf_op jit(solution)/shard_map/face_rows/pallas_call | solution.py:616
  3.8 0.1 collective-permute-start
  3.9 1.5 %collective-permute-done.got_ref = bf16[27,32,128]{2,1,0:T(8,128)(2,1)S(1)} collective-permute-done((bf16[27,32,128]{2,1,0:T(8,128)(2,1)S(1)}, bf16[27,32,128]{2,1,0:T(8,128)(2,1)S(1)}, u32[]{:S(2)}, u32[]{:S(2)}) %collective-permute-start) | collective-permute-done | bytes 221216 | tf_op jit(solution)/shard_map/ppermute | solution.py:577
  5.4 0.7 collective-permute-start.1
  6.1 0.0 copy-done.9
  6.1 0.0 copy-done.1
  6.1 0.0 copy-done
  6.1 0.0 copy-done.5
  6.1 0.0 copy-done.4
  6.1 0.0 copy-done.10
  6.2 0.0 copy-done.8
  6.2 0.0 copy-start.2
  6.2 2.9 %prepare.1 = (s32[128]{0:T(128)S(1)}, s32[12,32]{1,0:T(8,128)S(1)}, bf16[32,32,512]{2,1,0:T(8,128)(2,1)S(1)}, bf16[32,32,512]{2,1,0:T(8,128)(2,1)S(1)}, bf16[2,3...) custom-call(s32[128]{0:T(128)S(1)} %copy-done.9, ...), custom_call_target="tpu_custom_call" | custom-call | flops 4000000 | bytes 12000000 | tf_op jit(solution)/shard_map/prepare/pallas_call | solution.py:636
  9.1 0.0 collective-permute-done.1.b_ref
  9.2 4.3 %collective-permute-start.2 = (bf16[8,32,128]{2,1,0:T(8,128)(2,1)S(1)}, bf16[8,32,128]{2,1,0:T(8,128)(2,1)S(1)}, u32[]{:S(2)}, u32[]{:S(2)}) collective-permute-start(bf16[8,32,128]{2,1,0:T(8,128)(2,1)S(1)} %slice.16), channel_id=1, source_target_pairs={{0,1},{2,3},{4,5},{6,7},{8,9},{10,11},{12,13},{14,15},{16,17},{18,... | collective-permute-start | bytes 196616 | tf_op jit(solution)/shard_map/ppermute | solution.py:577
  13.5 0.9 %collective-permute-done.2.c_ref = bf16[8,32,128]{2,1,0:T(8,128)(2,1)S(1)} collective-permute-done((bf16[8,32,128]{2,1,0:T(8,128)(2,1)S(1)}, bf16[8,32,128]{2,1,0:T(8,128)(2,1)S(1)}, u32[]{:S(2)}, u32[]{:S(2)}) %collective-permute-start.2) | collective-permute-done | bytes 65568 | tf_op jit(solution)/shard_map/ppermute | solution.py:577
  14.4 6.7 %fine_level.1 = (bf16[32,224,512]{2,1,0:T(8,128)(2,1)S(1)}, bf16[32,224,512]{2,1,0:T(8,128)(2,1)S(1)}, bf16[32,32,512]{2,1,0:T(8,128)(2,1)S(1)}, bf16[32,32,512]...) custom-call(s32[128]{0:T(128)S(1)} %get-tuple-element.60.meta, ...), custom_call_target="tpu_custom_call" | custom-call | flops 8000000 | bytes 24000000 | tf_op jit(solution)/shard_map/fine_level/pallas_call | solution.py:652
  21.1 0.4 collective-permute-start.3
  21.5 0.8 %collective-permute-start.4 = (bf16[8,32,128]{2,1,0:T(8,128)(2,1)S(1)}, bf16[8,32,128]{2,1,0:T(8,128)(2,1)S(1)}, u32[]{:S(2)}, u32[]{:S(2)}) collective-permute-start(bf16[8,32,128]{2,1,0:T(8,128)(2,1)S(1)} %get-tuple-element.76), channel_id=1, source_target_pairs={{1,2},{3,4},{5,6},{7,8},{9,10},{11,12},{13,14},{15,16},{17,18},{19... | collective-permute-start | bytes 196616 | tf_op jit(solution)/shard_map/ppermute | solution.py:577
  22.4 0.0 copy-start.3
  22.4 4.0 %window.1 = (bf16[4,32,224]{2,1,0:T(8,128)(2,1)S(1)}, f32[224,32]{1,0:T(8,128)S(1)}, bf16[32,224,128]{2,1,0:T(8,128)(2,1)S(1)}) custom-call(bf16[32,32,512]{2,1,0:T(8,128)(2,1)S(1)} %get-tuple-element.68.hidden_ref, bf16[32,224,512]{2,1,0:T(8,128)(2,1)S(1)} %get-tuple-element.69.tb_ref, bf16[2,512,128]{2,1,0:T(8,128)(2,1)S(1)} %copy-done.2, ...), custom_call_target="tpu_custom_call" | custom-call | flops 3000000 | bytes 9000000 | tf_op jit(solution)/shard_map/window/pallas_call | solution.py:671
  26.4 0.0 collective-permute-done.3.pin_ref
  26.5 0.0 collective-permute-done.4.pout_ref
  26.5 7.1 %coarse_and_merge.1 = (bf16[32,32,512]{2,1,0:T(8,128)(2,1)S(1)}, bf16[32,32,512]{2,1,0:T(8,128)(2,1)S(1)}, bf16[7,32,128]{2,1,0:T(8,128)(2,1)S(1)}, bf16[34,32,1...) custom-call(s32[128]{0:T(128)S(1)} %get-tuple-element.60.meta, bf16[32,224,512]{2,1,0:T(8,128)(2,1)S(1)} %get-tuple-element.67.ta_ref, ...), custom_call_target="tpu_custom_call" | custom-call | flops 9000000 | bytes 27000000 | tf_op jit(solution)/shard_map/coarse_and_merge/pallas_call | solution.py:682
  33.6 3.0 %collective-permute-start.5 = (bf16[34,32,128]{2,1,0:T(8,128)(2,1)S(1)}, bf16[34,32,128]{2,1,0:T(8,128)(2,1)S(1)}, u32[]{:S(2)}, u32[]{:S(2)}) collective-permute-start(bf16[34,32,128]{2,1,0:T(8,128)(2,1)S(1)} %get-tuple-element.81), channel_id=1, source_target_pairs={{0,1},{2,3},{4,5},{6,7},{8,9},{10,11},{12,13},{14,15},{16,17},{18,... | collective-permute-start | bytes 835592 | tf_op jit(solution)/shard_map/ppermute | solution.py:577
  36.6 1.2 %collective-permute-done.5.got_ref = bf16[34,32,128]{2,1,0:T(8,128)(2,1)S(1)} collective-permute-done((bf16[34,32,128]{2,1,0:T(8,128)(2,1)S(1)}, bf16[34,32,128]{2,1,0:T(8,128)(2,1)S(1)}, u32[]{:S(2)}, u32[]{:S(2)}) %collective-permute-start.5) | collective-permute-done | bytes 278560 | tf_op jit(solution)/shard_map/ppermute | solution.py:577
  37.9 1.6 %collective-permute-start.7 = (bf16[7,32,128]{2,1,0:T(8,128)(2,1)S(1)}, bf16[7,32,128]{2,1,0:T(8,128)(2,1)S(1)}, u32[]{:S(2)}, u32[]{:S(2)}) collective-permute-start(bf16[7,32,128]{2,1,0:T(8,128)(2,1)S(1)} %add_convert_fusion.5), channel_id=1, source_target_pairs={{0,2},{1,3},{2,0},{3,1},{4,6},{5,7},{6,4},{7,5},{8,10},{9,11},{10,... | collective-permute-start | bytes 172040 | tf_op jit(solution)/shard_map/ppermute | solution.py:595
  39.5 0.7 collective-permute-start.6
  40.2 2.0 %collective-permute-done.7 = bf16[7,32,128]{2,1,0:T(8,128)(2,1)S(1)} collective-permute-done((bf16[7,32,128]{2,1,0:T(8,128)(2,1)S(1)}, bf16[7,32,128]{2,1,0:T(8,128)(2,1)S(1)}, u32[]{:S(2)}, u32[]{:S(2)}) %collective-permute-start.7) | collective-permute-done | bytes 57376 | tf_op jit(solution)/shard_map/ppermute | solution.py:595
  42.2 5.2 %collective-permute-start.8 = (bf16[7,32,128]{2,1,0:T(8,128)(2,1)S(1)}, bf16[7,32,128]{2,1,0:T(8,128)(2,1)S(1)}, u32[]{:S(2)}, u32[]{:S(2)}) collective-permute-start(bf16[7,32,128]{2,1,0:T(8,128)(2,1)S(1)} %add_convert_fusion.4), channel_id=1, source_target_pairs={{0,6},{1,7},{2,4},{3,5},{4,2},{5,3},{6,0},{7,1},{8,14},{9,15},{10,... | collective-permute-start | bytes 172040 | tf_op jit(solution)/shard_map/ppermute | solution.py:595
  47.4 1.8 %face_table.1.t_ref = bf16[219,32,128]{2,1,0:T(8,128)(2,1)S(1)} custom-call(bf16[32,32,512]{2,1,0:T(8,128)(2,1)S(1)} %get-tuple-element.78.v_ref, bf16[32,32,512]{2,1,0:T(8,128)(2,1)S(1)} %get-tuple-element.79.y_ref, bf16[6,512,256]{2,1,0:T(8,128)(2,1)S(1)} %get-tuple-element.56.sel_ref, bf16[34,32,128]{2,1,0:T(8,128)(2,1)S(1)} %collective-permute-done.5.got_ref), custom_call_target="tpu_custom_call" | custom-call | flops 2000000 | bytes 6000000 | tf_op jit(solution)/shard_map/face_table/pallas_call | solution.py:708
  49.2 0.0 collective-permute-done.6.b_ref
  49.2 0.3 collective-permute-start.9
  49.5 0.6 collective-permute-done.8
  50.1 0.4 collective-permute-done.9.c_ref
  50.5 4.3 %collective-permute-start.10 = (bf16[7,32,128]{2,1,0:T(8,128)(2,1)S(1)}, bf16[7,32,128]{2,1,0:T(8,128)(2,1)S(1)}, u32[]{:S(2)}, u32[]{:S(2)}) collective-permute-start(bf16[7,32,128]{2,1,0:T(8,128)(2,1)S(1)} %add_convert_fusion.3), channel_id=1, source_target_pairs={{0,8},{1,9},{2,10},{3,11},{4,12},{5,13},{6,14},{7,15},{8,0},{9,1},... | collective-permute-start | bytes 172040 | tf_op jit(solution)/shard_map/ppermute | solution.py:595
  54.8 2.8 %last_level.4 = (bf16[262,32,128]{2,1,0:T(8,128)(2,1)S(1)}, bf16[32,32,512]{2,1,0:T(8,128)(2,1)}, bf16[32,32,512]{2,1,0:T(8,128)(2,1)}) custom-call(s32[12,32]{1,0:T(8,128)S(1)} %get-tuple-element.57.index, bf16[32,32,512]{2,1,0:T(8,128)(2,1)S(1)} %get-tuple-element.78.v_ref, bf16[32,32,512]{2,1,0:T(8,128)(2,1)S(1)} %get-tuple-element.79.y_ref, ...), custom_call_target="tpu_custom_call" | custom-call | flops 2000000 | bytes 6000000 | tf_op jit(solution)/shard_map/last_level/pallas_call | solution.py:730
  57.6 0.0 collective-permute-done.10
  57.6 4.4 %collective-permute-start.11 = (bf16[7,32,128]{2,1,0:T(8,128)(2,1)S(1)}, bf16[7,32,128]{2,1,0:T(8,128)(2,1)S(1)}, u32[]{:S(2)}, u32[]{:S(2)}) collective-permute-start(bf16[7,32,128]{2,1,0:T(8,128)(2,1)S(1)} %add_convert_fusion.2), channel_id=1, source_target_pairs={{0,24},{1,25},{2,26},{3,27},{4,28},{5,29},{6,30},{7,31},{8,16},{9,... | collective-permute-start | bytes 172040 | tf_op jit(solution)/shard_map/ppermute | solution.py:595
  62.0 2.6 %last_level.5 = (bf16[32,32,512]{2,1,0:T(8,128)(2,1)}, bf16[32,32,512]{2,1,0:T(8,128)(2,1)}) custom-call(s32[12,32]{1,0:T(8,128)S(1)} %get-tuple-element.57.index, bf16[32,32,512]{2,1,0:T(8,128)(2,1)S(1)} %get-tuple-element.78.v_ref, bf16[32,32,512]{2,1,0:T(8,128)(2,1)S(1)} %get-tuple-element.79.y_ref, ...), custom_call_target="tpu_custom_call", output_to_operand_aliasing={{0}: (9, {}), {1}: (10, {})} | custom-call | flops 2000000 | bytes 6000000 | tf_op jit(solution)/shard_map/last_level/pallas_call | solution.py:743
  64.7 0.0 collective-permute-done.11
  64.7 6.5 %collective-permute-start.12 = (bf16[7,32,128]{2,1,0:T(8,128)(2,1)S(1)}, bf16[7,32,128]{2,1,0:T(8,128)(2,1)S(1)}, u32[]{:S(2)}, u32[]{:S(2)}) collective-permute-start(bf16[7,32,128]{2,1,0:T(8,128)(2,1)S(1)} %add_convert_fusion.1), channel_id=1, source_target_pairs={{0,32},{1,33},{2,34},{3,35},{4,36},{5,37},{6,38},{7,39},{8,40},{9,... | collective-permute-start | bytes 172040 | tf_op jit(solution)/shard_map/ppermute | solution.py:595
  71.2 2.6 %last_level.6 = (bf16[32,32,512]{2,1,0:T(8,128)(2,1)}, bf16[32,32,512]{2,1,0:T(8,128)(2,1)}) custom-call(s32[12,32]{1,0:T(8,128)S(1)} %get-tuple-element.57.index, bf16[32,32,512]{2,1,0:T(8,128)(2,1)S(1)} %get-tuple-element.78.v_ref, bf16[32,32,512]{2,1,0:T(8,128)(2,1)S(1)} %get-tuple-element.79.y_ref, ...), custom_call_target="tpu_custom_call", output_to_operand_aliasing={{0}: (9, {}), {1}: (10, {})} | custom-call | flops 2000000 | bytes 6000000 | tf_op jit(solution)/shard_map/last_level/pallas_call | solution.py:743
  73.9 0.0 collective-permute-done.12
  73.9 4.0 %collective-permute-start.13 = (bf16[7,32,128]{2,1,0:T(8,128)(2,1)S(1)}, bf16[7,32,128]{2,1,0:T(8,128)(2,1)S(1)}, u32[]{:S(2)}, u32[]{:S(2)}) collective-permute-start(bf16[7,32,128]{2,1,0:T(8,128)(2,1)S(1)} %add_convert_fusion.one_ref), channel_id=1, source_target_pairs={{0,96},{1,97},{2,98},{3,99},{4,100},{5,101},{6,102},{7,103},{8,104... | collective-permute-start | bytes 172040 | tf_op jit(solution)/shard_map/ppermute | solution.py:595
  77.9 2.6 %last_level.7 = (bf16[32,32,512]{2,1,0:T(8,128)(2,1)}, bf16[32,32,512]{2,1,0:T(8,128)(2,1)}) custom-call(s32[12,32]{1,0:T(8,128)S(1)} %get-tuple-element.57.index, bf16[32,32,512]{2,1,0:T(8,128)(2,1)S(1)} %get-tuple-element.78.v_ref, bf16[32,32,512]{2,1,0:T(8,128)(2,1)S(1)} %get-tuple-element.79.y_ref, ...), custom_call_target="tpu_custom_call", output_to_operand_aliasing={{0}: (9, {}), {1}: (10, {})} | custom-call | flops 2000000 | bytes 6000000 | tf_op jit(solution)/shard_map/last_level/pallas_call | solution.py:743
  80.6 0.0 collective-permute-done.13.two_ref
  80.6 1.0 %weight_sums.1 = (f32[7,32,32]{2,1,0:T(8,128)}, f32[7,32,32]{2,1,0:T(8,128)}, f32[7,32,32]{2,1,0:T(8,128)}) custom-call(bf16[7,32,128]{2,1,0:T(8,128)(2,1)S(1)} %add_convert_fusion.one_ref, bf16[7,32,128]{2,1,0:T(8,128)(2,1)S(1)} %collective-permute-done.13.two_ref), custom_call_target="tpu_custom_call" | custom-call | flops 1000000 | bytes 3000000 | tf_op jit(solution)/shard_map/weight_sums/pallas_call | solution.py:757
  (25 shorter events, 0.2 us)
Async XLA Ops:
  0.6 5.5 %copy-start.9 = (s32[128]{0:T(128)S(1)}, s32[128]{0:T(128)}, u32[]{:S(2)}) copy-start(s32[128]{0:T(128)} %counts.1) | copy-start | bytes 1540
  0.6 5.5 %copy-start.1 = (bf16[32,32,512]{2,1,0:T(8,128)(2,1)S(1)}, bf16[32,32,512]{2,1,0:T(8,128)(2,1)}, u32[]{:S(2)}) copy-start(bf16[32,32,512]{2,1,0:T(8,128)(2,1)} %z_ref.1) | copy-start | bytes 3145732
  0.7 5.5 %copy-start = (bf16[32,32,512]{2,1,0:T(8,128)(2,1)S(1)}, bf16[32,32,512]{2,1,0:T(8,128)(2,1)}, u32[]{:S(2)}) copy-start(bf16[32,32,512]{2,1,0:T(8,128)(2,1)} %x_ref.1) | copy-start | bytes 3145732
  0.7 5.5 %copy-start.5 = (bf16[7,32,32]{2,1,0:T(8,128)(2,1)S(1)}, bf16[7,32,32]{2,1,0:T(8,128)(2,1)}, u32[]{:S(2)}) copy-start(bf16[7,32,32]{2,1,0:T(8,128)(2,1)} %w_out.3) | copy-start | bytes 43012
  0.7 5.5 %copy-start.4 = (bf16[7,32,32]{2,1,0:T(8,128)(2,1)S(1)}, bf16[7,32,32]{2,1,0:T(8,128)(2,1)}, u32[]{:S(2)}) copy-start(bf16[7,32,32]{2,1,0:T(8,128)(2,1)} %w_in.3) | copy-start | bytes 43012
  0.7 5.5 %copy-start.10 = (s32[32]{0:T(128)S(1)}, s32[32]{0:T(128)}, u32[]{:S(2)}) copy-start(s32[32]{0:T(128)} %octant.1) | copy-start | bytes 388
  0.7 5.5 %copy-start.8 = (s32[32,6]{0,1:T(8,128)S(1)}, s32[32,6]{0,1:T(8,128)}, u32[]{:S(2)}) copy-start(s32[32,6]{0,1:T(8,128)} %param.18) | copy-start | bytes 2308
  0.7 5.5 %copy-start.7 = (s32[32,6]{0,1:T(8,128)S(1)}, s32[32,6]{0,1:T(8,128)}, u32[]{:S(2)}) copy-start(s32[32,6]{0,1:T(8,128)} %param.17) | copy-start | bytes 2308
  3.8 1.6 %collective-permute-start = (bf16[27,32,128]{2,1,0:T(8,128)(2,1)S(1)}, bf16[27,32,128]{2,1,0:T(8,128)(2,1)S(1)}, u32[]{:S(2)}, u32[]{:S(2)}) collective-permute-start(bf16[27,32,128]{2,1,0:T(8,128)(2,1)S(1)} %get-tuple-element.55), channel_id=1, source_target_pairs={{0,1},{2,3},{4,5},{6,7},{8,9},{10,11},{12,13},{14,15},{16,17},{18,... | collective-permute-start | bytes 663560 | tf_op jit(solution)/shard_map/ppermute | solution.py:577
  5.4 3.7 %collective-permute-start.1 = (bf16[35,32,128]{2,1,0:T(8,128)(2,1)S(1)}, bf16[35,32,128]{2,1,0:T(8,128)(2,1)S(1)}, u32[]{:S(2)}, u32[]{:S(2)}) collective-permute-start(bf16[35,32,128]{2,1,0:T(8,128)(2,1)S(1)} %pad_maximum_fusion), channel_id=1, source_target_pairs={{1,2},{3,4},{5,6},{7,8},{9,10},{11,12},{13,14},{15,16},{17,18},{19... | collective-permute-start | bytes 860168 | tf_op jit(solution)/shard_map/ppermute | solution.py:577
  6.2 8.2 %copy-start.2 = (bf16[2,512,128]{2,1,0:T(8,128)(2,1)S(1)}, bf16[2,512,128]{2,1,0:T(8,128)(2,1)}, u32[]{:S(2)}) copy-start(bf16[2,512,128]{2,1,0:T(8,128)(2,1)} %constant.4.clone.rest_ref) | copy-start | bytes 786436
  9.2 5.3 %collective-permute-start.2 = (bf16[8,32,128]{2,1,0:T(8,128)(2,1)S(1)}, bf16[8,32,128]{2,1,0:T(8,128)(2,1)S(1)}, u32[]{:S(2)}, u32[]{:S(2)}) collective-permute-start(bf16[8,32,128]{2,1,0:T(8,128)(2,1)S(1)} %slice.16), channel_id=1, source_target_pairs={{0,1},{2,3},{4,5},{6,7},{8,9},{10,11},{12,13},{14,15},{16,17},{18,... | collective-permute-start | bytes 196616 | tf_op jit(solution)/shard_map/ppermute | solution.py:577
  14.4 8.0 %copy-start.6 = (bf16[7,32,32]{2,1,0:T(8,128)(2,1)S(1)}, bf16[7,32,32]{2,1,0:T(8,128)(2,1)}, u32[]{:S(2)}) copy-start(bf16[7,32,32]{2,1,0:T(8,128)(2,1)} %w_co.1) | copy-start | bytes 43012
  21.1 5.3 %collective-permute-start.3 = (bf16[8,32,128]{2,1,0:T(8,128)(2,1)S(1)}, bf16[8,32,128]{2,1,0:T(8,128)(2,1)S(1)}, u32[]{:S(2)}, u32[]{:S(2)}) collective-permute-start(bf16[8,32,128]{2,1,0:T(8,128)(2,1)S(1)} %get-tuple-element.75), channel_id=1, source_target_pairs={{0,1},{2,3},{4,5},{6,7},{8,9},{10,11},{12,13},{14,15},{16,17},{18,... | collective-permute-start | bytes 196616 | tf_op jit(solution)/shard_map/ppermute | solution.py:577
  21.5 4.9 %collective-permute-start.4 = (bf16[8,32,128]{2,1,0:T(8,128)(2,1)S(1)}, bf16[8,32,128]{2,1,0:T(8,128)(2,1)S(1)}, u32[]{:S(2)}, u32[]{:S(2)}) collective-permute-start(bf16[8,32,128]{2,1,0:T(8,128)(2,1)S(1)} %get-tuple-element.76), channel_id=1, source_target_pairs={{1,2},{3,4},{5,6},{7,8},{9,10},{11,12},{13,14},{15,16},{17,18},{19... | collective-permute-start | bytes 196616 | tf_op jit(solution)/shard_map/ppermute | solution.py:577
  22.4 4.1 %copy-start.3 = (bf16[256,1024]{1,0:T(8,128)(2,1)S(1)}, bf16[256,1024]{1,0:T(8,128)(2,1)}, u32[]{:S(2)}) copy-start(bf16[256,1024]{1,0:T(8,128)(2,1)} %constant.5.clone.place_ref) | copy-start | bytes 1572868
  33.6 4.2 %collective-permute-start.5 = (bf16[34,32,128]{2,1,0:T(8,128)(2,1)S(1)}, bf16[34,32,128]{2,1,0:T(8,128)(2,1)S(1)}, u32[]{:S(2)}, u32[]{:S(2)}) collective-permute-start(bf16[34,32,128]{2,1,0:T(8,128)(2,1)S(1)} %get-tuple-element.81), channel_id=1, source_target_pairs={{0,1},{2,3},{4,5},{6,7},{8,9},{10,11},{12,13},{14,15},{16,17},{18,... | collective-permute-start | bytes 835592 | tf_op jit(solution)/shard_map/ppermute | solution.py:577
  37.9 4.3 %collective-permute-start.7 = (bf16[7,32,128]{2,1,0:T(8,128)(2,1)S(1)}, bf16[7,32,128]{2,1,0:T(8,128)(2,1)S(1)}, u32[]{:S(2)}, u32[]{:S(2)}) collective-permute-start(bf16[7,32,128]{2,1,0:T(8,128)(2,1)S(1)} %add_convert_fusion.5), channel_id=1, source_target_pairs={{0,2},{1,3},{2,0},{3,1},{4,6},{5,7},{6,4},{7,5},{8,10},{9,11},{10,... | collective-permute-start | bytes 172040 | tf_op jit(solution)/shard_map/ppermute | solution.py:595
  39.5 9.7 %collective-permute-start.6 = (bf16[35,32,128]{2,1,0:T(8,128)(2,1)S(1)}, bf16[35,32,128]{2,1,0:T(8,128)(2,1)S(1)}, u32[]{:S(2)}, u32[]{:S(2)}) collective-permute-start(bf16[35,32,128]{2,1,0:T(8,128)(2,1)S(1)} %pad_maximum_fusion.1), channel_id=1, source_target_pairs={{1,2},{3,4},{5,6},{7,8},{9,10},{11,12},{13,14},{15,16},{17,18},{19... | collective-permute-start | bytes 860168 | tf_op jit(solution)/shard_map/ppermute | solution.py:577
  42.2 7.9 %collective-permute-start.8 = (bf16[7,32,128]{2,1,0:T(8,128)(2,1)S(1)}, bf16[7,32,128]{2,1,0:T(8,128)(2,1)S(1)}, u32[]{:S(2)}, u32[]{:S(2)}) collective-permute-start(bf16[7,32,128]{2,1,0:T(8,128)(2,1)S(1)} %add_convert_fusion.4), channel_id=1, source_target_pairs={{0,6},{1,7},{2,4},{3,5},{4,2},{5,3},{6,0},{7,1},{8,14},{9,15},{10,... | collective-permute-start | bytes 172040 | tf_op jit(solution)/shard_map/ppermute | solution.py:595
  49.2 1.3 %collective-permute-start.9 = (bf16[8,32,128]{2,1,0:T(8,128)(2,1)S(1)}, bf16[8,32,128]{2,1,0:T(8,128)(2,1)S(1)}, u32[]{:S(2)}, u32[]{:S(2)}) collective-permute-start(bf16[8,32,128]{2,1,0:T(8,128)(2,1)S(1)} %slice.19), channel_id=1, source_target_pairs={{0,1},{2,3},{4,5},{6,7},{8,9},{10,11},{12,13},{14,15},{16,17},{18,... | collective-permute-start | bytes 196616 | tf_op jit(solution)/shard_map/ppermute | solution.py:577
  50.5 7.0 %collective-permute-start.10 = (bf16[7,32,128]{2,1,0:T(8,128)(2,1)S(1)}, bf16[7,32,128]{2,1,0:T(8,128)(2,1)S(1)}, u32[]{:S(2)}, u32[]{:S(2)}) collective-permute-start(bf16[7,32,128]{2,1,0:T(8,128)(2,1)S(1)} %add_convert_fusion.3), channel_id=1, source_target_pairs={{0,8},{1,9},{2,10},{3,11},{4,12},{5,13},{6,14},{7,15},{8,0},{9,1},... | collective-permute-start | bytes 172040 | tf_op jit(solution)/shard_map/ppermute | solution.py:595
  57.6 7.1 %collective-permute-start.11 = (bf16[7,32,128]{2,1,0:T(8,128)(2,1)S(1)}, bf16[7,32,128]{2,1,0:T(8,128)(2,1)S(1)}, u32[]{:S(2)}, u32[]{:S(2)}) collective-permute-start(bf16[7,32,128]{2,1,0:T(8,128)(2,1)S(1)} %add_convert_fusion.2), channel_id=1, source_target_pairs={{0,24},{1,25},{2,26},{3,27},{4,28},{5,29},{6,30},{7,31},{8,16},{9,... | collective-permute-start | bytes 172040 | tf_op jit(solution)/shard_map/ppermute | solution.py:595
  64.7 9.2 %collective-permute-start.12 = (bf16[7,32,128]{2,1,0:T(8,128)(2,1)S(1)}, bf16[7,32,128]{2,1,0:T(8,128)(2,1)S(1)}, u32[]{:S(2)}, u32[]{:S(2)}) collective-permute-start(bf16[7,32,128]{2,1,0:T(8,128)(2,1)S(1)} %add_convert_fusion.1), channel_id=1, source_target_pairs={{0,32},{1,33},{2,34},{3,35},{4,36},{5,37},{6,38},{7,39},{8,40},{9,... | collective-permute-start | bytes 172040 | tf_op jit(solution)/shard_map/ppermute | solution.py:595
  73.9 6.7 %collective-permute-start.13 = (bf16[7,32,128]{2,1,0:T(8,128)(2,1)S(1)}, bf16[7,32,128]{2,1,0:T(8,128)(2,1)S(1)}, u32[]{:S(2)}, u32[]{:S(2)}) collective-permute-start(bf16[7,32,128]{2,1,0:T(8,128)(2,1)S(1)} %add_convert_fusion.one_ref), channel_id=1, source_target_pairs={{0,96},{1,97},{2,98},{3,99},{4,100},{5,101},{6,102},{7,103},{8,104... | collective-permute-start | bytes 172040 | tf_op jit(solution)/shard_map/ppermute | solution.py:595
